TPU v7x, 512 devices: a whole 4x8x8 slice. The times are simulated.
512 devices in a mesh: tok: 64 (over z, y), tp: 8 (over x, core).
Axes of the slice: x: 4, y: 8, z: 8, core: 2. Of those that a mesh axis runs over, the one named last changes fastest.
Arguments:
- activations: bfloat16 [8192, 4096], P('tok', 'tp'), may hold values from -6 to 6
- out_grad: bfloat16 [8192, 4096], P('tok', 'tp'), may hold values from -6 to 6
- routes: int32 [8192, 2], P('tok'), may hold values from 0 to 63, all different within a row; in each aligned block of 128 rows (0 to 127, 128 to 255, ...) at most 8 rows name the same one
- gate_vals: float32 [8192, 2], P('tok'), may hold values from 0.2 to 1
- w_gate: bfloat16 [64, 1536, 4096], P('tok', 'tp'), may hold values from -0.09375 to 0.09375
- w_up: bfloat16 [64, 1536, 4096], P('tok', 'tp'), may hold values from -0.09375 to 0.09375
- w_down: bfloat16 [64, 1536, 4096], P('tok', 'tp'), may hold values from -0.15625 to 0.15625
Outputs:
- in_grad: bfloat16 [8192, 4096], P('tok', 'tp')
Inputs may be any that keep to these rules, and one draw needn't show every extreme that they name: `routes`: each row names 2 different experts. In each aligned block of 128 rows (the tokens of one index of tok) no expert is named by more than 8 rows, a bound that some block reaches.
All inputs are finite; a program needn't handle non-finite values.
Results may differ from a plain program's by a relative error of at most 0.0057.
Values may be sent and summed in bfloat16 or wider, within the bound.
No kernel may reach another device: no remote copies, remote signals or barrier semaphores. Data moves between devices by JAX's collectives and lax.ppermute only.
A program may use at most 64 MiB of HBM per device.

v0:
```python
import jax
import jax.numpy as jnp
from jax import lax
from jax.sharding import PartitionSpec as P


def routing(routes, n_tok, capacity):
    tok_dev = routes.shape[0]
    top_k = routes.shape[1]
    flat = routes.reshape(-1)
    onehot = (flat[:, None] == jnp.arange(n_tok, dtype=jnp.int32)[None, :]).astype(jnp.int32)
    before = jnp.cumsum(onehot, axis=0) - onehot
    slot = jnp.sum(before * onehot, axis=1)
    position = flat * capacity + slot
    slot_count = n_tok * capacity
    hits = (position[:, None] == jnp.arange(slot_count, dtype=jnp.int32)[None, :]).astype(jnp.int32)
    hits = jnp.sum(hits.reshape(tok_dev, top_k, slot_count), axis=1)
    token_of = jnp.sum(hits * jnp.arange(tok_dev, dtype=jnp.int32)[:, None], axis=0)
    filled = jnp.sum(hits, axis=0) > 0
    return (position, token_of, filled)


def bucket(rows, token_of, filled):
    return jnp.where(filled[:, None], jnp.take(rows, token_of, axis=0), jnp.zeros((), rows.dtype))


def combine(returned, position, gate_vals):
    picked = jnp.take(returned, position, axis=0).reshape(
        gate_vals.shape[0], gate_vals.shape[1], returned.shape[1]
    )
    total = jnp.zeros((picked.shape[0], picked.shape[2]), jnp.float32)
    for column in range(gate_vals.shape[1]):
        total = total + gate_vals[:, column : column + 1] * picked[:, column].astype(jnp.float32)
    return total


def hidden_grads(gate_pre, up_pre, hidden_grad):
    sigma = jax.nn.sigmoid(gate_pre)
    silu_value = gate_pre * sigma
    slope = sigma * (1.0 + gate_pre * (1.0 - sigma))
    return (
        (hidden_grad * up_pre * slope).astype(jnp.bfloat16),
        (hidden_grad * silu_value).astype(jnp.bfloat16),
    )


def shards(activations, out_grad, routes, gate_vals, w_gate, w_up, w_down):
    n_tok = lax.axis_size("tok")
    tok_dev = routes.shape[0]
    top_k = routes.shape[1]
    capacity = max(2, 2 * tok_dev * top_k // n_tok)
    slot_count = n_tok * capacity
    gate_local = w_gate[0]
    up_local = w_up[0]
    down_local = w_down[0]
    contract_last = (((1,), (1,)), ((), ()))
    position, token_of, filled = routing(routes, n_tok, capacity)
    whole_x, whole_g = (
        lax.all_gather(activations, "tp", axis=1, tiled=True),
        lax.all_gather(out_grad, "tp", axis=1, tiled=True),
    )
    width = whole_x.shape[1]
    send_x = bucket(whole_x, token_of, filled).reshape(n_tok, capacity, width)
    send_g = bucket(whole_g, token_of, filled).reshape(n_tok, capacity, width)
    recv_x, recv_g = (
        lax.all_to_all(send_x, "tok", split_axis=0, concat_axis=0, tiled=True),
        lax.all_to_all(send_g, "tok", split_axis=0, concat_axis=0, tiled=True),
    )
    recv_x = recv_x.reshape(slot_count, width)
    recv_g = recv_g.reshape(slot_count, width)
    gate_pre = lax.dot_general(
        recv_x, gate_local, contract_last, preferred_element_type=jnp.float32
    )
    up_pre = lax.dot_general(recv_x, up_local, contract_last, preferred_element_type=jnp.float32)
    hidden_grad = lax.dot_general(
        recv_g, down_local, contract_last, preferred_element_type=jnp.float32
    )
    gate_grad, up_grad = hidden_grads(gate_pre, up_pre, hidden_grad)
    partial_value = jnp.dot(gate_grad, gate_local, preferred_element_type=jnp.float32)
    partial_value = partial_value + jnp.dot(up_grad, up_local, preferred_element_type=jnp.float32)
    partial_bf = partial_value.astype(jnp.bfloat16)
    full_width = partial_bf.shape[1]
    returned = lax.all_to_all(
        partial_bf.reshape(n_tok, capacity, full_width),
        "tok",
        split_axis=0,
        concat_axis=0,
        tiled=True,
    )
    combined = combine(returned.reshape(slot_count, full_width), position, gate_vals)
    summed = lax.psum_scatter(combined, "tp", scatter_dimension=1, tiled=True)
    return summed.astype(jnp.bfloat16)


def solution(mesh):
    placed = (
        P("tok", "tp"),
        P("tok", "tp"),
        P("tok", None),
        P("tok", None),
        P("tok", "tp", None),
        P("tok", "tp", None),
        P("tok", "tp", None),
    )
    return jax.shard_map(
        shards, mesh=mesh, in_specs=placed, out_specs=P("tok", "tp"), check_vma=False
    )
```

profile of v0, /device:TPU:6, one launch (start us, length us, event | category | flops | bytes accessed | tf_op | source)
XLA Modules:
  0.0 563.0 jit_solution(14401200045992333486)
XLA Ops:
  6.5 0.0 copy-start
  6.5 0.0 all-gather.3.cloned.1.call-start
  6.5 0.7 all-gather.3.cloned.1.call-update
  7.3 0.0 all-gather.5.cloned.1.call-start
  7.3 0.7 all-gather.5.cloned.1.call-update
  8.0 0.8 copy.23
  8.8 0.1 eq.40
  8.9 0.1 reshape.106
  9.1 0.6 reduce-window.6
  9.7 0.2 slice_reduce_fusion
  9.9 0.1 fusion.43
  10.0 0.1 reduce_sum.41
  10.2 0.1 copy.26
  10.3 0.7 compare_and_fusion.1
  11.0 0.1 convert_reduce_fusion.1
  11.2 30.4 %all-gather.3.cloned.1.call-done = bf16[128,4096]{1,0:T(8,128)(2,1)} async-done(((bf16[128,512]{1,0:T(8,128)(2,1)}), bf16[128,4096]{1,0:T(8,128)(2,1)}) %all-gather.3.cloned.1.call-update) | async-done | bytes 1048592 | tf_op jit(solution)/shard_map/all_gather | solution.py:60
  41.6 9.9 %gather_fusion.1 = bf16[512,4096]{1,0:T(8,128)(2,1)} fusion(bf16[128,4096]{1,0:T(8,128)(2,1)} %all-gather.3.cloned.1.call-done, s32[1024]{0:T(1024)S(1)} %pad_clamp_fusion.1), kind=kCustom, calls=%fused_computation.clone | custom fusion | bytes 8390656 | tf_op jit(solution)/shard_map/jit(_take)/gather | solution.py:24
  51.5 20.9 %all-gather.5.cloned.1.call-done = bf16[128,4096]{1,0:T(8,128)(2,1)} async-done(((bf16[128,512]{1,0:T(8,128)(2,1)}), bf16[128,4096]{1,0:T(8,128)(2,1)}) %all-gather.5.cloned.1.call-update) | async-done | bytes 1048592 | tf_op jit(solution)/shard_map/all_gather | solution.py:59
  72.3 9.9 %gather_fusion.2 = bf16[512,4096]{1,0:T(8,128)(2,1)} fusion(bf16[128,4096]{1,0:T(8,128)(2,1)} %all-gather.5.cloned.1.call-done, s32[1024]{0:T(1024)S(1)} %pad_clamp_fusion.1), kind=kCustom, calls=%fused_computation.1.clone | custom fusion | bytes 8390656 | tf_op jit(solution)/shard_map/jit(_take)/gather | solution.py:24
  82.3 5.4 fusion.7
  87.6 111.0 %all_to_all.15 = bf16[64,8,4096]{2,1,0:T(8,128)(2,1)} all-to-all(bf16[64,8,4096]{2,1,0:T(8,128)(2,1)S(1)} %get-tuple-element.12), channel_id=1, replica_groups=mesh['tok'=64,'tp'=8] {'tok'}, dimensions={0} | all-to-all | bytes 8388608 | tf_op jit(solution)/shard_map/all_to_all | solution.py:66
  198.6 0.0 copy-start.1
  198.6 14.4 %all-to-all-start = ((bf16[64,8,4096]{2,1,0:T(8,128)(2,1)}), bf16[64,8,4096]{2,1,0:T(8,128)(2,1)}, u32[]{:S(2)}, u32[]{:S(2)}) async-start(bf16[64,8,4096]{2,1,0:T(8,128)(2,1)} %get-tuple-element.13), calls=%async_computation | async-start | bytes 8388608 | tf_op jit(solution)/shard_map/all_to_all | solution.py:67
  213.0 0.0 copy-done.1
  213.0 3.7 fusion.1
  216.8 105.2 %all-to-all-done = bf16[64,8,4096]{2,1,0:T(8,128)(2,1)} async-done(((bf16[64,8,4096]{2,1,0:T(8,128)(2,1)}), bf16[64,8,4096]{2,1,0:T(8,128)(2,1)}, u32[]{:S(2)}, u32[]{:S(2)}) %all-to-all-start) | async-done | bytes 4194336 | tf_op jit(solution)/shard_map/all_to_all | solution.py:67
  321.9 5.0 fusion.5
  326.9 0.0 copy-done
  326.9 8.3 %fusion.10 = f32[512,4096]{1,0:T(8,128)} fusion(bf16[1,192,4096]{2,1,0:T(8,128)(2,1)S(1)} %copy-done.1, f32[512,192]{0,1:T(8,128)} %fusion.5, bf16[1,192,4096]{2,1,0:T(8,128)(2,1)S(1)} %copy-done, bf16[64,8,4096]{2,1,0:T(8,128)(2,1)} %all_to_all.15, f32[512,192]{0,1:T(8,128)S(1)} %fusion.1), kind=kOutput, calls=%fused_computation.19 | convolution fusion | flops 1611595776 | bytes 16515072 | tf_op jit(solution)/shard_map/dot_general | solution.py:79
  335.2 6.8 %fusion = bf16[64,8,4096]{2,1,0:T(8,128)(2,1)} fusion(f32[512,4096]{1,0:T(8,128)} %fusion.10, bf16[1,192,4096]{2,1,0:T(8,128)(2,1)S(1)} %copy-done, f32[512,192]{0,1:T(8,128)} %fusion.5, f32[512,192]{0,1:T(8,128)S(1)} %fusion.1), kind=kOutput, calls=%fused_computation.4 | convolution fusion | flops 810090496 | bytes 14942208 | tf_op jit(solution)/shard_map/dot_general | solution.py:80
  342.0 0.0 copy-start.2
  342.0 0.0 copy-start.3
  342.0 26.5 %all-to-all-start.2 = ((bf16[64,8,4096]{2,1,0:T(8,128)(2,1)}), bf16[64,8,4096]{2,1,0:T(8,128)(2,1)}, u32[]{:S(2)}, u32[]{:S(2)}) async-start(bf16[64,8,4096]{2,1,0:T(8,128)(2,1)} %fusion), calls=%async_computation.2 | async-start | bytes 8388608 | tf_op jit(solution)/shard_map/all_to_all | solution.py:83
  368.6 0.3 reduce-scatter.2.cloned.1.call-start
  368.8 0.0 copy-done.2
  368.8 0.1 copy.27
  369.0 0.1 mul.84
  369.1 0.0 copy-done.3
  369.1 102.4 %all-to-all-done.2 = bf16[64,8,4096]{2,1,0:T(8,128)(2,1)} async-done(((bf16[64,8,4096]{2,1,0:T(8,128)(2,1)}), bf16[64,8,4096]{2,1,0:T(8,128)(2,1)}, u32[]{:S(2)}, u32[]{:S(2)}) %all-to-all-start.2) | async-done | bytes 4194336 | tf_op jit(solution)/shard_map/all_to_all | solution.py:83
  471.5 7.9 %gather_fusion = bf16[256,4096]{1,0:T(8,128)(2,1)} fusion(bf16[512,4096]{1,0:T(8,128)(2,1)} %bitcast.10, s32[1024]{0:T(1024)S(1)} %pad_clamp_fusion), kind=kCustom, calls=%fused_computation.2 | custom fusion | bytes 4195328 | tf_op jit(solution)/shard_map/jit(_take)/gather | solution.py:28
  479.4 4.4 gather.10
  483.8 4.0 copy_select_fusion
  487.9 1.8 fusion.9
  489.7 0.0 reduce-scatter.2.cloned.1.call-update
  489.7 65.1 %reduce-scatter.2.cloned.1.call-done = f32[128,512]{1,0:T(8,128)} async-done(((f32[128,4096]{1,0:T(8,128)}), f32[128,512]{1,0:T(8,128)}) %reduce-scatter.2.cloned.1.call-update) | async-done | bytes 262160 | tf_op jit(solution)/shard_map/reduce_scatter | solution.py:91
  554.8 1.6 convert_element_type.45
  (11 shorter events, 0.1 us)
Async XLA Ops:
  6.5 320.4 %copy-start = (bf16[1,192,4096]{2,1,0:T(8,128)(2,1)S(1)}, bf16[1,192,4096]{2,1,0:T(8,128)(2,1)}, u32[]{:S(2)}) copy-start(bf16[1,192,4096]{2,1,0:T(8,128)(2,1)} %param.14) | copy-start | bytes 4718596
  6.5 35.0 %all-gather.3.cloned.1.call-start = ((), (), s32[]{:S(2)}) async-start(), calls=%async_computation.4 | async-start | bytes 1179648 | tf_op jit(solution)/shard_map/all_gather | solution.py:60
  7.3 65.1 %all-gather.5.cloned.1.call-start = ((), (), s32[]{:S(2)}) async-start(), calls=%async_computation.5 | async-start | bytes 1179648 | tf_op jit(solution)/shard_map/all_gather | solution.py:59
  198.6 14.4 %copy-start.1 = (bf16[1,192,4096]{2,1,0:T(8,128)(2,1)S(1)}, bf16[1,192,4096]{2,1,0:T(8,128)(2,1)}, u32[]{:S(2)}) copy-start(bf16[1,192,4096]{2,1,0:T(8,128)(2,1)} %param.13) | copy-start | bytes 4718596
  198.6 123.3 %all-to-all-start = ((bf16[64,8,4096]{2,1,0:T(8,128)(2,1)}), bf16[64,8,4096]{2,1,0:T(8,128)(2,1)}, u32[]{:S(2)}, u32[]{:S(2)}) async-start(bf16[64,8,4096]{2,1,0:T(8,128)(2,1)} %get-tuple-element.13), calls=%async_computation | async-start | bytes 8388608 | tf_op jit(solution)/shard_map/all_to_all | solution.py:67
  342.0 26.8 %copy-start.2 = (s32[128,2]{0,1:T(2,128)S(1)}, s32[128,2]{0,1:T(2,128)}, u32[]{:S(2)}) copy-start(s32[128,2]{0,1:T(2,128)} %param.11) | copy-start | bytes 3076
  342.0 27.1 %copy-start.3 = (f32[128,2]{0,1:T(2,128)S(1)}, f32[128,2]{0,1:T(2,128)}, u32[]{:S(2)}) copy-start(f32[128,2]{0,1:T(2,128)} %param.12) | copy-start | bytes 3076
  342.0 129.5 %all-to-all-start.2 = ((bf16[64,8,4096]{2,1,0:T(8,128)(2,1)}), bf16[64,8,4096]{2,1,0:T(8,128)(2,1)}, u32[]{:S(2)}, u32[]{:S(2)}) async-start(bf16[64,8,4096]{2,1,0:T(8,128)(2,1)} %fusion), calls=%async_computation.2 | async-start | bytes 8388608 | tf_op jit(solution)/shard_map/all_to_all | solution.py:83
  368.6 186.3 %reduce-scatter.2.cloned.1.call-start = ((), (), s32[]{:S(2)}) async-start(), calls=%async_computation.6 | async-start | bytes 2359296 | tf_op jit(solution)/shard_map/reduce_scatter | solution.py:91
Sparse Core Ops, SparseCore 0:
  9.5 32.0 all-gather.2
  43.7 28.5 all-gather.4
  489.8 64.9 reduce-scatter.1
where the time goes:
time: 567 us; the launch traced here: 563 us
  waiting for transfers between devices  325 us (57%)
  blocking collectives  111 us (20%)
  starting transfers between devices  41.2 us (7%)
  local copies, waits for them, and re-layouts  33.9 us (6%)
  matrix products  23.8 us (4%)
  other arithmetic  14.5 us (3%)
  between operations  13.2 us (2%)
    all_to_all x1, blocking collectives, shards(): lax.all_to_all(send_x, 'tok', split_axis=0, concat_axis=0, tiled=True)  111 us
    all_to_all x1, waiting for transfers between devices, shards(): lax.all_to_all(send_g, 'tok', split_axis=0, concat_axis=0, tiled=True)  105 us
    all_to_all x1, waiting for transfers between devices, shards(): lax.all_to_all(partial_bf.reshape(n_tok, capacity, full_width), 'tok', sp...  102 us
    reduce_scatter x1, waiting for transfers between devices, shards(): summed = lax.psum_scatter(combined, 'tp', scatter_dimension=1, tiled=True)  65.1 us
    all_gather x1, waiting for transfers between devices, shards(): lax.all_gather(out_grad, 'tp', axis=1, tiled=True)  30.4 us
    all_to_all x1, starting transfers between devices, shards(): lax.all_to_all(partial_bf.reshape(n_tok, capacity, full_width), 'tok', sp...  26.5 us
    all_gather x1, waiting for transfers between devices, shards(): lax.all_gather(activations, 'tp', axis=1, tiled=True)  20.9 us
    gather x2, local copies, waits for them, and re-layouts, bucket(): jnp.take(rows, token_of, axis=0)  19.8 us
  transfers between devices with their start and end apart: 5, of which 5 were waited for; matrix products, arithmetic and copies ran while one was open for 3% of the time, Pallas kernels for 0%

commit v1 on v0

v1 whole, which is shorter than its diff:
```python
import functools

import jax
import jax.numpy as jnp
from jax import lax
from jax.experimental import pallas as pl
from jax.experimental.pallas import tpu as pltpu
from jax.sharding import PartitionSpec as P

CONTRACT_LAST = (((1,), (1,)), ((), ()))


def dispatch_kernel(n_tok, capacity, routes_ref, gates_ref, x_ref, g_ref, send_x_ref, send_g_ref, hi_ref, lo_ref):
    top_k, tok_dev = routes_ref.shape
    expert = lax.broadcasted_iota(jnp.int32, (n_tok, tok_dev), 0)
    named = jnp.zeros((n_tok, tok_dev), jnp.float32)
    weight = jnp.zeros((n_tok, tok_dev), jnp.float32)
    for k in range(top_k):
        hit = routes_ref[k : k + 1, :] == expert
        named = named + jnp.where(hit, 1.0, 0.0)
        weight = weight + jnp.where(hit, gates_ref[k : k + 1, :], 0.0)
    earlier = lax.broadcasted_iota(jnp.int32, (tok_dev, tok_dev), 0)
    later = lax.broadcasted_iota(jnp.int32, (tok_dev, tok_dev), 1)
    ahead = jnp.where(earlier < later, 1.0, 0.0).astype(jnp.bfloat16)
    before = jnp.dot(named.astype(jnp.bfloat16), ahead, preferred_element_type=jnp.float32)
    rows = n_tok * capacity
    slot = lax.broadcasted_iota(jnp.int32, (n_tok, capacity, tok_dev), 1).astype(jnp.float32)
    at_slot = before[:, None, :] == slot
    placed = jnp.where(at_slot, named[:, None, :], 0.0).reshape(rows, tok_dev)
    scaled = jnp.where(at_slot, weight[:, None, :], 0.0).reshape(rows, tok_dev)
    placed = placed.astype(jnp.bfloat16)
    send_x_ref[...] = jnp.dot(placed, x_ref[...], preferred_element_type=jnp.float32).astype(send_x_ref.dtype)
    send_g_ref[...] = jnp.dot(placed, g_ref[...], preferred_element_type=jnp.float32).astype(send_g_ref.dtype)
    scaled = scaled.T
    high = scaled.astype(jnp.bfloat16)
    hi_ref[...] = high
    lo_ref[...] = (scaled - high.astype(jnp.float32)).astype(jnp.bfloat16)


def dispatch(routes, gate_vals, activations, out_grad, n_tok, capacity):
    tok_dev, width = activations.shape
    rows = n_tok * capacity
    sent = jax.ShapeDtypeStruct((rows, width), activations.dtype)
    mixer = jax.ShapeDtypeStruct((tok_dev, rows), jnp.bfloat16)
    return pl.pallas_call(
        functools.partial(dispatch_kernel, n_tok, capacity),
        out_shape=(sent, sent, mixer, mixer),
        name="dispatch",
    )(routes.T, gate_vals.T, activations, out_grad)


def forward_kernel(x_ref, gate_ref, up_ref, gate_pre_ref, up_pre_ref):
    @pl.when(pl.program_id(0) == 0)
    def _():
        gate_pre_ref[...] = jnp.zeros_like(gate_pre_ref)
        up_pre_ref[...] = jnp.zeros_like(up_pre_ref)

    x = x_ref[...]
    gate_pre_ref[...] += lax.dot_general(x, gate_ref[...], CONTRACT_LAST, preferred_element_type=jnp.float32)
    up_pre_ref[...] += lax.dot_general(x, up_ref[...], CONTRACT_LAST, preferred_element_type=jnp.float32)


def forward(x, w_gate, w_up, steps):
    rows, width = x.shape
    hidden = w_gate.shape[0]
    chunk = width // steps
    by_step = lambda i: (0, i)
    fixed = lambda i: (0, 0)
    pre = jax.ShapeDtypeStruct((rows, hidden), jnp.float32)
    return pl.pallas_call(
        forward_kernel,
        grid=(steps,),
        in_specs=[
            pl.BlockSpec((rows, chunk), by_step),
            pl.BlockSpec((hidden, chunk), by_step),
            pl.BlockSpec((hidden, chunk), by_step),
        ],
        out_specs=[pl.BlockSpec((rows, hidden), fixed)] * 2,
        out_shape=(pre, pre),
        name="forward",
    )(x, w_gate, w_up)


def backward_kernel(steps, g_ref, down_ref, gate_pre_ref, up_pre_ref, gate_ref, up_ref, out_ref, acc_ref, gate_grad_ref, up_grad_ref):
    step = pl.program_id(0)

    @pl.when(step == 0)
    def _():
        acc_ref[...] = jnp.zeros_like(acc_ref)

    @pl.when(step < steps)
    def _():
        acc_ref[...] += lax.dot_general(g_ref[...], down_ref[...], CONTRACT_LAST, preferred_element_type=jnp.float32)

    @pl.when(step == steps - 1)
    def _():
        hidden_grad = acc_ref[...]
        gate_pre = gate_pre_ref[...]
        sigma = 1.0 / (1.0 + jnp.exp(-gate_pre))
        slope = sigma * (1.0 + gate_pre * (1.0 - sigma))
        gate_grad_ref[...] = (hidden_grad * up_pre_ref[...] * slope).astype(jnp.bfloat16)
        up_grad_ref[...] = (hidden_grad * (gate_pre * sigma)).astype(jnp.bfloat16)

    @pl.when(step >= steps)
    def _():
        value = jnp.dot(gate_grad_ref[...], gate_ref[...], preferred_element_type=jnp.float32)
        value = value + jnp.dot(up_grad_ref[...], up_ref[...], preferred_element_type=jnp.float32)
        out_ref[0] = value.astype(out_ref.dtype)


def backward(g, w_down, gate_pre, up_pre, w_gate, w_up, steps, blocks):
    rows, width = g.shape
    hidden = w_down.shape[0]
    chunk = width // steps
    block = width // blocks
    by_step = lambda i: (0, jnp.minimum(i, steps - 1))
    by_block = lambda i: (0, jnp.maximum(i - steps, 0))
    fixed = lambda i: (0, 0)
    return pl.pallas_call(
        functools.partial(backward_kernel, steps),
        grid=(steps + blocks,),
        in_specs=[
            pl.BlockSpec((rows, chunk), by_step),
            pl.BlockSpec((hidden, chunk), by_step),
            pl.BlockSpec((rows, hidden), fixed),
            pl.BlockSpec((rows, hidden), fixed),
            pl.BlockSpec((hidden, block), by_block),
            pl.BlockSpec((hidden, block), by_block),
        ],
        out_specs=pl.BlockSpec((1, rows, block), lambda i: (jnp.maximum(i - steps, 0), 0, 0)),
        out_shape=jax.ShapeDtypeStruct((blocks, rows, block), jnp.bfloat16),
        scratch_shapes=[
            pltpu.VMEM((rows, hidden), jnp.float32),
            pltpu.VMEM((rows, hidden), jnp.bfloat16),
            pltpu.VMEM((rows, hidden), jnp.bfloat16),
        ],
        name="backward",
    )(g, w_down, gate_pre, up_pre, w_gate, w_up)


def combine_kernel(hi_ref, lo_ref, back_ref, out_ref):
    back = back_ref[...]
    total = jnp.dot(hi_ref[...], back, preferred_element_type=jnp.float32)
    total = total + jnp.dot(lo_ref[...], back, preferred_element_type=jnp.float32)
    out_ref[...] = total.astype(out_ref.dtype)


def combine(high, low, back):
    return pl.pallas_call(
        combine_kernel,
        out_shape=jax.ShapeDtypeStruct((high.shape[0], back.shape[1]), jnp.bfloat16),
        name="combine",
    )(high, low, back)


def exchange(rows, n_tok):
    blocks = rows.reshape(n_tok, rows.shape[0] // n_tok, rows.shape[1])
    return lax.all_to_all(blocks, "tok", split_axis=0, concat_axis=0, tiled=True).reshape(rows.shape)


def shards(activations, out_grad, routes, gate_vals, w_gate, w_up, w_down):
    n_tok = lax.axis_size("tok")
    n_tp = lax.axis_size("tp")
    tok_dev, top_k = routes.shape
    capacity = max(2, 2 * tok_dev * top_k // n_tok)
    send_x, send_g, high, low = dispatch(routes, gate_vals, activations, out_grad, n_tok, capacity)
    whole_x = lax.all_gather(exchange(send_x, n_tok), "tp", axis=1, tiled=True)
    whole_g = lax.all_gather(exchange(send_g, n_tok), "tp", axis=1, tiled=True)
    gate_pre, up_pre = forward(whole_x, w_gate[0], w_up[0], 4)
    partial = backward(whole_g, w_down[0], gate_pre, up_pre, w_gate[0], w_up[0], 4, n_tp)
    expert_sum = lax.psum_scatter(partial, "tp", scatter_dimension=0, tiled=False)
    return combine(high, low, exchange(expert_sum, n_tok))


def solution(mesh):
    placed = (
        P("tok", "tp"),
        P("tok", "tp"),
        P("tok", None),
        P("tok", None),
        P("tok", "tp", None),
        P("tok", "tp", None),
        P("tok", "tp", None),
    )
    return jax.shard_map(
        shards, mesh=mesh, in_specs=placed, out_specs=P("tok", "tp"), check_vma=False
    )
```

time: 567 us -> 212 us (0.37)
  waiting for transfers between devices: 325 us -> 79.6 us
  starting transfers between devices: 41.2 us -> 0.09 us
  local copies, waits for them, and re-layouts: 33.9 us -> 0 us
  matrix products: 23.8 us -> 0 us
  Pallas kernels: 0 us -> 23.5 us
  blocking collectives: 111 us -> 93 us
  other arithmetic: 14.5 us -> 0 us
    all_to_all x2 -> x0, waiting for transfers between devices: 208 us -> none  [the longest x1 105 us: shards(): lax.all_to_all(send_g, 'tok', split_axis=0, concat_axis=0, tiled=True)]
    all_to_all x2 -> x0, starting transfers between devices: 40.9 us -> none  [the longest x1 26.5 us: shards(): lax.all_to_all(partial_bf.reshape(n_tok, capacity, full_width), 'tok', sp...]
    gather x4 -> x0, local copies, waits for them, and re-layouts: 32.2 us -> none  [the longest x2 19.8 us: bucket(): jnp.take(rows, token_of, axis=0)]
    dot_general x4 -> x0, matrix products: 23.8 us -> none  [the longest x1 8.3 us: shards(): jnp.dot(gate_grad, gate_local, preferred_element_type=jnp.float32)]
    pallas_call x0 -> x4, Pallas kernels: none -> 23.5 us  [the longest x1 12.6 us: backward(): pl.pallas_call(functools.partial(backward_kernel, steps), grid=(steps + b...]
    reduce_scatter x1, waiting for transfers between devices: 65.1 us -> 41.7 us  [shards(): lax.psum_scatter(partial, 'tp', scatter_dimension=0, tiled=False)]
    all_to_all x1 -> x3, blocking collectives: 111 us -> 93 us  [exchange(): lax.all_to_all(blocks, 'tok', split_axis=0, concat_axis=0, tiled=True)]
    all_gather x2, waiting for transfers between devices: 51.2 us -> 37.9 us  [the longest x1 33.3 us: shards(): whole_g = lax.all_gather(exchange(send_g, n_tok), 'tp', axis=1, tiled=True)]
  transfers between devices with their start and end apart: 5 -> 3, of which waited for: 5 -> 3; matrix products, arithmetic and copies ran while one was open for 3% -> 0% of each run, Pallas kernels for 0% -> 3%
where the time goes in v1:
time: 212 us; the launch traced here: 209 us
  blocking collectives  93 us (44%)
  waiting for transfers between devices  79.6 us (38%)
  Pallas kernels  23.5 us (11%)
  between operations  13.1 us (6%)
    all_to_all x3, blocking collectives, exchange(): lax.all_to_all(blocks, 'tok', split_axis=0, concat_axis=0, tiled=True)  93 us
    reduce_scatter x1, waiting for transfers between devices, shards(): lax.psum_scatter(partial, 'tp', scatter_dimension=0, tiled=False)  41.7 us
    all_gather x1, waiting for transfers between devices, shards(): whole_g = lax.all_gather(exchange(send_g, n_tok), 'tp', axis=1, tiled=True)  33.3 us
    pallas_call x1, Pallas kernels, backward(): pl.pallas_call(functools.partial(backward_kernel, steps), grid=(steps + b...  12.6 us
    pallas_call x1, Pallas kernels, forward(): pl.pallas_call(forward_kernel, grid=(steps,), in_specs=[pl.BlockSpec((row...  6.28 us
    all_gather x1, waiting for transfers between devices, shards(): whole_x = lax.all_gather(exchange(send_x, n_tok), 'tp', axis=1, tiled=True)  4.57 us
  transfers between devices with their start and end apart: 3, of which 3 were waited for; matrix products, arithmetic and copies ran while one was open for 0% of the time, Pallas kernels for 3%

profile of v1, /device:TPU:6, one launch (start us, length us, event | category | flops | bytes accessed | tf_op | source)
XLA Modules:
  0.0 209.3 jit_solution(5112117513827785723)
XLA Ops:
  6.5 0.0 all-gather.5.cloned.1.call-start
  6.5 2.5 %dispatch.1 = (bf16[512,512]{1,0:T(8,128)(2,1)}, bf16[512,512]{1,0:T(8,128)(2,1)}, bf16[128,512]{1,0:T(8,128)(2,1)}, bf16[128,512]{1,0:T(8,128)(2,1)}) custom-call(s32[2,128]{1,0:T(2,128)} %bitcast.22, f32[2,128]{1,0:T(2,128)} %bitcast.23, bf16[128,512]{1,0:T(8,128)(2,1)} %x_ref.1, bf16[128,512]{1,0:T(8,128)(2,1)} %g_ref.1), custom_call_target="tpu_custom_call" | custom-call | tf_op jit(solution)/shard_map/dispatch/pallas_call | solution.py:45
  9.0 36.4 %all_to_all.15 = bf16[64,8,512]{2,1,0:T(8,128)(2,1)} all-to-all(bf16[64,8,512]{2,1,0:T(8,128)(2,1)} %bitcast.21), channel_id=1, replica_groups=mesh['tok'=64,'tp'=8] {'tok'}, dimensions={0} | all-to-all | bytes 1048576 | tf_op jit(solution)/shard_map/all_to_all | solution.py:158
  45.4 0.0 all-gather.5.cloned.1.call-update
  45.5 0.0 all-gather.3.cloned.1.call-start
  45.5 24.1 %all_to_all.16 = bf16[64,8,512]{2,1,0:T(8,128)(2,1)} all-to-all(bf16[64,8,512]{2,1,0:T(8,128)(2,1)} %bitcast.19), channel_id=1, replica_groups=mesh['tok'=64,'tp'=8] {'tok'}, dimensions={0} | all-to-all | bytes 1048576 | tf_op jit(solution)/shard_map/all_to_all | solution.py:158
  69.6 0.0 all-gather.3.cloned.1.call-update
  69.6 0.0 reduce-scatter.2.cloned.1.call-start
  69.6 4.6 %all-gather.5.cloned.1.call-done.x_ref = bf16[512,4096]{1,0:T(8,128)(2,1)} async-done(((bf16[512,512]{1,0:T(8,128)(2,1)}), bf16[512,4096]{1,0:T(8,128)(2,1)}) %all-gather.5.cloned.1.call-update) | async-done | bytes 4194320 | tf_op jit(solution)/shard_map/all_gather | solution.py:167
  74.2 6.3 %forward.1 = (f32[512,192]{1,0:T(8,128)}, f32[512,192]{1,0:T(8,128)}) custom-call(bf16[512,4096]{1,0:T(8,128)(2,1)} %all-gather.5.cloned.1.call-done.x_ref, bf16[192,4096]{1,0:T(8,128)(2,1)} %bitcast.11, bf16[192,4096]{1,0:T(8,128)(2,1)} %bitcast.13), custom_call_target="tpu_custom_call" | custom-call | tf_op jit(solution)/shard_map/forward/pallas_call | solution.py:70
  80.5 33.3 %all-gather.3.cloned.1.call-done.g_ref = bf16[512,4096]{1,0:T(8,128)(2,1)} async-done(((bf16[512,512]{1,0:T(8,128)(2,1)}), bf16[512,4096]{1,0:T(8,128)(2,1)}) %all-gather.3.cloned.1.call-update) | async-done | bytes 4194320 | tf_op jit(solution)/shard_map/all_gather | solution.py:168
  113.8 12.6 %backward.1 = bf16[8,512,512]{2,1,0:T(8,128)(2,1)} custom-call(bf16[512,4096]{1,0:T(8,128)(2,1)} %all-gather.3.cloned.1.call-done.g_ref, bf16[192,4096]{1,0:T(8,128)(2,1)} %bitcast.18, f32[512,192]{1,0:T(8,128)} %get-tuple-element.15.gate_pre_ref, f32[512,192]{1,0:T(8,128)} %get-tuple-element.16.up_pre_ref, bf16[192,4096]{1,0:T(8,128)(2,1)} %bitcast.12, ...), custom_call_target="tpu_custom_call" | custom-call | tf_op jit(solution)/shard_map/backward/pallas_call | solution.py:119
  126.4 0.0 reduce-scatter.2.cloned.1.call-update
  126.4 41.7 %reduce-scatter.2.cloned.1.call-done = bf16[1,512,512]{2,1,0:T(8,128)(2,1)} async-done(((bf16[8,512,512]{2,1,0:T(8,128)(2,1)}), bf16[1,512,512]{2,1,0:T(8,128)(2,1)}) %reduce-scatter.2.cloned.1.call-update) | async-done | bytes 524304 | tf_op jit(solution)/shard_map/reduce_scatter | solution.py:171
  168.1 32.6 %all_to_all.17 = bf16[64,8,512]{2,1,0:T(8,128)(2,1)} all-to-all(bf16[64,8,512]{2,1,0:T(8,128)(2,1)} %bitcast.20), channel_id=1, replica_groups=mesh['tok'=64,'tp'=8] {'tok'}, dimensions={0} | all-to-all | bytes 1048576 | tf_op jit(solution)/shard_map/all_to_all | solution.py:158
  200.6 2.1 %combine.1 = bf16[128,512]{1,0:T(8,128)(2,1)} custom-call(bf16[128,512]{1,0:T(8,128)(2,1)} %get-tuple-element.11.hi_ref, bf16[128,512]{1,0:T(8,128)(2,1)} %get-tuple-element.12.lo_ref, bf16[512,512]{1,0:T(8,128)(2,1)} %bitcast.15), custom_call_target="tpu_custom_call" | custom-call | tf_op jit(solution)/shard_map/combine/pallas_call | solution.py:149
Async XLA Ops:
  6.5 67.7 %all-gather.5.cloned.1.call-start = ((), (), s32[]{:S(2)}) async-start(), calls=%async_computation.5 | async-start | bytes 4718592 | tf_op jit(solution)/shard_map/all_gather | solution.py:167
  45.5 68.4 %all-gather.3.cloned.1.call-start = ((), (), s32[]{:S(2)}) async-start(), calls=%async_computation.4 | async-start | bytes 4718592 | tf_op jit(solution)/shard_map/all_gather | solution.py:168
  69.6 98.5 %reduce-scatter.2.cloned.1.call-start = ((), (), s32[]{:S(2)}) async-start(), calls=%async_computation.6 | async-start | bytes 4718592 | tf_op jit(solution)/shard_map/reduce_scatter | solution.py:171
Sparse Core Ops, SparseCore 0:
  45.6 28.5 all-gather.4
  76.3 37.4 all-gather.2
  126.5 41.5 reduce-scatter.1

commit v2 on v1

v2 whole, which is shorter than its diff:
```python
import functools

import jax
import jax.numpy as jnp
from jax import lax
from jax.experimental import pallas as pl
from jax.experimental.pallas import tpu as pltpu
from jax.sharding import PartitionSpec as P

OFFSETS = (0, 3, 1, 2)
CHIPS = 4
CORES = 2
CONTRACT_LAST = (((1,), (1,)), ((), ()))
CONTRACT_FIRST = (((0,), (0,)), ((), ()))
BIG = pltpu.CompilerParams(vmem_limit_bytes=40 * 1024 * 1024)


def dispatch_kernel(n_tok, capacity, routes_ref, gates_ref, x_ref, g_ref, send_ref, hi_ref, lo_ref):
    top_k, tok_dev = routes_ref.shape
    width = x_ref.shape[1]
    expert = lax.broadcasted_iota(jnp.int32, (n_tok, tok_dev), 0)
    named = jnp.zeros((n_tok, tok_dev), jnp.float32)
    weight = jnp.zeros((n_tok, tok_dev), jnp.float32)
    for k in range(top_k):
        hit = routes_ref[k : k + 1, :] == expert
        named = named + jnp.where(hit, 1.0, 0.0)
        weight = weight + jnp.where(hit, gates_ref[k : k + 1, :], 0.0)
    earlier = lax.broadcasted_iota(jnp.int32, (tok_dev, tok_dev), 0)
    later = lax.broadcasted_iota(jnp.int32, (tok_dev, tok_dev), 1)
    ahead = jnp.where(earlier < later, 1.0, 0.0).astype(jnp.bfloat16)
    before = jnp.dot(named.astype(jnp.bfloat16), ahead, preferred_element_type=jnp.float32)
    rows = n_tok * capacity
    slot = lax.broadcasted_iota(jnp.int32, (n_tok, capacity, tok_dev), 1).astype(jnp.float32)
    at_slot = before[:, None, :] == slot
    placed = jnp.where(at_slot, named[:, None, :], 0.0).reshape(rows, tok_dev)
    scaled = jnp.where(at_slot, weight[:, None, :], 0.0).reshape(rows, tok_dev)
    placed = placed.astype(jnp.bfloat16)
    send_ref[:, :width] = jnp.dot(placed, x_ref[...], preferred_element_type=jnp.float32).astype(send_ref.dtype)
    send_ref[:, width:] = jnp.dot(placed, g_ref[...], preferred_element_type=jnp.float32).astype(send_ref.dtype)
    scaled = scaled.T
    high = scaled.astype(jnp.bfloat16)
    hi_ref[...] = high
    lo_ref[...] = (scaled - high.astype(jnp.float32)).astype(jnp.bfloat16)


def dispatch(routes, gate_vals, activations, out_grad, n_tok, capacity):
    tok_dev, width = activations.shape
    rows = n_tok * capacity
    mixer = jax.ShapeDtypeStruct((tok_dev, rows), jnp.bfloat16)
    return pl.pallas_call(
        functools.partial(dispatch_kernel, n_tok, capacity),
        out_shape=(jax.ShapeDtypeStruct((rows, 2 * width), activations.dtype), mixer, mixer),
        name="dispatch",
    )(routes.T, gate_vals.T, activations, out_grad)


def pack_kernel(blocks_ref, *refs):
    keep_ref, give_ref = refs[6:]
    hidden = refs[0].shape[0]
    for n in range(3):
        keep_ref[0, n * hidden : (n + 1) * hidden, :] = refs[n][...]
        give_ref[0, n * hidden : (n + 1) * hidden, :] = refs[3 + n][...]


def pack(blocks, weights):
    hidden, width = weights[0].shape
    block = width // (CHIPS * CORES)
    packed = jax.ShapeDtypeStruct((CHIPS, 3 * hidden, block), weights[0].dtype)
    keep = pl.BlockSpec((hidden, block), lambda i, blocks_ref: (0, blocks_ref[i]))
    give = pl.BlockSpec((hidden, block), lambda i, blocks_ref: (0, blocks_ref[i + CHIPS]))
    out = pl.BlockSpec((1, 3 * hidden, block), lambda i, blocks_ref: (i, 0, 0))
    return pl.pallas_call(
        pack_kernel,
        grid_spec=pltpu.PrefetchScalarGridSpec(
            num_scalar_prefetch=1,
            grid=(CHIPS,),
            in_specs=[keep] * 3 + [give] * 3,
            out_specs=[out, out],
        ),
        out_shape=(packed, packed),
        name="pack",
    )(blocks, *weights, *weights)


def products(weight, rows):
    block = weight.shape[1]
    split = weight.shape[0] // 3 * 2
    wide = lax.dot_general(weight[:split], rows[:, :block], CONTRACT_LAST, preferred_element_type=jnp.float32)
    narrow = lax.dot_general(weight[split:], rows[:, block:], CONTRACT_LAST, preferred_element_type=jnp.float32)
    return wide, narrow, split


def first_kernel(own_ref, left_ref, right_ref, keep_ref, sib_ref, out_ref):
    for n, weights in enumerate((keep_ref, sib_ref)):
        wide, narrow = 0.0, 0.0
        for r, rows in enumerate((own_ref, left_ref, right_ref)):
            a, b, split = products(weights[r], rows[...])
            wide, narrow = wide + a, narrow + b
        out_ref[n, :split, :] = wide
        out_ref[n, split:, :] = narrow


def first(own, left, right, keep, sib):
    rows, width = own.shape
    _, depth, block = keep.shape
    half = rows // 2
    by_half = pl.BlockSpec((half, width), lambda i: (i, 0))
    weights = pl.BlockSpec((CHIPS - 1, depth, block), lambda i: (0, 0, 0))
    return pl.pallas_call(
        first_kernel,
        grid=(2,),
        in_specs=[by_half] * 3 + [weights] * 2,
        out_specs=pl.BlockSpec((CORES, depth, half), lambda i: (0, 0, i)),
        out_shape=jax.ShapeDtypeStruct((CORES, depth, rows), jnp.float32),
        compiler_params=BIG,
        name="first",
    )(own, left, right, keep, sib)


def second_kernel(low_ref, high_ref, keep_ref, sib_ref, sum_ref, out_ref):
    def add(rows_ref):
        for n, weights in enumerate((keep_ref, sib_ref)):
            wide, narrow, split = products(weights[0], rows_ref[...])
            out_ref[n, :split, :] = sum_ref[n, :split, :] + wide
            out_ref[n, split:, :] = sum_ref[n, split:, :] + narrow

    @pl.when(pl.program_id(0) == 0)
    def _():
        add(low_ref)

    @pl.when(pl.program_id(0) == 1)
    def _():
        add(high_ref)


def second(low, high, keep, sib, sums):
    half, width = low.shape
    _, depth, block = keep.shape
    whole = pl.BlockSpec((half, width), lambda i: (0, 0))
    weights = pl.BlockSpec((1, depth, block), lambda i: (CHIPS - 1, 0, 0))
    by_half = pl.BlockSpec((CORES, depth, half), lambda i: (0, 0, i))
    return pl.pallas_call(
        second_kernel,
        grid=(2,),
        in_specs=[whole] * 2 + [weights] * 2 + [by_half],
        out_specs=by_half,
        out_shape=jax.ShapeDtypeStruct(sums.shape, sums.dtype),
        compiler_params=BIG,
        name="second",
    )(low, high, keep, sib, sums)


def chip_sum(grads_ref, keep_ref, sib_ref):
    depth = grads_ref.shape[1]
    return jnp.dot(grads_ref[0].T, keep_ref[0, :depth, :], preferred_element_type=jnp.float32) + jnp.dot(
        grads_ref[1].T, sib_ref[0, :depth, :], preferred_element_type=jnp.float32
    )


def grads_kernel(mine_ref, theirs_ref, keep_ref, sib_ref, grads_ref, low_ref, high_ref):
    hidden = mine_ref.shape[1] // 3
    for n in range(CORES):
        gate_pre = mine_ref[n, :hidden, :] + theirs_ref[1 - n, :hidden, :]
        up_pre = mine_ref[n, hidden : 2 * hidden, :] + theirs_ref[1 - n, hidden : 2 * hidden, :]
        hidden_grad = mine_ref[n, 2 * hidden :, :] + theirs_ref[1 - n, 2 * hidden :, :]
        sigma = 1.0 / (1.0 + jnp.exp(-gate_pre))
        slope = sigma * (1.0 + gate_pre * (1.0 - sigma))
        grads_ref[n, :hidden, :] = (hidden_grad * up_pre * slope).astype(grads_ref.dtype)
        grads_ref[n, hidden:, :] = (hidden_grad * (gate_pre * sigma)).astype(grads_ref.dtype)
    value = chip_sum(grads_ref, keep_ref, sib_ref).astype(low_ref.dtype)

    @pl.when(pl.program_id(0) == 0)
    def _():
        low_ref[...] = value

    @pl.when(pl.program_id(0) == 1)
    def _():
        high_ref[...] = value


def grads(mine, theirs, keep, sib):
    _, depth, rows = mine.shape
    block = keep.shape[2]
    half = rows // 2
    wide = depth // 3 * 2
    by_half = pl.BlockSpec((CORES, depth, half), lambda i: (0, 0, i))
    weights = pl.BlockSpec((1, depth, block), lambda i: (CHIPS - 1, 0, 0))
    whole = pl.BlockSpec((half, block), lambda i: (0, 0))
    part = jax.ShapeDtypeStruct((half, block), jnp.bfloat16)
    return pl.pallas_call(
        grads_kernel,
        grid=(2,),
        in_specs=[by_half] * 2 + [weights] * 2,
        out_specs=[pl.BlockSpec((CORES, wide, half), lambda i: (0, 0, i)), whole, whole],
        out_shape=(jax.ShapeDtypeStruct((CORES, wide, rows), jnp.bfloat16), part, part),
        compiler_params=BIG,
        name="grads",
    )(mine, theirs, keep, sib)


def sides_kernel(grads_ref, keep_left_ref, sib_left_ref, keep_right_ref, sib_right_ref, low_ref, high_ref, left_ref, right_ref):
    to_left = chip_sum(grads_ref, keep_left_ref, sib_left_ref)
    to_right = chip_sum(grads_ref, keep_right_ref, sib_right_ref)

    @pl.when(pl.program_id(0) == 0)
    def _():
        left_ref[...] = to_left.astype(left_ref.dtype)
        right_ref[...] = (to_right + low_ref[...].astype(jnp.float32)).astype(right_ref.dtype)

    @pl.when(pl.program_id(0) == 1)
    def _():
        left_ref[...] = (to_left + high_ref[...].astype(jnp.float32)).astype(left_ref.dtype)
        right_ref[...] = to_right.astype(right_ref.dtype)


def sides(grads_value, keep, sib, low, high):
    _, wide, rows = grads_value.shape
    _, depth, block = keep.shape
    half = rows // 2
    left = pl.BlockSpec((1, depth, block), lambda i: (1, 0, 0))
    right = pl.BlockSpec((1, depth, block), lambda i: (2, 0, 0))
    whole = pl.BlockSpec((half, block), lambda i: (0, 0))
    by_half = pl.BlockSpec((half, block), lambda i: (i, 0))
    out = jax.ShapeDtypeStruct((rows, block), jnp.bfloat16)
    return pl.pallas_call(
        sides_kernel,
        grid=(2,),
        in_specs=[pl.BlockSpec((CORES, wide, half), lambda i: (0, 0, i)), left, left, right, right, whole, whole],
        out_specs=[by_half] * 2,
        out_shape=(out, out),
        compiler_params=BIG,
        name="sides",
    )(grads_value, keep, sib, keep, sib, low, high)


def total_kernel(grads_ref, keep_ref, sib_ref, a_ref, b_ref, out_ref):
    value = chip_sum(grads_ref, keep_ref, sib_ref)
    value = value + a_ref[...].astype(jnp.float32) + b_ref[...].astype(jnp.float32)
    out_ref[...] = value.astype(out_ref.dtype)


def total(grads_value, keep, sib, a, b):
    _, wide, rows = grads_value.shape
    _, depth, block = keep.shape
    half = rows // 2
    own = pl.BlockSpec((1, depth, block), lambda i: (0, 0, 0))
    by_half = pl.BlockSpec((half, block), lambda i: (i, 0))
    return pl.pallas_call(
        total_kernel,
        grid=(2,),
        in_specs=[pl.BlockSpec((CORES, wide, half), lambda i: (0, 0, i)), own, own, by_half, by_half],
        out_specs=by_half,
        out_shape=jax.ShapeDtypeStruct((rows, block), jnp.bfloat16),
        compiler_params=BIG,
        name="total",
    )(grads_value, keep, sib, a, b)


def combine_kernel(hi_ref, lo_ref, back_ref, out_ref):
    back = back_ref[...]
    value = jnp.dot(hi_ref[...], back, preferred_element_type=jnp.float32)
    value = value + jnp.dot(lo_ref[...], back, preferred_element_type=jnp.float32)
    out_ref[...] = value.astype(out_ref.dtype)


def combine(high, low, back):
    return pl.pallas_call(
        combine_kernel,
        out_shape=jax.ShapeDtypeStruct((high.shape[0], back.shape[1]), jnp.bfloat16),
        name="combine",
    )(high, low, back)


def exchange(rows, n_tok):
    blocks = rows.reshape(n_tok, rows.shape[0] // n_tok, rows.shape[1])
    return lax.all_to_all(blocks, "tok", split_axis=0, concat_axis=0, tiled=True).reshape(rows.shape)


def send(value, to):
    return lax.ppermute(value, "tp", [(i, to(i)) for i in range(CHIPS * CORES)])


def to_right(value):
    return send(value, lambda i: (i + CORES) % (CHIPS * CORES))


def to_left(value):
    return send(value, lambda i: (i - CORES) % (CHIPS * CORES))


def to_sibling(value):
    return send(value, lambda i: i ^ 1)


def expert(own, weights):
    place = lax.axis_index("tp").astype(jnp.int32)
    chip, core = place >> 1, place & 1
    keep_blocks = ((chip + jnp.array(OFFSETS, jnp.int32)) & (CHIPS - 1)) * CORES + core
    blocks = jnp.concatenate([keep_blocks, keep_blocks ^ 1])
    keep, give = pack(blocks, weights)
    sib = to_sibling(give)
    left, right = to_right(own), to_left(own)
    half = own.shape[0] // 2
    opposite_low, opposite_high = to_right(left[:half]), to_left(right[half:])
    mine = first(own, left, right, keep, sib)
    mine = second(opposite_low, opposite_high, keep, sib, mine)
    theirs = to_sibling(mine)
    grads_value, part_low, part_high = grads(mine, theirs, keep, sib)
    got_low, got_high = to_right(part_low), to_left(part_high)
    for_left, for_right = sides(grads_value, keep, sib, got_low, got_high)
    from_left, from_right = to_right(for_right), to_left(for_left)
    return total(grads_value, keep, sib, from_left, from_right)


def shards(activations, out_grad, routes, gate_vals, w_gate, w_up, w_down):
    n_tok = lax.axis_size("tok")
    tok_dev, top_k = routes.shape
    capacity = max(2, 2 * tok_dev * top_k // n_tok)
    sent, high, low = dispatch(routes, gate_vals, activations, out_grad, n_tok, capacity)
    weights, sent = lax.optimization_barrier(((w_gate[0], w_up[0], w_down[0]), sent))
    expert_sum = expert(exchange(sent, n_tok), weights)
    return combine(high, low, exchange(expert_sum, n_tok))


def solution(mesh):
    placed = (
        P("tok", "tp"),
        P("tok", "tp"),
        P("tok", None),
        P("tok", None),
        P("tok", "tp", None),
        P("tok", "tp", None),
        P("tok", "tp", None),
    )
    return jax.shard_map(
        shards, mesh=mesh, in_specs=placed, out_specs=P("tok", "tp"), check_vma=False
    )
```

time: 212 us -> 165 us (0.78)
  blocking collectives: 93 us -> 28.2 us
  starting transfers between devices: 0.09 us -> 43.8 us
  between operations: 13.1 us -> 0.19 us
  waiting for transfers between devices: 79.6 us -> 70.4 us
  Pallas kernels: 23.5 us -> 19.1 us
    all_to_all x3 -> x1, blocking collectives: 93 us -> 28.2 us  [exchange(): lax.all_to_all(blocks, 'tok', split_axis=0, concat_axis=0, tiled=True)]
    ppermute x0 -> x10, waiting for transfers between devices: none -> 49 us  [send(): return lax.ppermute(value, 'tp', [(i, to(i)) for i in range(CHIPS * CORES)])]
    reduce_scatter x1 -> x0, waiting for transfers between devices: 41.7 us -> none  [shards(): lax.psum_scatter(partial, 'tp', scatter_dimension=0, tiled=False)]
    all_gather x2 -> x0, waiting for transfers between devices: 37.9 us -> none  [the longest x1 33.3 us: shards(): whole_g = lax.all_gather(exchange(send_g, n_tok), 'tp', axis=1, tiled=True)]
    ppermute x0 -> x10, starting transfers between devices: none -> 27.2 us  [send(): return lax.ppermute(value, 'tp', [(i, to(i)) for i in range(CHIPS * CORES)])]
    all_to_all x0 -> x1, waiting for transfers between devices: none -> 21.4 us  [exchange(): lax.all_to_all(blocks, 'tok', split_axis=0, concat_axis=0, tiled=True)]
    all_to_all x0 -> x1, starting transfers between devices: none -> 16.6 us  [exchange(): lax.all_to_all(blocks, 'tok', split_axis=0, concat_axis=0, tiled=True)]
    pallas_call x2 -> x6, Pallas kernels: 18.8 us -> 14.3 us  [the longest x1 5.82 us: pack(): pl.pallas_call(pack_kernel, grid_spec=pltpu.PrefetchScalarGridSpec(num_sc...]
  transfers between devices with their start and end apart: 3 -> 11, of which waited for: 3 -> 9; matrix products, arithmetic and copies ran while one was open for 0% -> 0% of each run, Pallas kernels for 3% -> 5%
where the time goes in v2:
time: 165 us; the launch traced here: 164 us
  waiting for transfers between devices  70.4 us (43%)
  starting transfers between devices  43.8 us (27%)
  blocking collectives  28.2 us (17%)
  Pallas kernels  19.1 us (12%)
  local copies, waits for them, and re-layouts  1.73 us (1%)
    ppermute x10, waiting for transfers between devices, send(): return lax.ppermute(value, 'tp', [(i, to(i)) for i in range(CHIPS * CORES)])  49 us
    all_to_all x1, blocking collectives, exchange(): lax.all_to_all(blocks, 'tok', split_axis=0, concat_axis=0, tiled=True)  28.2 us
    ppermute x10, starting transfers between devices, send(): return lax.ppermute(value, 'tp', [(i, to(i)) for i in range(CHIPS * CORES)])  27.2 us
    all_to_all x1, waiting for transfers between devices, exchange(): lax.all_to_all(blocks, 'tok', split_axis=0, concat_axis=0, tiled=True)  21.4 us
    all_to_all x1, starting transfers between devices, exchange(): lax.all_to_all(blocks, 'tok', split_axis=0, concat_axis=0, tiled=True)  16.6 us
    pallas_call x1, Pallas kernels, pack(): pl.pallas_call(pack_kernel, grid_spec=pltpu.PrefetchScalarGridSpec(num_sc...  5.82 us
  transfers between devices with their start and end apart: 11, of which 9 were waited for; matrix products, arithmetic and copies ran while one was open for 0% of the time, Pallas kernels for 5%

profile of v2, /device:TPU:6, one launch (start us, length us, event | category | flops | bytes accessed | tf_op | source)
XLA Modules:
  0.0 164.0 jit_solution(12116743326431346504)
XLA Ops:
  0.0 0.0 copy-start.1
  0.0 2.6 %dispatch.1 = (bf16[512,1024]{1,0:T(8,128)(2,1)}, bf16[128,512]{1,0:T(8,128)(2,1)}, bf16[128,512]{1,0:T(8,128)(2,1)}) custom-call(s32[2,128]{1,0:T(2,128)} %bitcast.21, f32[2,128]{1,0:T(2,128)} %bitcast.22, bf16[128,512]{1,0:T(8,128)(2,1)} %x_ref.1, bf16[128,512]{1,0:T(8,128)(2,1)} %g_ref.1), custom_call_target="tpu_custom_call" | custom-call | tf_op jit(solution)/shard_map/dispatch/pallas_call | solution.py:50
  2.7 16.6 %all-to-all-start = ((bf16[64,8,1024]{2,1,0:T(8,128)(2,1)}), bf16[64,8,1024]{2,1,0:T(8,128)(2,1)S(1)}, u32[]{:S(2)}, u32[]{:S(2)}) async-start(bf16[64,8,1024]{2,1,0:T(8,128)(2,1)} %bitcast.20), calls=%async_computation | async-start | bytes 2097152 | tf_op jit(solution)/shard_map/all_to_all | solution.py:276
  19.3 0.0 copy-done.1
  19.3 0.6 pad_add_fusion.blocks_ref
  19.9 5.8 %pack.1 = (bf16[4,576,512]{2,1,0:T(8,128)(2,1)}, bf16[4,576,512]{2,1,0:T(8,128)(2,1)}) custom-call(s32[8]{0:T(128)} %pad_add_fusion.blocks_ref, bf16[192,4096]{1,0:T(8,128)(2,1)} %bitcast.13, bf16[192,4096]{1,0:T(8,128)(2,1)} %bitcast.15, bf16[192,4096]{1,0:T(8,128)(2,1)} %bitcast.17, bf16[192,4096]{1,0:T(8,128)(2,1)} %bitcast.14, ...), custom_call_target="tpu_custom_call" | custom-call | tf_op jit(solution)/shard_map/pack/pallas_call | solution.py:72
  25.7 1.9 %collective-permute-start.4 = (bf16[4,576,512]{2,1,0:T(8,128)(2,1)}, bf16[4,576,512]{2,1,0:T(8,128)(2,1)S(1)}, u32[]{:S(2)}, u32[]{:S(2)}) collective-permute-start(bf16[4,576,512]{2,1,0:T(8,128)(2,1)} %get-tuple-element.27), channel_id=1, source_target_pairs={{0,1},{1,0},{2,3},{3,2},{4,5},{5,4},{6,7},{7,6},{8,9},{9,8},{10,11... | collective-permute-start | bytes 7077896 | tf_op jit(solution)/shard_map/ppermute | solution.py:280
  27.6 21.4 %all-to-all-done = bf16[64,8,1024]{2,1,0:T(8,128)(2,1)S(1)} async-done(((bf16[64,8,1024]{2,1,0:T(8,128)(2,1)}), bf16[64,8,1024]{2,1,0:T(8,128)(2,1)S(1)}, u32[]{:S(2)}, u32[]{:S(2)}) %all-to-all-start) | async-done | bytes 1048608 | tf_op jit(solution)/shard_map/all_to_all | solution.py:276
  49.0 2.4 %collective-permute-start = (bf16[512,1024]{1,0:T(8,128)(2,1)S(1)}, bf16[512,1024]{1,0:T(8,128)(2,1)S(1)}, u32[]{:S(2)}, u32[]{:S(2)}) collective-permute-start(bf16[512,1024]{1,0:T(8,128)(2,1)S(1)} %bitcast.9), channel_id=1, source_target_pairs={{0,2},{1,3},{2,4},{3,5},{4,6},{5,7},{6,0},{7,1},{8,10},{9,11},{10,... | collective-permute-start | bytes 3145736 | tf_op jit(solution)/shard_map/ppermute | solution.py:280
  51.4 3.5 %collective-permute-start.2 = (bf16[512,1024]{1,0:T(8,128)(2,1)S(1)}, bf16[512,1024]{1,0:T(8,128)(2,1)S(1)}, u32[]{:S(2)}, u32[]{:S(2)}) collective-permute-start(bf16[512,1024]{1,0:T(8,128)(2,1)S(1)} %bitcast.10), channel_id=1, source_target_pairs={{0,6},{1,7},{2,0},{3,1},{4,2},{5,3},{6,4},{7,5},{8,14},{9,15},{10,... | collective-permute-start | bytes 3145736 | tf_op jit(solution)/shard_map/ppermute | solution.py:280
  54.9 18.3 %collective-permute-done.left_ref = bf16[512,1024]{1,0:T(8,128)(2,1)S(1)} collective-permute-done((bf16[512,1024]{1,0:T(8,128)(2,1)S(1)}, bf16[512,1024]{1,0:T(8,128)(2,1)S(1)}, u32[]{:S(2)}, u32[]{:S(2)}) %collective-permute-start) | collective-permute-done | bytes 1048608 | tf_op jit(solution)/shard_map/ppermute | solution.py:280
  73.2 3.6 %collective-permute-start.1 = (bf16[256,1024]{1,0:T(8,128)(2,1)S(1)}, bf16[256,1024]{1,0:T(8,128)(2,1)S(1)}, u32[]{:S(2)}, u32[]{:S(2)}) collective-permute-start(bf16[256,1024]{1,0:T(8,128)(2,1)S(1)} %slice.8), channel_id=1, source_target_pairs={{0,2},{1,3},{2,4},{3,5},{4,6},{5,7},{6,0},{7,1},{8,10},{9,11},{10,... | collective-permute-start | bytes 1572872 | tf_op jit(solution)/shard_map/ppermute | solution.py:280
  76.8 0.0 collective-permute-done.2.right_ref
  76.9 2.2 %collective-permute-start.3 = (bf16[256,1024]{1,0:T(8,128)(2,1)S(1)}, bf16[256,1024]{1,0:T(8,128)(2,1)S(1)}, u32[]{:S(2)}, u32[]{:S(2)}) collective-permute-start(bf16[256,1024]{1,0:T(8,128)(2,1)S(1)} %slice.9), channel_id=1, source_target_pairs={{0,6},{1,7},{2,0},{3,1},{4,2},{5,3},{6,4},{7,5},{8,14},{9,15},{10,... | collective-permute-start | bytes 1572872 | tf_op jit(solution)/shard_map/ppermute | solution.py:280
  79.1 0.0 collective-permute-done.4.sib_ref.sib_left_ref.sib_right_ref
  79.1 0.0 copy-start
  79.2 1.7 %copy-done = bf16[4,576,512]{2,1,0:T(8,128)(2,1)S(1)} copy-done((bf16[4,576,512]{2,1,0:T(8,128)(2,1)S(1)}, bf16[4,576,512]{2,1,0:T(8,128)(2,1)}, u32[]{:S(2)}) %copy-start) | copy-done | bytes 2359320
  80.8 2.6 %first.1.sum_ref = f32[2,576,512]{2,1,0:T(8,128)S(1)} custom-call(bf16[512,1024]{1,0:T(8,128)(2,1)S(1)} %bitcast.11, bf16[512,1024]{1,0:T(8,128)(2,1)S(1)} %collective-permute-done.left_ref, bf16[512,1024]{1,0:T(8,128)(2,1)S(1)} %collective-permute-done.2.right_ref, bf16[4,576,512]{2,1,0:T(8,128)(2,1)S(1)} %copy-done, ...), custom_call_target="tpu_custom_call" | custom-call | tf_op jit(solution)/shard_map/first/pallas_call | solution.py:109
  83.5 1.8 %collective-permute-done.1.low_ref = bf16[256,1024]{1,0:T(8,128)(2,1)S(1)} collective-permute-done((bf16[256,1024]{1,0:T(8,128)(2,1)S(1)}, bf16[256,1024]{1,0:T(8,128)(2,1)S(1)}, u32[]{:S(2)}, u32[]{:S(2)}) %collective-permute-start.1) | collective-permute-done | bytes 524320 | tf_op jit(solution)/shard_map/ppermute | solution.py:280
  85.2 4.6 %collective-permute-done.3.high_ref = bf16[256,1024]{1,0:T(8,128)(2,1)S(1)} collective-permute-done((bf16[256,1024]{1,0:T(8,128)(2,1)S(1)}, bf16[256,1024]{1,0:T(8,128)(2,1)S(1)}, u32[]{:S(2)}, u32[]{:S(2)}) %collective-permute-start.3) | collective-permute-done | bytes 524320 | tf_op jit(solution)/shard_map/ppermute | solution.py:280
  89.8 1.5 second.1.mine_ref
  91.3 1.9 %collective-permute-start.5 = (f32[2,576,512]{2,1,0:T(8,128)S(1)}, f32[2,576,512]{2,1,0:T(8,128)S(1)}, u32[]{:S(2)}, u32[]{:S(2)}) collective-permute-start(f32[2,576,512]{2,1,0:T(8,128)S(1)} %second.1.mine_ref), channel_id=1, source_target_pairs={{0,1},{1,0},{2,3},{3,2},{4,5},{5,4},{6,7},{7,6},{8,9},{9,8},{10,11... | collective-permute-start | bytes 7077896 | tf_op jit(solution)/shard_map/ppermute | solution.py:280
  93.3 4.5 %collective-permute-done.5.theirs_ref = f32[2,576,512]{2,1,0:T(8,128)S(1)} collective-permute-done((f32[2,576,512]{2,1,0:T(8,128)S(1)}, f32[2,576,512]{2,1,0:T(8,128)S(1)}, u32[]{:S(2)}, u32[]{:S(2)}) %collective-permute-start.5) | collective-permute-done | bytes 2359328 | tf_op jit(solution)/shard_map/ppermute | solution.py:280
  97.8 1.6 grads.1
  99.4 1.9 %collective-permute-start.6 = (bf16[256,512]{1,0:T(8,128)(2,1)S(1)}, bf16[256,512]{1,0:T(8,128)(2,1)S(1)}, u32[]{:S(2)}, u32[]{:S(2)}) collective-permute-start(bf16[256,512]{1,0:T(8,128)(2,1)S(1)} %get-tuple-element.29), channel_id=1, source_target_pairs={{0,2},{1,3},{2,4},{3,5},{4,6},{5,7},{6,0},{7,1},{8,10},{9,11},{10,... | collective-permute-start | bytes 786440 | tf_op jit(solution)/shard_map/ppermute | solution.py:280
  101.3 3.9 %collective-permute-start.7 = (bf16[256,512]{1,0:T(8,128)(2,1)S(1)}, bf16[256,512]{1,0:T(8,128)(2,1)S(1)}, u32[]{:S(2)}, u32[]{:S(2)}) collective-permute-start(bf16[256,512]{1,0:T(8,128)(2,1)S(1)} %get-tuple-element.30), channel_id=1, source_target_pairs={{0,6},{1,7},{2,0},{3,1},{4,2},{5,3},{6,4},{7,5},{8,14},{9,15},{10,... | collective-permute-start | bytes 786440 | tf_op jit(solution)/shard_map/ppermute | solution.py:280
  105.2 4.4 %collective-permute-done.6.low_ref = bf16[256,512]{1,0:T(8,128)(2,1)S(1)} collective-permute-done((bf16[256,512]{1,0:T(8,128)(2,1)S(1)}, bf16[256,512]{1,0:T(8,128)(2,1)S(1)}, u32[]{:S(2)}, u32[]{:S(2)}) %collective-permute-start.6) | collective-permute-done | bytes 262176 | tf_op jit(solution)/shard_map/ppermute | solution.py:280
  109.6 3.1 %collective-permute-done.7.high_ref = bf16[256,512]{1,0:T(8,128)(2,1)S(1)} collective-permute-done((bf16[256,512]{1,0:T(8,128)(2,1)S(1)}, bf16[256,512]{1,0:T(8,128)(2,1)S(1)}, u32[]{:S(2)}, u32[]{:S(2)}) %collective-permute-start.7) | collective-permute-done | bytes 262176 | tf_op jit(solution)/shard_map/ppermute | solution.py:280
  112.8 1.7 %sides.1 = (bf16[512,512]{1,0:T(8,128)(2,1)S(1)}, bf16[512,512]{1,0:T(8,128)(2,1)S(1)}) custom-call(bf16[2,384,512]{2,1,0:T(8,128)(2,1)S(1)} %get-tuple-element.28.grads_ref, bf16[4,576,512]{2,1,0:T(8,128)(2,1)S(1)} %copy-done, bf16[4,576,512]{2,1,0:T(8,128)(2,1)S(1)} %collective-permute-done.4.sib_ref.sib_left_ref.sib_right_ref, ...), custom_call_target="tpu_custom_call" | custom-call | tf_op jit(solution)/shard_map/sides/pallas_call | solution.py:225
  114.5 1.9 %collective-permute-start.8 = (bf16[512,512]{1,0:T(8,128)(2,1)S(1)}, bf16[512,512]{1,0:T(8,128)(2,1)S(1)}, u32[]{:S(2)}, u32[]{:S(2)}) collective-permute-start(bf16[512,512]{1,0:T(8,128)(2,1)S(1)} %get-tuple-element.31), channel_id=1, source_target_pairs={{0,2},{1,3},{2,4},{3,5},{4,6},{5,7},{6,0},{7,1},{8,10},{9,11},{10,... | collective-permute-start | bytes 1572872 | tf_op jit(solution)/shard_map/ppermute | solution.py:280
  116.4 3.9 %collective-permute-start.9 = (bf16[512,512]{1,0:T(8,128)(2,1)S(1)}, bf16[512,512]{1,0:T(8,128)(2,1)S(1)}, u32[]{:S(2)}, u32[]{:S(2)}) collective-permute-start(bf16[512,512]{1,0:T(8,128)(2,1)S(1)} %get-tuple-element.32), channel_id=1, source_target_pairs={{0,6},{1,7},{2,0},{3,1},{4,2},{5,3},{6,4},{7,5},{8,14},{9,15},{10,... | collective-permute-start | bytes 1572872 | tf_op jit(solution)/shard_map/ppermute | solution.py:280
  120.3 9.2 %collective-permute-done.8.a_ref = bf16[512,512]{1,0:T(8,128)(2,1)S(1)} collective-permute-done((bf16[512,512]{1,0:T(8,128)(2,1)S(1)}, bf16[512,512]{1,0:T(8,128)(2,1)S(1)}, u32[]{:S(2)}, u32[]{:S(2)}) %collective-permute-start.8) | collective-permute-done | bytes 524320 | tf_op jit(solution)/shard_map/ppermute | solution.py:280
  129.5 3.1 %collective-permute-done.9.b_ref = bf16[512,512]{1,0:T(8,128)(2,1)S(1)} collective-permute-done((bf16[512,512]{1,0:T(8,128)(2,1)S(1)}, bf16[512,512]{1,0:T(8,128)(2,1)S(1)}, u32[]{:S(2)}, u32[]{:S(2)}) %collective-permute-start.9) | collective-permute-done | bytes 524320 | tf_op jit(solution)/shard_map/ppermute | solution.py:280
  132.6 1.0 total.1
  133.7 28.2 %all_to_all.10 = bf16[64,8,512]{2,1,0:T(8,128)(2,1)} all-to-all(bf16[64,8,512]{2,1,0:T(8,128)(2,1)S(1)} %bitcast.12), channel_id=1, replica_groups=mesh['tok'=64,'tp'=8] {'tok'}, dimensions={0} | all-to-all | bytes 1048576 | tf_op jit(solution)/shard_map/all_to_all | solution.py:276
  161.8 2.1 %combine.1 = bf16[128,512]{1,0:T(8,128)(2,1)} custom-call(bf16[128,512]{1,0:T(8,128)(2,1)} %get-tuple-element.19.hi_ref, bf16[128,512]{1,0:T(8,128)(2,1)} %get-tuple-element.20.lo_ref, bf16[512,512]{1,0:T(8,128)(2,1)} %bitcast.19), custom_call_target="tpu_custom_call" | custom-call | tf_op jit(solution)/shard_map/combine/pallas_call | solution.py:267
  (3 shorter events, 0.1 us)
Async XLA Ops:
  0.0 19.3 %copy-start.1 = (s32[4]{0:T(128)S(1)}, s32[4]{0:T(128)}, u32[]{:S(2)}) copy-start(s32[4]{0:T(128)} %constant.4.clone) | copy-start | bytes 52
  2.7 46.4 %all-to-all-start = ((bf16[64,8,1024]{2,1,0:T(8,128)(2,1)}), bf16[64,8,1024]{2,1,0:T(8,128)(2,1)S(1)}, u32[]{:S(2)}, u32[]{:S(2)}) async-start(bf16[64,8,1024]{2,1,0:T(8,128)(2,1)} %bitcast.20), calls=%async_computation | async-start | bytes 2097152 | tf_op jit(solution)/shard_map/all_to_all | solution.py:276
  25.7 53.5 %collective-permute-start.4 = (bf16[4,576,512]{2,1,0:T(8,128)(2,1)}, bf16[4,576,512]{2,1,0:T(8,128)(2,1)S(1)}, u32[]{:S(2)}, u32[]{:S(2)}) collective-permute-start(bf16[4,576,512]{2,1,0:T(8,128)(2,1)} %get-tuple-element.27), channel_id=1, source_target_pairs={{0,1},{1,0},{2,3},{3,2},{4,5},{5,4},{6,7},{7,6},{8,9},{9,8},{10,11... | collective-permute-start | bytes 7077896 | tf_op jit(solution)/shard_map/ppermute | solution.py:280
  49.0 24.1 %collective-permute-start = (bf16[512,1024]{1,0:T(8,128)(2,1)S(1)}, bf16[512,1024]{1,0:T(8,128)(2,1)S(1)}, u32[]{:S(2)}, u32[]{:S(2)}) collective-permute-start(bf16[512,1024]{1,0:T(8,128)(2,1)S(1)} %bitcast.9), channel_id=1, source_target_pairs={{0,2},{1,3},{2,4},{3,5},{4,6},{5,7},{6,0},{7,1},{8,10},{9,11},{10,... | collective-permute-start | bytes 3145736 | tf_op jit(solution)/shard_map/ppermute | solution.py:280
  51.4 25.4 %collective-permute-start.2 = (bf16[512,1024]{1,0:T(8,128)(2,1)S(1)}, bf16[512,1024]{1,0:T(8,128)(2,1)S(1)}, u32[]{:S(2)}, u32[]{:S(2)}) collective-permute-start(bf16[512,1024]{1,0:T(8,128)(2,1)S(1)} %bitcast.10), channel_id=1, source_target_pairs={{0,6},{1,7},{2,0},{3,1},{4,2},{5,3},{6,4},{7,5},{8,14},{9,15},{10,... | collective-permute-start | bytes 3145736 | tf_op jit(solution)/shard_map/ppermute | solution.py:280
  73.2 12.0 %collective-permute-start.1 = (bf16[256,1024]{1,0:T(8,128)(2,1)S(1)}, bf16[256,1024]{1,0:T(8,128)(2,1)S(1)}, u32[]{:S(2)}, u32[]{:S(2)}) collective-permute-start(bf16[256,1024]{1,0:T(8,128)(2,1)S(1)} %slice.8), channel_id=1, source_target_pairs={{0,2},{1,3},{2,4},{3,5},{4,6},{5,7},{6,0},{7,1},{8,10},{9,11},{10,... | collective-permute-start | bytes 1572872 | tf_op jit(solution)/shard_map/ppermute | solution.py:280
  76.9 12.9 %collective-permute-start.3 = (bf16[256,1024]{1,0:T(8,128)(2,1)S(1)}, bf16[256,1024]{1,0:T(8,128)(2,1)S(1)}, u32[]{:S(2)}, u32[]{:S(2)}) collective-permute-start(bf16[256,1024]{1,0:T(8,128)(2,1)S(1)} %slice.9), channel_id=1, source_target_pairs={{0,6},{1,7},{2,0},{3,1},{4,2},{5,3},{6,4},{7,5},{8,14},{9,15},{10,... | collective-permute-start | bytes 1572872 | tf_op jit(solution)/shard_map/ppermute | solution.py:280
  79.1 1.7 %copy-start = (bf16[4,576,512]{2,1,0:T(8,128)(2,1)S(1)}, bf16[4,576,512]{2,1,0:T(8,128)(2,1)}, u32[]{:S(2)}) copy-start(bf16[4,576,512]{2,1,0:T(8,128)(2,1)} %get-tuple-element.26.keep_ref.keep_left_ref.keep_right_ref) | copy-start | bytes 7077892
  91.3 6.4 %collective-permute-start.5 = (f32[2,576,512]{2,1,0:T(8,128)S(1)}, f32[2,576,512]{2,1,0:T(8,128)S(1)}, u32[]{:S(2)}, u32[]{:S(2)}) collective-permute-start(f32[2,576,512]{2,1,0:T(8,128)S(1)} %second.1.mine_ref), channel_id=1, source_target_pairs={{0,1},{1,0},{2,3},{3,2},{4,5},{5,4},{6,7},{7,6},{8,9},{9,8},{10,11... | collective-permute-start | bytes 7077896 | tf_op jit(solution)/shard_map/ppermute | solution.py:280
  99.4 10.2 %collective-permute-start.6 = (bf16[256,512]{1,0:T(8,128)(2,1)S(1)}, bf16[256,512]{1,0:T(8,128)(2,1)S(1)}, u32[]{:S(2)}, u32[]{:S(2)}) collective-permute-start(bf16[256,512]{1,0:T(8,128)(2,1)S(1)} %get-tuple-element.29), channel_id=1, source_target_pairs={{0,2},{1,3},{2,4},{3,5},{4,6},{5,7},{6,0},{7,1},{8,10},{9,11},{10,... | collective-permute-start | bytes 786440 | tf_op jit(solution)/shard_map/ppermute | solution.py:280
  101.3 11.5 %collective-permute-start.7 = (bf16[256,512]{1,0:T(8,128)(2,1)S(1)}, bf16[256,512]{1,0:T(8,128)(2,1)S(1)}, u32[]{:S(2)}, u32[]{:S(2)}) collective-permute-start(bf16[256,512]{1,0:T(8,128)(2,1)S(1)} %get-tuple-element.30), channel_id=1, source_target_pairs={{0,6},{1,7},{2,0},{3,1},{4,2},{5,3},{6,4},{7,5},{8,14},{9,15},{10,... | collective-permute-start | bytes 786440 | tf_op jit(solution)/shard_map/ppermute | solution.py:280
  114.5 15.0 %collective-permute-start.8 = (bf16[512,512]{1,0:T(8,128)(2,1)S(1)}, bf16[512,512]{1,0:T(8,128)(2,1)S(1)}, u32[]{:S(2)}, u32[]{:S(2)}) collective-permute-start(bf16[512,512]{1,0:T(8,128)(2,1)S(1)} %get-tuple-element.31), channel_id=1, source_target_pairs={{0,2},{1,3},{2,4},{3,5},{4,6},{5,7},{6,0},{7,1},{8,10},{9,11},{10,... | collective-permute-start | bytes 1572872 | tf_op jit(solution)/shard_map/ppermute | solution.py:280
  116.4 16.2 %collective-permute-start.9 = (bf16[512,512]{1,0:T(8,128)(2,1)S(1)}, bf16[512,512]{1,0:T(8,128)(2,1)S(1)}, u32[]{:S(2)}, u32[]{:S(2)}) collective-permute-start(bf16[512,512]{1,0:T(8,128)(2,1)S(1)} %get-tuple-element.32), channel_id=1, source_target_pairs={{0,6},{1,7},{2,0},{3,1},{4,2},{5,3},{6,4},{7,5},{8,14},{9,15},{10,... | collective-permute-start | bytes 1572872 | tf_op jit(solution)/shard_map/ppermute | solution.py:280

commit v3 on v2

--- a/solution.py
+++ b/solution.py
@@ -90,31 +90,40 @@
     return wide, narrow, split
 
 
-def first_kernel(own_ref, left_ref, right_ref, keep_ref, sib_ref, out_ref):
-    for n, weights in enumerate((keep_ref, sib_ref)):
-        wide, narrow = 0.0, 0.0
-        for r, rows in enumerate((own_ref, left_ref, right_ref)):
-            a, b, split = products(weights[r], rows[...])
-            wide, narrow = wide + a, narrow + b
-        out_ref[n, :split, :] = wide
-        out_ref[n, split:, :] = narrow
+def first_kernel(own_ref, left_low_ref, left_high_ref, right_low_ref, right_high_ref, keep_ref, sib_ref, out_ref):
+    def add(left_ref, right_ref):
+        for n, weights in enumerate((keep_ref, sib_ref)):
+            wide, narrow = 0.0, 0.0
+            for r, rows in enumerate((own_ref, left_ref, right_ref)):
+                a, b, split = products(weights[r], rows[...])
+                wide, narrow = wide + a, narrow + b
+            out_ref[n, :split, :] = wide
+            out_ref[n, split:, :] = narrow
+
+    @pl.when(pl.program_id(0) == 0)
+    def _():
+        add(left_low_ref, right_low_ref)
+
+    @pl.when(pl.program_id(0) == 1)
+    def _():
+        add(left_high_ref, right_high_ref)
 
 
 def first(own, left, right, keep, sib):
     rows, width = own.shape
     _, depth, block = keep.shape
     half = rows // 2
-    by_half = pl.BlockSpec((half, width), lambda i: (i, 0))
+    whole = pl.BlockSpec((half, width), lambda i: (0, 0))
     weights = pl.BlockSpec((CHIPS - 1, depth, block), lambda i: (0, 0, 0))
     return pl.pallas_call(
         first_kernel,
         grid=(2,),
-        in_specs=[by_half] * 3 + [weights] * 2,
+        in_specs=[pl.BlockSpec((half, width), lambda i: (i, 0))] + [whole] * 4 + [weights] * 2,
         out_specs=pl.BlockSpec((CORES, depth, half), lambda i: (0, 0, i)),
         out_shape=jax.ShapeDtypeStruct((CORES, depth, rows), jnp.float32),
         compiler_params=BIG,
         name="first",
-    )(own, left, right, keep, sib)
+    )(own, *left, *right, keep, sib)
 
 
 def second_kernel(low_ref, high_ref, keep_ref, sib_ref, sum_ref, out_ref):
@@ -150,14 +159,14 @@
     )(low, high, keep, sib, sums)
 
 
-def chip_sum(grads_ref, keep_ref, sib_ref):
-    depth = grads_ref.shape[1]
-    return jnp.dot(grads_ref[0].T, keep_ref[0, :depth, :], preferred_element_type=jnp.float32) + jnp.dot(
-        grads_ref[1].T, sib_ref[0, :depth, :], preferred_element_type=jnp.float32
+def chip_sum(grads, keep, sib):
+    depth = grads.shape[1]
+    return jnp.dot(grads[0].T, keep[:depth, :], preferred_element_type=jnp.float32) + jnp.dot(
+        grads[1].T, sib[:depth, :], preferred_element_type=jnp.float32
     )
 
 
-def grads_kernel(mine_ref, theirs_ref, keep_ref, sib_ref, grads_ref, low_ref, high_ref):
+def grads_kernel(mine_ref, theirs_ref, keep_ref, sib_ref, grads_ref, opposite_low_ref, opposite_high_ref, left_low_ref, right_high_ref):
     hidden = mine_ref.shape[1] // 3
     for n in range(CORES):
         gate_pre = mine_ref[n, :hidden, :] + theirs_ref[1 - n, :hidden, :]
@@ -167,15 +176,19 @@
         slope = sigma * (1.0 + gate_pre * (1.0 - sigma))
         grads_ref[n, :hidden, :] = (hidden_grad * up_pre * slope).astype(grads_ref.dtype)
         grads_ref[n, hidden:, :] = (hidden_grad * (gate_pre * sigma)).astype(grads_ref.dtype)
-    value = chip_sum(grads_ref, keep_ref, sib_ref).astype(low_ref.dtype)
+
+    def store(out_ref, block):
+        out_ref[...] = chip_sum(grads_ref[...], keep_ref[block], sib_ref[block]).astype(out_ref.dtype)
 
     @pl.when(pl.program_id(0) == 0)
     def _():
-        low_ref[...] = value
+        store(opposite_low_ref, 3)
+        store(left_low_ref, 1)
 
     @pl.when(pl.program_id(0) == 1)
     def _():
-        high_ref[...] = value
+        store(opposite_high_ref, 3)
+        store(right_high_ref, 2)
 
 
 def grads(mine, theirs, keep, sib):
@@ -184,59 +197,65 @@
     half = rows // 2
     wide = depth // 3 * 2
     by_half = pl.BlockSpec((CORES, depth, half), lambda i: (0, 0, i))
-    weights = pl.BlockSpec((1, depth, block), lambda i: (CHIPS - 1, 0, 0))
+    weights = pl.BlockSpec(keep.shape, lambda i: (0, 0, 0))
     whole = pl.BlockSpec((half, block), lambda i: (0, 0))
     part = jax.ShapeDtypeStruct((half, block), jnp.bfloat16)
     return pl.pallas_call(
         grads_kernel,
         grid=(2,),
         in_specs=[by_half] * 2 + [weights] * 2,
-        out_specs=[pl.BlockSpec((CORES, wide, half), lambda i: (0, 0, i)), whole, whole],
-        out_shape=(jax.ShapeDtypeStruct((CORES, wide, rows), jnp.bfloat16), part, part),
+        out_specs=[pl.BlockSpec((CORES, wide, half), lambda i: (0, 0, i))] + [whole] * 4,
+        out_shape=(jax.ShapeDtypeStruct((CORES, wide, rows), jnp.bfloat16),) + (part,) * 4,
         compiler_params=BIG,
         name="grads",
     )(mine, theirs, keep, sib)
 
 
-def sides_kernel(grads_ref, keep_left_ref, sib_left_ref, keep_right_ref, sib_right_ref, low_ref, high_ref, left_ref, right_ref):
-    to_left = chip_sum(grads_ref, keep_left_ref, sib_left_ref)
-    to_right = chip_sum(grads_ref, keep_right_ref, sib_right_ref)
-
-    @pl.when(pl.program_id(0) == 0)
-    def _():
-        left_ref[...] = to_left.astype(left_ref.dtype)
-        right_ref[...] = (to_right + low_ref[...].astype(jnp.float32)).astype(right_ref.dtype)
-
-    @pl.when(pl.program_id(0) == 1)
-    def _():
-        left_ref[...] = (to_left + high_ref[...].astype(jnp.float32)).astype(left_ref.dtype)
-        right_ref[...] = to_right.astype(right_ref.dtype)
+def sides_kernel(grads_low_ref, grads_high_ref, keep_ref, sib_ref, low_ref, high_ref, right_low_ref, left_high_ref):
+    value = chip_sum(grads_low_ref[...], keep_ref[1], sib_ref[1]) + low_ref[...].astype(jnp.float32)
+    right_low_ref[...] = value.astype(right_low_ref.dtype)
+    value = chip_sum(grads_high_ref[...], keep_ref[0], sib_ref[0]) + high_ref[...].astype(jnp.float32)
+    left_high_ref[...] = value.astype(left_high_ref.dtype)
 
 
 def sides(grads_value, keep, sib, low, high):
     _, wide, rows = grads_value.shape
     _, depth, block = keep.shape
     half = rows // 2
-    left = pl.BlockSpec((1, depth, block), lambda i: (1, 0, 0))
-    right = pl.BlockSpec((1, depth, block), lambda i: (2, 0, 0))
+    weights = pl.BlockSpec((pl.Element(2), pl.Element(depth), pl.Element(block)), lambda i: (1, 0, 0))
     whole = pl.BlockSpec((half, block), lambda i: (0, 0))
-    by_half = pl.BlockSpec((half, block), lambda i: (i, 0))
-    out = jax.ShapeDtypeStruct((rows, block), jnp.bfloat16)
+    out = jax.ShapeDtypeStruct((half, block), jnp.bfloat16)
     return pl.pallas_call(
         sides_kernel,
-        grid=(2,),
-        in_specs=[pl.BlockSpec((CORES, wide, half), lambda i: (0, 0, i)), left, left, right, right, whole, whole],
-        out_specs=[by_half] * 2,
+        grid=(1,),
+        in_specs=[
+            pl.BlockSpec((CORES, wide, half), lambda i: (0, 0, 0)),
+            pl.BlockSpec((CORES, wide, half), lambda i: (0, 0, 1)),
+            weights,
+            weights,
+            whole,
+            whole,
+        ],
+        out_specs=[whole] * 2,
         out_shape=(out, out),
         compiler_params=BIG,
         name="sides",
-    )(grads_value, keep, sib, keep, sib, low, high)
-
-
-def total_kernel(grads_ref, keep_ref, sib_ref, a_ref, b_ref, out_ref):
-    value = chip_sum(grads_ref, keep_ref, sib_ref)
-    value = value + a_ref[...].astype(jnp.float32) + b_ref[...].astype(jnp.float32)
-    out_ref[...] = value.astype(out_ref.dtype)
+    )(grads_value, grads_value, keep, sib, low, high)
+
+
+def total_kernel(grads_ref, keep_ref, sib_ref, a_low_ref, a_high_ref, b_low_ref, b_high_ref, out_ref):
+    value = chip_sum(grads_ref[...], keep_ref[0], sib_ref[0])
+
+    def store(a_ref, b_ref):
+        out_ref[...] = (value + a_ref[...].astype(jnp.float32) + b_ref[...].astype(jnp.float32)).astype(out_ref.dtype)
+
+    @pl.when(pl.program_id(0) == 0)
+    def _():
+        store(a_low_ref, b_low_ref)
+
+    @pl.when(pl.program_id(0) == 1)
+    def _():
+        store(a_high_ref, b_high_ref)
 
 
 def total(grads_value, keep, sib, a, b):
@@ -244,16 +263,16 @@
     _, depth, block = keep.shape
     half = rows // 2
     own = pl.BlockSpec((1, depth, block), lambda i: (0, 0, 0))
-    by_half = pl.BlockSpec((half, block), lambda i: (i, 0))
+    whole = pl.BlockSpec((half, block), lambda i: (0, 0))
     return pl.pallas_call(
         total_kernel,
         grid=(2,),
-        in_specs=[pl.BlockSpec((CORES, wide, half), lambda i: (0, 0, i)), own, own, by_half, by_half],
-        out_specs=by_half,
+        in_specs=[pl.BlockSpec((CORES, wide, half), lambda i: (0, 0, i)), own, own] + [whole] * 4,
+        out_specs=pl.BlockSpec((half, block), lambda i: (i, 0)),
         out_shape=jax.ShapeDtypeStruct((rows, block), jnp.bfloat16),
         compiler_params=BIG,
         name="total",
-    )(grads_value, keep, sib, a, b)
+    )(grads_value, keep, sib, *a, *b)
 
 
 def combine_kernel(hi_ref, lo_ref, back_ref, out_ref):
@@ -299,17 +318,20 @@
     blocks = jnp.concatenate([keep_blocks, keep_blocks ^ 1])
     keep, give = pack(blocks, weights)
     sib = to_sibling(give)
-    left, right = to_right(own), to_left(own)
     half = own.shape[0] // 2
-    opposite_low, opposite_high = to_right(left[:half]), to_left(right[half:])
-    mine = first(own, left, right, keep, sib)
+    low, high = own[:half], own[half:]
+    left_low, right_high = to_right(low), to_left(high)
+    left_high, right_low = to_right(high), to_left(low)
+    opposite_low, opposite_high = to_right(left_low), to_left(right_high)
+    mine = first(own, (left_low, left_high), (right_low, right_high), keep, sib)
     mine = second(opposite_low, opposite_high, keep, sib, mine)
     theirs = to_sibling(mine)
-    grads_value, part_low, part_high = grads(mine, theirs, keep, sib)
+    grads_value, part_low, part_high, for_left_low, for_right_high = grads(mine, theirs, keep, sib)
     got_low, got_high = to_right(part_low), to_left(part_high)
-    for_left, for_right = sides(grads_value, keep, sib, got_low, got_high)
-    from_left, from_right = to_right(for_right), to_left(for_left)
-    return total(grads_value, keep, sib, from_left, from_right)
+    from_left_high, from_right_low = to_right(for_right_high), to_left(for_left_low)
+    for_right_low, for_left_high = sides(grads_value, keep, sib, got_low, got_high)
+    from_left_low, from_right_high = to_right(for_right_low), to_left(for_left_high)
+    return total(grads_value, keep, sib, (from_left_low, from_left_high), (from_right_low, from_right_high))
 
 
 def shards(activations, out_grad, routes, gate_vals, w_gate, w_up, w_down):

time: 165 us -> 155 us (0.939)
  waiting for transfers between devices: 70.4 us -> 51.5 us
  starting transfers between devices: 43.8 us -> 55.5 us
  blocking collectives: 28.2 us -> 25.6 us
    ppermute x10 -> x14, waiting for transfers between devices: 49 us -> 30.1 us  [send(): return lax.ppermute(value, 'tp', [(i, to(i)) for i in range(CHIPS * CORES)])]
    ppermute x10 -> x14, starting transfers between devices: 27.2 us -> 38.9 us  [send(): return lax.ppermute(value, 'tp', [(i, to(i)) for i in range(CHIPS * CORES)])]
    all_to_all x1, blocking collectives: 28.2 us -> 25.6 us  [exchange(): lax.all_to_all(blocks, 'tok', split_axis=0, concat_axis=0, tiled=True)]
  transfers between devices with their start and end apart: 11 -> 15, of which waited for: 9 -> 9; matrix products, arithmetic and copies ran while one was open for 0% -> 0% of each run, Pallas kernels for 5% -> 6%
where the time goes in v3:
time: 155 us; the launch traced here: 154 us
  starting transfers between devices  55.5 us (36%)
  waiting for transfers between devices  51.5 us (33%)
  blocking collectives  25.6 us (17%)
  Pallas kernels  19 us (12%)
  local copies, waits for them, and re-layouts  1.74 us (1%)
    ppermute x14, starting transfers between devices, send(): return lax.ppermute(value, 'tp', [(i, to(i)) for i in range(CHIPS * CORES)])  38.9 us
    ppermute x14, waiting for transfers between devices, send(): return lax.ppermute(value, 'tp', [(i, to(i)) for i in range(CHIPS * CORES)])  30.1 us
    all_to_all x1, blocking collectives, exchange(): lax.all_to_all(blocks, 'tok', split_axis=0, concat_axis=0, tiled=True)  25.6 us
    all_to_all x1, waiting for transfers between devices, exchange(): lax.all_to_all(blocks, 'tok', split_axis=0, concat_axis=0, tiled=True)  21.4 us
    all_to_all x1, starting transfers between devices, exchange(): lax.all_to_all(blocks, 'tok', split_axis=0, concat_axis=0, tiled=True)  16.6 us
    pallas_call x1, Pallas kernels, pack(): pl.pallas_call(pack_kernel, grid_spec=pltpu.PrefetchScalarGridSpec(num_sc...  5.83 us
  transfers between devices with their start and end apart: 15, of which 9 were waited for; matrix products, arithmetic and copies ran while one was open for 0% of the time, Pallas kernels for 6%

profile of v3, /device:TPU:6, one launch (start us, length us, event | category | flops | bytes accessed | tf_op | source)
XLA Modules:
  0.0 154.1 jit_solution(9171488054537281584)
XLA Ops:
  0.0 0.0 copy-start.1
  0.0 2.6 %dispatch.1 = (bf16[512,1024]{1,0:T(8,128)(2,1)}, bf16[128,512]{1,0:T(8,128)(2,1)}, bf16[128,512]{1,0:T(8,128)(2,1)}) custom-call(s32[2,128]{1,0:T(2,128)} %bitcast.23, f32[2,128]{1,0:T(2,128)} %bitcast.24, bf16[128,512]{1,0:T(8,128)(2,1)} %x_ref.1, bf16[128,512]{1,0:T(8,128)(2,1)} %g_ref.1), custom_call_target="tpu_custom_call" | custom-call | tf_op jit(solution)/shard_map/dispatch/pallas_call | solution.py:50
  2.6 16.6 %all-to-all-start = ((bf16[64,8,1024]{2,1,0:T(8,128)(2,1)}), bf16[64,8,1024]{2,1,0:T(8,128)(2,1)S(1)}, u32[]{:S(2)}, u32[]{:S(2)}) async-start(bf16[64,8,1024]{2,1,0:T(8,128)(2,1)} %bitcast.22), calls=%async_computation | async-start | bytes 2097152 | tf_op jit(solution)/shard_map/all_to_all | solution.py:295
  19.2 0.0 copy-done.1
  19.3 0.6 pad_add_fusion.blocks_ref
  19.8 5.8 %pack.1 = (bf16[4,576,512]{2,1,0:T(8,128)(2,1)}, bf16[4,576,512]{2,1,0:T(8,128)(2,1)}) custom-call(s32[8]{0:T(128)} %pad_add_fusion.blocks_ref, bf16[192,4096]{1,0:T(8,128)(2,1)} %bitcast.15, bf16[192,4096]{1,0:T(8,128)(2,1)} %bitcast.17, bf16[192,4096]{1,0:T(8,128)(2,1)} %bitcast.19, bf16[192,4096]{1,0:T(8,128)(2,1)} %bitcast.16, ...), custom_call_target="tpu_custom_call" | custom-call | tf_op jit(solution)/shard_map/pack/pallas_call | solution.py:72
  25.7 1.9 %collective-permute-start.4 = (bf16[4,576,512]{2,1,0:T(8,128)(2,1)}, bf16[4,576,512]{2,1,0:T(8,128)(2,1)S(1)}, u32[]{:S(2)}, u32[]{:S(2)}) collective-permute-start(bf16[4,576,512]{2,1,0:T(8,128)(2,1)} %get-tuple-element.29), channel_id=1, source_target_pairs={{0,1},{1,0},{2,3},{3,2},{4,5},{5,4},{6,7},{7,6},{8,9},{9,8},{10,11... | collective-permute-start | bytes 7077896 | tf_op jit(solution)/shard_map/ppermute | solution.py:299
  27.6 21.4 %all-to-all-done = bf16[64,8,1024]{2,1,0:T(8,128)(2,1)S(1)} async-done(((bf16[64,8,1024]{2,1,0:T(8,128)(2,1)}), bf16[64,8,1024]{2,1,0:T(8,128)(2,1)S(1)}, u32[]{:S(2)}, u32[]{:S(2)}) %all-to-all-start) | async-done | bytes 1048608 | tf_op jit(solution)/shard_map/all_to_all | solution.py:295
  49.0 0.1 slice_bitcast_fusion
  49.1 2.4 %collective-permute-start = (bf16[256,1024]{1,0:T(8,128)(2,1)S(1)}, bf16[256,1024]{1,0:T(8,128)(2,1)S(1)}, u32[]{:S(2)}, u32[]{:S(2)}) collective-permute-start(bf16[256,1024]{1,0:T(8,128)(2,1)S(1)} %get-tuple-element.40), channel_id=1, source_target_pairs={{0,2},{1,3},{2,4},{3,5},{4,6},{5,7},{6,0},{7,1},{8,10},{9,11},{10,... | collective-permute-start | bytes 1572872 | tf_op jit(solution)/shard_map/ppermute | solution.py:299
  51.5 3.5 %collective-permute-start.2 = (bf16[256,1024]{1,0:T(8,128)(2,1)S(1)}, bf16[256,1024]{1,0:T(8,128)(2,1)S(1)}, u32[]{:S(2)}, u32[]{:S(2)}) collective-permute-start(bf16[256,1024]{1,0:T(8,128)(2,1)S(1)} %get-tuple-element.39), channel_id=1, source_target_pairs={{0,6},{1,7},{2,0},{3,1},{4,2},{5,3},{6,4},{7,5},{8,14},{9,15},{10,... | collective-permute-start | bytes 1572872 | tf_op jit(solution)/shard_map/ppermute | solution.py:299
  54.9 3.6 %collective-permute-start.5 = (bf16[256,1024]{1,0:T(8,128)(2,1)S(1)}, bf16[256,1024]{1,0:T(8,128)(2,1)S(1)}, u32[]{:S(2)}, u32[]{:S(2)}) collective-permute-start(bf16[256,1024]{1,0:T(8,128)(2,1)S(1)} %get-tuple-element.39), channel_id=1, source_target_pairs={{0,2},{1,3},{2,4},{3,5},{4,6},{5,7},{6,0},{7,1},{8,10},{9,11},{10,... | collective-permute-start | bytes 1572872 | tf_op jit(solution)/shard_map/ppermute | solution.py:299
  58.5 2.3 %collective-permute-start.6 = (bf16[256,1024]{1,0:T(8,128)(2,1)S(1)}, bf16[256,1024]{1,0:T(8,128)(2,1)S(1)}, u32[]{:S(2)}, u32[]{:S(2)}) collective-permute-start(bf16[256,1024]{1,0:T(8,128)(2,1)S(1)} %get-tuple-element.40), channel_id=1, source_target_pairs={{0,6},{1,7},{2,0},{3,1},{4,2},{5,3},{6,4},{7,5},{8,14},{9,15},{10,... | collective-permute-start | bytes 1572872 | tf_op jit(solution)/shard_map/ppermute | solution.py:299
  60.8 5.0 %collective-permute-done.left_low_ref = bf16[256,1024]{1,0:T(8,128)(2,1)S(1)} collective-permute-done((bf16[256,1024]{1,0:T(8,128)(2,1)S(1)}, bf16[256,1024]{1,0:T(8,128)(2,1)S(1)}, u32[]{:S(2)}, u32[]{:S(2)}) %collective-permute-start) | collective-permute-done | bytes 524320 | tf_op jit(solution)/shard_map/ppermute | solution.py:299
  65.8 3.6 %collective-permute-start.1 = (bf16[256,1024]{1,0:T(8,128)(2,1)S(1)}, bf16[256,1024]{1,0:T(8,128)(2,1)S(1)}, u32[]{:S(2)}, u32[]{:S(2)}) collective-permute-start(bf16[256,1024]{1,0:T(8,128)(2,1)S(1)} %collective-permute-done.left_low_ref), channel_id=1, source_target_pairs={{0,2},{1,3},{2,4},{3,5},{4,6},{5,7},{6,0},{7,1},{8,10},{9,11},{10,... | collective-permute-start | bytes 1572872 | tf_op jit(solution)/shard_map/ppermute | solution.py:299
  69.4 0.0 collective-permute-done.2.right_high_ref
  69.4 2.3 %collective-permute-start.3 = (bf16[256,1024]{1,0:T(8,128)(2,1)S(1)}, bf16[256,1024]{1,0:T(8,128)(2,1)S(1)}, u32[]{:S(2)}, u32[]{:S(2)}) collective-permute-start(bf16[256,1024]{1,0:T(8,128)(2,1)S(1)} %collective-permute-done.2.right_high_ref), channel_id=1, source_target_pairs={{0,6},{1,7},{2,0},{3,1},{4,2},{5,3},{6,4},{7,5},{8,14},{9,15},{10,... | collective-permute-start | bytes 1572872 | tf_op jit(solution)/shard_map/ppermute | solution.py:299
  71.7 0.0 collective-permute-done.4.sib_ref
  71.7 5.4 %collective-permute-done.5.left_high_ref = bf16[256,1024]{1,0:T(8,128)(2,1)S(1)} collective-permute-done((bf16[256,1024]{1,0:T(8,128)(2,1)S(1)}, bf16[256,1024]{1,0:T(8,128)(2,1)S(1)}, u32[]{:S(2)}, u32[]{:S(2)}) %collective-permute-start.5) | collective-permute-done | bytes 524320 | tf_op jit(solution)/shard_map/ppermute | solution.py:299
  77.1 3.6 %collective-permute-done.6.right_low_ref = bf16[256,1024]{1,0:T(8,128)(2,1)S(1)} collective-permute-done((bf16[256,1024]{1,0:T(8,128)(2,1)S(1)}, bf16[256,1024]{1,0:T(8,128)(2,1)S(1)}, u32[]{:S(2)}, u32[]{:S(2)}) %collective-permute-start.6) | collective-permute-done | bytes 524320 | tf_op jit(solution)/shard_map/ppermute | solution.py:299
  80.7 0.0 copy-start
  80.7 1.7 %copy-done = bf16[4,576,512]{2,1,0:T(8,128)(2,1)S(1)} copy-done((bf16[4,576,512]{2,1,0:T(8,128)(2,1)S(1)}, bf16[4,576,512]{2,1,0:T(8,128)(2,1)}, u32[]{:S(2)}) %copy-start) | copy-done | bytes 2359320
  82.3 2.7 %first.1.sum_ref = f32[2,576,512]{2,1,0:T(8,128)S(1)} custom-call(bf16[512,1024]{1,0:T(8,128)(2,1)S(1)} %bitcast.13, bf16[256,1024]{1,0:T(8,128)(2,1)S(1)} %collective-permute-done.left_low_ref, bf16[256,1024]{1,0:T(8,128)(2,1)S(1)} %collective-permute-done.5.left_high_ref, bf16[256,1024]{1,0:T(8,128)(2,1)S(1)} %collective-permute-done.6.right_low_ref, ...), custom_call_target="tpu_custom_call" | custom-call | tf_op jit(solution)/shard_map/first/pallas_call | solution.py:118
  85.0 0.0 collective-permute-done.1.low_ref
  85.1 2.8 %collective-permute-done.3.high_ref = bf16[256,1024]{1,0:T(8,128)(2,1)S(1)} collective-permute-done((bf16[256,1024]{1,0:T(8,128)(2,1)S(1)}, bf16[256,1024]{1,0:T(8,128)(2,1)S(1)}, u32[]{:S(2)}, u32[]{:S(2)}) %collective-permute-start.3) | collective-permute-done | bytes 524320 | tf_op jit(solution)/shard_map/ppermute | solution.py:299
  87.8 1.5 second.1.mine_ref
  89.3 1.9 %collective-permute-start.7 = (f32[2,576,512]{2,1,0:T(8,128)S(1)}, f32[2,576,512]{2,1,0:T(8,128)S(1)}, u32[]{:S(2)}, u32[]{:S(2)}) collective-permute-start(f32[2,576,512]{2,1,0:T(8,128)S(1)} %second.1.mine_ref), channel_id=1, source_target_pairs={{0,1},{1,0},{2,3},{3,2},{4,5},{5,4},{6,7},{7,6},{8,9},{9,8},{10,11... | collective-permute-start | bytes 7077896 | tf_op jit(solution)/shard_map/ppermute | solution.py:299
  91.2 4.5 %collective-permute-done.7.theirs_ref = f32[2,576,512]{2,1,0:T(8,128)S(1)} collective-permute-done((f32[2,576,512]{2,1,0:T(8,128)S(1)}, f32[2,576,512]{2,1,0:T(8,128)S(1)}, u32[]{:S(2)}, u32[]{:S(2)}) %collective-permute-start.7) | collective-permute-done | bytes 2359328 | tf_op jit(solution)/shard_map/ppermute | solution.py:299
  95.8 2.3 %grads.1 = (bf16[2,384,512]{2,1,0:T(8,128)(2,1)S(1)}, bf16[256,512]{1,0:T(8,128)(2,1)S(1)}, bf16[256,512]{1,0:T(8,128)(2,1)S(1)}, bf16[256,512]{1,0:T(8,128)(2,1)S(1)}, bf16[256,512]{1,0:T(8,128)(2,1)S(1)}) custom-call(f32[2,576,512]{2,1,0:T(8,128)S(1)} %second.1.mine_ref, f32[2,576,512]{2,1,0:T(8,128)S(1)} %collective-permute-done.7.theirs_ref, ...), custom_call_target="tpu_custom_call" | custom-call | tf_op jit(solution)/shard_map/grads/pallas_call | solution.py:203
  98.1 2.2 %collective-permute-start.8 = (bf16[256,512]{1,0:T(8,128)(2,1)S(1)}, bf16[256,512]{1,0:T(8,128)(2,1)S(1)}, u32[]{:S(2)}, u32[]{:S(2)}) collective-permute-start(bf16[256,512]{1,0:T(8,128)(2,1)S(1)} %get-tuple-element.31), channel_id=1, source_target_pairs={{0,2},{1,3},{2,4},{3,5},{4,6},{5,7},{6,0},{7,1},{8,10},{9,11},{10,... | collective-permute-start | bytes 786440 | tf_op jit(solution)/shard_map/ppermute | solution.py:299
  100.3 3.7 %collective-permute-start.9 = (bf16[256,512]{1,0:T(8,128)(2,1)S(1)}, bf16[256,512]{1,0:T(8,128)(2,1)S(1)}, u32[]{:S(2)}, u32[]{:S(2)}) collective-permute-start(bf16[256,512]{1,0:T(8,128)(2,1)S(1)} %get-tuple-element.32), channel_id=1, source_target_pairs={{0,6},{1,7},{2,0},{3,1},{4,2},{5,3},{6,4},{7,5},{8,14},{9,15},{10,... | collective-permute-start | bytes 786440 | tf_op jit(solution)/shard_map/ppermute | solution.py:299
  103.9 3.4 %collective-permute-start.11 = (bf16[256,512]{1,0:T(8,128)(2,1)S(1)}, bf16[256,512]{1,0:T(8,128)(2,1)S(1)}, u32[]{:S(2)}, u32[]{:S(2)}) collective-permute-start(bf16[256,512]{1,0:T(8,128)(2,1)S(1)} %get-tuple-element.34), channel_id=1, source_target_pairs={{0,2},{1,3},{2,4},{3,5},{4,6},{5,7},{6,0},{7,1},{8,10},{9,11},{10,... | collective-permute-start | bytes 786440 | tf_op jit(solution)/shard_map/ppermute | solution.py:299
  107.3 2.5 %collective-permute-start.12 = (bf16[256,512]{1,0:T(8,128)(2,1)S(1)}, bf16[256,512]{1,0:T(8,128)(2,1)S(1)}, u32[]{:S(2)}, u32[]{:S(2)}) collective-permute-start(bf16[256,512]{1,0:T(8,128)(2,1)S(1)} %get-tuple-element.35), channel_id=1, source_target_pairs={{0,6},{1,7},{2,0},{3,1},{4,2},{5,3},{6,4},{7,5},{8,14},{9,15},{10,... | collective-permute-start | bytes 786440 | tf_op jit(solution)/shard_map/ppermute | solution.py:299
  109.8 0.0 collective-permute-done.8.low_ref
  109.8 1.7 %collective-permute-done.9.high_ref = bf16[256,512]{1,0:T(8,128)(2,1)S(1)} collective-permute-done((bf16[256,512]{1,0:T(8,128)(2,1)S(1)}, bf16[256,512]{1,0:T(8,128)(2,1)S(1)}, u32[]{:S(2)}, u32[]{:S(2)}) %collective-permute-start.9) | collective-permute-done | bytes 262176 | tf_op jit(solution)/shard_map/ppermute | solution.py:299
  111.5 0.7 sides.1
  112.2 3.0 %collective-permute-start.10 = (bf16[256,512]{1,0:T(8,128)(2,1)S(1)}, bf16[256,512]{1,0:T(8,128)(2,1)S(1)}, u32[]{:S(2)}, u32[]{:S(2)}) collective-permute-start(bf16[256,512]{1,0:T(8,128)(2,1)S(1)} %get-tuple-element.33), channel_id=1, source_target_pairs={{0,2},{1,3},{2,4},{3,5},{4,6},{5,7},{6,0},{7,1},{8,10},{9,11},{10,... | collective-permute-start | bytes 786440 | tf_op jit(solution)/shard_map/ppermute | solution.py:299
  115.2 2.9 %collective-permute-start.13 = (bf16[256,512]{1,0:T(8,128)(2,1)S(1)}, bf16[256,512]{1,0:T(8,128)(2,1)S(1)}, u32[]{:S(2)}, u32[]{:S(2)}) collective-permute-start(bf16[256,512]{1,0:T(8,128)(2,1)S(1)} %get-tuple-element.36), channel_id=1, source_target_pairs={{0,6},{1,7},{2,0},{3,1},{4,2},{5,3},{6,4},{7,5},{8,14},{9,15},{10,... | collective-permute-start | bytes 786440 | tf_op jit(solution)/shard_map/ppermute | solution.py:299
  118.0 0.0 collective-permute-done.11.a_high_ref
  118.1 0.0 collective-permute-done.12.b_low_ref
  118.1 3.2 %collective-permute-done.10.a_low_ref = bf16[256,512]{1,0:T(8,128)(2,1)S(1)} collective-permute-done((bf16[256,512]{1,0:T(8,128)(2,1)S(1)}, bf16[256,512]{1,0:T(8,128)(2,1)S(1)}, u32[]{:S(2)}, u32[]{:S(2)}) %collective-permute-start.10) | collective-permute-done | bytes 262176 | tf_op jit(solution)/shard_map/ppermute | solution.py:299
  121.3 3.9 %collective-permute-done.13.b_high_ref = bf16[256,512]{1,0:T(8,128)(2,1)S(1)} collective-permute-done((bf16[256,512]{1,0:T(8,128)(2,1)S(1)}, bf16[256,512]{1,0:T(8,128)(2,1)S(1)}, u32[]{:S(2)}, u32[]{:S(2)}) %collective-permute-start.13) | collective-permute-done | bytes 262176 | tf_op jit(solution)/shard_map/ppermute | solution.py:299
  125.2 1.2 total.1
  126.4 25.6 %all_to_all.10 = bf16[64,8,512]{2,1,0:T(8,128)(2,1)} all-to-all(bf16[64,8,512]{2,1,0:T(8,128)(2,1)S(1)} %bitcast.14), channel_id=1, replica_groups=mesh['tok'=64,'tp'=8] {'tok'}, dimensions={0} | all-to-all | bytes 1048576 | tf_op jit(solution)/shard_map/all_to_all | solution.py:295
  152.0 2.1 %combine.1 = bf16[128,512]{1,0:T(8,128)(2,1)} custom-call(bf16[128,512]{1,0:T(8,128)(2,1)} %get-tuple-element.21.hi_ref, bf16[128,512]{1,0:T(8,128)(2,1)} %get-tuple-element.22.lo_ref, bf16[512,512]{1,0:T(8,128)(2,1)} %bitcast.21), custom_call_target="tpu_custom_call" | custom-call | tf_op jit(solution)/shard_map/combine/pallas_call | solution.py:286
  (1 shorter events, 0.0 us)
Async XLA Ops:
  0.0 19.2 %copy-start.1 = (s32[4]{0:T(128)S(1)}, s32[4]{0:T(128)}, u32[]{:S(2)}) copy-start(s32[4]{0:T(128)} %constant.4.clone) | copy-start | bytes 52
  2.6 46.4 %all-to-all-start = ((bf16[64,8,1024]{2,1,0:T(8,128)(2,1)}), bf16[64,8,1024]{2,1,0:T(8,128)(2,1)S(1)}, u32[]{:S(2)}, u32[]{:S(2)}) async-start(bf16[64,8,1024]{2,1,0:T(8,128)(2,1)} %bitcast.22), calls=%async_computation | async-start | bytes 2097152 | tf_op jit(solution)/shard_map/all_to_all | solution.py:295
  25.7 46.0 %collective-permute-start.4 = (bf16[4,576,512]{2,1,0:T(8,128)(2,1)}, bf16[4,576,512]{2,1,0:T(8,128)(2,1)S(1)}, u32[]{:S(2)}, u32[]{:S(2)}) collective-permute-start(bf16[4,576,512]{2,1,0:T(8,128)(2,1)} %get-tuple-element.29), channel_id=1, source_target_pairs={{0,1},{1,0},{2,3},{3,2},{4,5},{5,4},{6,7},{7,6},{8,9},{9,8},{10,11... | collective-permute-start | bytes 7077896 | tf_op jit(solution)/shard_map/ppermute | solution.py:299
  49.1 16.8 %collective-permute-start = (bf16[256,1024]{1,0:T(8,128)(2,1)S(1)}, bf16[256,1024]{1,0:T(8,128)(2,1)S(1)}, u32[]{:S(2)}, u32[]{:S(2)}) collective-permute-start(bf16[256,1024]{1,0:T(8,128)(2,1)S(1)} %get-tuple-element.40), channel_id=1, source_target_pairs={{0,2},{1,3},{2,4},{3,5},{4,6},{5,7},{6,0},{7,1},{8,10},{9,11},{10,... | collective-permute-start | bytes 1572872 | tf_op jit(solution)/shard_map/ppermute | solution.py:299
  51.5 18.0 %collective-permute-start.2 = (bf16[256,1024]{1,0:T(8,128)(2,1)S(1)}, bf16[256,1024]{1,0:T(8,128)(2,1)S(1)}, u32[]{:S(2)}, u32[]{:S(2)}) collective-permute-start(bf16[256,1024]{1,0:T(8,128)(2,1)S(1)} %get-tuple-element.39), channel_id=1, source_target_pairs={{0,6},{1,7},{2,0},{3,1},{4,2},{5,3},{6,4},{7,5},{8,14},{9,15},{10,... | collective-permute-start | bytes 1572872 | tf_op jit(solution)/shard_map/ppermute | solution.py:299
  54.9 22.1 %collective-permute-start.5 = (bf16[256,1024]{1,0:T(8,128)(2,1)S(1)}, bf16[256,1024]{1,0:T(8,128)(2,1)S(1)}, u32[]{:S(2)}, u32[]{:S(2)}) collective-permute-start(bf16[256,1024]{1,0:T(8,128)(2,1)S(1)} %get-tuple-element.39), channel_id=1, source_target_pairs={{0,2},{1,3},{2,4},{3,5},{4,6},{5,7},{6,0},{7,1},{8,10},{9,11},{10,... | collective-permute-start | bytes 1572872 | tf_op jit(solution)/shard_map/ppermute | solution.py:299
  58.5 22.1 %collective-permute-start.6 = (bf16[256,1024]{1,0:T(8,128)(2,1)S(1)}, bf16[256,1024]{1,0:T(8,128)(2,1)S(1)}, u32[]{:S(2)}, u32[]{:S(2)}) collective-permute-start(bf16[256,1024]{1,0:T(8,128)(2,1)S(1)} %get-tuple-element.40), channel_id=1, source_target_pairs={{0,6},{1,7},{2,0},{3,1},{4,2},{5,3},{6,4},{7,5},{8,14},{9,15},{10,... | collective-permute-start | bytes 1572872 | tf_op jit(solution)/shard_map/ppermute | solution.py:299
  65.8 19.2 %collective-permute-start.1 = (bf16[256,1024]{1,0:T(8,128)(2,1)S(1)}, bf16[256,1024]{1,0:T(8,128)(2,1)S(1)}, u32[]{:S(2)}, u32[]{:S(2)}) collective-permute-start(bf16[256,1024]{1,0:T(8,128)(2,1)S(1)} %collective-permute-done.left_low_ref), channel_id=1, source_target_pairs={{0,2},{1,3},{2,4},{3,5},{4,6},{5,7},{6,0},{7,1},{8,10},{9,11},{10,... | collective-permute-start | bytes 1572872 | tf_op jit(solution)/shard_map/ppermute | solution.py:299
  69.4 18.4 %collective-permute-start.3 = (bf16[256,1024]{1,0:T(8,128)(2,1)S(1)}, bf16[256,1024]{1,0:T(8,128)(2,1)S(1)}, u32[]{:S(2)}, u32[]{:S(2)}) collective-permute-start(bf16[256,1024]{1,0:T(8,128)(2,1)S(1)} %collective-permute-done.2.right_high_ref), channel_id=1, source_target_pairs={{0,6},{1,7},{2,0},{3,1},{4,2},{5,3},{6,4},{7,5},{8,14},{9,15},{10,... | collective-permute-start | bytes 1572872 | tf_op jit(solution)/shard_map/ppermute | solution.py:299
  80.7 1.7 %copy-start = (bf16[4,576,512]{2,1,0:T(8,128)(2,1)S(1)}, bf16[4,576,512]{2,1,0:T(8,128)(2,1)}, u32[]{:S(2)}) copy-start(bf16[4,576,512]{2,1,0:T(8,128)(2,1)} %get-tuple-element.28.keep_ref) | copy-start | bytes 7077892
  89.3 6.4 %collective-permute-start.7 = (f32[2,576,512]{2,1,0:T(8,128)S(1)}, f32[2,576,512]{2,1,0:T(8,128)S(1)}, u32[]{:S(2)}, u32[]{:S(2)}) collective-permute-start(f32[2,576,512]{2,1,0:T(8,128)S(1)} %second.1.mine_ref), channel_id=1, source_target_pairs={{0,1},{1,0},{2,3},{3,2},{4,5},{5,4},{6,7},{7,6},{8,9},{9,8},{10,11... | collective-permute-start | bytes 7077896 | tf_op jit(solution)/shard_map/ppermute | solution.py:299
  98.1 11.7 %collective-permute-start.8 = (bf16[256,512]{1,0:T(8,128)(2,1)S(1)}, bf16[256,512]{1,0:T(8,128)(2,1)S(1)}, u32[]{:S(2)}, u32[]{:S(2)}) collective-permute-start(bf16[256,512]{1,0:T(8,128)(2,1)S(1)} %get-tuple-element.31), channel_id=1, source_target_pairs={{0,2},{1,3},{2,4},{3,5},{4,6},{5,7},{6,0},{7,1},{8,10},{9,11},{10,... | collective-permute-start | bytes 786440 | tf_op jit(solution)/shard_map/ppermute | solution.py:299
  100.3 11.2 %collective-permute-start.9 = (bf16[256,512]{1,0:T(8,128)(2,1)S(1)}, bf16[256,512]{1,0:T(8,128)(2,1)S(1)}, u32[]{:S(2)}, u32[]{:S(2)}) collective-permute-start(bf16[256,512]{1,0:T(8,128)(2,1)S(1)} %get-tuple-element.32), channel_id=1, source_target_pairs={{0,6},{1,7},{2,0},{3,1},{4,2},{5,3},{6,4},{7,5},{8,14},{9,15},{10,... | collective-permute-start | bytes 786440 | tf_op jit(solution)/shard_map/ppermute | solution.py:299
  103.9 14.1 %collective-permute-start.11 = (bf16[256,512]{1,0:T(8,128)(2,1)S(1)}, bf16[256,512]{1,0:T(8,128)(2,1)S(1)}, u32[]{:S(2)}, u32[]{:S(2)}) collective-permute-start(bf16[256,512]{1,0:T(8,128)(2,1)S(1)} %get-tuple-element.34), channel_id=1, source_target_pairs={{0,2},{1,3},{2,4},{3,5},{4,6},{5,7},{6,0},{7,1},{8,10},{9,11},{10,... | collective-permute-start | bytes 786440 | tf_op jit(solution)/shard_map/ppermute | solution.py:299
  107.3 10.7 %collective-permute-start.12 = (bf16[256,512]{1,0:T(8,128)(2,1)S(1)}, bf16[256,512]{1,0:T(8,128)(2,1)S(1)}, u32[]{:S(2)}, u32[]{:S(2)}) collective-permute-start(bf16[256,512]{1,0:T(8,128)(2,1)S(1)} %get-tuple-element.35), channel_id=1, source_target_pairs={{0,6},{1,7},{2,0},{3,1},{4,2},{5,3},{6,4},{7,5},{8,14},{9,15},{10,... | collective-permute-start | bytes 786440 | tf_op jit(solution)/shard_map/ppermute | solution.py:299
  112.2 9.1 %collective-permute-start.10 = (bf16[256,512]{1,0:T(8,128)(2,1)S(1)}, bf16[256,512]{1,0:T(8,128)(2,1)S(1)}, u32[]{:S(2)}, u32[]{:S(2)}) collective-permute-start(bf16[256,512]{1,0:T(8,128)(2,1)S(1)} %get-tuple-element.33), channel_id=1, source_target_pairs={{0,2},{1,3},{2,4},{3,5},{4,6},{5,7},{6,0},{7,1},{8,10},{9,11},{10,... | collective-permute-start | bytes 786440 | tf_op jit(solution)/shard_map/ppermute | solution.py:299
  115.2 10.1 %collective-permute-start.13 = (bf16[256,512]{1,0:T(8,128)(2,1)S(1)}, bf16[256,512]{1,0:T(8,128)(2,1)S(1)}, u32[]{:S(2)}, u32[]{:S(2)}) collective-permute-start(bf16[256,512]{1,0:T(8,128)(2,1)S(1)} %get-tuple-element.36), channel_id=1, source_target_pairs={{0,6},{1,7},{2,0},{3,1},{4,2},{5,3},{6,4},{7,5},{8,14},{9,15},{10,... | collective-permute-start | bytes 786440 | tf_op jit(solution)/shard_map/ppermute | solution.py:299

commit v4 on v2

v4 whole, which is shorter than its diff:
```python
import functools

import jax
import jax.numpy as jnp
from jax import lax
from jax.experimental import pallas as pl
from jax.experimental.pallas import tpu as pltpu
from jax.sharding import PartitionSpec as P

CHIPS = 4
CORES = 2
CONTRACT_LAST = (((1,), (1,)), ((), ()))
BIG = pltpu.CompilerParams(vmem_limit_bytes=40 * 1024 * 1024)


def places(routes_ref, values, n_tok, capacity):
    top_k, tok_dev = routes_ref.shape
    expert = lax.broadcasted_iota(jnp.int32, (n_tok, tok_dev), 0)
    named = jnp.zeros((n_tok, tok_dev), jnp.float32)
    weight = jnp.zeros((n_tok, tok_dev), jnp.float32)
    for k in range(top_k):
        hit = routes_ref[k : k + 1, :] == expert
        named = named + jnp.where(hit, 1.0, 0.0)
        weight = weight + jnp.where(hit, values[k], 0.0)
    earlier = lax.broadcasted_iota(jnp.int32, (tok_dev, tok_dev), 0)
    later = lax.broadcasted_iota(jnp.int32, (tok_dev, tok_dev), 1)
    ahead = jnp.where(earlier < later, 1.0, 0.0).astype(jnp.bfloat16)
    before = jnp.dot(named.astype(jnp.bfloat16), ahead, preferred_element_type=jnp.float32)
    before = jnp.where(named > 0.0, before, -1.0)
    slot = lax.broadcasted_iota(jnp.int32, (n_tok, capacity, tok_dev), 1).astype(jnp.float32)
    placed = jnp.where(before[:, None, :] == slot, weight[:, None, :], 0.0)
    return placed.reshape(n_tok * capacity, tok_dev)


def dispatch_kernel(n_tok, capacity, routes_ref, x_ref, g_ref, send_ref):
    width = x_ref.shape[1]
    placed = places(routes_ref, (1.0,) * routes_ref.shape[0], n_tok, capacity).astype(jnp.bfloat16)
    send_ref[:, :width] = jnp.dot(placed, x_ref[...], preferred_element_type=jnp.float32).astype(send_ref.dtype)
    send_ref[:, width:] = jnp.dot(placed, g_ref[...], preferred_element_type=jnp.float32).astype(send_ref.dtype)


def dispatch(routes, activations, out_grad, n_tok, capacity):
    width = activations.shape[1]
    return pl.pallas_call(
        functools.partial(dispatch_kernel, n_tok, capacity),
        out_shape=jax.ShapeDtypeStruct((n_tok * capacity, 2 * width), activations.dtype),
        name="dispatch",
    )(routes.T, activations, out_grad)


def mixer_kernel(n_tok, capacity, routes_ref, gates_ref, hi_ref, lo_ref):
    gates = [gates_ref[k : k + 1, :] for k in range(gates_ref.shape[0])]
    scaled = places(routes_ref, gates, n_tok, capacity).T
    high = scaled.astype(jnp.bfloat16)
    hi_ref[...] = high
    lo_ref[...] = (scaled - high.astype(jnp.float32)).astype(jnp.bfloat16)


def mixer(routes, gate_vals, n_tok, capacity):
    part = jax.ShapeDtypeStruct((routes.shape[0], n_tok * capacity), jnp.bfloat16)
    return pl.pallas_call(
        functools.partial(mixer_kernel, n_tok, capacity),
        out_shape=(part, part),
        name="mixer",
    )(routes.T, gate_vals.T)


def pack_kernel(blocks_ref, *refs):
    keep_ref, give_ref = refs[6:]
    hidden = refs[0].shape[0]
    for n in range(3):
        keep_ref[0, n * hidden : (n + 1) * hidden, :] = refs[n][...]
        give_ref[0, n * hidden : (n + 1) * hidden, :] = refs[3 + n][...]


def pack(blocks, weights):
    hidden, width = weights[0].shape
    block = width // (CHIPS * CORES)
    packed = jax.ShapeDtypeStruct((CHIPS, 3 * hidden, block), weights[0].dtype)
    keep = pl.BlockSpec((hidden, block), lambda i, blocks_ref: (0, blocks_ref[i]))
    give = pl.BlockSpec((hidden, block), lambda i, blocks_ref: (0, blocks_ref[i + CHIPS]))
    out = pl.BlockSpec((1, 3 * hidden, block), lambda i, blocks_ref: (i, 0, 0))
    return pl.pallas_call(
        pack_kernel,
        grid_spec=pltpu.PrefetchScalarGridSpec(
            num_scalar_prefetch=1,
            grid=(CHIPS,),
            in_specs=[keep] * 3 + [give] * 3,
            out_specs=[out, out],
        ),
        out_shape=(packed, packed),
        name="pack",
    )(blocks, *weights, *weights)


def products(weight, rows):
    block = weight.shape[1]
    split = weight.shape[0] // 3 * 2
    wide = lax.dot_general(weight[:split], rows[:, :block], CONTRACT_LAST, preferred_element_type=jnp.float32)
    narrow = lax.dot_general(weight[split:], rows[:, block:], CONTRACT_LAST, preferred_element_type=jnp.float32)
    return wide, narrow, split


def first_kernel(own_ref, same_ref, other_ref, keep_ref, sib_ref, out_ref):
    for n, weights in enumerate((keep_ref, sib_ref)):
        wide, narrow = 0.0, 0.0
        for r, rows in enumerate((own_ref, same_ref, other_ref)):
            a, b, split = products(weights[r], rows[...])
            wide, narrow = wide + a, narrow + b
        out_ref[n, :split, :] = wide
        out_ref[n, split:, :] = narrow


def first(own, same, other, keep, sib):
    rows, width = own.shape
    _, depth, block = keep.shape
    half = rows // 2
    weights = pl.BlockSpec((CHIPS - 1, depth, block), lambda i: (0, 0, 0))
    return pl.pallas_call(
        first_kernel,
        grid=(2,),
        in_specs=[pl.BlockSpec((half, width), lambda i: (i, 0))] * 3 + [weights] * 2,
        out_specs=pl.BlockSpec((CORES, depth, half), lambda i: (0, 0, i)),
        out_shape=jax.ShapeDtypeStruct((CORES, depth, rows), jnp.float32),
        compiler_params=BIG,
        name="first",
    )(own, same, other, keep, sib)


def second_kernel(rows_ref, keep_ref, sib_ref, sum_ref, out_ref):
    for n, weights in enumerate((keep_ref, sib_ref)):
        wide, narrow, split = products(weights[0], rows_ref[...])
        out_ref[n, :split, :] = sum_ref[n, :split, :] + wide
        out_ref[n, split:, :] = sum_ref[n, split:, :] + narrow


def second(opposite, keep, sib, sums):
    rows, width = opposite.shape
    _, depth, block = keep.shape
    half = rows // 2
    weights = pl.BlockSpec((1, depth, block), lambda i: (CHIPS - 1, 0, 0))
    by_half = pl.BlockSpec((CORES, depth, half), lambda i: (0, 0, i))
    return pl.pallas_call(
        second_kernel,
        grid=(2,),
        in_specs=[pl.BlockSpec((half, width), lambda i: (i, 0))] + [weights] * 2 + [by_half],
        out_specs=by_half,
        out_shape=jax.ShapeDtypeStruct(sums.shape, sums.dtype),
        compiler_params=BIG,
        name="second",
    )(opposite, keep, sib, sums)


def chip_sum(grads, keep, sib):
    depth = grads.shape[1]
    return jnp.dot(grads[0].T, keep[:depth, :], preferred_element_type=jnp.float32) + jnp.dot(
        grads[1].T, sib[:depth, :], preferred_element_type=jnp.float32
    )


def grads_kernel(mine_ref, theirs_ref, keep_ref, sib_ref, grads_ref, opposite_ref, other_ref):
    hidden = mine_ref.shape[1] // 3
    for n in range(CORES):
        gate_pre = mine_ref[n, :hidden, :] + theirs_ref[1 - n, :hidden, :]
        up_pre = mine_ref[n, hidden : 2 * hidden, :] + theirs_ref[1 - n, hidden : 2 * hidden, :]
        hidden_grad = mine_ref[n, 2 * hidden :, :] + theirs_ref[1 - n, 2 * hidden :, :]
        sigma = 1.0 / (1.0 + jnp.exp(-gate_pre))
        slope = sigma * (1.0 + gate_pre * (1.0 - sigma))
        grads_ref[n, :hidden, :] = (hidden_grad * up_pre * slope).astype(grads_ref.dtype)
        grads_ref[n, hidden:, :] = (hidden_grad * (gate_pre * sigma)).astype(grads_ref.dtype)
    opposite_ref[...] = chip_sum(grads_ref[...], keep_ref[1], sib_ref[1]).astype(opposite_ref.dtype)
    other_ref[...] = chip_sum(grads_ref[...], keep_ref[0], sib_ref[0]).astype(other_ref.dtype)


def grads(mine, theirs, keep, sib):
    _, depth, rows = mine.shape
    block = keep.shape[2]
    half = rows // 2
    wide = depth // 3 * 2
    by_half = pl.BlockSpec((CORES, depth, half), lambda i: (0, 0, i))
    weights = pl.BlockSpec((2, depth, block), lambda i: (1, 0, 0))
    part = jax.ShapeDtypeStruct((rows, block), jnp.bfloat16)
    return pl.pallas_call(
        grads_kernel,
        grid=(2,),
        in_specs=[by_half] * 2 + [weights] * 2,
        out_specs=[pl.BlockSpec((CORES, wide, half), lambda i: (0, 0, i))] + [pl.BlockSpec((half, block), lambda i: (i, 0))] * 2,
        out_shape=(jax.ShapeDtypeStruct((CORES, wide, rows), jnp.bfloat16), part, part),
        compiler_params=BIG,
        name="grads",
    )(mine, theirs, keep, sib)


def add_kernel(grads_ref, keep_ref, sib_ref, *refs):
    value = chip_sum(grads_ref[...], keep_ref[0], sib_ref[0])
    for got_ref in refs[:-1]:
        value = value + got_ref[...].astype(jnp.float32)
    refs[-1][...] = value.astype(refs[-1].dtype)


def add(grads_value, keep, sib, got, at):
    _, wide, rows = grads_value.shape
    _, depth, block = keep.shape
    half = rows // 2
    weights = pl.BlockSpec((1, depth, block), lambda i: (at, 0, 0))
    by_half = pl.BlockSpec((half, block), lambda i: (i, 0))
    return pl.pallas_call(
        add_kernel,
        grid=(2,),
        in_specs=[pl.BlockSpec((CORES, wide, half), lambda i: (0, 0, i)), weights, weights] + [by_half] * len(got),
        out_specs=by_half,
        out_shape=jax.ShapeDtypeStruct((rows, block), jnp.bfloat16),
        compiler_params=BIG,
        name="add",
    )(grads_value, keep, sib, *got)


def combine_kernel(hi_ref, lo_ref, back_ref, out_ref):
    back = back_ref[...]
    value = jnp.dot(hi_ref[...], back, preferred_element_type=jnp.float32)
    value = value + jnp.dot(lo_ref[...], back, preferred_element_type=jnp.float32)
    out_ref[...] = value.astype(out_ref.dtype)


def combine(high, low, back):
    return pl.pallas_call(
        combine_kernel,
        out_shape=jax.ShapeDtypeStruct((high.shape[0], back.shape[1]), jnp.bfloat16),
        name="combine",
    )(high, low, back)


def exchange(rows, n_tok):
    blocks = rows.reshape(n_tok, rows.shape[0] // n_tok, rows.shape[1])
    return lax.all_to_all(blocks, "tok", split_axis=0, concat_axis=0, tiled=True).reshape(rows.shape)


def send(value, to):
    pairs = []
    for i in range(CHIPS * CORES):
        chip, core = to(i // CORES, i % CORES)
        pairs.append((i, chip % CHIPS * CORES + core))
    return lax.ppermute(value, "tp", pairs)


def from_near(value):
    return send(value, lambda chip, core: (chip + 1 - 2 * core, core))


def to_near(value):
    return send(value, lambda chip, core: (chip - 1 + 2 * core, core))


def to_near_other(value):
    return send(value, lambda chip, core: (chip - 1 + 2 * core, 1 - core))


def to_sibling(value):
    return send(value, lambda chip, core: (chip, 1 - core))


def block_order(chip, core):
    near = chip - 1 + 2 * core
    chips = jnp.stack([chip, near, near, chip + 2]) & (CHIPS - 1)
    return chips * CORES + jnp.stack([core, core, 1 - core, core])


def expert(own, weights):
    place = lax.axis_index("tp").astype(jnp.int32)
    chip, core = place >> 1, place & 1
    keep, give = pack(jnp.concatenate([block_order(chip, core), block_order(chip, 1 - core)]), weights)
    sib = to_sibling(give)
    same = from_near(own)
    other = to_near_other(own)
    opposite = from_near(same)
    mine = first(own, same, other, keep, sib)
    mine = second(opposite, keep, sib, mine)
    theirs = to_sibling(mine)
    grads_value, for_opposite, for_other = grads(mine, theirs, keep, sib)
    passing = to_near(for_opposite)
    from_other = to_near_other(for_other)
    from_far = to_near(add(grads_value, keep, sib, (passing,), 1))
    return add(grads_value, keep, sib, (from_far, from_other), 0)


def shards(activations, out_grad, routes, gate_vals, w_gate, w_up, w_down):
    n_tok = lax.axis_size("tok")
    tok_dev, top_k = routes.shape
    capacity = max(2, 2 * tok_dev * top_k // n_tok)
    sent = dispatch(routes, activations, out_grad, n_tok, capacity)
    weights, sent, gate_vals = lax.optimization_barrier(((w_gate[0], w_up[0], w_down[0]), sent, gate_vals))
    high, low = mixer(routes, gate_vals, n_tok, capacity)
    expert_sum = expert(exchange(sent, n_tok), weights)
    return combine(high, low, exchange(expert_sum, n_tok))


def solution(mesh):
    placed = (
        P("tok", "tp"),
        P("tok", "tp"),
        P("tok", None),
        P("tok", None),
        P("tok", "tp", None),
        P("tok", "tp", None),
        P("tok", "tp", None),
    )
    return jax.shard_map(
        shards, mesh=mesh, in_specs=placed, out_specs=P("tok", "tp"), check_vma=False
    )
```

time: 165 us -> 158 us (0.958)
  the two profiles are of different devices: /device:TPU:6 before, /device:TPU:8 now
where the time goes in v4:
time: 158 us; the launch traced here: 157 us
  waiting for transfers between devices  86.7 us (55%)
  starting transfers between devices  45.8 us (29%)
  Pallas kernels  21.1 us (13%)
  local copies, waits for them, and re-layouts  2.45 us (2%)
    ppermute x8, waiting for transfers between devices, send(): return lax.ppermute(value, 'tp', pairs)  48 us
    all_to_all x2, waiting for transfers between devices, exchange(): lax.all_to_all(blocks, 'tok', split_axis=0, concat_axis=0, tiled=True)  38.7 us
    all_to_all x2, starting transfers between devices, exchange(): lax.all_to_all(blocks, 'tok', split_axis=0, concat_axis=0, tiled=True)  23.6 us
    ppermute x8, starting transfers between devices, send(): return lax.ppermute(value, 'tp', pairs)  22.2 us
    pallas_call x1, Pallas kernels, pack(): pl.pallas_call(pack_kernel, grid_spec=pltpu.PrefetchScalarGridSpec(num_sc...  5.8 us
  transfers between devices with their start and end apart: 10, of which 9 were waited for; matrix products, arithmetic and copies ran while one was open for 0% of the time, Pallas kernels for 7%

profile of v4, /device:TPU:8, one launch (start us, length us, event | category | flops | bytes accessed | tf_op | source)
XLA Modules:
  0.0 156.9 jit_solution(17233024079887782486)
XLA Ops:
  0.0 2.5 %dispatch.1 = bf16[512,1024]{1,0:T(8,128)(2,1)} custom-call(s32[2,128]{1,0:T(2,128)} %bitcast.26, bf16[128,512]{1,0:T(8,128)(2,1)} %x_ref.1, bf16[128,512]{1,0:T(8,128)(2,1)} %g_ref.1), custom_call_target="tpu_custom_call" | custom-call | tf_op jit(solution)/shard_map/dispatch/pallas_call | solution.py:44
  2.5 16.6 %all-to-all-start = ((bf16[64,8,1024]{2,1,0:T(8,128)(2,1)}), bf16[64,8,1024]{2,1,0:T(8,128)(2,1)S(1)}, u32[]{:S(2)}, u32[]{:S(2)}) async-start(bf16[64,8,1024]{2,1,0:T(8,128)(2,1)} %bitcast.24), calls=%async_computation | async-start | bytes 2097152 | tf_op jit(solution)/shard_map/all_to_all | solution.py:235
  19.1 0.1 fusion.1
  19.2 0.6 pad_add_fusion.blocks_ref
  19.8 5.8 %pack.1 = (bf16[4,576,512]{2,1,0:T(8,128)(2,1)}, bf16[4,576,512]{2,1,0:T(8,128)(2,1)}) custom-call(s32[8]{0:T(128)} %pad_add_fusion.blocks_ref, bf16[192,4096]{1,0:T(8,128)(2,1)} %bitcast.18, bf16[192,4096]{1,0:T(8,128)(2,1)} %bitcast.20, bf16[192,4096]{1,0:T(8,128)(2,1)} %bitcast.22, bf16[192,4096]{1,0:T(8,128)(2,1)} %bitcast.19, ...), custom_call_target="tpu_custom_call" | custom-call | tf_op jit(solution)/shard_map/pack/pallas_call | solution.py:83
  25.6 1.9 %collective-permute-start.2 = (bf16[4,576,512]{2,1,0:T(8,128)(2,1)}, bf16[4,576,512]{2,1,0:T(8,128)(2,1)S(1)}, u32[]{:S(2)}, u32[]{:S(2)}) collective-permute-start(bf16[4,576,512]{2,1,0:T(8,128)(2,1)} %get-tuple-element.25), channel_id=1, source_target_pairs={{0,1},{1,0},{2,3},{3,2},{4,5},{5,4},{6,7},{7,6},{8,9},{9,8},{10,11... | collective-permute-start | bytes 7077896 | tf_op jit(solution)/shard_map/ppermute | solution.py:243
  27.5 20.9 %all-to-all-done = bf16[64,8,1024]{2,1,0:T(8,128)(2,1)S(1)} async-done(((bf16[64,8,1024]{2,1,0:T(8,128)(2,1)}), bf16[64,8,1024]{2,1,0:T(8,128)(2,1)S(1)}, u32[]{:S(2)}, u32[]{:S(2)}) %all-to-all-start) | async-done | bytes 1048608 | tf_op jit(solution)/shard_map/all_to_all | solution.py:235
  48.4 3.4 %collective-permute-start = (bf16[512,1024]{1,0:T(8,128)(2,1)S(1)}, bf16[512,1024]{1,0:T(8,128)(2,1)S(1)}, u32[]{:S(2)}, u32[]{:S(2)}) collective-permute-start(bf16[512,1024]{1,0:T(8,128)(2,1)S(1)} %bitcast.15), channel_id=1, source_target_pairs={{0,2},{1,7},{2,4},{3,1},{4,6},{5,3},{6,0},{7,5},{8,10},{9,15},{10,... | collective-permute-start | bytes 3145736 | tf_op jit(solution)/shard_map/ppermute | solution.py:243
  51.8 1.9 %collective-permute-start.3 = (bf16[512,1024]{1,0:T(8,128)(2,1)S(1)}, bf16[512,1024]{1,0:T(8,128)(2,1)S(1)}, u32[]{:S(2)}, u32[]{:S(2)}) collective-permute-start(bf16[512,1024]{1,0:T(8,128)(2,1)S(1)} %bitcast.16), channel_id=1, source_target_pairs={{0,7},{1,2},{2,1},{3,4},{4,3},{5,6},{6,5},{7,0},{8,15},{9,10},{10,... | collective-permute-start | bytes 3145736 | tf_op jit(solution)/shard_map/ppermute | solution.py:243
  53.7 20.9 %collective-permute-done.same_ref = bf16[512,1024]{1,0:T(8,128)(2,1)S(1)} collective-permute-done((bf16[512,1024]{1,0:T(8,128)(2,1)S(1)}, bf16[512,1024]{1,0:T(8,128)(2,1)S(1)}, u32[]{:S(2)}, u32[]{:S(2)}) %collective-permute-start) | collective-permute-done | bytes 1048608 | tf_op jit(solution)/shard_map/ppermute | solution.py:243
  74.6 2.2 %collective-permute-start.1 = (bf16[512,1024]{1,0:T(8,128)(2,1)S(1)}, bf16[512,1024]{1,0:T(8,128)(2,1)S(1)}, u32[]{:S(2)}, u32[]{:S(2)}) collective-permute-start(bf16[512,1024]{1,0:T(8,128)(2,1)S(1)} %collective-permute-done.same_ref), channel_id=1, source_target_pairs={{0,2},{1,7},{2,4},{3,1},{4,6},{5,3},{6,0},{7,5},{8,10},{9,15},{10,... | collective-permute-start | bytes 3145736 | tf_op jit(solution)/shard_map/ppermute | solution.py:243
  76.8 0.0 collective-permute-done.2.sib_ref
  76.8 0.7 collective-permute-done.3.other_ref
  77.5 0.0 copy-start
  77.5 1.7 %copy-done = bf16[4,576,512]{2,1,0:T(8,128)(2,1)S(1)} copy-done((bf16[4,576,512]{2,1,0:T(8,128)(2,1)S(1)}, bf16[4,576,512]{2,1,0:T(8,128)(2,1)}, u32[]{:S(2)}) %copy-start) | copy-done | bytes 2359320
  79.2 2.6 %first.1.sum_ref = f32[2,576,512]{2,1,0:T(8,128)S(1)} custom-call(bf16[512,1024]{1,0:T(8,128)(2,1)S(1)} %bitcast.17, bf16[512,1024]{1,0:T(8,128)(2,1)S(1)} %collective-permute-done.same_ref, bf16[512,1024]{1,0:T(8,128)(2,1)S(1)} %collective-permute-done.3.other_ref, bf16[4,576,512]{2,1,0:T(8,128)(2,1)S(1)} %copy-done, ...), custom_call_target="tpu_custom_call" | custom-call | tf_op jit(solution)/shard_map/first/pallas_call | solution.py:119
  81.8 10.7 %collective-permute-done.1.rows_ref = bf16[512,1024]{1,0:T(8,128)(2,1)S(1)} collective-permute-done((bf16[512,1024]{1,0:T(8,128)(2,1)S(1)}, bf16[512,1024]{1,0:T(8,128)(2,1)S(1)}, u32[]{:S(2)}, u32[]{:S(2)}) %collective-permute-start.1) | collective-permute-done | bytes 1048608 | tf_op jit(solution)/shard_map/ppermute | solution.py:243
  92.5 1.5 second.1.mine_ref
  94.0 1.9 %collective-permute-start.4 = (f32[2,576,512]{2,1,0:T(8,128)S(1)}, f32[2,576,512]{2,1,0:T(8,128)S(1)}, u32[]{:S(2)}, u32[]{:S(2)}) collective-permute-start(f32[2,576,512]{2,1,0:T(8,128)S(1)} %second.1.mine_ref), channel_id=1, source_target_pairs={{0,1},{1,0},{2,3},{3,2},{4,5},{5,4},{6,7},{7,6},{8,9},{9,8},{10,11... | collective-permute-start | bytes 7077896 | tf_op jit(solution)/shard_map/ppermute | solution.py:243
  95.9 4.5 %collective-permute-done.4.theirs_ref = f32[2,576,512]{2,1,0:T(8,128)S(1)} collective-permute-done((f32[2,576,512]{2,1,0:T(8,128)S(1)}, f32[2,576,512]{2,1,0:T(8,128)S(1)}, u32[]{:S(2)}, u32[]{:S(2)}) %collective-permute-start.4) | collective-permute-done | bytes 2359328 | tf_op jit(solution)/shard_map/ppermute | solution.py:243
  100.4 2.1 %grads.1 = (bf16[2,384,512]{2,1,0:T(8,128)(2,1)S(1)}, bf16[512,512]{1,0:T(8,128)(2,1)S(1)}, bf16[512,512]{1,0:T(8,128)(2,1)S(1)}) custom-call(f32[2,576,512]{2,1,0:T(8,128)S(1)} %second.1.mine_ref, f32[2,576,512]{2,1,0:T(8,128)S(1)} %collective-permute-done.4.theirs_ref, bf16[4,576,512]{2,1,0:T(8,128)(2,1)S(1)} %copy-done, ...), custom_call_target="tpu_custom_call" | custom-call | tf_op jit(solution)/shard_map/grads/pallas_call | solution.py:183
  102.5 3.2 %collective-permute-start.5 = (bf16[512,512]{1,0:T(8,128)(2,1)S(1)}, bf16[512,512]{1,0:T(8,128)(2,1)S(1)}, u32[]{:S(2)}, u32[]{:S(2)}) collective-permute-start(bf16[512,512]{1,0:T(8,128)(2,1)S(1)} %get-tuple-element.27), channel_id=1, source_target_pairs={{0,6},{1,3},{2,0},{3,5},{4,2},{5,7},{6,4},{7,1},{8,14},{9,11},{10,... | collective-permute-start | bytes 1572872 | tf_op jit(solution)/shard_map/ppermute | solution.py:243
  105.7 3.3 %collective-permute-start.7 = (bf16[512,512]{1,0:T(8,128)(2,1)S(1)}, bf16[512,512]{1,0:T(8,128)(2,1)S(1)}, u32[]{:S(2)}, u32[]{:S(2)}) collective-permute-start(bf16[512,512]{1,0:T(8,128)(2,1)S(1)} %get-tuple-element.28), channel_id=1, source_target_pairs={{0,7},{1,2},{2,1},{3,4},{4,3},{5,6},{6,5},{7,0},{8,15},{9,10},{10,... | collective-permute-start | bytes 1572872 | tf_op jit(solution)/shard_map/ppermute | solution.py:243
  109.0 4.5 %collective-permute-done.5.refs_0_ = bf16[512,512]{1,0:T(8,128)(2,1)S(1)} collective-permute-done((bf16[512,512]{1,0:T(8,128)(2,1)S(1)}, bf16[512,512]{1,0:T(8,128)(2,1)S(1)}, u32[]{:S(2)}, u32[]{:S(2)}) %collective-permute-start.5) | collective-permute-done | bytes 524320 | tf_op jit(solution)/shard_map/ppermute | solution.py:243
  113.6 1.0 add.60
  114.6 4.4 %collective-permute-start.6 = (bf16[512,512]{1,0:T(8,128)(2,1)S(1)}, bf16[512,512]{1,0:T(8,128)(2,1)S(1)}, u32[]{:S(2)}, u32[]{:S(2)}) collective-permute-start(bf16[512,512]{1,0:T(8,128)(2,1)S(1)} %add.60), channel_id=1, source_target_pairs={{0,6},{1,3},{2,0},{3,5},{4,2},{5,7},{6,4},{7,1},{8,14},{9,11},{10,... | collective-permute-start | bytes 1572872 | tf_op jit(solution)/shard_map/ppermute | solution.py:243
  119.0 0.5 collective-permute-done.7.refs_1_
  119.6 6.1 %collective-permute-done.6.refs_0_ = bf16[512,512]{1,0:T(8,128)(2,1)S(1)} collective-permute-done((bf16[512,512]{1,0:T(8,128)(2,1)S(1)}, bf16[512,512]{1,0:T(8,128)(2,1)S(1)}, u32[]{:S(2)}, u32[]{:S(2)}) %collective-permute-start.6) | collective-permute-done | bytes 524320 | tf_op jit(solution)/shard_map/ppermute | solution.py:243
  125.7 1.7 %add.61 = bf16[512,512]{1,0:T(8,128)(2,1)} custom-call(bf16[2,384,512]{2,1,0:T(8,128)(2,1)S(1)} %get-tuple-element.26.grads_ref, bf16[4,576,512]{2,1,0:T(8,128)(2,1)S(1)} %copy-done, bf16[4,576,512]{2,1,0:T(8,128)(2,1)S(1)} %collective-permute-done.2.sib_ref, bf16[512,512]{1,0:T(8,128)(2,1)S(1)} %collective-permute-done.6.refs_0_, ...), custom_call_target="tpu_custom_call" | custom-call | tf_op jit(solution)/shard_map/add/pallas_call | solution.py:207
  127.4 7.0 %all-to-all-start.1 = ((bf16[64,8,512]{2,1,0:T(8,128)(2,1)}), bf16[64,8,512]{2,1,0:T(8,128)(2,1)S(1)}, u32[]{:S(2)}, u32[]{:S(2)}) async-start(bf16[64,8,512]{2,1,0:T(8,128)(2,1)} %bitcast.13), calls=%async_computation.1 | async-start | bytes 1048576 | tf_op jit(solution)/shard_map/all_to_all | solution.py:235
  134.4 1.7 %mixer.1 = (bf16[128,512]{1,0:T(8,128)(2,1)}, bf16[128,512]{1,0:T(8,128)(2,1)}) custom-call(s32[2,128]{1,0:T(2,128)} %bitcast.27, f32[2,128]{1,0:T(2,128)} %bitcast.28), custom_call_target="tpu_custom_call" | custom-call | tf_op jit(solution)/shard_map/mixer/pallas_call | solution.py:61
  136.1 17.9 %all-to-all-done.1 = bf16[64,8,512]{2,1,0:T(8,128)(2,1)S(1)} async-done(((bf16[64,8,512]{2,1,0:T(8,128)(2,1)}), bf16[64,8,512]{2,1,0:T(8,128)(2,1)S(1)}, u32[]{:S(2)}, u32[]{:S(2)}) %all-to-all-start.1) | async-done | bytes 524320 | tf_op jit(solution)/shard_map/all_to_all | solution.py:235
  154.0 0.0 copy-start.1
  154.0 0.8 copy-done.1
  154.7 2.1 %combine.1 = bf16[128,512]{1,0:T(8,128)(2,1)} custom-call(bf16[128,512]{1,0:T(8,128)(2,1)} %get-tuple-element.18.hi_ref, bf16[128,512]{1,0:T(8,128)(2,1)} %get-tuple-element.19.lo_ref, bf16[512,512]{1,0:T(8,128)(2,1)} %bitcast.25), custom_call_target="tpu_custom_call" | custom-call | tf_op jit(solution)/shard_map/combine/pallas_call | solution.py:226
Async XLA Ops:
  2.5 45.8 %all-to-all-start = ((bf16[64,8,1024]{2,1,0:T(8,128)(2,1)}), bf16[64,8,1024]{2,1,0:T(8,128)(2,1)S(1)}, u32[]{:S(2)}, u32[]{:S(2)}) async-start(bf16[64,8,1024]{2,1,0:T(8,128)(2,1)} %bitcast.24), calls=%async_computation | async-start | bytes 2097152 | tf_op jit(solution)/shard_map/all_to_all | solution.py:235
  25.6 51.2 %collective-permute-start.2 = (bf16[4,576,512]{2,1,0:T(8,128)(2,1)}, bf16[4,576,512]{2,1,0:T(8,128)(2,1)S(1)}, u32[]{:S(2)}, u32[]{:S(2)}) collective-permute-start(bf16[4,576,512]{2,1,0:T(8,128)(2,1)} %get-tuple-element.25), channel_id=1, source_target_pairs={{0,1},{1,0},{2,3},{3,2},{4,5},{5,4},{6,7},{7,6},{8,9},{9,8},{10,11... | collective-permute-start | bytes 7077896 | tf_op jit(solution)/shard_map/ppermute | solution.py:243
  48.4 26.2 %collective-permute-start = (bf16[512,1024]{1,0:T(8,128)(2,1)S(1)}, bf16[512,1024]{1,0:T(8,128)(2,1)S(1)}, u32[]{:S(2)}, u32[]{:S(2)}) collective-permute-start(bf16[512,1024]{1,0:T(8,128)(2,1)S(1)} %bitcast.15), channel_id=1, source_target_pairs={{0,2},{1,7},{2,4},{3,1},{4,6},{5,3},{6,0},{7,5},{8,10},{9,15},{10,... | collective-permute-start | bytes 3145736 | tf_op jit(solution)/shard_map/ppermute | solution.py:243
  51.8 25.7 %collective-permute-start.3 = (bf16[512,1024]{1,0:T(8,128)(2,1)S(1)}, bf16[512,1024]{1,0:T(8,128)(2,1)S(1)}, u32[]{:S(2)}, u32[]{:S(2)}) collective-permute-start(bf16[512,1024]{1,0:T(8,128)(2,1)S(1)} %bitcast.16), channel_id=1, source_target_pairs={{0,7},{1,2},{2,1},{3,4},{4,3},{5,6},{6,5},{7,0},{8,15},{9,10},{10,... | collective-permute-start | bytes 3145736 | tf_op jit(solution)/shard_map/ppermute | solution.py:243
  74.6 17.9 %collective-permute-start.1 = (bf16[512,1024]{1,0:T(8,128)(2,1)S(1)}, bf16[512,1024]{1,0:T(8,128)(2,1)S(1)}, u32[]{:S(2)}, u32[]{:S(2)}) collective-permute-start(bf16[512,1024]{1,0:T(8,128)(2,1)S(1)} %collective-permute-done.same_ref), channel_id=1, source_target_pairs={{0,2},{1,7},{2,4},{3,1},{4,6},{5,3},{6,0},{7,5},{8,10},{9,15},{10,... | collective-permute-start | bytes 3145736 | tf_op jit(solution)/shard_map/ppermute | solution.py:243
  77.5 1.7 %copy-start = (bf16[4,576,512]{2,1,0:T(8,128)(2,1)S(1)}, bf16[4,576,512]{2,1,0:T(8,128)(2,1)}, u32[]{:S(2)}) copy-start(bf16[4,576,512]{2,1,0:T(8,128)(2,1)} %get-tuple-element.24.keep_ref) | copy-start | bytes 7077892
  94.0 6.4 %collective-permute-start.4 = (f32[2,576,512]{2,1,0:T(8,128)S(1)}, f32[2,576,512]{2,1,0:T(8,128)S(1)}, u32[]{:S(2)}, u32[]{:S(2)}) collective-permute-start(f32[2,576,512]{2,1,0:T(8,128)S(1)} %second.1.mine_ref), channel_id=1, source_target_pairs={{0,1},{1,0},{2,3},{3,2},{4,5},{5,4},{6,7},{7,6},{8,9},{9,8},{10,11... | collective-permute-start | bytes 7077896 | tf_op jit(solution)/shard_map/ppermute | solution.py:243
  102.5 11.1 %collective-permute-start.5 = (bf16[512,512]{1,0:T(8,128)(2,1)S(1)}, bf16[512,512]{1,0:T(8,128)(2,1)S(1)}, u32[]{:S(2)}, u32[]{:S(2)}) collective-permute-start(bf16[512,512]{1,0:T(8,128)(2,1)S(1)} %get-tuple-element.27), channel_id=1, source_target_pairs={{0,6},{1,3},{2,0},{3,5},{4,2},{5,7},{6,4},{7,1},{8,14},{9,11},{10,... | collective-permute-start | bytes 1572872 | tf_op jit(solution)/shard_map/ppermute | solution.py:243
  105.7 13.8 %collective-permute-start.7 = (bf16[512,512]{1,0:T(8,128)(2,1)S(1)}, bf16[512,512]{1,0:T(8,128)(2,1)S(1)}, u32[]{:S(2)}, u32[]{:S(2)}) collective-permute-start(bf16[512,512]{1,0:T(8,128)(2,1)S(1)} %get-tuple-element.28), channel_id=1, source_target_pairs={{0,7},{1,2},{2,1},{3,4},{4,3},{5,6},{6,5},{7,0},{8,15},{9,10},{10,... | collective-permute-start | bytes 1572872 | tf_op jit(solution)/shard_map/ppermute | solution.py:243
  114.6 11.1 %collective-permute-start.6 = (bf16[512,512]{1,0:T(8,128)(2,1)S(1)}, bf16[512,512]{1,0:T(8,128)(2,1)S(1)}, u32[]{:S(2)}, u32[]{:S(2)}) collective-permute-start(bf16[512,512]{1,0:T(8,128)(2,1)S(1)} %add.60), channel_id=1, source_target_pairs={{0,6},{1,3},{2,0},{3,5},{4,2},{5,7},{6,4},{7,1},{8,14},{9,11},{10,... | collective-permute-start | bytes 1572872 | tf_op jit(solution)/shard_map/ppermute | solution.py:243
  127.4 26.5 %all-to-all-start.1 = ((bf16[64,8,512]{2,1,0:T(8,128)(2,1)}), bf16[64,8,512]{2,1,0:T(8,128)(2,1)S(1)}, u32[]{:S(2)}, u32[]{:S(2)}) async-start(bf16[64,8,512]{2,1,0:T(8,128)(2,1)} %bitcast.13), calls=%async_computation.1 | async-start | bytes 1048576 | tf_op jit(solution)/shard_map/all_to_all | solution.py:235
  154.0 0.8 copy-start.1

commit v5 on v4

--- a/solution.py
+++ b/solution.py
@@ -101,54 +101,72 @@
     return wide, narrow, split
 
 
-def first_kernel(own_ref, same_ref, other_ref, keep_ref, sib_ref, out_ref):
-    for n, weights in enumerate((keep_ref, sib_ref)):
-        wide, narrow = 0.0, 0.0
-        for r, rows in enumerate((own_ref, same_ref, other_ref)):
-            a, b, split = products(weights[r], rows[...])
-            wide, narrow = wide + a, narrow + b
-        out_ref[n, :split, :] = wide
-        out_ref[n, split:, :] = narrow
-
-
-def first(own, same, other, keep, sib):
+def first_kernel(own_ref, same_low_ref, same_high_ref, keep_ref, sib_ref, out_ref):
+    def store(same_ref):
+        for n, weights in enumerate((keep_ref, sib_ref)):
+            wide, narrow, split = products(weights[0], own_ref[...])
+            same_wide, same_narrow, _ = products(weights[1], same_ref[...])
+            out_ref[n, :split, :] = wide + same_wide
+            out_ref[n, split:, :] = narrow + same_narrow
+
+    @pl.when(pl.program_id(0) == 0)
+    def _():
+        store(same_low_ref)
+
+    @pl.when(pl.program_id(0) == 1)
+    def _():
+        store(same_high_ref)
+
+
+def first(own, same_low, same_high, keep, sib):
     rows, width = own.shape
     _, depth, block = keep.shape
     half = rows // 2
-    weights = pl.BlockSpec((CHIPS - 1, depth, block), lambda i: (0, 0, 0))
+    whole = pl.BlockSpec((half, width), lambda i: (0, 0))
+    weights = pl.BlockSpec((2, depth, block), lambda i: (0, 0, 0))
     return pl.pallas_call(
         first_kernel,
         grid=(2,),
-        in_specs=[pl.BlockSpec((half, width), lambda i: (i, 0))] * 3 + [weights] * 2,
+        in_specs=[pl.BlockSpec((half, width), lambda i: (i, 0)), whole, whole, weights, weights],
         out_specs=pl.BlockSpec((CORES, depth, half), lambda i: (0, 0, i)),
         out_shape=jax.ShapeDtypeStruct((CORES, depth, rows), jnp.float32),
         compiler_params=BIG,
         name="first",
-    )(own, same, other, keep, sib)
-
-
-def second_kernel(rows_ref, keep_ref, sib_ref, sum_ref, out_ref):
-    for n, weights in enumerate((keep_ref, sib_ref)):
-        wide, narrow, split = products(weights[0], rows_ref[...])
-        out_ref[n, :split, :] = sum_ref[n, :split, :] + wide
-        out_ref[n, split:, :] = sum_ref[n, split:, :] + narrow
-
-
-def second(opposite, keep, sib, sums):
-    rows, width = opposite.shape
+    )(own, same_low, same_high, keep, sib)
+
+
+def second_kernel(other_ref, low_ref, high_ref, keep_ref, sib_ref, sum_ref, out_ref):
+    def add(rows_ref):
+        for n, weights in enumerate((keep_ref, sib_ref)):
+            wide, narrow, split = products(weights[0], other_ref[...])
+            far_wide, far_narrow, _ = products(weights[1], rows_ref[...])
+            out_ref[n, :split, :] = sum_ref[n, :split, :] + (wide + far_wide)
+            out_ref[n, split:, :] = sum_ref[n, split:, :] + (narrow + far_narrow)
+
+    @pl.when(pl.program_id(0) == 0)
+    def _():
+        add(low_ref)
+
+    @pl.when(pl.program_id(0) == 1)
+    def _():
+        add(high_ref)
+
+
+def second(other, low, high, keep, sib, sums):
+    half, width = low.shape
     _, depth, block = keep.shape
-    half = rows // 2
-    weights = pl.BlockSpec((1, depth, block), lambda i: (CHIPS - 1, 0, 0))
+    whole = pl.BlockSpec((half, width), lambda i: (0, 0))
+    weights = pl.BlockSpec((2, depth, block), lambda i: (1, 0, 0))
     by_half = pl.BlockSpec((CORES, depth, half), lambda i: (0, 0, i))
     return pl.pallas_call(
         second_kernel,
         grid=(2,),
-        in_specs=[pl.BlockSpec((half, width), lambda i: (i, 0))] + [weights] * 2 + [by_half],
+        in_specs=[pl.BlockSpec((half, width), lambda i: (i, 0)), whole, whole, weights, weights, by_half],
         out_specs=by_half,
         out_shape=jax.ShapeDtypeStruct(sums.shape, sums.dtype),
         compiler_params=BIG,
         name="second",
-    )(opposite, keep, sib, sums)
+    )(other, low, high, keep, sib, sums)
 
 
 def chip_sum(grads, keep, sib):
@@ -270,14 +288,16 @@
     chip, core = place >> 1, place & 1
     keep, give = pack(jnp.concatenate([block_order(chip, core), block_order(chip, 1 - core)]), weights)
     sib = to_sibling(give)
-    same = from_near(own)
-    other = to_near_other(own)
-    opposite = from_near(same)
-    mine = first(own, same, other, keep, sib)
-    mine = second(opposite, keep, sib, mine)
+    half = own.shape[0] // 2
+    same_low, same_high = from_near(own[:half]), from_near(own[half:])
+    same_low, later = lax.optimization_barrier((same_low, own))
+    other = to_near_other(later)
+    opposite_low, opposite_high = from_near(same_low), from_near(same_high)
+    mine = first(own, same_low, same_high, keep, sib)
+    mine = second(other, opposite_low, opposite_high, keep, sib, mine)
     theirs = to_sibling(mine)
     grads_value, for_opposite, for_other = grads(mine, theirs, keep, sib)
-    passing = to_near(for_opposite)
+    passing, for_other = lax.optimization_barrier((to_near(for_opposite), for_other))
     from_other = to_near_other(for_other)
     from_far = to_near(add(grads_value, keep, sib, (passing,), 1))
     return add(grads_value, keep, sib, (from_far, from_other), 0)
@@ -290,7 +310,8 @@
     sent = dispatch(routes, activations, out_grad, n_tok, capacity)
     weights, sent, gate_vals = lax.optimization_barrier(((w_gate[0], w_up[0], w_down[0]), sent, gate_vals))
     high, low = mixer(routes, gate_vals, n_tok, capacity)
-    expert_sum = expert(exchange(sent, n_tok), weights)
+    own, high, low = lax.optimization_barrier((exchange(sent, n_tok), high, low))
+    expert_sum = expert(own, weights)
     return combine(high, low, exchange(expert_sum, n_tok))
 
 

time: 158 us -> 159 us (level)
  blocking collectives: 0 us -> 26.1 us
  waiting for transfers between devices: 86.7 us -> 64.5 us
    all_to_all x0 -> x1, blocking collectives: none -> 26.1 us  [exchange(): lax.all_to_all(blocks, 'tok', split_axis=0, concat_axis=0, tiled=True)]
    all_to_all x2 -> x1, waiting for transfers between devices: 38.7 us -> 19.2 us  [exchange(): lax.all_to_all(blocks, 'tok', split_axis=0, concat_axis=0, tiled=True)]
    all_to_all x2 -> x1, starting transfers between devices: 23.6 us -> 16.6 us  [exchange(): lax.all_to_all(blocks, 'tok', split_axis=0, concat_axis=0, tiled=True)]
    ppermute x8 -> x10, starting transfers between devices: 22.2 us -> 28.3 us  [send(): return lax.ppermute(value, 'tp', pairs)]
    ppermute x8 -> x10, waiting for transfers between devices: 48 us -> 45.3 us  [send(): return lax.ppermute(value, 'tp', pairs)]
  transfers between devices with their start and end apart: 10 -> 11, of which waited for: 9 -> 9; matrix products, arithmetic and copies ran while one was open for 0% -> 0% of each run, Pallas kernels for 7% -> 6%
where the time goes in v5:
time: 159 us; the launch traced here: 158 us
  waiting for transfers between devices  64.5 us (41%)
  starting transfers between devices  44.9 us (28%)
  blocking collectives  26.1 us (16%)
  Pallas kernels  20.5 us (13%)
  local copies, waits for them, and re-layouts  1.73 us (1%)
    ppermute x10, waiting for transfers between devices, send(): return lax.ppermute(value, 'tp', pairs)  45.3 us
    ppermute x10, starting transfers between devices, send(): return lax.ppermute(value, 'tp', pairs)  28.3 us
    all_to_all x1, blocking collectives, exchange(): lax.all_to_all(blocks, 'tok', split_axis=0, concat_axis=0, tiled=True)  26.1 us
    all_to_all x1, waiting for transfers between devices, exchange(): lax.all_to_all(blocks, 'tok', split_axis=0, concat_axis=0, tiled=True)  19.2 us
    all_to_all x1, starting transfers between devices, exchange(): lax.all_to_all(blocks, 'tok', split_axis=0, concat_axis=0, tiled=True)  16.6 us
    pallas_call x1, Pallas kernels, pack(): pl.pallas_call(pack_kernel, grid_spec=pltpu.PrefetchScalarGridSpec(num_sc...  5.8 us
  transfers between devices with their start and end apart: 11, of which 9 were waited for; matrix products, arithmetic and copies ran while one was open for 0% of the time, Pallas kernels for 6%

profile of v5, /device:TPU:8, one launch (start us, length us, event | category | flops | bytes accessed | tf_op | source)
XLA Modules:
  0.0 158.5 jit_solution(11717700519281629430)
XLA Ops:
  0.0 2.5 %dispatch.1 = bf16[512,1024]{1,0:T(8,128)(2,1)} custom-call(s32[2,128]{1,0:T(2,128)} %bitcast.27, bf16[128,512]{1,0:T(8,128)(2,1)} %x_ref.1, bf16[128,512]{1,0:T(8,128)(2,1)} %g_ref.1), custom_call_target="tpu_custom_call" | custom-call | tf_op jit(solution)/shard_map/dispatch/pallas_call | solution.py:44
  2.5 16.6 %all-to-all-start = ((bf16[64,8,1024]{2,1,0:T(8,128)(2,1)}), bf16[64,8,1024]{2,1,0:T(8,128)(2,1)S(1)}, u32[]{:S(2)}, u32[]{:S(2)}) async-start(bf16[64,8,1024]{2,1,0:T(8,128)(2,1)} %bitcast.25), calls=%async_computation | async-start | bytes 2097152 | tf_op jit(solution)/shard_map/all_to_all | solution.py:253
  19.1 0.1 fusion.1
  19.2 0.6 pad_add_fusion.blocks_ref
  19.8 5.8 %pack.1 = (bf16[4,576,512]{2,1,0:T(8,128)(2,1)}, bf16[4,576,512]{2,1,0:T(8,128)(2,1)}) custom-call(s32[8]{0:T(128)} %pad_add_fusion.blocks_ref, bf16[192,4096]{1,0:T(8,128)(2,1)} %bitcast.19, bf16[192,4096]{1,0:T(8,128)(2,1)} %bitcast.21, bf16[192,4096]{1,0:T(8,128)(2,1)} %bitcast.23, bf16[192,4096]{1,0:T(8,128)(2,1)} %bitcast.20, ...), custom_call_target="tpu_custom_call" | custom-call | tf_op jit(solution)/shard_map/pack/pallas_call | solution.py:83
  25.6 1.9 %collective-permute-start.5 = (bf16[4,576,512]{2,1,0:T(8,128)(2,1)}, bf16[4,576,512]{2,1,0:T(8,128)(2,1)S(1)}, u32[]{:S(2)}, u32[]{:S(2)}) collective-permute-start(bf16[4,576,512]{2,1,0:T(8,128)(2,1)} %get-tuple-element.37), channel_id=1, source_target_pairs={{0,1},{1,0},{2,3},{3,2},{4,5},{5,4},{6,7},{7,6},{8,9},{9,8},{10,11... | collective-permute-start | bytes 7077896 | tf_op jit(solution)/shard_map/ppermute | solution.py:261
  27.5 1.7 %mixer.1 = (bf16[128,512]{1,0:T(8,128)(2,1)}, bf16[128,512]{1,0:T(8,128)(2,1)}) custom-call(s32[2,128]{1,0:T(2,128)} %bitcast.28, f32[2,128]{1,0:T(2,128)} %bitcast.29), custom_call_target="tpu_custom_call" | custom-call | tf_op jit(solution)/shard_map/mixer/pallas_call | solution.py:61
  29.2 19.2 %all-to-all-done = bf16[64,8,1024]{2,1,0:T(8,128)(2,1)S(1)} async-done(((bf16[64,8,1024]{2,1,0:T(8,128)(2,1)}), bf16[64,8,1024]{2,1,0:T(8,128)(2,1)S(1)}, u32[]{:S(2)}, u32[]{:S(2)}) %all-to-all-start) | async-done | bytes 1048608 | tf_op jit(solution)/shard_map/all_to_all | solution.py:253
  48.4 0.1 fusion.4
  48.4 3.4 %collective-permute-start = (bf16[256,1024]{1,0:T(8,128)(2,1)S(1)}, bf16[256,1024]{1,0:T(8,128)(2,1)S(1)}, u32[]{:S(2)}, u32[]{:S(2)}) collective-permute-start(bf16[256,1024]{1,0:T(8,128)(2,1)S(1)} %get-tuple-element.44), channel_id=1, source_target_pairs={{0,2},{1,7},{2,4},{3,1},{4,6},{5,3},{6,0},{7,5},{8,10},{9,15},{10,... | collective-permute-start | bytes 1572872 | tf_op jit(solution)/shard_map/ppermute | solution.py:261
  51.9 3.4 %collective-permute-start.3 = (bf16[256,1024]{1,0:T(8,128)(2,1)S(1)}, bf16[256,1024]{1,0:T(8,128)(2,1)S(1)}, u32[]{:S(2)}, u32[]{:S(2)}) collective-permute-start(bf16[256,1024]{1,0:T(8,128)(2,1)S(1)} %get-tuple-element.43), channel_id=1, source_target_pairs={{0,2},{1,7},{2,4},{3,1},{4,6},{5,3},{6,0},{7,5},{8,10},{9,15},{10,... | collective-permute-start | bytes 1572872 | tf_op jit(solution)/shard_map/ppermute | solution.py:261
  55.3 5.5 %collective-permute-done.same_low_ref = bf16[256,1024]{1,0:T(8,128)(2,1)S(1)} collective-permute-done((bf16[256,1024]{1,0:T(8,128)(2,1)S(1)}, bf16[256,1024]{1,0:T(8,128)(2,1)S(1)}, u32[]{:S(2)}, u32[]{:S(2)}) %collective-permute-start) | collective-permute-done | bytes 524320 | tf_op jit(solution)/shard_map/ppermute | solution.py:261
  60.7 1.9 %collective-permute-start.1 = (bf16[512,1024]{1,0:T(8,128)(2,1)S(1)}, bf16[512,1024]{1,0:T(8,128)(2,1)S(1)}, u32[]{:S(2)}, u32[]{:S(2)}) collective-permute-start(bf16[512,1024]{1,0:T(8,128)(2,1)S(1)} %bitcast.16), channel_id=1, source_target_pairs={{0,7},{1,2},{2,1},{3,4},{4,3},{5,6},{6,5},{7,0},{8,15},{9,10},{10,... | collective-permute-start | bytes 3145736 | tf_op jit(solution)/shard_map/ppermute | solution.py:261
  62.7 3.7 %collective-permute-done.3.same_high_ref = bf16[256,1024]{1,0:T(8,128)(2,1)S(1)} collective-permute-done((bf16[256,1024]{1,0:T(8,128)(2,1)S(1)}, bf16[256,1024]{1,0:T(8,128)(2,1)S(1)}, u32[]{:S(2)}, u32[]{:S(2)}) %collective-permute-start.3) | collective-permute-done | bytes 524320 | tf_op jit(solution)/shard_map/ppermute | solution.py:261
  66.4 2.9 %collective-permute-start.4 = (bf16[256,1024]{1,0:T(8,128)(2,1)S(1)}, bf16[256,1024]{1,0:T(8,128)(2,1)S(1)}, u32[]{:S(2)}, u32[]{:S(2)}) collective-permute-start(bf16[256,1024]{1,0:T(8,128)(2,1)S(1)} %collective-permute-done.3.same_high_ref), channel_id=1, source_target_pairs={{0,2},{1,7},{2,4},{3,1},{4,6},{5,3},{6,0},{7,5},{8,10},{9,15},{10,... | collective-permute-start | bytes 1572872 | tf_op jit(solution)/shard_map/ppermute | solution.py:261
  69.2 3.4 %collective-permute-start.2 = (bf16[256,1024]{1,0:T(8,128)(2,1)S(1)}, bf16[256,1024]{1,0:T(8,128)(2,1)S(1)}, u32[]{:S(2)}, u32[]{:S(2)}) collective-permute-start(bf16[256,1024]{1,0:T(8,128)(2,1)S(1)} %collective-permute-done.same_low_ref), channel_id=1, source_target_pairs={{0,2},{1,7},{2,4},{3,1},{4,6},{5,3},{6,0},{7,5},{8,10},{9,15},{10,... | collective-permute-start | bytes 1572872 | tf_op jit(solution)/shard_map/ppermute | solution.py:261
  72.6 0.0 collective-permute-done.5.sib_ref
  72.6 0.0 copy-start
  72.6 1.7 %copy-done = bf16[4,576,512]{2,1,0:T(8,128)(2,1)S(1)} copy-done((bf16[4,576,512]{2,1,0:T(8,128)(2,1)S(1)}, bf16[4,576,512]{2,1,0:T(8,128)(2,1)}, u32[]{:S(2)}) %copy-start) | copy-done | bytes 2359320
  74.3 2.0 %first.1.sum_ref = f32[2,576,512]{2,1,0:T(8,128)S(1)} custom-call(bf16[512,1024]{1,0:T(8,128)(2,1)S(1)} %bitcast.17, bf16[256,1024]{1,0:T(8,128)(2,1)S(1)} %collective-permute-done.same_low_ref, bf16[256,1024]{1,0:T(8,128)(2,1)S(1)} %collective-permute-done.3.same_high_ref, bf16[4,576,512]{2,1,0:T(8,128)(2,1)S(1)} %copy-done, ...), custom_call_target="tpu_custom_call" | custom-call | tf_op jit(solution)/shard_map/first/pallas_call | solution.py:127
  76.3 7.4 %collective-permute-done.4.high_ref = bf16[256,1024]{1,0:T(8,128)(2,1)S(1)} collective-permute-done((bf16[256,1024]{1,0:T(8,128)(2,1)S(1)}, bf16[256,1024]{1,0:T(8,128)(2,1)S(1)}, u32[]{:S(2)}, u32[]{:S(2)}) %collective-permute-start.4) | collective-permute-done | bytes 524320 | tf_op jit(solution)/shard_map/ppermute | solution.py:261
  83.7 5.6 %collective-permute-done.2.low_ref = bf16[256,1024]{1,0:T(8,128)(2,1)S(1)} collective-permute-done((bf16[256,1024]{1,0:T(8,128)(2,1)S(1)}, bf16[256,1024]{1,0:T(8,128)(2,1)S(1)}, u32[]{:S(2)}, u32[]{:S(2)}) %collective-permute-start.2) | collective-permute-done | bytes 524320 | tf_op jit(solution)/shard_map/ppermute | solution.py:261
  89.3 0.0 collective-permute-done.1.other_ref
  89.3 2.2 %second.1.mine_ref = f32[2,576,512]{2,1,0:T(8,128)S(1)} custom-call(bf16[512,1024]{1,0:T(8,128)(2,1)S(1)} %collective-permute-done.1.other_ref, bf16[256,1024]{1,0:T(8,128)(2,1)S(1)} %collective-permute-done.2.low_ref, bf16[256,1024]{1,0:T(8,128)(2,1)S(1)} %collective-permute-done.4.high_ref, bf16[4,576,512]{2,1,0:T(8,128)(2,1)S(1)} %copy-done, ...), custom_call_target="tpu_custom_call" | custom-call | tf_op jit(solution)/shard_map/second/pallas_call | solution.py:161
  91.5 1.9 %collective-permute-start.6 = (f32[2,576,512]{2,1,0:T(8,128)S(1)}, f32[2,576,512]{2,1,0:T(8,128)S(1)}, u32[]{:S(2)}, u32[]{:S(2)}) collective-permute-start(f32[2,576,512]{2,1,0:T(8,128)S(1)} %second.1.mine_ref), channel_id=1, source_target_pairs={{0,1},{1,0},{2,3},{3,2},{4,5},{5,4},{6,7},{7,6},{8,9},{9,8},{10,11... | collective-permute-start | bytes 7077896 | tf_op jit(solution)/shard_map/ppermute | solution.py:261
  93.4 4.5 %collective-permute-done.6.theirs_ref = f32[2,576,512]{2,1,0:T(8,128)S(1)} collective-permute-done((f32[2,576,512]{2,1,0:T(8,128)S(1)}, f32[2,576,512]{2,1,0:T(8,128)S(1)}, u32[]{:S(2)}, u32[]{:S(2)}) %collective-permute-start.6) | collective-permute-done | bytes 2359328 | tf_op jit(solution)/shard_map/ppermute | solution.py:261
  97.9 2.1 %grads.1 = (bf16[2,384,512]{2,1,0:T(8,128)(2,1)S(1)}, bf16[512,512]{1,0:T(8,128)(2,1)S(1)}, bf16[512,512]{1,0:T(8,128)(2,1)S(1)}) custom-call(f32[2,576,512]{2,1,0:T(8,128)S(1)} %second.1.mine_ref, f32[2,576,512]{2,1,0:T(8,128)S(1)} %collective-permute-done.6.theirs_ref, bf16[4,576,512]{2,1,0:T(8,128)(2,1)S(1)} %copy-done, ...), custom_call_target="tpu_custom_call" | custom-call | tf_op jit(solution)/shard_map/grads/pallas_call | solution.py:201
  100.0 3.0 %collective-permute-start.7 = (bf16[512,512]{1,0:T(8,128)(2,1)S(1)}, bf16[512,512]{1,0:T(8,128)(2,1)S(1)}, u32[]{:S(2)}, u32[]{:S(2)}) collective-permute-start(bf16[512,512]{1,0:T(8,128)(2,1)S(1)} %get-tuple-element.39), channel_id=1, source_target_pairs={{0,6},{1,3},{2,0},{3,5},{4,2},{5,7},{6,4},{7,1},{8,14},{9,11},{10,... | collective-permute-start | bytes 1572872 | tf_op jit(solution)/shard_map/ppermute | solution.py:261
  103.0 8.1 %collective-permute-done.7.refs_0_ = bf16[512,512]{1,0:T(8,128)(2,1)S(1)} collective-permute-done((bf16[512,512]{1,0:T(8,128)(2,1)S(1)}, bf16[512,512]{1,0:T(8,128)(2,1)S(1)}, u32[]{:S(2)}, u32[]{:S(2)}) %collective-permute-start.7) | collective-permute-done | bytes 524320 | tf_op jit(solution)/shard_map/ppermute | solution.py:261
  111.1 1.0 add.60
  112.1 4.2 %collective-permute-start.8 = (bf16[512,512]{1,0:T(8,128)(2,1)S(1)}, bf16[512,512]{1,0:T(8,128)(2,1)S(1)}, u32[]{:S(2)}, u32[]{:S(2)}) collective-permute-start(bf16[512,512]{1,0:T(8,128)(2,1)S(1)} %add.60), channel_id=1, source_target_pairs={{0,6},{1,3},{2,0},{3,5},{4,2},{5,7},{6,4},{7,1},{8,14},{9,11},{10,... | collective-permute-start | bytes 1572872 | tf_op jit(solution)/shard_map/ppermute | solution.py:261
  116.3 2.4 %collective-permute-start.9 = (bf16[512,512]{1,0:T(8,128)(2,1)S(1)}, bf16[512,512]{1,0:T(8,128)(2,1)S(1)}, u32[]{:S(2)}, u32[]{:S(2)}) collective-permute-start(bf16[512,512]{1,0:T(8,128)(2,1)S(1)} %get-tuple-element.42), channel_id=1, source_target_pairs={{0,7},{1,2},{2,1},{3,4},{4,3},{5,6},{6,5},{7,0},{8,15},{9,10},{10,... | collective-permute-start | bytes 1572872 | tf_op jit(solution)/shard_map/ppermute | solution.py:261
  118.7 4.5 %collective-permute-done.8.refs_0_ = bf16[512,512]{1,0:T(8,128)(2,1)S(1)} collective-permute-done((bf16[512,512]{1,0:T(8,128)(2,1)S(1)}, bf16[512,512]{1,0:T(8,128)(2,1)S(1)}, u32[]{:S(2)}, u32[]{:S(2)}) %collective-permute-start.8) | collective-permute-done | bytes 524320 | tf_op jit(solution)/shard_map/ppermute | solution.py:261
  123.2 6.1 %collective-permute-done.9.refs_1_ = bf16[512,512]{1,0:T(8,128)(2,1)S(1)} collective-permute-done((bf16[512,512]{1,0:T(8,128)(2,1)S(1)}, bf16[512,512]{1,0:T(8,128)(2,1)S(1)}, u32[]{:S(2)}, u32[]{:S(2)}) %collective-permute-start.9) | collective-permute-done | bytes 524320 | tf_op jit(solution)/shard_map/ppermute | solution.py:261
  129.2 1.0 add.61
  130.3 26.1 %all_to_all.10 = bf16[64,8,512]{2,1,0:T(8,128)(2,1)} all-to-all(bf16[64,8,512]{2,1,0:T(8,128)(2,1)S(1)} %bitcast.18), channel_id=1, replica_groups=mesh['tok'=64,'tp'=8] {'tok'}, dimensions={0} | all-to-all | bytes 1048576 | tf_op jit(solution)/shard_map/all_to_all | solution.py:253
  156.3 2.1 %combine.1 = bf16[128,512]{1,0:T(8,128)(2,1)} custom-call(bf16[128,512]{1,0:T(8,128)(2,1)} %get-tuple-element.28.hi_ref, bf16[128,512]{1,0:T(8,128)(2,1)} %get-tuple-element.29.lo_ref, bf16[512,512]{1,0:T(8,128)(2,1)} %bitcast.26), custom_call_target="tpu_custom_call" | custom-call | tf_op jit(solution)/shard_map/combine/pallas_call | solution.py:244
Async XLA Ops:
  2.5 45.8 %all-to-all-start = ((bf16[64,8,1024]{2,1,0:T(8,128)(2,1)}), bf16[64,8,1024]{2,1,0:T(8,128)(2,1)S(1)}, u32[]{:S(2)}, u32[]{:S(2)}) async-start(bf16[64,8,1024]{2,1,0:T(8,128)(2,1)} %bitcast.25), calls=%async_computation | async-start | bytes 2097152 | tf_op jit(solution)/shard_map/all_to_all | solution.py:253
  25.6 47.0 %collective-permute-start.5 = (bf16[4,576,512]{2,1,0:T(8,128)(2,1)}, bf16[4,576,512]{2,1,0:T(8,128)(2,1)S(1)}, u32[]{:S(2)}, u32[]{:S(2)}) collective-permute-start(bf16[4,576,512]{2,1,0:T(8,128)(2,1)} %get-tuple-element.37), channel_id=1, source_target_pairs={{0,1},{1,0},{2,3},{3,2},{4,5},{5,4},{6,7},{7,6},{8,9},{9,8},{10,11... | collective-permute-start | bytes 7077896 | tf_op jit(solution)/shard_map/ppermute | solution.py:261
  48.4 12.3 %collective-permute-start = (bf16[256,1024]{1,0:T(8,128)(2,1)S(1)}, bf16[256,1024]{1,0:T(8,128)(2,1)S(1)}, u32[]{:S(2)}, u32[]{:S(2)}) collective-permute-start(bf16[256,1024]{1,0:T(8,128)(2,1)S(1)} %get-tuple-element.44), channel_id=1, source_target_pairs={{0,2},{1,7},{2,4},{3,1},{4,6},{5,3},{6,0},{7,5},{8,10},{9,15},{10,... | collective-permute-start | bytes 1572872 | tf_op jit(solution)/shard_map/ppermute | solution.py:261
  51.9 14.5 %collective-permute-start.3 = (bf16[256,1024]{1,0:T(8,128)(2,1)S(1)}, bf16[256,1024]{1,0:T(8,128)(2,1)S(1)}, u32[]{:S(2)}, u32[]{:S(2)}) collective-permute-start(bf16[256,1024]{1,0:T(8,128)(2,1)S(1)} %get-tuple-element.43), channel_id=1, source_target_pairs={{0,2},{1,7},{2,4},{3,1},{4,6},{5,3},{6,0},{7,5},{8,10},{9,15},{10,... | collective-permute-start | bytes 1572872 | tf_op jit(solution)/shard_map/ppermute | solution.py:261
  60.7 28.6 %collective-permute-start.1 = (bf16[512,1024]{1,0:T(8,128)(2,1)S(1)}, bf16[512,1024]{1,0:T(8,128)(2,1)S(1)}, u32[]{:S(2)}, u32[]{:S(2)}) collective-permute-start(bf16[512,1024]{1,0:T(8,128)(2,1)S(1)} %bitcast.16), channel_id=1, source_target_pairs={{0,7},{1,2},{2,1},{3,4},{4,3},{5,6},{6,5},{7,0},{8,15},{9,10},{10,... | collective-permute-start | bytes 3145736 | tf_op jit(solution)/shard_map/ppermute | solution.py:261
  66.4 17.3 %collective-permute-start.4 = (bf16[256,1024]{1,0:T(8,128)(2,1)S(1)}, bf16[256,1024]{1,0:T(8,128)(2,1)S(1)}, u32[]{:S(2)}, u32[]{:S(2)}) collective-permute-start(bf16[256,1024]{1,0:T(8,128)(2,1)S(1)} %collective-permute-done.3.same_high_ref), channel_id=1, source_target_pairs={{0,2},{1,7},{2,4},{3,1},{4,6},{5,3},{6,0},{7,5},{8,10},{9,15},{10,... | collective-permute-start | bytes 1572872 | tf_op jit(solution)/shard_map/ppermute | solution.py:261
  69.2 20.1 %collective-permute-start.2 = (bf16[256,1024]{1,0:T(8,128)(2,1)S(1)}, bf16[256,1024]{1,0:T(8,128)(2,1)S(1)}, u32[]{:S(2)}, u32[]{:S(2)}) collective-permute-start(bf16[256,1024]{1,0:T(8,128)(2,1)S(1)} %collective-permute-done.same_low_ref), channel_id=1, source_target_pairs={{0,2},{1,7},{2,4},{3,1},{4,6},{5,3},{6,0},{7,5},{8,10},{9,15},{10,... | collective-permute-start | bytes 1572872 | tf_op jit(solution)/shard_map/ppermute | solution.py:261
  72.6 1.7 %copy-start = (bf16[4,576,512]{2,1,0:T(8,128)(2,1)S(1)}, bf16[4,576,512]{2,1,0:T(8,128)(2,1)}, u32[]{:S(2)}) copy-start(bf16[4,576,512]{2,1,0:T(8,128)(2,1)} %get-tuple-element.36.keep_ref) | copy-start | bytes 7077892
  91.5 6.4 %collective-permute-start.6 = (f32[2,576,512]{2,1,0:T(8,128)S(1)}, f32[2,576,512]{2,1,0:T(8,128)S(1)}, u32[]{:S(2)}, u32[]{:S(2)}) collective-permute-start(f32[2,576,512]{2,1,0:T(8,128)S(1)} %second.1.mine_ref), channel_id=1, source_target_pairs={{0,1},{1,0},{2,3},{3,2},{4,5},{5,4},{6,7},{7,6},{8,9},{9,8},{10,11... | collective-permute-start | bytes 7077896 | tf_op jit(solution)/shard_map/ppermute | solution.py:261
  100.0 11.1 %collective-permute-start.7 = (bf16[512,512]{1,0:T(8,128)(2,1)S(1)}, bf16[512,512]{1,0:T(8,128)(2,1)S(1)}, u32[]{:S(2)}, u32[]{:S(2)}) collective-permute-start(bf16[512,512]{1,0:T(8,128)(2,1)S(1)} %get-tuple-element.39), channel_id=1, source_target_pairs={{0,6},{1,3},{2,0},{3,5},{4,2},{5,7},{6,4},{7,1},{8,14},{9,11},{10,... | collective-permute-start | bytes 1572872 | tf_op jit(solution)/shard_map/ppermute | solution.py:261
  112.1 11.1 %collective-permute-start.8 = (bf16[512,512]{1,0:T(8,128)(2,1)S(1)}, bf16[512,512]{1,0:T(8,128)(2,1)S(1)}, u32[]{:S(2)}, u32[]{:S(2)}) collective-permute-start(bf16[512,512]{1,0:T(8,128)(2,1)S(1)} %add.60), channel_id=1, source_target_pairs={{0,6},{1,3},{2,0},{3,5},{4,2},{5,7},{6,4},{7,1},{8,14},{9,11},{10,... | collective-permute-start | bytes 1572872 | tf_op jit(solution)/shard_map/ppermute | solution.py:261
  116.3 12.9 %collective-permute-start.9 = (bf16[512,512]{1,0:T(8,128)(2,1)S(1)}, bf16[512,512]{1,0:T(8,128)(2,1)S(1)}, u32[]{:S(2)}, u32[]{:S(2)}) collective-permute-start(bf16[512,512]{1,0:T(8,128)(2,1)S(1)} %get-tuple-element.42), channel_id=1, source_target_pairs={{0,7},{1,2},{2,1},{3,4},{4,3},{5,6},{6,5},{7,0},{8,15},{9,10},{10,... | collective-permute-start | bytes 1572872 | tf_op jit(solution)/shard_map/ppermute | solution.py:261

commit v6 on v5

--- a/solution.py
+++ b/solution.py
@@ -176,7 +176,7 @@
     )
 
 
-def grads_kernel(mine_ref, theirs_ref, keep_ref, sib_ref, grads_ref, opposite_ref, other_ref):
+def grads_kernel(mine_ref, theirs_ref, keep_ref, sib_ref, grads_ref, low_ref, high_ref, other_ref):
     hidden = mine_ref.shape[1] // 3
     for n in range(CORES):
         gate_pre = mine_ref[n, :hidden, :] + theirs_ref[1 - n, :hidden, :]
@@ -186,8 +186,16 @@
         slope = sigma * (1.0 + gate_pre * (1.0 - sigma))
         grads_ref[n, :hidden, :] = (hidden_grad * up_pre * slope).astype(grads_ref.dtype)
         grads_ref[n, hidden:, :] = (hidden_grad * (gate_pre * sigma)).astype(grads_ref.dtype)
-    opposite_ref[...] = chip_sum(grads_ref[...], keep_ref[1], sib_ref[1]).astype(opposite_ref.dtype)
     other_ref[...] = chip_sum(grads_ref[...], keep_ref[0], sib_ref[0]).astype(other_ref.dtype)
+    value = chip_sum(grads_ref[...], keep_ref[1], sib_ref[1]).astype(low_ref.dtype)
+
+    @pl.when(pl.program_id(0) == 0)
+    def _():
+        low_ref[...] = value
+
+    @pl.when(pl.program_id(0) == 1)
+    def _():
+        high_ref[...] = value
 
 
 def grads(mine, theirs, keep, sib):
@@ -197,40 +205,79 @@
     wide = depth // 3 * 2
     by_half = pl.BlockSpec((CORES, depth, half), lambda i: (0, 0, i))
     weights = pl.BlockSpec((2, depth, block), lambda i: (1, 0, 0))
-    part = jax.ShapeDtypeStruct((rows, block), jnp.bfloat16)
+    whole = pl.BlockSpec((half, block), lambda i: (0, 0))
+    part = jax.ShapeDtypeStruct((half, block), jnp.bfloat16)
     return pl.pallas_call(
         grads_kernel,
         grid=(2,),
         in_specs=[by_half] * 2 + [weights] * 2,
-        out_specs=[pl.BlockSpec((CORES, wide, half), lambda i: (0, 0, i))] + [pl.BlockSpec((half, block), lambda i: (i, 0))] * 2,
-        out_shape=(jax.ShapeDtypeStruct((CORES, wide, rows), jnp.bfloat16), part, part),
+        out_specs=[
+            pl.BlockSpec((CORES, wide, half), lambda i: (0, 0, i)),
+            whole,
+            whole,
+            pl.BlockSpec((half, block), lambda i: (i, 0)),
+        ],
+        out_shape=(
+            jax.ShapeDtypeStruct((CORES, wide, rows), jnp.bfloat16),
+            part,
+            part,
+            jax.ShapeDtypeStruct((rows, block), jnp.bfloat16),
+        ),
         compiler_params=BIG,
         name="grads",
     )(mine, theirs, keep, sib)
 
 
-def add_kernel(grads_ref, keep_ref, sib_ref, *refs):
-    value = chip_sum(grads_ref[...], keep_ref[0], sib_ref[0])
-    for got_ref in refs[:-1]:
-        value = value + got_ref[...].astype(jnp.float32)
-    refs[-1][...] = value.astype(refs[-1].dtype)
-
-
-def add(grads_value, keep, sib, got, at):
+def near_kernel(grads_ref, keep_ref, sib_ref, got_ref, out_ref):
+    value = chip_sum(grads_ref[...], keep_ref[0], sib_ref[0]) + got_ref[...].astype(jnp.float32)
+    out_ref[...] = value.astype(out_ref.dtype)
+
+
+def near(grads_value, keep, sib, got, part):
+    _, wide, _ = grads_value.shape
+    _, depth, block = keep.shape
+    half = got.shape[0]
+    weights = pl.BlockSpec((1, depth, block), lambda i: (1, 0, 0))
+    whole = pl.BlockSpec((half, block), lambda i: (0, 0))
+    return pl.pallas_call(
+        near_kernel,
+        grid=(1,),
+        in_specs=[pl.BlockSpec((CORES, wide, half), lambda i: (0, 0, part)), weights, weights, whole],
+        out_specs=whole,
+        out_shape=jax.ShapeDtypeStruct(got.shape, jnp.bfloat16),
+        compiler_params=BIG,
+        name="near",
+    )(grads_value, keep, sib, got)
+
+
+def total_kernel(grads_ref, keep_ref, sib_ref, low_ref, high_ref, other_ref, out_ref):
+    value = chip_sum(grads_ref[...], keep_ref[0], sib_ref[0]) + other_ref[...].astype(jnp.float32)
+
+    @pl.when(pl.program_id(0) == 0)
+    def _():
+        out_ref[...] = (value + low_ref[...].astype(jnp.float32)).astype(out_ref.dtype)
+
+    @pl.when(pl.program_id(0) == 1)
+    def _():
+        out_ref[...] = (value + high_ref[...].astype(jnp.float32)).astype(out_ref.dtype)
+
+
+def total(grads_value, keep, sib, low, high, other):
     _, wide, rows = grads_value.shape
     _, depth, block = keep.shape
     half = rows // 2
-    weights = pl.BlockSpec((1, depth, block), lambda i: (at, 0, 0))
+    weights = pl.BlockSpec((1, depth, block), lambda i: (0, 0, 0))
+    whole = pl.BlockSpec((half, block), lambda i: (0, 0))
     by_half = pl.BlockSpec((half, block), lambda i: (i, 0))
     return pl.pallas_call(
-        add_kernel,
+        total_kernel,
         grid=(2,),
-        in_specs=[pl.BlockSpec((CORES, wide, half), lambda i: (0, 0, i)), weights, weights] + [by_half] * len(got),
+        in_specs=[pl.BlockSpec((CORES, wide, half), lambda i: (0, 0, i)), weights, weights, whole, whole, by_half],
         out_specs=by_half,
         out_shape=jax.ShapeDtypeStruct((rows, block), jnp.bfloat16),
         compiler_params=BIG,
-        name="add",
-    )(grads_value, keep, sib, *got)
+        name="total",
+    )(grads_value, keep, sib, low, high, other)
 
 
 def combine_kernel(hi_ref, lo_ref, back_ref, out_ref):
@@ -296,11 +343,12 @@
     mine = first(own, same_low, same_high, keep, sib)
     mine = second(other, opposite_low, opposite_high, keep, sib, mine)
     theirs = to_sibling(mine)
-    grads_value, for_opposite, for_other = grads(mine, theirs, keep, sib)
-    passing, for_other = lax.optimization_barrier((to_near(for_opposite), for_other))
+    grads_value, part_low, part_high, for_other = grads(mine, theirs, keep, sib)
+    passing_low, passing_high = to_near(part_low), to_near(part_high)
     from_other = to_near_other(for_other)
-    from_far = to_near(add(grads_value, keep, sib, (passing,), 1))
-    return add(grads_value, keep, sib, (from_far, from_other), 0)
+    from_low = to_near(near(grads_value, keep, sib, passing_low, 0))
+    from_high = to_near(near(grads_value, keep, sib, passing_high, 1))
+    return total(grads_value, keep, sib, from_low, from_high, from_other)
 
 
 def shards(activations, out_grad, routes, gate_vals, w_gate, w_up, w_down):

time: 159 us -> 153 us (0.962)
  the two profiles are of different devices: /device:TPU:8 before, /device:TPU:6 now
where the time goes in v6:
time: 153 us; the launch traced here: 151 us
  waiting for transfers between devices  55.3 us (36%)
  starting transfers between devices  47.3 us (31%)
  blocking collectives  25.1 us (16%)
  Pallas kernels  20.5 us (13%)
  local copies, waits for them, and re-layouts  1.73 us (1%)
    ppermute x12, waiting for transfers between devices, send(): return lax.ppermute(value, 'tp', pairs)  35.6 us
    ppermute x12, starting transfers between devices, send(): return lax.ppermute(value, 'tp', pairs)  30.7 us
    all_to_all x1, blocking collectives, exchange(): lax.all_to_all(blocks, 'tok', split_axis=0, concat_axis=0, tiled=True)  25.1 us
    all_to_all x1, waiting for transfers between devices, exchange(): lax.all_to_all(blocks, 'tok', split_axis=0, concat_axis=0, tiled=True)  19.7 us
    all_to_all x1, starting transfers between devices, exchange(): lax.all_to_all(blocks, 'tok', split_axis=0, concat_axis=0, tiled=True)  16.6 us
    pallas_call x1, Pallas kernels, pack(): pl.pallas_call(pack_kernel, grid_spec=pltpu.PrefetchScalarGridSpec(num_sc...  5.8 us
  transfers between devices with their start and end apart: 13, of which 10 were waited for; matrix products, arithmetic and copies ran while one was open for 0% of the time, Pallas kernels for 7%

profile of v6, /device:TPU:6, one launch (start us, length us, event | category | flops | bytes accessed | tf_op | source)
XLA Modules:
  0.0 150.9 jit_solution(14604844218458129534)
XLA Ops:
  0.0 2.5 %dispatch.1 = bf16[512,1024]{1,0:T(8,128)(2,1)} custom-call(s32[2,128]{1,0:T(2,128)} %bitcast.27, bf16[128,512]{1,0:T(8,128)(2,1)} %x_ref.1, bf16[128,512]{1,0:T(8,128)(2,1)} %g_ref.1), custom_call_target="tpu_custom_call" | custom-call | tf_op jit(solution)/shard_map/dispatch/pallas_call | solution.py:44
  2.5 16.6 %all-to-all-start = ((bf16[64,8,1024]{2,1,0:T(8,128)(2,1)}), bf16[64,8,1024]{2,1,0:T(8,128)(2,1)S(1)}, u32[]{:S(2)}, u32[]{:S(2)}) async-start(bf16[64,8,1024]{2,1,0:T(8,128)(2,1)} %bitcast.25), calls=%async_computation | async-start | bytes 2097152 | tf_op jit(solution)/shard_map/all_to_all | solution.py:300
  19.1 0.1 fusion.1
  19.2 0.6 pad_add_fusion.blocks_ref
  19.8 5.8 %pack.1 = (bf16[4,576,512]{2,1,0:T(8,128)(2,1)}, bf16[4,576,512]{2,1,0:T(8,128)(2,1)}) custom-call(s32[8]{0:T(128)} %pad_add_fusion.blocks_ref, bf16[192,4096]{1,0:T(8,128)(2,1)} %bitcast.19, bf16[192,4096]{1,0:T(8,128)(2,1)} %bitcast.21, bf16[192,4096]{1,0:T(8,128)(2,1)} %bitcast.23, bf16[192,4096]{1,0:T(8,128)(2,1)} %bitcast.20, ...), custom_call_target="tpu_custom_call" | custom-call | tf_op jit(solution)/shard_map/pack/pallas_call | solution.py:83
  25.6 1.9 %collective-permute-start.5 = (bf16[4,576,512]{2,1,0:T(8,128)(2,1)}, bf16[4,576,512]{2,1,0:T(8,128)(2,1)S(1)}, u32[]{:S(2)}, u32[]{:S(2)}) collective-permute-start(bf16[4,576,512]{2,1,0:T(8,128)(2,1)} %get-tuple-element.36), channel_id=1, source_target_pairs={{0,1},{1,0},{2,3},{3,2},{4,5},{5,4},{6,7},{7,6},{8,9},{9,8},{10,11... | collective-permute-start | bytes 7077896 | tf_op jit(solution)/shard_map/ppermute | solution.py:308
  27.5 1.7 %mixer.1 = (bf16[128,512]{1,0:T(8,128)(2,1)}, bf16[128,512]{1,0:T(8,128)(2,1)}) custom-call(s32[2,128]{1,0:T(2,128)} %bitcast.28, f32[2,128]{1,0:T(2,128)} %bitcast.29), custom_call_target="tpu_custom_call" | custom-call | tf_op jit(solution)/shard_map/mixer/pallas_call | solution.py:61
  29.2 19.7 %all-to-all-done = bf16[64,8,1024]{2,1,0:T(8,128)(2,1)S(1)} async-done(((bf16[64,8,1024]{2,1,0:T(8,128)(2,1)}), bf16[64,8,1024]{2,1,0:T(8,128)(2,1)S(1)}, u32[]{:S(2)}, u32[]{:S(2)}) %all-to-all-start) | async-done | bytes 1048608 | tf_op jit(solution)/shard_map/all_to_all | solution.py:300
  48.9 0.1 fusion.4
  49.0 2.4 %collective-permute-start = (bf16[256,1024]{1,0:T(8,128)(2,1)S(1)}, bf16[256,1024]{1,0:T(8,128)(2,1)S(1)}, u32[]{:S(2)}, u32[]{:S(2)}) collective-permute-start(bf16[256,1024]{1,0:T(8,128)(2,1)S(1)} %get-tuple-element.42), channel_id=1, source_target_pairs={{0,2},{1,7},{2,4},{3,1},{4,6},{5,3},{6,0},{7,5},{8,10},{9,15},{10,... | collective-permute-start | bytes 1572872 | tf_op jit(solution)/shard_map/ppermute | solution.py:308
  51.4 3.4 %collective-permute-start.3 = (bf16[256,1024]{1,0:T(8,128)(2,1)S(1)}, bf16[256,1024]{1,0:T(8,128)(2,1)S(1)}, u32[]{:S(2)}, u32[]{:S(2)}) collective-permute-start(bf16[256,1024]{1,0:T(8,128)(2,1)S(1)} %get-tuple-element.41), channel_id=1, source_target_pairs={{0,2},{1,7},{2,4},{3,1},{4,6},{5,3},{6,0},{7,5},{8,10},{9,15},{10,... | collective-permute-start | bytes 1572872 | tf_op jit(solution)/shard_map/ppermute | solution.py:308
  54.8 5.3 %collective-permute-done.same_low_ref = bf16[256,1024]{1,0:T(8,128)(2,1)S(1)} collective-permute-done((bf16[256,1024]{1,0:T(8,128)(2,1)S(1)}, bf16[256,1024]{1,0:T(8,128)(2,1)S(1)}, u32[]{:S(2)}, u32[]{:S(2)}) %collective-permute-start) | collective-permute-done | bytes 524320 | tf_op jit(solution)/shard_map/ppermute | solution.py:308
  60.1 1.9 %collective-permute-start.1 = (bf16[512,1024]{1,0:T(8,128)(2,1)S(1)}, bf16[512,1024]{1,0:T(8,128)(2,1)S(1)}, u32[]{:S(2)}, u32[]{:S(2)}) collective-permute-start(bf16[512,1024]{1,0:T(8,128)(2,1)S(1)} %bitcast.16), channel_id=1, source_target_pairs={{0,7},{1,2},{2,1},{3,4},{4,3},{5,6},{6,5},{7,0},{8,15},{9,10},{10,... | collective-permute-start | bytes 3145736 | tf_op jit(solution)/shard_map/ppermute | solution.py:308
  62.0 4.4 %collective-permute-done.3.same_high_ref = bf16[256,1024]{1,0:T(8,128)(2,1)S(1)} collective-permute-done((bf16[256,1024]{1,0:T(8,128)(2,1)S(1)}, bf16[256,1024]{1,0:T(8,128)(2,1)S(1)}, u32[]{:S(2)}, u32[]{:S(2)}) %collective-permute-start.3) | collective-permute-done | bytes 524320 | tf_op jit(solution)/shard_map/ppermute | solution.py:308
  66.4 2.9 %collective-permute-start.4 = (bf16[256,1024]{1,0:T(8,128)(2,1)S(1)}, bf16[256,1024]{1,0:T(8,128)(2,1)S(1)}, u32[]{:S(2)}, u32[]{:S(2)}) collective-permute-start(bf16[256,1024]{1,0:T(8,128)(2,1)S(1)} %collective-permute-done.3.same_high_ref), channel_id=1, source_target_pairs={{0,2},{1,7},{2,4},{3,1},{4,6},{5,3},{6,0},{7,5},{8,10},{9,15},{10,... | collective-permute-start | bytes 1572872 | tf_op jit(solution)/shard_map/ppermute | solution.py:308
  69.3 2.9 %collective-permute-start.2 = (bf16[256,1024]{1,0:T(8,128)(2,1)S(1)}, bf16[256,1024]{1,0:T(8,128)(2,1)S(1)}, u32[]{:S(2)}, u32[]{:S(2)}) collective-permute-start(bf16[256,1024]{1,0:T(8,128)(2,1)S(1)} %collective-permute-done.same_low_ref), channel_id=1, source_target_pairs={{0,2},{1,7},{2,4},{3,1},{4,6},{5,3},{6,0},{7,5},{8,10},{9,15},{10,... | collective-permute-start | bytes 1572872 | tf_op jit(solution)/shard_map/ppermute | solution.py:308
  72.2 0.0 collective-permute-done.5.sib_ref
  72.2 0.0 copy-start
  72.2 1.7 %copy-done = bf16[4,576,512]{2,1,0:T(8,128)(2,1)S(1)} copy-done((bf16[4,576,512]{2,1,0:T(8,128)(2,1)S(1)}, bf16[4,576,512]{2,1,0:T(8,128)(2,1)}, u32[]{:S(2)}) %copy-start) | copy-done | bytes 2359320
  73.8 2.0 %first.1.sum_ref = f32[2,576,512]{2,1,0:T(8,128)S(1)} custom-call(bf16[512,1024]{1,0:T(8,128)(2,1)S(1)} %bitcast.17, bf16[256,1024]{1,0:T(8,128)(2,1)S(1)} %collective-permute-done.same_low_ref, bf16[256,1024]{1,0:T(8,128)(2,1)S(1)} %collective-permute-done.3.same_high_ref, bf16[4,576,512]{2,1,0:T(8,128)(2,1)S(1)} %copy-done, ...), custom_call_target="tpu_custom_call" | custom-call | tf_op jit(solution)/shard_map/first/pallas_call | solution.py:127
  75.8 6.7 %collective-permute-done.4.high_ref = bf16[256,1024]{1,0:T(8,128)(2,1)S(1)} collective-permute-done((bf16[256,1024]{1,0:T(8,128)(2,1)S(1)}, bf16[256,1024]{1,0:T(8,128)(2,1)S(1)}, u32[]{:S(2)}, u32[]{:S(2)}) %collective-permute-start.4) | collective-permute-done | bytes 524320 | tf_op jit(solution)/shard_map/ppermute | solution.py:308
  82.5 5.6 %collective-permute-done.2.low_ref = bf16[256,1024]{1,0:T(8,128)(2,1)S(1)} collective-permute-done((bf16[256,1024]{1,0:T(8,128)(2,1)S(1)}, bf16[256,1024]{1,0:T(8,128)(2,1)S(1)}, u32[]{:S(2)}, u32[]{:S(2)}) %collective-permute-start.2) | collective-permute-done | bytes 524320 | tf_op jit(solution)/shard_map/ppermute | solution.py:308
  88.2 0.0 collective-permute-done.1.other_ref
  88.2 2.2 %second.1.mine_ref = f32[2,576,512]{2,1,0:T(8,128)S(1)} custom-call(bf16[512,1024]{1,0:T(8,128)(2,1)S(1)} %collective-permute-done.1.other_ref, bf16[256,1024]{1,0:T(8,128)(2,1)S(1)} %collective-permute-done.2.low_ref, bf16[256,1024]{1,0:T(8,128)(2,1)S(1)} %collective-permute-done.4.high_ref, bf16[4,576,512]{2,1,0:T(8,128)(2,1)S(1)} %copy-done, ...), custom_call_target="tpu_custom_call" | custom-call | tf_op jit(solution)/shard_map/second/pallas_call | solution.py:161
  90.4 1.9 %collective-permute-start.6 = (f32[2,576,512]{2,1,0:T(8,128)S(1)}, f32[2,576,512]{2,1,0:T(8,128)S(1)}, u32[]{:S(2)}, u32[]{:S(2)}) collective-permute-start(f32[2,576,512]{2,1,0:T(8,128)S(1)} %second.1.mine_ref), channel_id=1, source_target_pairs={{0,1},{1,0},{2,3},{3,2},{4,5},{5,4},{6,7},{7,6},{8,9},{9,8},{10,11... | collective-permute-start | bytes 7077896 | tf_op jit(solution)/shard_map/ppermute | solution.py:308
  92.3 4.5 %collective-permute-done.6.theirs_ref = f32[2,576,512]{2,1,0:T(8,128)S(1)} collective-permute-done((f32[2,576,512]{2,1,0:T(8,128)S(1)}, f32[2,576,512]{2,1,0:T(8,128)S(1)}, u32[]{:S(2)}, u32[]{:S(2)}) %collective-permute-start.6) | collective-permute-done | bytes 2359328 | tf_op jit(solution)/shard_map/ppermute | solution.py:308
  96.8 2.2 %grads.1 = (bf16[2,384,512]{2,1,0:T(8,128)(2,1)S(1)}, bf16[256,512]{1,0:T(8,128)(2,1)S(1)}, bf16[256,512]{1,0:T(8,128)(2,1)S(1)}, bf16[512,512]{1,0:T(8,128)(2,1)S(1)}) custom-call(f32[2,576,512]{2,1,0:T(8,128)S(1)} %second.1.mine_ref, f32[2,576,512]{2,1,0:T(8,128)S(1)} %collective-permute-done.6.theirs_ref, bf16[4,576,512]{2,1,0:T(8,128)(2,1)S(1)} %copy-done, ...), custom_call_target="tpu_custom_call" | custom-call | tf_op jit(solution)/shard_map/grads/pallas_call | solution.py:210
  99.0 2.7 %collective-permute-start.7 = (bf16[256,512]{1,0:T(8,128)(2,1)S(1)}, bf16[256,512]{1,0:T(8,128)(2,1)S(1)}, u32[]{:S(2)}, u32[]{:S(2)}) collective-permute-start(bf16[256,512]{1,0:T(8,128)(2,1)S(1)} %get-tuple-element.38), channel_id=1, source_target_pairs={{0,6},{1,3},{2,0},{3,5},{4,2},{5,7},{6,4},{7,1},{8,14},{9,11},{10,... | collective-permute-start | bytes 786440 | tf_op jit(solution)/shard_map/ppermute | solution.py:308
  101.7 2.4 %collective-permute-start.9 = (bf16[256,512]{1,0:T(8,128)(2,1)S(1)}, bf16[256,512]{1,0:T(8,128)(2,1)S(1)}, u32[]{:S(2)}, u32[]{:S(2)}) collective-permute-start(bf16[256,512]{1,0:T(8,128)(2,1)S(1)} %get-tuple-element.39), channel_id=1, source_target_pairs={{0,6},{1,3},{2,0},{3,5},{4,2},{5,7},{6,4},{7,1},{8,14},{9,11},{10,... | collective-permute-start | bytes 786440 | tf_op jit(solution)/shard_map/ppermute | solution.py:308
  104.2 3.9 %collective-permute-start.11 = (bf16[512,512]{1,0:T(8,128)(2,1)S(1)}, bf16[512,512]{1,0:T(8,128)(2,1)S(1)}, u32[]{:S(2)}, u32[]{:S(2)}) collective-permute-start(bf16[512,512]{1,0:T(8,128)(2,1)S(1)} %get-tuple-element.40), channel_id=1, source_target_pairs={{0,7},{1,2},{2,1},{3,4},{4,3},{5,6},{6,5},{7,0},{8,15},{9,10},{10,... | collective-permute-start | bytes 1572872 | tf_op jit(solution)/shard_map/ppermute | solution.py:308
  108.1 0.4 collective-permute-done.7.got_ref
  108.4 0.5 near.2
  108.9 1.9 %collective-permute-start.8 = (bf16[256,512]{1,0:T(8,128)(2,1)S(1)}, bf16[256,512]{1,0:T(8,128)(2,1)S(1)}, u32[]{:S(2)}, u32[]{:S(2)}) collective-permute-start(bf16[256,512]{1,0:T(8,128)(2,1)S(1)} %near.2), channel_id=1, source_target_pairs={{0,6},{1,3},{2,0},{3,5},{4,2},{5,7},{6,4},{7,1},{8,14},{9,11},{10,... | collective-permute-start | bytes 786440 | tf_op jit(solution)/shard_map/ppermute | solution.py:308
  110.8 0.4 collective-permute-done.9.got_ref
  111.2 0.5 near.3
  111.7 2.4 %collective-permute-start.10 = (bf16[256,512]{1,0:T(8,128)(2,1)S(1)}, bf16[256,512]{1,0:T(8,128)(2,1)S(1)}, u32[]{:S(2)}, u32[]{:S(2)}) collective-permute-start(bf16[256,512]{1,0:T(8,128)(2,1)S(1)} %near.3), channel_id=1, source_target_pairs={{0,6},{1,3},{2,0},{3,5},{4,2},{5,7},{6,4},{7,1},{8,14},{9,11},{10,... | collective-permute-start | bytes 786440 | tf_op jit(solution)/shard_map/ppermute | solution.py:308
  114.2 5.5 %collective-permute-done.8.low_ref = bf16[256,512]{1,0:T(8,128)(2,1)S(1)} collective-permute-done((bf16[256,512]{1,0:T(8,128)(2,1)S(1)}, bf16[256,512]{1,0:T(8,128)(2,1)S(1)}, u32[]{:S(2)}, u32[]{:S(2)}) %collective-permute-start.8) | collective-permute-done | bytes 262176 | tf_op jit(solution)/shard_map/ppermute | solution.py:308
  119.7 2.8 %collective-permute-done.10.high_ref = bf16[256,512]{1,0:T(8,128)(2,1)S(1)} collective-permute-done((bf16[256,512]{1,0:T(8,128)(2,1)S(1)}, bf16[256,512]{1,0:T(8,128)(2,1)S(1)}, u32[]{:S(2)}, u32[]{:S(2)}) %collective-permute-start.10) | collective-permute-done | bytes 262176 | tf_op jit(solution)/shard_map/ppermute | solution.py:308
  122.5 0.0 collective-permute-done.11.other_ref
  122.5 1.1 total.1
  123.6 25.1 %all_to_all.10 = bf16[64,8,512]{2,1,0:T(8,128)(2,1)} all-to-all(bf16[64,8,512]{2,1,0:T(8,128)(2,1)S(1)} %bitcast.18), channel_id=1, replica_groups=mesh['tok'=64,'tp'=8] {'tok'}, dimensions={0} | all-to-all | bytes 1048576 | tf_op jit(solution)/shard_map/all_to_all | solution.py:300
  148.7 2.1 %combine.1 = bf16[128,512]{1,0:T(8,128)(2,1)} custom-call(bf16[128,512]{1,0:T(8,128)(2,1)} %get-tuple-element.27.hi_ref, bf16[128,512]{1,0:T(8,128)(2,1)} %get-tuple-element.28.lo_ref, bf16[512,512]{1,0:T(8,128)(2,1)} %bitcast.26), custom_call_target="tpu_custom_call" | custom-call | tf_op jit(solution)/shard_map/combine/pallas_call | solution.py:291
Async XLA Ops:
  2.5 46.4 %all-to-all-start = ((bf16[64,8,1024]{2,1,0:T(8,128)(2,1)}), bf16[64,8,1024]{2,1,0:T(8,128)(2,1)S(1)}, u32[]{:S(2)}, u32[]{:S(2)}) async-start(bf16[64,8,1024]{2,1,0:T(8,128)(2,1)} %bitcast.25), calls=%async_computation | async-start | bytes 2097152 | tf_op jit(solution)/shard_map/all_to_all | solution.py:300
  25.6 46.5 %collective-permute-start.5 = (bf16[4,576,512]{2,1,0:T(8,128)(2,1)}, bf16[4,576,512]{2,1,0:T(8,128)(2,1)S(1)}, u32[]{:S(2)}, u32[]{:S(2)}) collective-permute-start(bf16[4,576,512]{2,1,0:T(8,128)(2,1)} %get-tuple-element.36), channel_id=1, source_target_pairs={{0,1},{1,0},{2,3},{3,2},{4,5},{5,4},{6,7},{7,6},{8,9},{9,8},{10,11... | collective-permute-start | bytes 7077896 | tf_op jit(solution)/shard_map/ppermute | solution.py:308
  49.0 11.1 %collective-permute-start = (bf16[256,1024]{1,0:T(8,128)(2,1)S(1)}, bf16[256,1024]{1,0:T(8,128)(2,1)S(1)}, u32[]{:S(2)}, u32[]{:S(2)}) collective-permute-start(bf16[256,1024]{1,0:T(8,128)(2,1)S(1)} %get-tuple-element.42), channel_id=1, source_target_pairs={{0,2},{1,7},{2,4},{3,1},{4,6},{5,3},{6,0},{7,5},{8,10},{9,15},{10,... | collective-permute-start | bytes 1572872 | tf_op jit(solution)/shard_map/ppermute | solution.py:308
  51.4 15.0 %collective-permute-start.3 = (bf16[256,1024]{1,0:T(8,128)(2,1)S(1)}, bf16[256,1024]{1,0:T(8,128)(2,1)S(1)}, u32[]{:S(2)}, u32[]{:S(2)}) collective-permute-start(bf16[256,1024]{1,0:T(8,128)(2,1)S(1)} %get-tuple-element.41), channel_id=1, source_target_pairs={{0,2},{1,7},{2,4},{3,1},{4,6},{5,3},{6,0},{7,5},{8,10},{9,15},{10,... | collective-permute-start | bytes 1572872 | tf_op jit(solution)/shard_map/ppermute | solution.py:308
  60.1 28.1 %collective-permute-start.1 = (bf16[512,1024]{1,0:T(8,128)(2,1)S(1)}, bf16[512,1024]{1,0:T(8,128)(2,1)S(1)}, u32[]{:S(2)}, u32[]{:S(2)}) collective-permute-start(bf16[512,1024]{1,0:T(8,128)(2,1)S(1)} %bitcast.16), channel_id=1, source_target_pairs={{0,7},{1,2},{2,1},{3,4},{4,3},{5,6},{6,5},{7,0},{8,15},{9,10},{10,... | collective-permute-start | bytes 3145736 | tf_op jit(solution)/shard_map/ppermute | solution.py:308
  66.4 16.2 %collective-permute-start.4 = (bf16[256,1024]{1,0:T(8,128)(2,1)S(1)}, bf16[256,1024]{1,0:T(8,128)(2,1)S(1)}, u32[]{:S(2)}, u32[]{:S(2)}) collective-permute-start(bf16[256,1024]{1,0:T(8,128)(2,1)S(1)} %collective-permute-done.3.same_high_ref), channel_id=1, source_target_pairs={{0,2},{1,7},{2,4},{3,1},{4,6},{5,3},{6,0},{7,5},{8,10},{9,15},{10,... | collective-permute-start | bytes 1572872 | tf_op jit(solution)/shard_map/ppermute | solution.py:308
  69.3 18.9 %collective-permute-start.2 = (bf16[256,1024]{1,0:T(8,128)(2,1)S(1)}, bf16[256,1024]{1,0:T(8,128)(2,1)S(1)}, u32[]{:S(2)}, u32[]{:S(2)}) collective-permute-start(bf16[256,1024]{1,0:T(8,128)(2,1)S(1)} %collective-permute-done.same_low_ref), channel_id=1, source_target_pairs={{0,2},{1,7},{2,4},{3,1},{4,6},{5,3},{6,0},{7,5},{8,10},{9,15},{10,... | collective-permute-start | bytes 1572872 | tf_op jit(solution)/shard_map/ppermute | solution.py:308
  72.2 1.7 %copy-start = (bf16[4,576,512]{2,1,0:T(8,128)(2,1)S(1)}, bf16[4,576,512]{2,1,0:T(8,128)(2,1)}, u32[]{:S(2)}) copy-start(bf16[4,576,512]{2,1,0:T(8,128)(2,1)} %get-tuple-element.35.keep_ref) | copy-start | bytes 7077892
  90.4 6.4 %collective-permute-start.6 = (f32[2,576,512]{2,1,0:T(8,128)S(1)}, f32[2,576,512]{2,1,0:T(8,128)S(1)}, u32[]{:S(2)}, u32[]{:S(2)}) collective-permute-start(f32[2,576,512]{2,1,0:T(8,128)S(1)} %second.1.mine_ref), channel_id=1, source_target_pairs={{0,1},{1,0},{2,3},{3,2},{4,5},{5,4},{6,7},{7,6},{8,9},{9,8},{10,11... | collective-permute-start | bytes 7077896 | tf_op jit(solution)/shard_map/ppermute | solution.py:308
  99.0 9.5 %collective-permute-start.7 = (bf16[256,512]{1,0:T(8,128)(2,1)S(1)}, bf16[256,512]{1,0:T(8,128)(2,1)S(1)}, u32[]{:S(2)}, u32[]{:S(2)}) collective-permute-start(bf16[256,512]{1,0:T(8,128)(2,1)S(1)} %get-tuple-element.38), channel_id=1, source_target_pairs={{0,6},{1,3},{2,0},{3,5},{4,2},{5,7},{6,4},{7,1},{8,14},{9,11},{10,... | collective-permute-start | bytes 786440 | tf_op jit(solution)/shard_map/ppermute | solution.py:308
  101.7 9.5 %collective-permute-start.9 = (bf16[256,512]{1,0:T(8,128)(2,1)S(1)}, bf16[256,512]{1,0:T(8,128)(2,1)S(1)}, u32[]{:S(2)}, u32[]{:S(2)}) collective-permute-start(bf16[256,512]{1,0:T(8,128)(2,1)S(1)} %get-tuple-element.39), channel_id=1, source_target_pairs={{0,6},{1,3},{2,0},{3,5},{4,2},{5,7},{6,4},{7,1},{8,14},{9,11},{10,... | collective-permute-start | bytes 786440 | tf_op jit(solution)/shard_map/ppermute | solution.py:308
  104.2 18.3 %collective-permute-start.11 = (bf16[512,512]{1,0:T(8,128)(2,1)S(1)}, bf16[512,512]{1,0:T(8,128)(2,1)S(1)}, u32[]{:S(2)}, u32[]{:S(2)}) collective-permute-start(bf16[512,512]{1,0:T(8,128)(2,1)S(1)} %get-tuple-element.40), channel_id=1, source_target_pairs={{0,7},{1,2},{2,1},{3,4},{4,3},{5,6},{6,5},{7,0},{8,15},{9,10},{10,... | collective-permute-start | bytes 1572872 | tf_op jit(solution)/shard_map/ppermute | solution.py:308
  108.9 10.8 %collective-permute-start.8 = (bf16[256,512]{1,0:T(8,128)(2,1)S(1)}, bf16[256,512]{1,0:T(8,128)(2,1)S(1)}, u32[]{:S(2)}, u32[]{:S(2)}) collective-permute-start(bf16[256,512]{1,0:T(8,128)(2,1)S(1)} %near.2), channel_id=1, source_target_pairs={{0,6},{1,3},{2,0},{3,5},{4,2},{5,7},{6,4},{7,1},{8,14},{9,11},{10,... | collective-permute-start | bytes 786440 | tf_op jit(solution)/shard_map/ppermute | solution.py:308
  111.7 10.8 %collective-permute-start.10 = (bf16[256,512]{1,0:T(8,128)(2,1)S(1)}, bf16[256,512]{1,0:T(8,128)(2,1)S(1)}, u32[]{:S(2)}, u32[]{:S(2)}) collective-permute-start(bf16[256,512]{1,0:T(8,128)(2,1)S(1)} %near.3), channel_id=1, source_target_pairs={{0,6},{1,3},{2,0},{3,5},{4,2},{5,7},{6,4},{7,1},{8,14},{9,11},{10,... | collective-permute-start | bytes 786440 | tf_op jit(solution)/shard_map/ppermute | solution.py:308

commit v7 on v6

--- a/solution.py
+++ b/solution.py
@@ -135,8 +135,8 @@
     )(own, same_low, same_high, keep, sib)
 
 
-def second_kernel(other_ref, low_ref, high_ref, keep_ref, sib_ref, sum_ref, out_ref):
-    def add(rows_ref):
+def second_kernel(other_low_ref, other_high_ref, low_ref, high_ref, keep_ref, sib_ref, sum_ref, out_ref):
+    def add(other_ref, rows_ref):
         for n, weights in enumerate((keep_ref, sib_ref)):
             wide, narrow, split = products(weights[0], other_ref[...])
             far_wide, far_narrow, _ = products(weights[1], rows_ref[...])
@@ -145,15 +145,15 @@
 
     @pl.when(pl.program_id(0) == 0)
     def _():
-        add(low_ref)
+        add(other_low_ref, low_ref)
 
     @pl.when(pl.program_id(0) == 1)
     def _():
-        add(high_ref)
-
-
-def second(other, low, high, keep, sib, sums):
-    half, width = low.shape
+        add(other_high_ref, high_ref)
+
+
+def second(other, opposite, keep, sib, sums):
+    half, width = other[0].shape
     _, depth, block = keep.shape
     whole = pl.BlockSpec((half, width), lambda i: (0, 0))
     weights = pl.BlockSpec((2, depth, block), lambda i: (1, 0, 0))
@@ -161,12 +161,12 @@
     return pl.pallas_call(
         second_kernel,
         grid=(2,),
-        in_specs=[pl.BlockSpec((half, width), lambda i: (i, 0)), whole, whole, weights, weights, by_half],
+        in_specs=[whole] * 4 + [weights, weights, by_half],
         out_specs=by_half,
         out_shape=jax.ShapeDtypeStruct(sums.shape, sums.dtype),
         compiler_params=BIG,
         name="second",
-    )(other, low, high, keep, sib, sums)
+    )(*other, *opposite, keep, sib, sums)
 
 
 def chip_sum(grads, keep, sib):
@@ -336,12 +336,12 @@
     keep, give = pack(jnp.concatenate([block_order(chip, core), block_order(chip, 1 - core)]), weights)
     sib = to_sibling(give)
     half = own.shape[0] // 2
-    same_low, same_high = from_near(own[:half]), from_near(own[half:])
-    same_low, later = lax.optimization_barrier((same_low, own))
-    other = to_near_other(later)
-    opposite_low, opposite_high = from_near(same_low), from_near(same_high)
-    mine = first(own, same_low, same_high, keep, sib)
-    mine = second(other, opposite_low, opposite_high, keep, sib, mine)
+    halves = (own[:half], own[half:])
+    same = [from_near(rows) for rows in halves]
+    other = [to_near_other(rows) for rows in halves]
+    opposite = [from_near(rows) for rows in same]
+    mine = first(own, *same, keep, sib)
+    mine = second(other, opposite, keep, sib, mine)
     theirs = to_sibling(mine)
     grads_value, part_low, part_high, for_other = grads(mine, theirs, keep, sib)
     passing_low, passing_high = to_near(part_low), to_near(part_high)

time: 153 us -> 153 us (level)
  starting transfers between devices: 47.3 us -> 51.9 us
  waiting for transfers between devices: 55.3 us -> 50.7 us
    ppermute x12 -> x13, waiting for transfers between devices: 35.6 us -> 31 us  [send(): return lax.ppermute(value, 'tp', pairs)]
    ppermute x12 -> x13, starting transfers between devices: 30.7 us -> 35.3 us  [send(): return lax.ppermute(value, 'tp', pairs)]
  transfers between devices with their start and end apart: 13 -> 14, of which waited for: 10 -> 11; matrix products, arithmetic and copies ran while one was open for 0% -> 0% of each run, Pallas kernels for 7% -> 7%
where the time goes in v7:
time: 153 us; the launch traced here: 151 us
  starting transfers between devices  51.9 us (34%)
  waiting for transfers between devices  50.7 us (33%)
  blocking collectives  24.8 us (16%)
  Pallas kernels  20.5 us (13%)
  local copies, waits for them, and re-layouts  1.73 us (1%)
    ppermute x13, starting transfers between devices, send(): return lax.ppermute(value, 'tp', pairs)  35.3 us
    ppermute x13, waiting for transfers between devices, send(): return lax.ppermute(value, 'tp', pairs)  31 us
    all_to_all x1, blocking collectives, exchange(): lax.all_to_all(blocks, 'tok', split_axis=0, concat_axis=0, tiled=True)  24.8 us
    all_to_all x1, waiting for transfers between devices, exchange(): lax.all_to_all(blocks, 'tok', split_axis=0, concat_axis=0, tiled=True)  19.7 us
    all_to_all x1, starting transfers between devices, exchange(): lax.all_to_all(blocks, 'tok', split_axis=0, concat_axis=0, tiled=True)  16.6 us
    pallas_call x1, Pallas kernels, pack(): pl.pallas_call(pack_kernel, grid_spec=pltpu.PrefetchScalarGridSpec(num_sc...  5.8 us
  transfers between devices with their start and end apart: 14, of which 11 were waited for; matrix products, arithmetic and copies ran while one was open for 0% of the time, Pallas kernels for 7%

profile of v7, /device:TPU:6, one launch (start us, length us, event | category | flops | bytes accessed | tf_op | source)
XLA Modules:
  0.0 150.6 jit_solution(16527545853100410747)
XLA Ops:
  0.0 2.5 %dispatch.1 = bf16[512,1024]{1,0:T(8,128)(2,1)} custom-call(s32[2,128]{1,0:T(2,128)} %bitcast.26, bf16[128,512]{1,0:T(8,128)(2,1)} %x_ref.1, bf16[128,512]{1,0:T(8,128)(2,1)} %g_ref.1), custom_call_target="tpu_custom_call" | custom-call | tf_op jit(solution)/shard_map/dispatch/pallas_call | solution.py:44
  2.5 16.6 %all-to-all-start = ((bf16[64,8,1024]{2,1,0:T(8,128)(2,1)}), bf16[64,8,1024]{2,1,0:T(8,128)(2,1)S(1)}, u32[]{:S(2)}, u32[]{:S(2)}) async-start(bf16[64,8,1024]{2,1,0:T(8,128)(2,1)} %bitcast.24), calls=%async_computation | async-start | bytes 2097152 | tf_op jit(solution)/shard_map/all_to_all | solution.py:300
  19.1 0.1 fusion.1
  19.2 0.6 pad_add_fusion.blocks_ref
  19.8 5.8 %pack.1 = (bf16[4,576,512]{2,1,0:T(8,128)(2,1)}, bf16[4,576,512]{2,1,0:T(8,128)(2,1)}) custom-call(s32[8]{0:T(128)} %pad_add_fusion.blocks_ref, bf16[192,4096]{1,0:T(8,128)(2,1)} %bitcast.18, bf16[192,4096]{1,0:T(8,128)(2,1)} %bitcast.20, bf16[192,4096]{1,0:T(8,128)(2,1)} %bitcast.22, bf16[192,4096]{1,0:T(8,128)(2,1)} %bitcast.19, ...), custom_call_target="tpu_custom_call" | custom-call | tf_op jit(solution)/shard_map/pack/pallas_call | solution.py:83
  25.6 1.9 %collective-permute-start.6 = (bf16[4,576,512]{2,1,0:T(8,128)(2,1)}, bf16[4,576,512]{2,1,0:T(8,128)(2,1)S(1)}, u32[]{:S(2)}, u32[]{:S(2)}) collective-permute-start(bf16[4,576,512]{2,1,0:T(8,128)(2,1)} %get-tuple-element.32), channel_id=1, source_target_pairs={{0,1},{1,0},{2,3},{3,2},{4,5},{5,4},{6,7},{7,6},{8,9},{9,8},{10,11... | collective-permute-start | bytes 7077896 | tf_op jit(solution)/shard_map/ppermute | solution.py:308
  27.5 1.7 %mixer.1 = (bf16[128,512]{1,0:T(8,128)(2,1)}, bf16[128,512]{1,0:T(8,128)(2,1)}) custom-call(s32[2,128]{1,0:T(2,128)} %bitcast.27, f32[2,128]{1,0:T(2,128)} %bitcast.28), custom_call_target="tpu_custom_call" | custom-call | tf_op jit(solution)/shard_map/mixer/pallas_call | solution.py:61
  29.2 19.7 %all-to-all-done = bf16[64,8,1024]{2,1,0:T(8,128)(2,1)S(1)} async-done(((bf16[64,8,1024]{2,1,0:T(8,128)(2,1)}), bf16[64,8,1024]{2,1,0:T(8,128)(2,1)S(1)}, u32[]{:S(2)}, u32[]{:S(2)}) %all-to-all-start) | async-done | bytes 1048608 | tf_op jit(solution)/shard_map/all_to_all | solution.py:300
  48.9 0.1 fusion.4
  49.0 2.4 %collective-permute-start.4 = (bf16[256,1024]{1,0:T(8,128)(2,1)S(1)}, bf16[256,1024]{1,0:T(8,128)(2,1)S(1)}, u32[]{:S(2)}, u32[]{:S(2)}) collective-permute-start(bf16[256,1024]{1,0:T(8,128)(2,1)S(1)} %get-tuple-element.37), channel_id=1, source_target_pairs={{0,2},{1,7},{2,4},{3,1},{4,6},{5,3},{6,0},{7,5},{8,10},{9,15},{10,... | collective-permute-start | bytes 1572872 | tf_op jit(solution)/shard_map/ppermute | solution.py:308
  51.4 3.4 %collective-permute-start.2 = (bf16[256,1024]{1,0:T(8,128)(2,1)S(1)}, bf16[256,1024]{1,0:T(8,128)(2,1)S(1)}, u32[]{:S(2)}, u32[]{:S(2)}) collective-permute-start(bf16[256,1024]{1,0:T(8,128)(2,1)S(1)} %get-tuple-element.38), channel_id=1, source_target_pairs={{0,2},{1,7},{2,4},{3,1},{4,6},{5,3},{6,0},{7,5},{8,10},{9,15},{10,... | collective-permute-start | bytes 1572872 | tf_op jit(solution)/shard_map/ppermute | solution.py:308
  54.8 1.9 %collective-permute-start.1 = (bf16[256,1024]{1,0:T(8,128)(2,1)S(1)}, bf16[256,1024]{1,0:T(8,128)(2,1)S(1)}, u32[]{:S(2)}, u32[]{:S(2)}) collective-permute-start(bf16[256,1024]{1,0:T(8,128)(2,1)S(1)} %get-tuple-element.37), channel_id=1, source_target_pairs={{0,7},{1,2},{2,1},{3,4},{4,3},{5,6},{6,5},{7,0},{8,15},{9,10},{10,... | collective-permute-start | bytes 1572872 | tf_op jit(solution)/shard_map/ppermute | solution.py:308
  56.7 3.6 %collective-permute-start = (bf16[256,1024]{1,0:T(8,128)(2,1)S(1)}, bf16[256,1024]{1,0:T(8,128)(2,1)S(1)}, u32[]{:S(2)}, u32[]{:S(2)}) collective-permute-start(bf16[256,1024]{1,0:T(8,128)(2,1)S(1)} %get-tuple-element.38), channel_id=1, source_target_pairs={{0,7},{1,2},{2,1},{3,4},{4,3},{5,6},{6,5},{7,0},{8,15},{9,10},{10,... | collective-permute-start | bytes 1572872 | tf_op jit(solution)/shard_map/ppermute | solution.py:308
  60.4 0.0 collective-permute-done.4.same_high_ref
  60.4 4.6 %collective-permute-start.5 = (bf16[256,1024]{1,0:T(8,128)(2,1)S(1)}, bf16[256,1024]{1,0:T(8,128)(2,1)S(1)}, u32[]{:S(2)}, u32[]{:S(2)}) collective-permute-start(bf16[256,1024]{1,0:T(8,128)(2,1)S(1)} %collective-permute-done.4.same_high_ref), channel_id=1, source_target_pairs={{0,2},{1,7},{2,4},{3,1},{4,6},{5,3},{6,0},{7,5},{8,10},{9,15},{10,... | collective-permute-start | bytes 1572872 | tf_op jit(solution)/shard_map/ppermute | solution.py:308
  65.0 6.6 %collective-permute-done.2.same_low_ref = bf16[256,1024]{1,0:T(8,128)(2,1)S(1)} collective-permute-done((bf16[256,1024]{1,0:T(8,128)(2,1)S(1)}, bf16[256,1024]{1,0:T(8,128)(2,1)S(1)}, u32[]{:S(2)}, u32[]{:S(2)}) %collective-permute-start.2) | collective-permute-done | bytes 524320 | tf_op jit(solution)/shard_map/ppermute | solution.py:308
  71.6 2.6 %collective-permute-start.3 = (bf16[256,1024]{1,0:T(8,128)(2,1)S(1)}, bf16[256,1024]{1,0:T(8,128)(2,1)S(1)}, u32[]{:S(2)}, u32[]{:S(2)}) collective-permute-start(bf16[256,1024]{1,0:T(8,128)(2,1)S(1)} %collective-permute-done.2.same_low_ref), channel_id=1, source_target_pairs={{0,2},{1,7},{2,4},{3,1},{4,6},{5,3},{6,0},{7,5},{8,10},{9,15},{10,... | collective-permute-start | bytes 1572872 | tf_op jit(solution)/shard_map/ppermute | solution.py:308
  74.2 0.0 collective-permute-done.6.sib_ref
  74.2 0.0 copy-start
  74.2 1.7 %copy-done = bf16[4,576,512]{2,1,0:T(8,128)(2,1)S(1)} copy-done((bf16[4,576,512]{2,1,0:T(8,128)(2,1)S(1)}, bf16[4,576,512]{2,1,0:T(8,128)(2,1)}, u32[]{:S(2)}) %copy-start) | copy-done | bytes 2359320
  75.9 2.0 %first.1.sum_ref = f32[2,576,512]{2,1,0:T(8,128)S(1)} custom-call(bf16[512,1024]{1,0:T(8,128)(2,1)S(1)} %bitcast.16, bf16[256,1024]{1,0:T(8,128)(2,1)S(1)} %collective-permute-done.2.same_low_ref, bf16[256,1024]{1,0:T(8,128)(2,1)S(1)} %collective-permute-done.4.same_high_ref, bf16[4,576,512]{2,1,0:T(8,128)(2,1)S(1)} %copy-done, ...), custom_call_target="tpu_custom_call" | custom-call | tf_op jit(solution)/shard_map/first/pallas_call | solution.py:127
  77.9 0.0 collective-permute-done.1.other_high_ref
  77.9 4.3 %collective-permute-done.other_low_ref = bf16[256,1024]{1,0:T(8,128)(2,1)S(1)} collective-permute-done((bf16[256,1024]{1,0:T(8,128)(2,1)S(1)}, bf16[256,1024]{1,0:T(8,128)(2,1)S(1)}, u32[]{:S(2)}, u32[]{:S(2)}) %collective-permute-start) | collective-permute-done | bytes 524320 | tf_op jit(solution)/shard_map/ppermute | solution.py:308
  82.2 0.3 collective-permute-done.5.high_ref
  82.5 5.6 %collective-permute-done.3.low_ref = bf16[256,1024]{1,0:T(8,128)(2,1)S(1)} collective-permute-done((bf16[256,1024]{1,0:T(8,128)(2,1)S(1)}, bf16[256,1024]{1,0:T(8,128)(2,1)S(1)}, u32[]{:S(2)}, u32[]{:S(2)}) %collective-permute-start.3) | collective-permute-done | bytes 524320 | tf_op jit(solution)/shard_map/ppermute | solution.py:308
  88.2 2.2 %second.1.mine_ref = f32[2,576,512]{2,1,0:T(8,128)S(1)} custom-call(bf16[256,1024]{1,0:T(8,128)(2,1)S(1)} %collective-permute-done.other_low_ref, bf16[256,1024]{1,0:T(8,128)(2,1)S(1)} %collective-permute-done.1.other_high_ref, bf16[256,1024]{1,0:T(8,128)(2,1)S(1)} %collective-permute-done.3.low_ref, bf16[256,1024]{1,0:T(8,128)(2,1)S(1)} %collective-permute-done.5.high_ref, ...), custom_call_target="tpu_custom_call" | custom-call | tf_op jit(solution)/shard_map/second/pallas_call | solution.py:161
  90.3 1.9 %collective-permute-start.7 = (f32[2,576,512]{2,1,0:T(8,128)S(1)}, f32[2,576,512]{2,1,0:T(8,128)S(1)}, u32[]{:S(2)}, u32[]{:S(2)}) collective-permute-start(f32[2,576,512]{2,1,0:T(8,128)S(1)} %second.1.mine_ref), channel_id=1, source_target_pairs={{0,1},{1,0},{2,3},{3,2},{4,5},{5,4},{6,7},{7,6},{8,9},{9,8},{10,11... | collective-permute-start | bytes 7077896 | tf_op jit(solution)/shard_map/ppermute | solution.py:308
  92.3 4.5 %collective-permute-done.7.theirs_ref = f32[2,576,512]{2,1,0:T(8,128)S(1)} collective-permute-done((f32[2,576,512]{2,1,0:T(8,128)S(1)}, f32[2,576,512]{2,1,0:T(8,128)S(1)}, u32[]{:S(2)}, u32[]{:S(2)}) %collective-permute-start.7) | collective-permute-done | bytes 2359328 | tf_op jit(solution)/shard_map/ppermute | solution.py:308
  96.8 2.2 %grads.1 = (bf16[2,384,512]{2,1,0:T(8,128)(2,1)S(1)}, bf16[256,512]{1,0:T(8,128)(2,1)S(1)}, bf16[256,512]{1,0:T(8,128)(2,1)S(1)}, bf16[512,512]{1,0:T(8,128)(2,1)S(1)}) custom-call(f32[2,576,512]{2,1,0:T(8,128)S(1)} %second.1.mine_ref, f32[2,576,512]{2,1,0:T(8,128)S(1)} %collective-permute-done.7.theirs_ref, bf16[4,576,512]{2,1,0:T(8,128)(2,1)S(1)} %copy-done, ...), custom_call_target="tpu_custom_call" | custom-call | tf_op jit(solution)/shard_map/grads/pallas_call | solution.py:210
  99.0 2.7 %collective-permute-start.8 = (bf16[256,512]{1,0:T(8,128)(2,1)S(1)}, bf16[256,512]{1,0:T(8,128)(2,1)S(1)}, u32[]{:S(2)}, u32[]{:S(2)}) collective-permute-start(bf16[256,512]{1,0:T(8,128)(2,1)S(1)} %get-tuple-element.34), channel_id=1, source_target_pairs={{0,6},{1,3},{2,0},{3,5},{4,2},{5,7},{6,4},{7,1},{8,14},{9,11},{10,... | collective-permute-start | bytes 786440 | tf_op jit(solution)/shard_map/ppermute | solution.py:308
  101.7 2.4 %collective-permute-start.10 = (bf16[256,512]{1,0:T(8,128)(2,1)S(1)}, bf16[256,512]{1,0:T(8,128)(2,1)S(1)}, u32[]{:S(2)}, u32[]{:S(2)}) collective-permute-start(bf16[256,512]{1,0:T(8,128)(2,1)S(1)} %get-tuple-element.35), channel_id=1, source_target_pairs={{0,6},{1,3},{2,0},{3,5},{4,2},{5,7},{6,4},{7,1},{8,14},{9,11},{10,... | collective-permute-start | bytes 786440 | tf_op jit(solution)/shard_map/ppermute | solution.py:308
  104.1 3.4 %collective-permute-start.12 = (bf16[512,512]{1,0:T(8,128)(2,1)S(1)}, bf16[512,512]{1,0:T(8,128)(2,1)S(1)}, u32[]{:S(2)}, u32[]{:S(2)}) collective-permute-start(bf16[512,512]{1,0:T(8,128)(2,1)S(1)} %get-tuple-element.36), channel_id=1, source_target_pairs={{0,7},{1,2},{2,1},{3,4},{4,3},{5,6},{6,5},{7,0},{8,15},{9,10},{10,... | collective-permute-start | bytes 1572872 | tf_op jit(solution)/shard_map/ppermute | solution.py:308
  107.6 0.8 collective-permute-done.8.got_ref
  108.4 0.5 near.2
  108.9 1.9 %collective-permute-start.9 = (bf16[256,512]{1,0:T(8,128)(2,1)S(1)}, bf16[256,512]{1,0:T(8,128)(2,1)S(1)}, u32[]{:S(2)}, u32[]{:S(2)}) collective-permute-start(bf16[256,512]{1,0:T(8,128)(2,1)S(1)} %near.2), channel_id=1, source_target_pairs={{0,6},{1,3},{2,0},{3,5},{4,2},{5,7},{6,4},{7,1},{8,14},{9,11},{10,... | collective-permute-start | bytes 786440 | tf_op jit(solution)/shard_map/ppermute | solution.py:308
  110.8 0.4 collective-permute-done.10.got_ref
  111.2 0.5 near.3
  111.7 2.4 %collective-permute-start.11 = (bf16[256,512]{1,0:T(8,128)(2,1)S(1)}, bf16[256,512]{1,0:T(8,128)(2,1)S(1)}, u32[]{:S(2)}, u32[]{:S(2)}) collective-permute-start(bf16[256,512]{1,0:T(8,128)(2,1)S(1)} %near.3), channel_id=1, source_target_pairs={{0,6},{1,3},{2,0},{3,5},{4,2},{5,7},{6,4},{7,1},{8,14},{9,11},{10,... | collective-permute-start | bytes 786440 | tf_op jit(solution)/shard_map/ppermute | solution.py:308
  114.2 1.2 collective-permute-done.12.other_ref
  115.3 4.3 %collective-permute-done.9.low_ref = bf16[256,512]{1,0:T(8,128)(2,1)S(1)} collective-permute-done((bf16[256,512]{1,0:T(8,128)(2,1)S(1)}, bf16[256,512]{1,0:T(8,128)(2,1)S(1)}, u32[]{:S(2)}, u32[]{:S(2)}) %collective-permute-start.9) | collective-permute-done | bytes 262176 | tf_op jit(solution)/shard_map/ppermute | solution.py:308
  119.7 2.8 %collective-permute-done.11.high_ref = bf16[256,512]{1,0:T(8,128)(2,1)S(1)} collective-permute-done((bf16[256,512]{1,0:T(8,128)(2,1)S(1)}, bf16[256,512]{1,0:T(8,128)(2,1)S(1)}, u32[]{:S(2)}, u32[]{:S(2)}) %collective-permute-start.11) | collective-permute-done | bytes 262176 | tf_op jit(solution)/shard_map/ppermute | solution.py:308
  122.5 1.1 total.1
  123.6 24.8 %all_to_all.10 = bf16[64,8,512]{2,1,0:T(8,128)(2,1)} all-to-all(bf16[64,8,512]{2,1,0:T(8,128)(2,1)S(1)} %bitcast.17), channel_id=1, replica_groups=mesh['tok'=64,'tp'=8] {'tok'}, dimensions={0} | all-to-all | bytes 1048576 | tf_op jit(solution)/shard_map/all_to_all | solution.py:300
  148.4 2.1 %combine.1 = bf16[128,512]{1,0:T(8,128)(2,1)} custom-call(bf16[128,512]{1,0:T(8,128)(2,1)} %get-tuple-element.25.hi_ref, bf16[128,512]{1,0:T(8,128)(2,1)} %get-tuple-element.26.lo_ref, bf16[512,512]{1,0:T(8,128)(2,1)} %bitcast.25), custom_call_target="tpu_custom_call" | custom-call | tf_op jit(solution)/shard_map/combine/pallas_call | solution.py:291
Async XLA Ops:
  2.5 46.4 %all-to-all-start = ((bf16[64,8,1024]{2,1,0:T(8,128)(2,1)}), bf16[64,8,1024]{2,1,0:T(8,128)(2,1)S(1)}, u32[]{:S(2)}, u32[]{:S(2)}) async-start(bf16[64,8,1024]{2,1,0:T(8,128)(2,1)} %bitcast.24), calls=%async_computation | async-start | bytes 2097152 | tf_op jit(solution)/shard_map/all_to_all | solution.py:300
  25.6 48.6 %collective-permute-start.6 = (bf16[4,576,512]{2,1,0:T(8,128)(2,1)}, bf16[4,576,512]{2,1,0:T(8,128)(2,1)S(1)}, u32[]{:S(2)}, u32[]{:S(2)}) collective-permute-start(bf16[4,576,512]{2,1,0:T(8,128)(2,1)} %get-tuple-element.32), channel_id=1, source_target_pairs={{0,1},{1,0},{2,3},{3,2},{4,5},{5,4},{6,7},{7,6},{8,9},{9,8},{10,11... | collective-permute-start | bytes 7077896 | tf_op jit(solution)/shard_map/ppermute | solution.py:308
  49.0 11.4 %collective-permute-start.4 = (bf16[256,1024]{1,0:T(8,128)(2,1)S(1)}, bf16[256,1024]{1,0:T(8,128)(2,1)S(1)}, u32[]{:S(2)}, u32[]{:S(2)}) collective-permute-start(bf16[256,1024]{1,0:T(8,128)(2,1)S(1)} %get-tuple-element.37), channel_id=1, source_target_pairs={{0,2},{1,7},{2,4},{3,1},{4,6},{5,3},{6,0},{7,5},{8,10},{9,15},{10,... | collective-permute-start | bytes 1572872 | tf_op jit(solution)/shard_map/ppermute | solution.py:308
  51.4 20.2 %collective-permute-start.2 = (bf16[256,1024]{1,0:T(8,128)(2,1)S(1)}, bf16[256,1024]{1,0:T(8,128)(2,1)S(1)}, u32[]{:S(2)}, u32[]{:S(2)}) collective-permute-start(bf16[256,1024]{1,0:T(8,128)(2,1)S(1)} %get-tuple-element.38), channel_id=1, source_target_pairs={{0,2},{1,7},{2,4},{3,1},{4,6},{5,3},{6,0},{7,5},{8,10},{9,15},{10,... | collective-permute-start | bytes 1572872 | tf_op jit(solution)/shard_map/ppermute | solution.py:308
  54.8 23.1 %collective-permute-start.1 = (bf16[256,1024]{1,0:T(8,128)(2,1)S(1)}, bf16[256,1024]{1,0:T(8,128)(2,1)S(1)}, u32[]{:S(2)}, u32[]{:S(2)}) collective-permute-start(bf16[256,1024]{1,0:T(8,128)(2,1)S(1)} %get-tuple-element.37), channel_id=1, source_target_pairs={{0,7},{1,2},{2,1},{3,4},{4,3},{5,6},{6,5},{7,0},{8,15},{9,10},{10,... | collective-permute-start | bytes 1572872 | tf_op jit(solution)/shard_map/ppermute | solution.py:308
  56.7 25.5 %collective-permute-start = (bf16[256,1024]{1,0:T(8,128)(2,1)S(1)}, bf16[256,1024]{1,0:T(8,128)(2,1)S(1)}, u32[]{:S(2)}, u32[]{:S(2)}) collective-permute-start(bf16[256,1024]{1,0:T(8,128)(2,1)S(1)} %get-tuple-element.38), channel_id=1, source_target_pairs={{0,7},{1,2},{2,1},{3,4},{4,3},{5,6},{6,5},{7,0},{8,15},{9,10},{10,... | collective-permute-start | bytes 1572872 | tf_op jit(solution)/shard_map/ppermute | solution.py:308
  60.4 22.1 %collective-permute-start.5 = (bf16[256,1024]{1,0:T(8,128)(2,1)S(1)}, bf16[256,1024]{1,0:T(8,128)(2,1)S(1)}, u32[]{:S(2)}, u32[]{:S(2)}) collective-permute-start(bf16[256,1024]{1,0:T(8,128)(2,1)S(1)} %collective-permute-done.4.same_high_ref), channel_id=1, source_target_pairs={{0,2},{1,7},{2,4},{3,1},{4,6},{5,3},{6,0},{7,5},{8,10},{9,15},{10,... | collective-permute-start | bytes 1572872 | tf_op jit(solution)/shard_map/ppermute | solution.py:308
  71.6 16.5 %collective-permute-start.3 = (bf16[256,1024]{1,0:T(8,128)(2,1)S(1)}, bf16[256,1024]{1,0:T(8,128)(2,1)S(1)}, u32[]{:S(2)}, u32[]{:S(2)}) collective-permute-start(bf16[256,1024]{1,0:T(8,128)(2,1)S(1)} %collective-permute-done.2.same_low_ref), channel_id=1, source_target_pairs={{0,2},{1,7},{2,4},{3,1},{4,6},{5,3},{6,0},{7,5},{8,10},{9,15},{10,... | collective-permute-start | bytes 1572872 | tf_op jit(solution)/shard_map/ppermute | solution.py:308
  74.2 1.7 %copy-start = (bf16[4,576,512]{2,1,0:T(8,128)(2,1)S(1)}, bf16[4,576,512]{2,1,0:T(8,128)(2,1)}, u32[]{:S(2)}) copy-start(bf16[4,576,512]{2,1,0:T(8,128)(2,1)} %get-tuple-element.31.keep_ref) | copy-start | bytes 7077892
  90.3 6.4 %collective-permute-start.7 = (f32[2,576,512]{2,1,0:T(8,128)S(1)}, f32[2,576,512]{2,1,0:T(8,128)S(1)}, u32[]{:S(2)}, u32[]{:S(2)}) collective-permute-start(f32[2,576,512]{2,1,0:T(8,128)S(1)} %second.1.mine_ref), channel_id=1, source_target_pairs={{0,1},{1,0},{2,3},{3,2},{4,5},{5,4},{6,7},{7,6},{8,9},{9,8},{10,11... | collective-permute-start | bytes 7077896 | tf_op jit(solution)/shard_map/ppermute | solution.py:308
  99.0 9.5 %collective-permute-start.8 = (bf16[256,512]{1,0:T(8,128)(2,1)S(1)}, bf16[256,512]{1,0:T(8,128)(2,1)S(1)}, u32[]{:S(2)}, u32[]{:S(2)}) collective-permute-start(bf16[256,512]{1,0:T(8,128)(2,1)S(1)} %get-tuple-element.34), channel_id=1, source_target_pairs={{0,6},{1,3},{2,0},{3,5},{4,2},{5,7},{6,4},{7,1},{8,14},{9,11},{10,... | collective-permute-start | bytes 786440 | tf_op jit(solution)/shard_map/ppermute | solution.py:308
  101.7 9.5 %collective-permute-start.10 = (bf16[256,512]{1,0:T(8,128)(2,1)S(1)}, bf16[256,512]{1,0:T(8,128)(2,1)S(1)}, u32[]{:S(2)}, u32[]{:S(2)}) collective-permute-start(bf16[256,512]{1,0:T(8,128)(2,1)S(1)} %get-tuple-element.35), channel_id=1, source_target_pairs={{0,6},{1,3},{2,0},{3,5},{4,2},{5,7},{6,4},{7,1},{8,14},{9,11},{10,... | collective-permute-start | bytes 786440 | tf_op jit(solution)/shard_map/ppermute | solution.py:308
  104.1 11.2 %collective-permute-start.12 = (bf16[512,512]{1,0:T(8,128)(2,1)S(1)}, bf16[512,512]{1,0:T(8,128)(2,1)S(1)}, u32[]{:S(2)}, u32[]{:S(2)}) collective-permute-start(bf16[512,512]{1,0:T(8,128)(2,1)S(1)} %get-tuple-element.36), channel_id=1, source_target_pairs={{0,7},{1,2},{2,1},{3,4},{4,3},{5,6},{6,5},{7,0},{8,15},{9,10},{10,... | collective-permute-start | bytes 1572872 | tf_op jit(solution)/shard_map/ppermute | solution.py:308
  108.9 10.8 %collective-permute-start.9 = (bf16[256,512]{1,0:T(8,128)(2,1)S(1)}, bf16[256,512]{1,0:T(8,128)(2,1)S(1)}, u32[]{:S(2)}, u32[]{:S(2)}) collective-permute-start(bf16[256,512]{1,0:T(8,128)(2,1)S(1)} %near.2), channel_id=1, source_target_pairs={{0,6},{1,3},{2,0},{3,5},{4,2},{5,7},{6,4},{7,1},{8,14},{9,11},{10,... | collective-permute-start | bytes 786440 | tf_op jit(solution)/shard_map/ppermute | solution.py:308
  111.7 10.8 %collective-permute-start.11 = (bf16[256,512]{1,0:T(8,128)(2,1)S(1)}, bf16[256,512]{1,0:T(8,128)(2,1)S(1)}, u32[]{:S(2)}, u32[]{:S(2)}) collective-permute-start(bf16[256,512]{1,0:T(8,128)(2,1)S(1)} %near.3), channel_id=1, source_target_pairs={{0,6},{1,3},{2,0},{3,5},{4,2},{5,7},{6,4},{7,1},{8,14},{9,11},{10,... | collective-permute-start | bytes 786440 | tf_op jit(solution)/shard_map/ppermute | solution.py:308

commit v8 on v7

--- a/solution.py
+++ b/solution.py
@@ -135,38 +135,28 @@
     )(own, same_low, same_high, keep, sib)
 
 
-def second_kernel(other_low_ref, other_high_ref, low_ref, high_ref, keep_ref, sib_ref, sum_ref, out_ref):
-    def add(other_ref, rows_ref):
-        for n, weights in enumerate((keep_ref, sib_ref)):
-            wide, narrow, split = products(weights[0], other_ref[...])
-            far_wide, far_narrow, _ = products(weights[1], rows_ref[...])
-            out_ref[n, :split, :] = sum_ref[n, :split, :] + (wide + far_wide)
-            out_ref[n, split:, :] = sum_ref[n, split:, :] + (narrow + far_narrow)
-
-    @pl.when(pl.program_id(0) == 0)
-    def _():
-        add(other_low_ref, low_ref)
-
-    @pl.when(pl.program_id(0) == 1)
-    def _():
-        add(other_high_ref, high_ref)
-
-
-def second(other, opposite, keep, sib, sums):
-    half, width = other[0].shape
+def second_kernel(other_ref, opposite_ref, keep_ref, sib_ref, sum_ref, out_ref):
+    for n, weights in enumerate((keep_ref, sib_ref)):
+        wide, narrow, split = products(weights[0], other_ref[...])
+        far_wide, far_narrow, _ = products(weights[1], opposite_ref[...])
+        out_ref[n, :split, :] = sum_ref[n, :split, :] + (wide + far_wide)
+        out_ref[n, split:, :] = sum_ref[n, split:, :] + (narrow + far_narrow)
+
+
+def second(other, opposite, keep, sib, sums, part):
+    half, width = other.shape
     _, depth, block = keep.shape
     whole = pl.BlockSpec((half, width), lambda i: (0, 0))
     weights = pl.BlockSpec((2, depth, block), lambda i: (1, 0, 0))
-    by_half = pl.BlockSpec((CORES, depth, half), lambda i: (0, 0, i))
     return pl.pallas_call(
         second_kernel,
-        grid=(2,),
-        in_specs=[whole] * 4 + [weights, weights, by_half],
-        out_specs=by_half,
-        out_shape=jax.ShapeDtypeStruct(sums.shape, sums.dtype),
+        grid=(1,),
+        in_specs=[whole, whole, weights, weights, pl.BlockSpec((CORES, depth, half), lambda i: (0, 0, part))],
+        out_specs=pl.BlockSpec((CORES, depth, half), lambda i: (0, 0, 0)),
+        out_shape=jax.ShapeDtypeStruct((CORES, depth, half), sums.dtype),
         compiler_params=BIG,
         name="second",
-    )(*other, *opposite, keep, sib, sums)
+    )(other, opposite, keep, sib, sums)
 
 
 def chip_sum(grads, keep, sib):
@@ -176,7 +166,7 @@
     )
 
 
-def grads_kernel(mine_ref, theirs_ref, keep_ref, sib_ref, grads_ref, low_ref, high_ref, other_ref):
+def grads_kernel(mine_ref, theirs_ref, keep_ref, sib_ref, grads_ref, part_ref):
     hidden = mine_ref.shape[1] // 3
     for n in range(CORES):
         gate_pre = mine_ref[n, :hidden, :] + theirs_ref[1 - n, :hidden, :]
@@ -186,43 +176,21 @@
         slope = sigma * (1.0 + gate_pre * (1.0 - sigma))
         grads_ref[n, :hidden, :] = (hidden_grad * up_pre * slope).astype(grads_ref.dtype)
         grads_ref[n, hidden:, :] = (hidden_grad * (gate_pre * sigma)).astype(grads_ref.dtype)
-    other_ref[...] = chip_sum(grads_ref[...], keep_ref[0], sib_ref[0]).astype(other_ref.dtype)
-    value = chip_sum(grads_ref[...], keep_ref[1], sib_ref[1]).astype(low_ref.dtype)
-
-    @pl.when(pl.program_id(0) == 0)
-    def _():
-        low_ref[...] = value
-
-    @pl.when(pl.program_id(0) == 1)
-    def _():
-        high_ref[...] = value
+    part_ref[...] = chip_sum(grads_ref[...], keep_ref[0], sib_ref[0]).astype(part_ref.dtype)
 
 
 def grads(mine, theirs, keep, sib):
-    _, depth, rows = mine.shape
+    _, depth, half = mine.shape
     block = keep.shape[2]
-    half = rows // 2
     wide = depth // 3 * 2
-    by_half = pl.BlockSpec((CORES, depth, half), lambda i: (0, 0, i))
-    weights = pl.BlockSpec((2, depth, block), lambda i: (1, 0, 0))
-    whole = pl.BlockSpec((half, block), lambda i: (0, 0))
-    part = jax.ShapeDtypeStruct((half, block), jnp.bfloat16)
+    whole = pl.BlockSpec((CORES, depth, half), lambda i: (0, 0, 0))
+    weights = pl.BlockSpec((1, depth, block), lambda i: (CHIPS - 1, 0, 0))
     return pl.pallas_call(
         grads_kernel,
-        grid=(2,),
-        in_specs=[by_half] * 2 + [weights] * 2,
-        out_specs=[
-            pl.BlockSpec((CORES, wide, half), lambda i: (0, 0, i)),
-            whole,
-            whole,
-            pl.BlockSpec((half, block), lambda i: (i, 0)),
-        ],
-        out_shape=(
-            jax.ShapeDtypeStruct((CORES, wide, rows), jnp.bfloat16),
-            part,
-            part,
-            jax.ShapeDtypeStruct((rows, block), jnp.bfloat16),
-        ),
+        grid=(1,),
+        in_specs=[whole, whole, weights, weights],
+        out_specs=[pl.BlockSpec((CORES, wide, half), lambda i: (0, 0, 0)), pl.BlockSpec((half, block), lambda i: (0, 0))],
+        out_shape=(jax.ShapeDtypeStruct((CORES, wide, half), jnp.bfloat16), jax.ShapeDtypeStruct((half, block), jnp.bfloat16)),
         compiler_params=BIG,
         name="grads",
     )(mine, theirs, keep, sib)
@@ -233,16 +201,15 @@
     out_ref[...] = value.astype(out_ref.dtype)
 
 
-def near(grads_value, keep, sib, got, part):
-    _, wide, _ = grads_value.shape
+def near(grads_value, keep, sib, got):
+    _, wide, half = grads_value.shape
     _, depth, block = keep.shape
-    half = got.shape[0]
     weights = pl.BlockSpec((1, depth, block), lambda i: (1, 0, 0))
     whole = pl.BlockSpec((half, block), lambda i: (0, 0))
     return pl.pallas_call(
         near_kernel,
         grid=(1,),
-        in_specs=[pl.BlockSpec((CORES, wide, half), lambda i: (0, 0, part)), weights, weights, whole],
+        in_specs=[pl.BlockSpec((CORES, wide, half), lambda i: (0, 0, 0)), weights, weights, whole],
         out_specs=whole,
         out_shape=jax.ShapeDtypeStruct(got.shape, jnp.bfloat16),
         compiler_params=BIG,
@@ -250,34 +217,37 @@
     )(grads_value, keep, sib, got)
 
 
-def total_kernel(grads_ref, keep_ref, sib_ref, low_ref, high_ref, other_ref, out_ref):
-    value = chip_sum(grads_ref[...], keep_ref[0], sib_ref[0]) + other_ref[...].astype(jnp.float32)
+def rows_kernel(low_ref, high_ref, keep_ref, sib_ref, *refs):
+    def store(grads_ref, more):
+        value = chip_sum(grads_ref[...], keep_ref[0], sib_ref[0])
+        for ref in more:
+            value = value + ref[...].astype(jnp.float32)
+        refs[-1][...] = value.astype(refs[-1].dtype)
 
     @pl.when(pl.program_id(0) == 0)
     def _():
-        out_ref[...] = (value + low_ref[...].astype(jnp.float32)).astype(out_ref.dtype)
+        store(low_ref, (refs[0], refs[2]) if len(refs) > 1 else ())
 
     @pl.when(pl.program_id(0) == 1)
     def _():
-        out_ref[...] = (value + high_ref[...].astype(jnp.float32)).astype(out_ref.dtype)
-
-
-def total(grads_value, keep, sib, low, high, other):
-    _, wide, rows = grads_value.shape
+        store(high_ref, (refs[1], refs[2]) if len(refs) > 1 else ())
+
+
+def all_rows(grads_values, keep, sib, at, more=()):
+    _, wide, half = grads_values[0].shape
     _, depth, block = keep.shape
-    half = rows // 2
-    weights = pl.BlockSpec((1, depth, block), lambda i: (0, 0, 0))
+    by_half = pl.BlockSpec((half, block), lambda i: (i, 0))
     whole = pl.BlockSpec((half, block), lambda i: (0, 0))
-    by_half = pl.BlockSpec((half, block), lambda i: (i, 0))
-    return pl.pallas_call(
-        total_kernel,
+    weights = pl.BlockSpec((1, depth, block), lambda i: (at, 0, 0))
+    return pl.pallas_call(
+        rows_kernel,
         grid=(2,),
-        in_specs=[pl.BlockSpec((CORES, wide, half), lambda i: (0, 0, i)), weights, weights, whole, whole, by_half],
+        in_specs=[pl.BlockSpec((CORES, wide, half), lambda i: (0, 0, 0))] * 2 + [weights, weights] + [whole, whole, by_half][: len(more)],
         out_specs=by_half,
-        out_shape=jax.ShapeDtypeStruct((rows, block), jnp.bfloat16),
-        compiler_params=BIG,
-        name="total",
-    )(grads_value, keep, sib, low, high, other)
+        out_shape=jax.ShapeDtypeStruct((2 * half, block), jnp.bfloat16),
+        compiler_params=BIG,
+        name="all_rows",
+    )(*grads_values, keep, sib, *more)
 
 
 def combine_kernel(hi_ref, lo_ref, back_ref, out_ref):
@@ -341,14 +311,14 @@
     other = [to_near_other(rows) for rows in halves]
     opposite = [from_near(rows) for rows in same]
     mine = first(own, *same, keep, sib)
-    mine = second(other, opposite, keep, sib, mine)
-    theirs = to_sibling(mine)
-    grads_value, part_low, part_high, for_other = grads(mine, theirs, keep, sib)
-    passing_low, passing_high = to_near(part_low), to_near(part_high)
-    from_other = to_near_other(for_other)
-    from_low = to_near(near(grads_value, keep, sib, passing_low, 0))
-    from_high = to_near(near(grads_value, keep, sib, passing_high, 1))
-    return total(grads_value, keep, sib, from_low, from_high, from_other)
+    values, far = [], []
+    for part in range(2):
+        rows = second(other[part], opposite[part], keep, sib, mine, part)
+        value, for_opposite = grads(rows, to_sibling(rows), keep, sib)
+        values.append(value)
+        far.append(to_near(near(value, keep, sib, to_near(for_opposite))))
+    from_other = to_near_other(all_rows(values, keep, sib, 2))
+    return all_rows(values, keep, sib, 0, (*far, from_other))
 
 
 def shards(activations, out_grad, routes, gate_vals, w_gate, w_up, w_down):

time: 153 us -> 147 us (0.961)
  the two profiles are of different devices: /device:TPU:6 before, /device:TPU:1 now
where the time goes in v8:
time: 147 us
  starting transfers between devices  71.5 us (49%)
  waiting for transfers between devices  27.7 us (19%)
  blocking collectives  24.8 us (17%)
  Pallas kernels  19.9 us (14%)
  local copies, waits for them, and re-layouts  1.73 us (1%)
    ppermute x14, starting transfers between devices, send(): return lax.ppermute(value, 'tp', pairs)  54.3 us
    all_to_all x1, blocking collectives, exchange(): lax.all_to_all(blocks, 'tok', split_axis=0, concat_axis=0, tiled=True)  24.8 us
    all_to_all x1, starting transfers between devices, exchange(): lax.all_to_all(blocks, 'tok', split_axis=0, concat_axis=0, tiled=True)  17.1 us
    all_to_all x1, waiting for transfers between devices, exchange(): lax.all_to_all(blocks, 'tok', split_axis=0, concat_axis=0, tiled=True)  16.4 us
    ppermute x14, waiting for transfers between devices, send(): return lax.ppermute(value, 'tp', pairs)  11.3 us
    pallas_call x1, Pallas kernels, pack(): pl.pallas_call(pack_kernel, grid_spec=pltpu.PrefetchScalarGridSpec(num_sc...  5.82 us
  transfers between devices with their start and end apart: 15, of which 5 were waited for; matrix products, arithmetic and copies ran while one was open for 1% of the time, Pallas kernels for 10%

profile of v8, /device:TPU:1, one launch (start us, length us, event | category | flops | bytes accessed | tf_op | source)
XLA Modules:
  0.0 146.6 jit_solution(16627116161861522854)
XLA Ops:
  0.0 2.5 %dispatch.1 = bf16[512,1024]{1,0:T(8,128)(2,1)} custom-call(s32[2,128]{1,0:T(2,128)} %bitcast.26, bf16[128,512]{1,0:T(8,128)(2,1)} %x_ref.1, bf16[128,512]{1,0:T(8,128)(2,1)} %g_ref.1), custom_call_target="tpu_custom_call" | custom-call | tf_op jit(solution)/shard_map/dispatch/pallas_call | solution.py:44
  2.5 17.1 %all-to-all-start = ((bf16[64,8,1024]{2,1,0:T(8,128)(2,1)}), bf16[64,8,1024]{2,1,0:T(8,128)(2,1)S(1)}, u32[]{:S(2)}, u32[]{:S(2)}) async-start(bf16[64,8,1024]{2,1,0:T(8,128)(2,1)} %bitcast.24), calls=%async_computation | async-start | bytes 2097152 | tf_op jit(solution)/shard_map/all_to_all | solution.py:270
  19.7 0.1 fusion.1
  19.8 0.6 pad_add_fusion.blocks_ref
  20.4 5.8 %pack.1 = (bf16[4,576,512]{2,1,0:T(8,128)(2,1)}, bf16[4,576,512]{2,1,0:T(8,128)(2,1)}) custom-call(s32[8]{0:T(128)} %pad_add_fusion.blocks_ref, bf16[192,4096]{1,0:T(8,128)(2,1)} %bitcast.18, bf16[192,4096]{1,0:T(8,128)(2,1)} %bitcast.20, bf16[192,4096]{1,0:T(8,128)(2,1)} %bitcast.22, bf16[192,4096]{1,0:T(8,128)(2,1)} %bitcast.19, ...), custom_call_target="tpu_custom_call" | custom-call | tf_op jit(solution)/shard_map/pack/pallas_call | solution.py:83
  26.2 2.8 %collective-permute-start.3 = (bf16[4,576,512]{2,1,0:T(8,128)(2,1)}, bf16[4,576,512]{2,1,0:T(8,128)(2,1)S(1)}, u32[]{:S(2)}, u32[]{:S(2)}) collective-permute-start(bf16[4,576,512]{2,1,0:T(8,128)(2,1)} %get-tuple-element.32), channel_id=1, source_target_pairs={{0,1},{1,0},{2,3},{3,2},{4,5},{5,4},{6,7},{7,6},{8,9},{9,8},{10,11... | collective-permute-start | bytes 7077896 | tf_op jit(solution)/shard_map/ppermute | solution.py:278
  29.0 1.7 %mixer.1 = (bf16[128,512]{1,0:T(8,128)(2,1)}, bf16[128,512]{1,0:T(8,128)(2,1)}) custom-call(s32[2,128]{1,0:T(2,128)} %bitcast.27, f32[2,128]{1,0:T(2,128)} %bitcast.28), custom_call_target="tpu_custom_call" | custom-call | tf_op jit(solution)/shard_map/mixer/pallas_call | solution.py:61
  30.7 16.4 %all-to-all-done = bf16[64,8,1024]{2,1,0:T(8,128)(2,1)S(1)} async-done(((bf16[64,8,1024]{2,1,0:T(8,128)(2,1)}), bf16[64,8,1024]{2,1,0:T(8,128)(2,1)S(1)}, u32[]{:S(2)}, u32[]{:S(2)}) %all-to-all-start) | async-done | bytes 1048608 | tf_op jit(solution)/shard_map/all_to_all | solution.py:270
  47.1 0.1 fusion.4
  47.2 4.4 %collective-permute-start.1 = (bf16[256,1024]{1,0:T(8,128)(2,1)S(1)}, bf16[256,1024]{1,0:T(8,128)(2,1)S(1)}, u32[]{:S(2)}, u32[]{:S(2)}) collective-permute-start(bf16[256,1024]{1,0:T(8,128)(2,1)S(1)} %get-tuple-element.38), channel_id=1, source_target_pairs={{0,2},{1,7},{2,4},{3,1},{4,6},{5,3},{6,0},{7,5},{8,10},{9,15},{10,... | collective-permute-start | bytes 1572872 | tf_op jit(solution)/shard_map/ppermute | solution.py:278
  51.6 2.5 %collective-permute-start.4 = (bf16[256,1024]{1,0:T(8,128)(2,1)S(1)}, bf16[256,1024]{1,0:T(8,128)(2,1)S(1)}, u32[]{:S(2)}, u32[]{:S(2)}) collective-permute-start(bf16[256,1024]{1,0:T(8,128)(2,1)S(1)} %get-tuple-element.37), channel_id=1, source_target_pairs={{0,2},{1,7},{2,4},{3,1},{4,6},{5,3},{6,0},{7,5},{8,10},{9,15},{10,... | collective-permute-start | bytes 1572872 | tf_op jit(solution)/shard_map/ppermute | solution.py:278
  54.0 6.0 %collective-permute-start = (bf16[256,1024]{1,0:T(8,128)(2,1)S(1)}, bf16[256,1024]{1,0:T(8,128)(2,1)S(1)}, u32[]{:S(2)}, u32[]{:S(2)}) collective-permute-start(bf16[256,1024]{1,0:T(8,128)(2,1)S(1)} %get-tuple-element.38), channel_id=1, source_target_pairs={{0,7},{1,2},{2,1},{3,4},{4,3},{5,6},{6,5},{7,0},{8,15},{9,10},{10,... | collective-permute-start | bytes 1572872 | tf_op jit(solution)/shard_map/ppermute | solution.py:278
  60.0 0.0 collective-permute-done.1.same_low_ref
  60.0 3.7 %collective-permute-start.2 = (bf16[256,1024]{1,0:T(8,128)(2,1)S(1)}, bf16[256,1024]{1,0:T(8,128)(2,1)S(1)}, u32[]{:S(2)}, u32[]{:S(2)}) collective-permute-start(bf16[256,1024]{1,0:T(8,128)(2,1)S(1)} %collective-permute-done.1.same_low_ref), channel_id=1, source_target_pairs={{0,2},{1,7},{2,4},{3,1},{4,6},{5,3},{6,0},{7,5},{8,10},{9,15},{10,... | collective-permute-start | bytes 1572872 | tf_op jit(solution)/shard_map/ppermute | solution.py:278
  63.7 4.9 %collective-permute-start.6 = (bf16[256,1024]{1,0:T(8,128)(2,1)S(1)}, bf16[256,1024]{1,0:T(8,128)(2,1)S(1)}, u32[]{:S(2)}, u32[]{:S(2)}) collective-permute-start(bf16[256,1024]{1,0:T(8,128)(2,1)S(1)} %get-tuple-element.37), channel_id=1, source_target_pairs={{0,7},{1,2},{2,1},{3,4},{4,3},{5,6},{6,5},{7,0},{8,15},{9,10},{10,... | collective-permute-start | bytes 1572872 | tf_op jit(solution)/shard_map/ppermute | solution.py:278
  68.6 0.0 collective-permute-done.4.same_high_ref
  68.6 3.0 %collective-permute-start.7 = (bf16[256,1024]{1,0:T(8,128)(2,1)S(1)}, bf16[256,1024]{1,0:T(8,128)(2,1)S(1)}, u32[]{:S(2)}, u32[]{:S(2)}) collective-permute-start(bf16[256,1024]{1,0:T(8,128)(2,1)S(1)} %collective-permute-done.4.same_high_ref), channel_id=1, source_target_pairs={{0,2},{1,7},{2,4},{3,1},{4,6},{5,3},{6,0},{7,5},{8,10},{9,15},{10,... | collective-permute-start | bytes 1572872 | tf_op jit(solution)/shard_map/ppermute | solution.py:278
  71.6 0.0 collective-permute-done.3.sib_ref
  71.7 1.7 %copy-done = bf16[4,576,512]{2,1,0:T(8,128)(2,1)S(1)} copy-done((bf16[4,576,512]{2,1,0:T(8,128)(2,1)S(1)}, bf16[4,576,512]{2,1,0:T(8,128)(2,1)}, u32[]{:S(2)}) %copy-start) | copy-done | bytes 2359320
  73.3 2.0 %first.1.sum_ref = f32[2,576,512]{2,1,0:T(8,128)S(1)} custom-call(bf16[512,1024]{1,0:T(8,128)(2,1)S(1)} %bitcast.16, bf16[256,1024]{1,0:T(8,128)(2,1)S(1)} %collective-permute-done.1.same_low_ref, bf16[256,1024]{1,0:T(8,128)(2,1)S(1)} %collective-permute-done.4.same_high_ref, bf16[4,576,512]{2,1,0:T(8,128)(2,1)S(1)} %copy-done, ...), custom_call_target="tpu_custom_call" | custom-call | tf_op jit(solution)/shard_map/first/pallas_call | solution.py:127
  75.3 0.0 collective-permute-done.other_ref
  75.3 2.5 %collective-permute-done.2.opposite_ref = bf16[256,1024]{1,0:T(8,128)(2,1)S(1)} collective-permute-done((bf16[256,1024]{1,0:T(8,128)(2,1)S(1)}, bf16[256,1024]{1,0:T(8,128)(2,1)S(1)}, u32[]{:S(2)}, u32[]{:S(2)}) %collective-permute-start.2) | collective-permute-done | bytes 524320 | tf_op jit(solution)/shard_map/ppermute | solution.py:278
  77.9 0.9 second.2.mine_ref
  78.8 8.6 %collective-permute-start.5 = (f32[2,576,256]{2,1,0:T(8,128)S(1)}, f32[2,576,256]{2,1,0:T(8,128)S(1)}, u32[]{:S(2)}, u32[]{:S(2)}) collective-permute-start(f32[2,576,256]{2,1,0:T(8,128)S(1)} %second.2.mine_ref), channel_id=1, source_target_pairs={{0,1},{1,0},{2,3},{3,2},{4,5},{5,4},{6,7},{7,6},{8,9},{9,8},{10,11... | collective-permute-start | bytes 3538952 | tf_op jit(solution)/shard_map/ppermute | solution.py:278
  87.4 0.0 collective-permute-done.6.other_ref
  87.4 0.0 collective-permute-done.7.opposite_ref
  87.4 0.9 second.3.mine_ref
  88.3 5.4 %collective-permute-start.8 = (f32[2,576,256]{2,1,0:T(8,128)S(1)}, f32[2,576,256]{2,1,0:T(8,128)S(1)}, u32[]{:S(2)}, u32[]{:S(2)}) collective-permute-start(f32[2,576,256]{2,1,0:T(8,128)S(1)} %second.3.mine_ref), channel_id=1, source_target_pairs={{0,1},{1,0},{2,3},{3,2},{4,5},{5,4},{6,7},{7,6},{8,9},{9,8},{10,11... | collective-permute-start | bytes 3538952 | tf_op jit(solution)/shard_map/ppermute | solution.py:278
  93.7 0.0 collective-permute-done.5.theirs_ref
  93.7 0.6 grads.2
  94.3 1.9 %collective-permute-start.9 = (bf16[256,512]{1,0:T(8,128)(2,1)S(1)}, bf16[256,512]{1,0:T(8,128)(2,1)S(1)}, u32[]{:S(2)}, u32[]{:S(2)}) collective-permute-start(bf16[256,512]{1,0:T(8,128)(2,1)S(1)} %get-tuple-element.35), channel_id=1, source_target_pairs={{0,6},{1,3},{2,0},{3,5},{4,2},{5,7},{6,4},{7,1},{8,14},{9,11},{10,... | collective-permute-start | bytes 786440 | tf_op jit(solution)/shard_map/ppermute | solution.py:278
  96.2 0.0 collective-permute-done.8.theirs_ref
  96.2 0.6 grads.3
  96.8 3.1 %collective-permute-start.11 = (bf16[256,512]{1,0:T(8,128)(2,1)S(1)}, bf16[256,512]{1,0:T(8,128)(2,1)S(1)}, u32[]{:S(2)}, u32[]{:S(2)}) collective-permute-start(bf16[256,512]{1,0:T(8,128)(2,1)S(1)} %get-tuple-element.36), channel_id=1, source_target_pairs={{0,6},{1,3},{2,0},{3,5},{4,2},{5,7},{6,4},{7,1},{8,14},{9,11},{10,... | collective-permute-start | bytes 786440 | tf_op jit(solution)/shard_map/ppermute | solution.py:278
  99.9 1.0 all_rows.2
  100.9 3.9 %collective-permute-start.13 = (bf16[512,512]{1,0:T(8,128)(2,1)S(1)}, bf16[512,512]{1,0:T(8,128)(2,1)S(1)}, u32[]{:S(2)}, u32[]{:S(2)}) collective-permute-start(bf16[512,512]{1,0:T(8,128)(2,1)S(1)} %all_rows.2), channel_id=1, source_target_pairs={{0,7},{1,2},{2,1},{3,4},{4,3},{5,6},{6,5},{7,0},{8,15},{9,10},{10,... | collective-permute-start | bytes 1572872 | tf_op jit(solution)/shard_map/ppermute | solution.py:278
  104.8 0.0 collective-permute-done.9.got_ref
  104.8 0.5 near.2
  105.3 2.1 %collective-permute-start.10 = (bf16[256,512]{1,0:T(8,128)(2,1)S(1)}, bf16[256,512]{1,0:T(8,128)(2,1)S(1)}, u32[]{:S(2)}, u32[]{:S(2)}) collective-permute-start(bf16[256,512]{1,0:T(8,128)(2,1)S(1)} %near.2), channel_id=1, source_target_pairs={{0,6},{1,3},{2,0},{3,5},{4,2},{5,7},{6,4},{7,1},{8,14},{9,11},{10,... | collective-permute-start | bytes 786440 | tf_op jit(solution)/shard_map/ppermute | solution.py:278
  107.4 0.0 collective-permute-done.11.got_ref
  107.4 0.5 near.3
  107.8 2.1 %collective-permute-start.12 = (bf16[256,512]{1,0:T(8,128)(2,1)S(1)}, bf16[256,512]{1,0:T(8,128)(2,1)S(1)}, u32[]{:S(2)}, u32[]{:S(2)}) collective-permute-start(bf16[256,512]{1,0:T(8,128)(2,1)S(1)} %near.3), channel_id=1, source_target_pairs={{0,6},{1,3},{2,0},{3,5},{4,2},{5,7},{6,4},{7,1},{8,14},{9,11},{10,... | collective-permute-start | bytes 786440 | tf_op jit(solution)/shard_map/ppermute | solution.py:278
  109.9 2.0 %collective-permute-done.13.refs_2_ = bf16[512,512]{1,0:T(8,128)(2,1)S(1)} collective-permute-done((bf16[512,512]{1,0:T(8,128)(2,1)S(1)}, bf16[512,512]{1,0:T(8,128)(2,1)S(1)}, u32[]{:S(2)}, u32[]{:S(2)}) %collective-permute-start.13) | collective-permute-done | bytes 524320 | tf_op jit(solution)/shard_map/ppermute | solution.py:278
  111.9 4.0 %collective-permute-done.10.refs_0_ = bf16[256,512]{1,0:T(8,128)(2,1)S(1)} collective-permute-done((bf16[256,512]{1,0:T(8,128)(2,1)S(1)}, bf16[256,512]{1,0:T(8,128)(2,1)S(1)}, u32[]{:S(2)}, u32[]{:S(2)}) %collective-permute-start.10) | collective-permute-done | bytes 262176 | tf_op jit(solution)/shard_map/ppermute | solution.py:278
  115.9 2.8 %collective-permute-done.12.refs_1_ = bf16[256,512]{1,0:T(8,128)(2,1)S(1)} collective-permute-done((bf16[256,512]{1,0:T(8,128)(2,1)S(1)}, bf16[256,512]{1,0:T(8,128)(2,1)S(1)}, u32[]{:S(2)}, u32[]{:S(2)}) %collective-permute-start.12) | collective-permute-done | bytes 262176 | tf_op jit(solution)/shard_map/ppermute | solution.py:278
  118.7 1.0 all_rows.3
  119.7 24.8 %all_to_all.10 = bf16[64,8,512]{2,1,0:T(8,128)(2,1)} all-to-all(bf16[64,8,512]{2,1,0:T(8,128)(2,1)S(1)} %bitcast.17), channel_id=1, replica_groups=mesh['tok'=64,'tp'=8] {'tok'}, dimensions={0} | all-to-all | bytes 1048576 | tf_op jit(solution)/shard_map/all_to_all | solution.py:270
  144.4 2.1 %combine.1 = bf16[128,512]{1,0:T(8,128)(2,1)} custom-call(bf16[128,512]{1,0:T(8,128)(2,1)} %get-tuple-element.25.hi_ref, bf16[128,512]{1,0:T(8,128)(2,1)} %get-tuple-element.26.lo_ref, bf16[512,512]{1,0:T(8,128)(2,1)} %bitcast.25), custom_call_target="tpu_custom_call" | custom-call | tf_op jit(solution)/shard_map/combine/pallas_call | solution.py:261
  (1 shorter events, 0.0 us)
Async XLA Ops:
  2.5 44.6 %all-to-all-start = ((bf16[64,8,1024]{2,1,0:T(8,128)(2,1)}), bf16[64,8,1024]{2,1,0:T(8,128)(2,1)S(1)}, u32[]{:S(2)}, u32[]{:S(2)}) async-start(bf16[64,8,1024]{2,1,0:T(8,128)(2,1)} %bitcast.24), calls=%async_computation | async-start | bytes 2097152 | tf_op jit(solution)/shard_map/all_to_all | solution.py:270
  26.2 45.5 %collective-permute-start.3 = (bf16[4,576,512]{2,1,0:T(8,128)(2,1)}, bf16[4,576,512]{2,1,0:T(8,128)(2,1)S(1)}, u32[]{:S(2)}, u32[]{:S(2)}) collective-permute-start(bf16[4,576,512]{2,1,0:T(8,128)(2,1)} %get-tuple-element.32), channel_id=1, source_target_pairs={{0,1},{1,0},{2,3},{3,2},{4,5},{5,4},{6,7},{7,6},{8,9},{9,8},{10,11... | collective-permute-start | bytes 7077896 | tf_op jit(solution)/shard_map/ppermute | solution.py:278
  47.2 12.8 %collective-permute-start.1 = (bf16[256,1024]{1,0:T(8,128)(2,1)S(1)}, bf16[256,1024]{1,0:T(8,128)(2,1)S(1)}, u32[]{:S(2)}, u32[]{:S(2)}) collective-permute-start(bf16[256,1024]{1,0:T(8,128)(2,1)S(1)} %get-tuple-element.38), channel_id=1, source_target_pairs={{0,2},{1,7},{2,4},{3,1},{4,6},{5,3},{6,0},{7,5},{8,10},{9,15},{10,... | collective-permute-start | bytes 1572872 | tf_op jit(solution)/shard_map/ppermute | solution.py:278
  51.6 17.0 %collective-permute-start.4 = (bf16[256,1024]{1,0:T(8,128)(2,1)S(1)}, bf16[256,1024]{1,0:T(8,128)(2,1)S(1)}, u32[]{:S(2)}, u32[]{:S(2)}) collective-permute-start(bf16[256,1024]{1,0:T(8,128)(2,1)S(1)} %get-tuple-element.37), channel_id=1, source_target_pairs={{0,2},{1,7},{2,4},{3,1},{4,6},{5,3},{6,0},{7,5},{8,10},{9,15},{10,... | collective-permute-start | bytes 1572872 | tf_op jit(solution)/shard_map/ppermute | solution.py:278
  54.0 21.3 %collective-permute-start = (bf16[256,1024]{1,0:T(8,128)(2,1)S(1)}, bf16[256,1024]{1,0:T(8,128)(2,1)S(1)}, u32[]{:S(2)}, u32[]{:S(2)}) collective-permute-start(bf16[256,1024]{1,0:T(8,128)(2,1)S(1)} %get-tuple-element.38), channel_id=1, source_target_pairs={{0,7},{1,2},{2,1},{3,4},{4,3},{5,6},{6,5},{7,0},{8,15},{9,10},{10,... | collective-permute-start | bytes 1572872 | tf_op jit(solution)/shard_map/ppermute | solution.py:278
  60.0 17.8 %collective-permute-start.2 = (bf16[256,1024]{1,0:T(8,128)(2,1)S(1)}, bf16[256,1024]{1,0:T(8,128)(2,1)S(1)}, u32[]{:S(2)}, u32[]{:S(2)}) collective-permute-start(bf16[256,1024]{1,0:T(8,128)(2,1)S(1)} %collective-permute-done.1.same_low_ref), channel_id=1, source_target_pairs={{0,2},{1,7},{2,4},{3,1},{4,6},{5,3},{6,0},{7,5},{8,10},{9,15},{10,... | collective-permute-start | bytes 1572872 | tf_op jit(solution)/shard_map/ppermute | solution.py:278
  63.7 23.7 %collective-permute-start.6 = (bf16[256,1024]{1,0:T(8,128)(2,1)S(1)}, bf16[256,1024]{1,0:T(8,128)(2,1)S(1)}, u32[]{:S(2)}, u32[]{:S(2)}) collective-permute-start(bf16[256,1024]{1,0:T(8,128)(2,1)S(1)} %get-tuple-element.37), channel_id=1, source_target_pairs={{0,7},{1,2},{2,1},{3,4},{4,3},{5,6},{6,5},{7,0},{8,15},{9,10},{10,... | collective-permute-start | bytes 1572872 | tf_op jit(solution)/shard_map/ppermute | solution.py:278
  68.6 18.8 %collective-permute-start.7 = (bf16[256,1024]{1,0:T(8,128)(2,1)S(1)}, bf16[256,1024]{1,0:T(8,128)(2,1)S(1)}, u32[]{:S(2)}, u32[]{:S(2)}) collective-permute-start(bf16[256,1024]{1,0:T(8,128)(2,1)S(1)} %collective-permute-done.4.same_high_ref), channel_id=1, source_target_pairs={{0,2},{1,7},{2,4},{3,1},{4,6},{5,3},{6,0},{7,5},{8,10},{9,15},{10,... | collective-permute-start | bytes 1572872 | tf_op jit(solution)/shard_map/ppermute | solution.py:278
  71.7 1.7 %copy-start = (bf16[4,576,512]{2,1,0:T(8,128)(2,1)S(1)}, bf16[4,576,512]{2,1,0:T(8,128)(2,1)}, u32[]{:S(2)}) copy-start(bf16[4,576,512]{2,1,0:T(8,128)(2,1)} %get-tuple-element.31.keep_ref) | copy-start | bytes 7077892
  78.8 14.9 %collective-permute-start.5 = (f32[2,576,256]{2,1,0:T(8,128)S(1)}, f32[2,576,256]{2,1,0:T(8,128)S(1)}, u32[]{:S(2)}, u32[]{:S(2)}) collective-permute-start(f32[2,576,256]{2,1,0:T(8,128)S(1)} %second.2.mine_ref), channel_id=1, source_target_pairs={{0,1},{1,0},{2,3},{3,2},{4,5},{5,4},{6,7},{7,6},{8,9},{9,8},{10,11... | collective-permute-start | bytes 3538952 | tf_op jit(solution)/shard_map/ppermute | solution.py:278
  88.3 7.9 %collective-permute-start.8 = (f32[2,576,256]{2,1,0:T(8,128)S(1)}, f32[2,576,256]{2,1,0:T(8,128)S(1)}, u32[]{:S(2)}, u32[]{:S(2)}) collective-permute-start(f32[2,576,256]{2,1,0:T(8,128)S(1)} %second.3.mine_ref), channel_id=1, source_target_pairs={{0,1},{1,0},{2,3},{3,2},{4,5},{5,4},{6,7},{7,6},{8,9},{9,8},{10,11... | collective-permute-start | bytes 3538952 | tf_op jit(solution)/shard_map/ppermute | solution.py:278
  94.3 10.5 %collective-permute-start.9 = (bf16[256,512]{1,0:T(8,128)(2,1)S(1)}, bf16[256,512]{1,0:T(8,128)(2,1)S(1)}, u32[]{:S(2)}, u32[]{:S(2)}) collective-permute-start(bf16[256,512]{1,0:T(8,128)(2,1)S(1)} %get-tuple-element.35), channel_id=1, source_target_pairs={{0,6},{1,3},{2,0},{3,5},{4,2},{5,7},{6,4},{7,1},{8,14},{9,11},{10,... | collective-permute-start | bytes 786440 | tf_op jit(solution)/shard_map/ppermute | solution.py:278
  96.8 10.6 %collective-permute-start.11 = (bf16[256,512]{1,0:T(8,128)(2,1)S(1)}, bf16[256,512]{1,0:T(8,128)(2,1)S(1)}, u32[]{:S(2)}, u32[]{:S(2)}) collective-permute-start(bf16[256,512]{1,0:T(8,128)(2,1)S(1)} %get-tuple-element.36), channel_id=1, source_target_pairs={{0,6},{1,3},{2,0},{3,5},{4,2},{5,7},{6,4},{7,1},{8,14},{9,11},{10,... | collective-permute-start | bytes 786440 | tf_op jit(solution)/shard_map/ppermute | solution.py:278
  100.9 11.1 %collective-permute-start.13 = (bf16[512,512]{1,0:T(8,128)(2,1)S(1)}, bf16[512,512]{1,0:T(8,128)(2,1)S(1)}, u32[]{:S(2)}, u32[]{:S(2)}) collective-permute-start(bf16[512,512]{1,0:T(8,128)(2,1)S(1)} %all_rows.2), channel_id=1, source_target_pairs={{0,7},{1,2},{2,1},{3,4},{4,3},{5,6},{6,5},{7,0},{8,15},{9,10},{10,... | collective-permute-start | bytes 1572872 | tf_op jit(solution)/shard_map/ppermute | solution.py:278
  105.3 10.6 %collective-permute-start.10 = (bf16[256,512]{1,0:T(8,128)(2,1)S(1)}, bf16[256,512]{1,0:T(8,128)(2,1)S(1)}, u32[]{:S(2)}, u32[]{:S(2)}) collective-permute-start(bf16[256,512]{1,0:T(8,128)(2,1)S(1)} %near.2), channel_id=1, source_target_pairs={{0,6},{1,3},{2,0},{3,5},{4,2},{5,7},{6,4},{7,1},{8,14},{9,11},{10,... | collective-permute-start | bytes 786440 | tf_op jit(solution)/shard_map/ppermute | solution.py:278
  107.8 10.8 %collective-permute-start.12 = (bf16[256,512]{1,0:T(8,128)(2,1)S(1)}, bf16[256,512]{1,0:T(8,128)(2,1)S(1)}, u32[]{:S(2)}, u32[]{:S(2)}) collective-permute-start(bf16[256,512]{1,0:T(8,128)(2,1)S(1)} %near.3), channel_id=1, source_target_pairs={{0,6},{1,3},{2,0},{3,5},{4,2},{5,7},{6,4},{7,1},{8,14},{9,11},{10,... | collective-permute-start | bytes 786440 | tf_op jit(solution)/shard_map/ppermute | solution.py:278

commit v9 on v8

--- a/solution.py
+++ b/solution.py
@@ -48,19 +48,19 @@
     )(routes.T, activations, out_grad)
 
 
-def mixer_kernel(n_tok, capacity, routes_ref, gates_ref, hi_ref, lo_ref):
+def mixer_kernel(n_tok, capacity, routes_ref, gates_ref, out_ref):
     gates = [gates_ref[k : k + 1, :] for k in range(gates_ref.shape[0])]
     scaled = places(routes_ref, gates, n_tok, capacity).T
+    tokens = scaled.shape[0]
     high = scaled.astype(jnp.bfloat16)
-    hi_ref[...] = high
-    lo_ref[...] = (scaled - high.astype(jnp.float32)).astype(jnp.bfloat16)
+    out_ref[:tokens, :] = high
+    out_ref[tokens:, :] = (scaled - high.astype(jnp.float32)).astype(jnp.bfloat16)
 
 
 def mixer(routes, gate_vals, n_tok, capacity):
-    part = jax.ShapeDtypeStruct((routes.shape[0], n_tok * capacity), jnp.bfloat16)
     return pl.pallas_call(
         functools.partial(mixer_kernel, n_tok, capacity),
-        out_shape=(part, part),
+        out_shape=jax.ShapeDtypeStruct((2 * routes.shape[0], n_tok * capacity), jnp.bfloat16),
         name="mixer",
     )(routes.T, gate_vals.T)
 
@@ -135,28 +135,34 @@
     )(own, same_low, same_high, keep, sib)
 
 
-def second_kernel(other_ref, opposite_ref, keep_ref, sib_ref, sum_ref, out_ref):
+def second_kernel(other_ref, far_x_ref, far_g_ref, keep_ref, sib_ref, sum_ref, *refs):
+    out_ref = refs[-1]
     for n, weights in enumerate((keep_ref, sib_ref)):
         wide, narrow, split = products(weights[0], other_ref[...])
-        far_wide, far_narrow, _ = products(weights[1], opposite_ref[...])
-        out_ref[n, :split, :] = sum_ref[n, :split, :] + (wide + far_wide)
-        out_ref[n, split:, :] = sum_ref[n, split:, :] + (narrow + far_narrow)
-
-
-def second(other, opposite, keep, sib, sums, part):
+        far = weights[1]
+        wide = wide + lax.dot_general(far[:split], far_x_ref[...], CONTRACT_LAST, preferred_element_type=jnp.float32)
+        narrow = narrow + lax.dot_general(far[split:], far_g_ref[...], CONTRACT_LAST, preferred_element_type=jnp.float32)
+        out_ref[n, :split, :] = sum_ref[n, :split, :] + wide
+        out_ref[n, split:, :] = sum_ref[n, split:, :] + narrow
+
+
+def second(other, opposite, keep, sib, sums, part, before):
     half, width = other.shape
     _, depth, block = keep.shape
     whole = pl.BlockSpec((half, width), lambda i: (0, 0))
+    far_x = pl.BlockSpec((half, block), lambda i: (0, 0))
+    far_g = pl.BlockSpec((half, block), lambda i: (0, 2 - len(opposite)))
     weights = pl.BlockSpec((2, depth, block), lambda i: (1, 0, 0))
     return pl.pallas_call(
         second_kernel,
         grid=(1,),
-        in_specs=[whole, whole, weights, weights, pl.BlockSpec((CORES, depth, half), lambda i: (0, 0, part))],
+        in_specs=[whole, far_x, far_g, weights, weights, pl.BlockSpec((CORES, depth, half), lambda i: (0, 0, part))]
+        + [pl.BlockSpec(memory_space=pl.ANY) for _ in before],
         out_specs=pl.BlockSpec((CORES, depth, half), lambda i: (0, 0, 0)),
         out_shape=jax.ShapeDtypeStruct((CORES, depth, half), sums.dtype),
         compiler_params=BIG,
         name="second",
-    )(other, opposite, keep, sib, sums)
+    )(other, opposite[0], opposite[-1], keep, sib, sums, *before)
 
 
 def chip_sum(grads, keep, sib):
@@ -166,7 +172,8 @@
     )
 
 
-def grads_kernel(mine_ref, theirs_ref, keep_ref, sib_ref, grads_ref, part_ref):
+def grads_kernel(mine_ref, theirs_ref, keep_ref, sib_ref, *refs):
+    grads_ref, part_ref = refs[-2:]
     hidden = mine_ref.shape[1] // 3
     for n in range(CORES):
         gate_pre = mine_ref[n, :hidden, :] + theirs_ref[1 - n, :hidden, :]
@@ -179,7 +186,7 @@
     part_ref[...] = chip_sum(grads_ref[...], keep_ref[0], sib_ref[0]).astype(part_ref.dtype)
 
 
-def grads(mine, theirs, keep, sib):
+def grads(mine, theirs, keep, sib, before):
     _, depth, half = mine.shape
     block = keep.shape[2]
     wide = depth // 3 * 2
@@ -188,20 +195,21 @@
     return pl.pallas_call(
         grads_kernel,
         grid=(1,),
-        in_specs=[whole, whole, weights, weights],
+        in_specs=[whole, whole, weights, weights] + [pl.BlockSpec(memory_space=pl.ANY) for _ in before],
         out_specs=[pl.BlockSpec((CORES, wide, half), lambda i: (0, 0, 0)), pl.BlockSpec((half, block), lambda i: (0, 0))],
         out_shape=(jax.ShapeDtypeStruct((CORES, wide, half), jnp.bfloat16), jax.ShapeDtypeStruct((half, block), jnp.bfloat16)),
         compiler_params=BIG,
         name="grads",
-    )(mine, theirs, keep, sib)
-
-
-def near_kernel(grads_ref, keep_ref, sib_ref, got_ref, out_ref):
+    )(mine, theirs, keep, sib, *before)
+
+
+def near_kernel(grads_ref, keep_ref, sib_ref, got_ref, *refs):
+    out_ref = refs[-1]
     value = chip_sum(grads_ref[...], keep_ref[0], sib_ref[0]) + got_ref[...].astype(jnp.float32)
     out_ref[...] = value.astype(out_ref.dtype)
 
 
-def near(grads_value, keep, sib, got):
+def near(grads_value, keep, sib, got, before):
     _, wide, half = grads_value.shape
     _, depth, block = keep.shape
     weights = pl.BlockSpec((1, depth, block), lambda i: (1, 0, 0))
@@ -209,60 +217,82 @@
     return pl.pallas_call(
         near_kernel,
         grid=(1,),
-        in_specs=[pl.BlockSpec((CORES, wide, half), lambda i: (0, 0, 0)), weights, weights, whole],
+        in_specs=[pl.BlockSpec((CORES, wide, half), lambda i: (0, 0, 0)), weights, weights, whole]
+        + [pl.BlockSpec(memory_space=pl.ANY) for _ in before],
         out_specs=whole,
         out_shape=jax.ShapeDtypeStruct(got.shape, jnp.bfloat16),
         compiler_params=BIG,
         name="near",
-    )(grads_value, keep, sib, got)
-
-
-def rows_kernel(low_ref, high_ref, keep_ref, sib_ref, *refs):
-    def store(grads_ref, more):
-        value = chip_sum(grads_ref[...], keep_ref[0], sib_ref[0])
-        for ref in more:
-            value = value + ref[...].astype(jnp.float32)
-        refs[-1][...] = value.astype(refs[-1].dtype)
-
+    )(grads_value, keep, sib, got, *before)
+
+
+def other_kernel(low_ref, high_ref, keep_ref, sib_ref, out_ref):
     @pl.when(pl.program_id(0) == 0)
     def _():
-        store(low_ref, (refs[0], refs[2]) if len(refs) > 1 else ())
+        out_ref[...] = chip_sum(low_ref[...], keep_ref[0], sib_ref[0]).astype(out_ref.dtype)
 
     @pl.when(pl.program_id(0) == 1)
     def _():
-        store(high_ref, (refs[1], refs[2]) if len(refs) > 1 else ())
-
-
-def all_rows(grads_values, keep, sib, at, more=()):
+        out_ref[...] = chip_sum(high_ref[...], keep_ref[0], sib_ref[0]).astype(out_ref.dtype)
+
+
+def for_other(grads_values, keep, sib):
     _, wide, half = grads_values[0].shape
     _, depth, block = keep.shape
-    by_half = pl.BlockSpec((half, block), lambda i: (i, 0))
-    whole = pl.BlockSpec((half, block), lambda i: (0, 0))
-    weights = pl.BlockSpec((1, depth, block), lambda i: (at, 0, 0))
-    return pl.pallas_call(
-        rows_kernel,
+    weights = pl.BlockSpec((1, depth, block), lambda i: (2, 0, 0))
+    return pl.pallas_call(
+        other_kernel,
         grid=(2,),
-        in_specs=[pl.BlockSpec((CORES, wide, half), lambda i: (0, 0, 0))] * 2 + [weights, weights] + [whole, whole, by_half][: len(more)],
-        out_specs=by_half,
+        in_specs=[pl.BlockSpec((CORES, wide, half), lambda i: (0, 0, 0))] * 2 + [weights, weights],
+        out_specs=pl.BlockSpec((half, block), lambda i: (i, 0)),
         out_shape=jax.ShapeDtypeStruct((2 * half, block), jnp.bfloat16),
         compiler_params=BIG,
-        name="all_rows",
-    )(*grads_values, keep, sib, *more)
-
-
-def combine_kernel(hi_ref, lo_ref, back_ref, out_ref):
-    back = back_ref[...]
-    value = jnp.dot(hi_ref[...], back, preferred_element_type=jnp.float32)
-    value = value + jnp.dot(lo_ref[...], back, preferred_element_type=jnp.float32)
-    out_ref[...] = value.astype(out_ref.dtype)
-
-
-def combine(high, low, back):
+        name="for_other",
+    )(*grads_values, keep, sib)
+
+
+def total_kernel(grads_ref, keep_ref, sib_ref, far_ref, other_ref, *refs):
+    value = chip_sum(grads_ref[...], keep_ref[0], sib_ref[0])
+    value = value + far_ref[...].astype(jnp.float32) + other_ref[...].astype(jnp.float32)
+    refs[-1][...] = value.astype(refs[-1].dtype)
+
+
+def total(grads_value, keep, sib, far, other, part, before):
+    _, wide, half = grads_value.shape
+    _, depth, block = keep.shape
+    weights = pl.BlockSpec((1, depth, block), lambda i: (0, 0, 0))
+    by_part = pl.BlockSpec((half, block), lambda i: (part, 0))
+    return pl.pallas_call(
+        total_kernel,
+        grid=(1,),
+        in_specs=[
+            pl.BlockSpec((CORES, wide, half), lambda i: (0, 0, 0)),
+            weights,
+            weights,
+            pl.BlockSpec((half, block), lambda i: (0, 0)),
+            by_part,
+        ]
+        + [pl.BlockSpec(memory_space=pl.ANY) for _ in before],
+        out_specs=by_part,
+        out_shape=jax.ShapeDtypeStruct(other.shape, jnp.bfloat16),
+        input_output_aliases={5: 0} if before else {},
+        compiler_params=BIG,
+        name="total",
+    )(grads_value, keep, sib, far, other, *before)
+
+
+def combine_kernel(mix_ref, back_ref, out_ref):
+    tokens = out_ref.shape[0]
+    value = jnp.dot(mix_ref[...], back_ref[...], preferred_element_type=jnp.float32)
+    out_ref[...] = (value[:tokens] + value[tokens:]).astype(out_ref.dtype)
+
+
+def combine(mix, back):
     return pl.pallas_call(
         combine_kernel,
-        out_shape=jax.ShapeDtypeStruct((high.shape[0], back.shape[1]), jnp.bfloat16),
+        out_shape=jax.ShapeDtypeStruct((mix.shape[0] // 2, back.shape[1]), jnp.bfloat16),
         name="combine",
-    )(high, low, back)
+    )(mix, back)
 
 
 def exchange(rows, n_tok):
@@ -309,16 +339,20 @@
     halves = (own[:half], own[half:])
     same = [from_near(rows) for rows in halves]
     other = [to_near_other(rows) for rows in halves]
-    opposite = [from_near(rows) for rows in same]
+    width = own.shape[1] // 2
+    opposite = [(from_near(same[0]),), (from_near(same[1][:, :width]), from_near(same[1][:, width:]))]
     mine = first(own, *same, keep, sib)
-    values, far = [], []
+    values, passed, far, earlier = [], [], [], []
     for part in range(2):
-        rows = second(other[part], opposite[part], keep, sib, mine, part)
-        value, for_opposite = grads(rows, to_sibling(rows), keep, sib)
+        rows = second(other[part], opposite[part], keep, sib, mine, part, earlier)
+        earlier = [rows]
+        value, for_opposite = grads(rows, to_sibling(rows), keep, sib, values)
         values.append(value)
-        far.append(to_near(near(value, keep, sib, to_near(for_opposite))))
-    from_other = to_near_other(all_rows(values, keep, sib, 2))
-    return all_rows(values, keep, sib, 0, (*far, from_other))
+        passed.append(near(value, keep, sib, to_near(for_opposite), tuple(passed)))
+        far.append(to_near(passed[-1]))
+    from_other = to_near_other(for_other(values, keep, sib))
+    low = total(values[0], keep, sib, far[0], from_other, 0, ())
+    return total(values[1], keep, sib, far[1], from_other, 1, (low,))
 
 
 def shards(activations, out_grad, routes, gate_vals, w_gate, w_up, w_down):
@@ -327,10 +361,10 @@
     capacity = max(2, 2 * tok_dev * top_k // n_tok)
     sent = dispatch(routes, activations, out_grad, n_tok, capacity)
     weights, sent, gate_vals = lax.optimization_barrier(((w_gate[0], w_up[0], w_down[0]), sent, gate_vals))
-    high, low = mixer(routes, gate_vals, n_tok, capacity)
-    own, high, low = lax.optimization_barrier((exchange(sent, n_tok), high, low))
+    mix = mixer(routes, gate_vals, n_tok, capacity)
+    own, mix = lax.optimization_barrier((exchange(sent, n_tok), mix))
     expert_sum = expert(own, weights)
-    return combine(high, low, exchange(expert_sum, n_tok))
+    return combine(mix, exchange(expert_sum, n_tok))
 
 
 def solution(mesh):

time: 147 us -> 150 us (1.020)
  the two profiles are of different devices: /device:TPU:1 before, /device:TPU:8 now
where the time goes in v9:
time: 150 us; the launch traced here: 149 us
  starting transfers between devices  59.6 us (40%)
  waiting for transfers between devices  42.3 us (28%)
  blocking collectives  26.5 us (18%)
  Pallas kernels  19.9 us (13%)
    ppermute x15, starting transfers between devices, send(): return lax.ppermute(value, 'tp', pairs)  43 us
    all_to_all x1, blocking collectives, exchange(): lax.all_to_all(blocks, 'tok', split_axis=0, concat_axis=0, tiled=True)  26.5 us
    ppermute x15, waiting for transfers between devices, send(): return lax.ppermute(value, 'tp', pairs)  23.1 us
    all_to_all x1, waiting for transfers between devices, exchange(): lax.all_to_all(blocks, 'tok', split_axis=0, concat_axis=0, tiled=True)  19.2 us
    all_to_all x1, starting transfers between devices, exchange(): lax.all_to_all(blocks, 'tok', split_axis=0, concat_axis=0, tiled=True)  16.6 us
    pallas_call x1, Pallas kernels, pack(): pl.pallas_call(pack_kernel, grid_spec=pltpu.PrefetchScalarGridSpec(num_sc...  5.83 us
  transfers between devices with their start and end apart: 16, of which 8 were waited for; matrix products, arithmetic and copies ran while one was open for 1% of the time, Pallas kernels for 10%

profile of v9, /device:TPU:8, one launch (start us, length us, event | category | flops | bytes accessed | tf_op | source)
XLA Modules:
  0.0 149.4 jit_solution(2743700920056439377)
XLA Ops:
  0.0 2.5 %dispatch.1 = bf16[512,1024]{1,0:T(8,128)(2,1)} custom-call(s32[2,128]{1,0:T(2,128)} %bitcast.26, bf16[128,512]{1,0:T(8,128)(2,1)} %x_ref.1, bf16[128,512]{1,0:T(8,128)(2,1)} %g_ref.1), custom_call_target="tpu_custom_call" | custom-call | tf_op jit(solution)/shard_map/dispatch/pallas_call | solution.py:44
  2.5 16.6 %all-to-all-start = ((bf16[64,8,1024]{2,1,0:T(8,128)(2,1)}), bf16[64,8,1024]{2,1,0:T(8,128)(2,1)S(1)}, u32[]{:S(2)}, u32[]{:S(2)}) async-start(bf16[64,8,1024]{2,1,0:T(8,128)(2,1)} %bitcast.24), calls=%async_computation | async-start | bytes 2097152 | tf_op jit(solution)/shard_map/all_to_all | solution.py:300
  19.1 0.1 fusion.1
  19.2 0.6 pad_add_fusion.blocks_ref
  19.8 5.8 %pack.1 = (bf16[4,576,512]{2,1,0:T(8,128)(2,1)}, bf16[4,576,512]{2,1,0:T(8,128)(2,1)}) custom-call(s32[8]{0:T(128)} %pad_add_fusion.blocks_ref, bf16[192,4096]{1,0:T(8,128)(2,1)} %bitcast.18, bf16[192,4096]{1,0:T(8,128)(2,1)} %bitcast.20, bf16[192,4096]{1,0:T(8,128)(2,1)} %bitcast.22, bf16[192,4096]{1,0:T(8,128)(2,1)} %bitcast.19, ...), custom_call_target="tpu_custom_call" | custom-call | tf_op jit(solution)/shard_map/pack/pallas_call | solution.py:83
  25.6 1.9 %collective-permute-start.4 = (bf16[4,576,512]{2,1,0:T(8,128)(2,1)}, bf16[4,576,512]{2,1,0:T(8,128)(2,1)S(1)}, u32[]{:S(2)}, u32[]{:S(2)}) collective-permute-start(bf16[4,576,512]{2,1,0:T(8,128)(2,1)} %get-tuple-element.26), channel_id=1, source_target_pairs={{0,1},{1,0},{2,3},{3,2},{4,5},{5,4},{6,7},{7,6},{8,9},{9,8},{10,11... | collective-permute-start | bytes 7077896 | tf_op jit(solution)/shard_map/ppermute | solution.py:308
  27.5 1.7 %mixer.1.mix_ref = bf16[256,512]{1,0:T(8,128)(2,1)} custom-call(s32[2,128]{1,0:T(2,128)} %bitcast.27, f32[2,128]{1,0:T(2,128)} %bitcast.28), custom_call_target="tpu_custom_call" | custom-call | tf_op jit(solution)/shard_map/mixer/pallas_call | solution.py:61
  29.2 19.2 %all-to-all-done = bf16[64,8,1024]{2,1,0:T(8,128)(2,1)S(1)} async-done(((bf16[64,8,1024]{2,1,0:T(8,128)(2,1)}), bf16[64,8,1024]{2,1,0:T(8,128)(2,1)S(1)}, u32[]{:S(2)}, u32[]{:S(2)}) %all-to-all-start) | async-done | bytes 1048608 | tf_op jit(solution)/shard_map/all_to_all | solution.py:300
  48.4 0.1 fusion.4
  48.4 3.5 %collective-permute-start.5 = (bf16[256,1024]{1,0:T(8,128)(2,1)S(1)}, bf16[256,1024]{1,0:T(8,128)(2,1)S(1)}, u32[]{:S(2)}, u32[]{:S(2)}) collective-permute-start(bf16[256,1024]{1,0:T(8,128)(2,1)S(1)} %get-tuple-element.31), channel_id=1, source_target_pairs={{0,2},{1,7},{2,4},{3,1},{4,6},{5,3},{6,0},{7,5},{8,10},{9,15},{10,... | collective-permute-start | bytes 1572872 | tf_op jit(solution)/shard_map/ppermute | solution.py:308
  52.0 3.4 %collective-permute-start.1 = (bf16[256,1024]{1,0:T(8,128)(2,1)S(1)}, bf16[256,1024]{1,0:T(8,128)(2,1)S(1)}, u32[]{:S(2)}, u32[]{:S(2)}) collective-permute-start(bf16[256,1024]{1,0:T(8,128)(2,1)S(1)} %get-tuple-element.32), channel_id=1, source_target_pairs={{0,2},{1,7},{2,4},{3,1},{4,6},{5,3},{6,0},{7,5},{8,10},{9,15},{10,... | collective-permute-start | bytes 1572872 | tf_op jit(solution)/shard_map/ppermute | solution.py:308
  55.4 1.9 %collective-permute-start.6 = (bf16[256,1024]{1,0:T(8,128)(2,1)S(1)}, bf16[256,1024]{1,0:T(8,128)(2,1)S(1)}, u32[]{:S(2)}, u32[]{:S(2)}) collective-permute-start(bf16[256,1024]{1,0:T(8,128)(2,1)S(1)} %get-tuple-element.31), channel_id=1, source_target_pairs={{0,7},{1,2},{2,1},{3,4},{4,3},{5,6},{6,5},{7,0},{8,15},{9,10},{10,... | collective-permute-start | bytes 1572872 | tf_op jit(solution)/shard_map/ppermute | solution.py:308
  57.3 3.5 %collective-permute-done.5.same_low_ref = bf16[256,1024]{1,0:T(8,128)(2,1)S(1)} collective-permute-done((bf16[256,1024]{1,0:T(8,128)(2,1)S(1)}, bf16[256,1024]{1,0:T(8,128)(2,1)S(1)}, u32[]{:S(2)}, u32[]{:S(2)}) %collective-permute-start.5) | collective-permute-done | bytes 524320 | tf_op jit(solution)/shard_map/ppermute | solution.py:308
  60.9 2.2 %collective-permute-start.7 = (bf16[256,1024]{1,0:T(8,128)(2,1)S(1)}, bf16[256,1024]{1,0:T(8,128)(2,1)S(1)}, u32[]{:S(2)}, u32[]{:S(2)}) collective-permute-start(bf16[256,1024]{1,0:T(8,128)(2,1)S(1)} %collective-permute-done.5.same_low_ref), channel_id=1, source_target_pairs={{0,2},{1,7},{2,4},{3,1},{4,6},{5,3},{6,0},{7,5},{8,10},{9,15},{10,... | collective-permute-start | bytes 1572872 | tf_op jit(solution)/shard_map/ppermute | solution.py:308
  63.0 1.9 %collective-permute-start = (bf16[256,1024]{1,0:T(8,128)(2,1)S(1)}, bf16[256,1024]{1,0:T(8,128)(2,1)S(1)}, u32[]{:S(2)}, u32[]{:S(2)}) collective-permute-start(bf16[256,1024]{1,0:T(8,128)(2,1)S(1)} %get-tuple-element.32), channel_id=1, source_target_pairs={{0,7},{1,2},{2,1},{3,4},{4,3},{5,6},{6,5},{7,0},{8,15},{9,10},{10,... | collective-permute-start | bytes 1572872 | tf_op jit(solution)/shard_map/ppermute | solution.py:308
  65.0 6.4 %collective-permute-done.1.same_high_ref = bf16[256,1024]{1,0:T(8,128)(2,1)S(1)} collective-permute-done((bf16[256,1024]{1,0:T(8,128)(2,1)S(1)}, bf16[256,1024]{1,0:T(8,128)(2,1)S(1)}, u32[]{:S(2)}, u32[]{:S(2)}) %collective-permute-start.1) | collective-permute-done | bytes 524320 | tf_op jit(solution)/shard_map/ppermute | solution.py:308
  71.4 2.5 %collective-permute-start.2 = (bf16[256,512]{1,0:T(8,128)(2,1)S(1)}, bf16[256,512]{1,0:T(8,128)(2,1)S(1)}, u32[]{:S(2)}, u32[]{:S(2)}) collective-permute-start(bf16[256,512]{1,0:T(8,128)(2,1)S(1)} %get-tuple-element.34), channel_id=1, source_target_pairs={{0,2},{1,7},{2,4},{3,1},{4,6},{5,3},{6,0},{7,5},{8,10},{9,15},{10,... | collective-permute-start | bytes 786440 | tf_op jit(solution)/shard_map/ppermute | solution.py:308
  73.9 0.0 collective-permute-done.4.sib_ref
  74.0 4.4 %collective-permute-start.3 = (bf16[256,512]{1,0:T(8,128)(2,1)S(1)}, bf16[256,512]{1,0:T(8,128)(2,1)S(1)}, u32[]{:S(2)}, u32[]{:S(2)}) collective-permute-start(bf16[256,512]{1,0:T(8,128)(2,1)S(1)} %get-tuple-element.33), channel_id=1, source_target_pairs={{0,2},{1,7},{2,4},{3,1},{4,6},{5,3},{6,0},{7,5},{8,10},{9,15},{10,... | collective-permute-start | bytes 786440 | tf_op jit(solution)/shard_map/ppermute | solution.py:308
  78.4 2.0 %first.1.sum_ref = f32[2,576,512]{2,1,0:T(8,128)S(1)} custom-call(bf16[512,1024]{1,0:T(8,128)(2,1)S(1)} %bitcast.16, bf16[256,1024]{1,0:T(8,128)(2,1)S(1)} %collective-permute-done.5.same_low_ref, bf16[256,1024]{1,0:T(8,128)(2,1)S(1)} %collective-permute-done.1.same_high_ref, bf16[4,576,512]{2,1,0:T(8,128)(2,1)S(1)} %copy-done, ...), custom_call_target="tpu_custom_call" | custom-call | tf_op jit(solution)/shard_map/first/pallas_call | solution.py:127
  80.4 0.0 collective-permute-done.6.other_ref
  80.4 2.2 %collective-permute-done.7.far_x_ref.far_g_ref = bf16[256,1024]{1,0:T(8,128)(2,1)S(1)} collective-permute-done((bf16[256,1024]{1,0:T(8,128)(2,1)S(1)}, bf16[256,1024]{1,0:T(8,128)(2,1)S(1)}, u32[]{:S(2)}, u32[]{:S(2)}) %collective-permute-start.7) | collective-permute-done | bytes 524320 | tf_op jit(solution)/shard_map/ppermute | solution.py:308
  82.6 0.9 second.2.refs_0_.mine_ref
  83.5 1.9 %collective-permute-start.9 = (f32[2,576,256]{2,1,0:T(8,128)S(1)}, f32[2,576,256]{2,1,0:T(8,128)S(1)}, u32[]{:S(2)}, u32[]{:S(2)}) collective-permute-start(f32[2,576,256]{2,1,0:T(8,128)S(1)} %second.2.refs_0_.mine_ref), channel_id=1, source_target_pairs={{0,1},{1,0},{2,3},{3,2},{4,5},{5,4},{6,7},{7,6},{8,9},{9,8},{10,11... | collective-permute-start | bytes 3538952 | tf_op jit(solution)/shard_map/ppermute | solution.py:308
  85.5 0.0 collective-permute-done.other_ref
  85.5 0.7 collective-permute-done.2.far_x_ref
  86.1 2.8 %collective-permute-done.3.far_g_ref = bf16[256,512]{1,0:T(8,128)(2,1)S(1)} collective-permute-done((bf16[256,512]{1,0:T(8,128)(2,1)S(1)}, bf16[256,512]{1,0:T(8,128)(2,1)S(1)}, u32[]{:S(2)}, u32[]{:S(2)}) %collective-permute-start.3) | collective-permute-done | bytes 262176 | tf_op jit(solution)/shard_map/ppermute | solution.py:308
  88.9 0.9 second.3.mine_ref
  89.8 1.9 %collective-permute-start.8 = (f32[2,576,256]{2,1,0:T(8,128)S(1)}, f32[2,576,256]{2,1,0:T(8,128)S(1)}, u32[]{:S(2)}, u32[]{:S(2)}) collective-permute-start(f32[2,576,256]{2,1,0:T(8,128)S(1)} %second.3.mine_ref), channel_id=1, source_target_pairs={{0,1},{1,0},{2,3},{3,2},{4,5},{5,4},{6,7},{7,6},{8,9},{9,8},{10,11... | collective-permute-start | bytes 3538952 | tf_op jit(solution)/shard_map/ppermute | solution.py:308
  91.8 0.0 collective-permute-done.9.theirs_ref
  91.8 0.6 grads.2
  92.4 3.4 %collective-permute-start.11 = (bf16[256,512]{1,0:T(8,128)(2,1)S(1)}, bf16[256,512]{1,0:T(8,128)(2,1)S(1)}, u32[]{:S(2)}, u32[]{:S(2)}) collective-permute-start(bf16[256,512]{1,0:T(8,128)(2,1)S(1)} %get-tuple-element.30), channel_id=1, source_target_pairs={{0,6},{1,3},{2,0},{3,5},{4,2},{5,7},{6,4},{7,1},{8,14},{9,11},{10,... | collective-permute-start | bytes 786440 | tf_op jit(solution)/shard_map/ppermute | solution.py:308
  95.8 0.6 grads.3
  96.4 1.0 for_other.1
  97.4 3.4 %collective-permute-start.13 = (bf16[512,512]{1,0:T(8,128)(2,1)S(1)}, bf16[512,512]{1,0:T(8,128)(2,1)S(1)}, u32[]{:S(2)}, u32[]{:S(2)}) collective-permute-start(bf16[512,512]{1,0:T(8,128)(2,1)S(1)} %for_other.1), channel_id=1, source_target_pairs={{0,7},{1,2},{2,1},{3,4},{4,3},{5,6},{6,5},{7,0},{8,15},{9,10},{10,... | collective-permute-start | bytes 1572872 | tf_op jit(solution)/shard_map/ppermute | solution.py:308
  100.8 2.2 %collective-permute-start.10 = (bf16[256,512]{1,0:T(8,128)(2,1)S(1)}, bf16[256,512]{1,0:T(8,128)(2,1)S(1)}, u32[]{:S(2)}, u32[]{:S(2)}) collective-permute-start(bf16[256,512]{1,0:T(8,128)(2,1)S(1)} %get-tuple-element.29), channel_id=1, source_target_pairs={{0,6},{1,3},{2,0},{3,5},{4,2},{5,7},{6,4},{7,1},{8,14},{9,11},{10,... | collective-permute-start | bytes 786440 | tf_op jit(solution)/shard_map/ppermute | solution.py:308
  103.1 0.0 collective-permute-done.11.got_ref
  103.1 0.5 near.2.refs_0_
  103.5 2.7 %collective-permute-start.14 = (bf16[256,512]{1,0:T(8,128)(2,1)S(1)}, bf16[256,512]{1,0:T(8,128)(2,1)S(1)}, u32[]{:S(2)}, u32[]{:S(2)}) collective-permute-start(bf16[256,512]{1,0:T(8,128)(2,1)S(1)} %near.2.refs_0_), channel_id=1, source_target_pairs={{0,6},{1,3},{2,0},{3,5},{4,2},{5,7},{6,4},{7,1},{8,14},{9,11},{10,... | collective-permute-start | bytes 786440 | tf_op jit(solution)/shard_map/ppermute | solution.py:308
  106.3 4.0 %collective-permute-done.10.got_ref = bf16[256,512]{1,0:T(8,128)(2,1)S(1)} collective-permute-done((bf16[256,512]{1,0:T(8,128)(2,1)S(1)}, bf16[256,512]{1,0:T(8,128)(2,1)S(1)}, u32[]{:S(2)}, u32[]{:S(2)}) %collective-permute-start.10) | collective-permute-done | bytes 262176 | tf_op jit(solution)/shard_map/ppermute | solution.py:308
  110.3 0.5 near.3
  110.8 5.6 %collective-permute-start.12 = (bf16[256,512]{1,0:T(8,128)(2,1)S(1)}, bf16[256,512]{1,0:T(8,128)(2,1)S(1)}, u32[]{:S(2)}, u32[]{:S(2)}) collective-permute-start(bf16[256,512]{1,0:T(8,128)(2,1)S(1)} %near.3), channel_id=1, source_target_pairs={{0,6},{1,3},{2,0},{3,5},{4,2},{5,7},{6,4},{7,1},{8,14},{9,11},{10,... | collective-permute-start | bytes 786440 | tf_op jit(solution)/shard_map/ppermute | solution.py:308
  116.4 0.0 collective-permute-done.14.far_ref
  116.4 0.5 total.2.refs_0_
  116.9 3.4 %collective-permute-done.12.far_ref = bf16[256,512]{1,0:T(8,128)(2,1)S(1)} collective-permute-done((bf16[256,512]{1,0:T(8,128)(2,1)S(1)}, bf16[256,512]{1,0:T(8,128)(2,1)S(1)}, u32[]{:S(2)}, u32[]{:S(2)}) %collective-permute-start.12) | collective-permute-done | bytes 262176 | tf_op jit(solution)/shard_map/ppermute | solution.py:308
  120.3 0.5 total.3
  120.7 26.5 %all_to_all.10 = bf16[64,8,512]{2,1,0:T(8,128)(2,1)} all-to-all(bf16[64,8,512]{2,1,0:T(8,128)(2,1)S(1)} %bitcast.17), channel_id=1, replica_groups=mesh['tok'=64,'tp'=8] {'tok'}, dimensions={0} | all-to-all | bytes 1048576 | tf_op jit(solution)/shard_map/all_to_all | solution.py:300
  147.3 2.1 %combine.1 = bf16[128,512]{1,0:T(8,128)(2,1)} custom-call(bf16[256,512]{1,0:T(8,128)(2,1)} %mixer.1.mix_ref, bf16[512,512]{1,0:T(8,128)(2,1)} %bitcast.25), custom_call_target="tpu_custom_call" | custom-call | tf_op jit(solution)/shard_map/combine/pallas_call | solution.py:291
  (5 shorter events, 0.0 us)
Async XLA Ops:
  2.5 45.8 %all-to-all-start = ((bf16[64,8,1024]{2,1,0:T(8,128)(2,1)}), bf16[64,8,1024]{2,1,0:T(8,128)(2,1)S(1)}, u32[]{:S(2)}, u32[]{:S(2)}) async-start(bf16[64,8,1024]{2,1,0:T(8,128)(2,1)} %bitcast.24), calls=%async_computation | async-start | bytes 2097152 | tf_op jit(solution)/shard_map/all_to_all | solution.py:300
  25.6 48.3 %collective-permute-start.4 = (bf16[4,576,512]{2,1,0:T(8,128)(2,1)}, bf16[4,576,512]{2,1,0:T(8,128)(2,1)S(1)}, u32[]{:S(2)}, u32[]{:S(2)}) collective-permute-start(bf16[4,576,512]{2,1,0:T(8,128)(2,1)} %get-tuple-element.26), channel_id=1, source_target_pairs={{0,1},{1,0},{2,3},{3,2},{4,5},{5,4},{6,7},{7,6},{8,9},{9,8},{10,11... | collective-permute-start | bytes 7077896 | tf_op jit(solution)/shard_map/ppermute | solution.py:308
  48.4 30.0 %copy-start = (bf16[4,576,512]{2,1,0:T(8,128)(2,1)S(1)}, bf16[4,576,512]{2,1,0:T(8,128)(2,1)}, u32[]{:S(2)}) copy-start(bf16[4,576,512]{2,1,0:T(8,128)(2,1)} %get-tuple-element.25.keep_ref) | copy-start | bytes 7077892
  48.4 12.4 %collective-permute-start.5 = (bf16[256,1024]{1,0:T(8,128)(2,1)S(1)}, bf16[256,1024]{1,0:T(8,128)(2,1)S(1)}, u32[]{:S(2)}, u32[]{:S(2)}) collective-permute-start(bf16[256,1024]{1,0:T(8,128)(2,1)S(1)} %get-tuple-element.31), channel_id=1, source_target_pairs={{0,2},{1,7},{2,4},{3,1},{4,6},{5,3},{6,0},{7,5},{8,10},{9,15},{10,... | collective-permute-start | bytes 1572872 | tf_op jit(solution)/shard_map/ppermute | solution.py:308
  52.0 19.4 %collective-permute-start.1 = (bf16[256,1024]{1,0:T(8,128)(2,1)S(1)}, bf16[256,1024]{1,0:T(8,128)(2,1)S(1)}, u32[]{:S(2)}, u32[]{:S(2)}) collective-permute-start(bf16[256,1024]{1,0:T(8,128)(2,1)S(1)} %get-tuple-element.32), channel_id=1, source_target_pairs={{0,2},{1,7},{2,4},{3,1},{4,6},{5,3},{6,0},{7,5},{8,10},{9,15},{10,... | collective-permute-start | bytes 1572872 | tf_op jit(solution)/shard_map/ppermute | solution.py:308
  55.4 25.0 %collective-permute-start.6 = (bf16[256,1024]{1,0:T(8,128)(2,1)S(1)}, bf16[256,1024]{1,0:T(8,128)(2,1)S(1)}, u32[]{:S(2)}, u32[]{:S(2)}) collective-permute-start(bf16[256,1024]{1,0:T(8,128)(2,1)S(1)} %get-tuple-element.31), channel_id=1, source_target_pairs={{0,7},{1,2},{2,1},{3,4},{4,3},{5,6},{6,5},{7,0},{8,15},{9,10},{10,... | collective-permute-start | bytes 1572872 | tf_op jit(solution)/shard_map/ppermute | solution.py:308
  60.9 21.8 %collective-permute-start.7 = (bf16[256,1024]{1,0:T(8,128)(2,1)S(1)}, bf16[256,1024]{1,0:T(8,128)(2,1)S(1)}, u32[]{:S(2)}, u32[]{:S(2)}) collective-permute-start(bf16[256,1024]{1,0:T(8,128)(2,1)S(1)} %collective-permute-done.5.same_low_ref), channel_id=1, source_target_pairs={{0,2},{1,7},{2,4},{3,1},{4,6},{5,3},{6,0},{7,5},{8,10},{9,15},{10,... | collective-permute-start | bytes 1572872 | tf_op jit(solution)/shard_map/ppermute | solution.py:308
  63.0 22.4 %collective-permute-start = (bf16[256,1024]{1,0:T(8,128)(2,1)S(1)}, bf16[256,1024]{1,0:T(8,128)(2,1)S(1)}, u32[]{:S(2)}, u32[]{:S(2)}) collective-permute-start(bf16[256,1024]{1,0:T(8,128)(2,1)S(1)} %get-tuple-element.32), channel_id=1, source_target_pairs={{0,7},{1,2},{2,1},{3,4},{4,3},{5,6},{6,5},{7,0},{8,15},{9,10},{10,... | collective-permute-start | bytes 1572872 | tf_op jit(solution)/shard_map/ppermute | solution.py:308
  71.4 14.7 %collective-permute-start.2 = (bf16[256,512]{1,0:T(8,128)(2,1)S(1)}, bf16[256,512]{1,0:T(8,128)(2,1)S(1)}, u32[]{:S(2)}, u32[]{:S(2)}) collective-permute-start(bf16[256,512]{1,0:T(8,128)(2,1)S(1)} %get-tuple-element.34), channel_id=1, source_target_pairs={{0,2},{1,7},{2,4},{3,1},{4,6},{5,3},{6,0},{7,5},{8,10},{9,15},{10,... | collective-permute-start | bytes 786440 | tf_op jit(solution)/shard_map/ppermute | solution.py:308
  74.0 15.0 %collective-permute-start.3 = (bf16[256,512]{1,0:T(8,128)(2,1)S(1)}, bf16[256,512]{1,0:T(8,128)(2,1)S(1)}, u32[]{:S(2)}, u32[]{:S(2)}) collective-permute-start(bf16[256,512]{1,0:T(8,128)(2,1)S(1)} %get-tuple-element.33), channel_id=1, source_target_pairs={{0,2},{1,7},{2,4},{3,1},{4,6},{5,3},{6,0},{7,5},{8,10},{9,15},{10,... | collective-permute-start | bytes 786440 | tf_op jit(solution)/shard_map/ppermute | solution.py:308
  83.5 8.2 %collective-permute-start.9 = (f32[2,576,256]{2,1,0:T(8,128)S(1)}, f32[2,576,256]{2,1,0:T(8,128)S(1)}, u32[]{:S(2)}, u32[]{:S(2)}) collective-permute-start(f32[2,576,256]{2,1,0:T(8,128)S(1)} %second.2.refs_0_.mine_ref), channel_id=1, source_target_pairs={{0,1},{1,0},{2,3},{3,2},{4,5},{5,4},{6,7},{7,6},{8,9},{9,8},{10,11... | collective-permute-start | bytes 3538952 | tf_op jit(solution)/shard_map/ppermute | solution.py:308
  89.8 6.0 %collective-permute-start.8 = (f32[2,576,256]{2,1,0:T(8,128)S(1)}, f32[2,576,256]{2,1,0:T(8,128)S(1)}, u32[]{:S(2)}, u32[]{:S(2)}) collective-permute-start(f32[2,576,256]{2,1,0:T(8,128)S(1)} %second.3.mine_ref), channel_id=1, source_target_pairs={{0,1},{1,0},{2,3},{3,2},{4,5},{5,4},{6,7},{7,6},{8,9},{9,8},{10,11... | collective-permute-start | bytes 3538952 | tf_op jit(solution)/shard_map/ppermute | solution.py:308
  92.4 10.7 %collective-permute-start.11 = (bf16[256,512]{1,0:T(8,128)(2,1)S(1)}, bf16[256,512]{1,0:T(8,128)(2,1)S(1)}, u32[]{:S(2)}, u32[]{:S(2)}) collective-permute-start(bf16[256,512]{1,0:T(8,128)(2,1)S(1)} %get-tuple-element.30), channel_id=1, source_target_pairs={{0,6},{1,3},{2,0},{3,5},{4,2},{5,7},{6,4},{7,1},{8,14},{9,11},{10,... | collective-permute-start | bytes 786440 | tf_op jit(solution)/shard_map/ppermute | solution.py:308
  97.4 19.0 %collective-permute-start.13 = (bf16[512,512]{1,0:T(8,128)(2,1)S(1)}, bf16[512,512]{1,0:T(8,128)(2,1)S(1)}, u32[]{:S(2)}, u32[]{:S(2)}) collective-permute-start(bf16[512,512]{1,0:T(8,128)(2,1)S(1)} %for_other.1), channel_id=1, source_target_pairs={{0,7},{1,2},{2,1},{3,4},{4,3},{5,6},{6,5},{7,0},{8,15},{9,10},{10,... | collective-permute-start | bytes 1572872 | tf_op jit(solution)/shard_map/ppermute | solution.py:308
  100.8 9.5 %collective-permute-start.10 = (bf16[256,512]{1,0:T(8,128)(2,1)S(1)}, bf16[256,512]{1,0:T(8,128)(2,1)S(1)}, u32[]{:S(2)}, u32[]{:S(2)}) collective-permute-start(bf16[256,512]{1,0:T(8,128)(2,1)S(1)} %get-tuple-element.29), channel_id=1, source_target_pairs={{0,6},{1,3},{2,0},{3,5},{4,2},{5,7},{6,4},{7,1},{8,14},{9,11},{10,... | collective-permute-start | bytes 786440 | tf_op jit(solution)/shard_map/ppermute | solution.py:308
  103.5 12.9 %collective-permute-start.14 = (bf16[256,512]{1,0:T(8,128)(2,1)S(1)}, bf16[256,512]{1,0:T(8,128)(2,1)S(1)}, u32[]{:S(2)}, u32[]{:S(2)}) collective-permute-start(bf16[256,512]{1,0:T(8,128)(2,1)S(1)} %near.2.refs_0_), channel_id=1, source_target_pairs={{0,6},{1,3},{2,0},{3,5},{4,2},{5,7},{6,4},{7,1},{8,14},{9,11},{10,... | collective-permute-start | bytes 786440 | tf_op jit(solution)/shard_map/ppermute | solution.py:308
  110.8 9.5 %collective-permute-start.12 = (bf16[256,512]{1,0:T(8,128)(2,1)S(1)}, bf16[256,512]{1,0:T(8,128)(2,1)S(1)}, u32[]{:S(2)}, u32[]{:S(2)}) collective-permute-start(bf16[256,512]{1,0:T(8,128)(2,1)S(1)} %near.3), channel_id=1, source_target_pairs={{0,6},{1,3},{2,0},{3,5},{4,2},{5,7},{6,4},{7,1},{8,14},{9,11},{10,... | collective-permute-start | bytes 786440 | tf_op jit(solution)/shard_map/ppermute | solution.py:308

commit v10 on v8

--- a/solution.py
+++ b/solution.py
@@ -166,7 +166,7 @@
     )
 
 
-def grads_kernel(mine_ref, theirs_ref, keep_ref, sib_ref, grads_ref, part_ref):
+def grads_kernel(mine_ref, theirs_ref, keep_ref, sib_ref, grads_ref, part_ref, other_ref):
     hidden = mine_ref.shape[1] // 3
     for n in range(CORES):
         gate_pre = mine_ref[n, :hidden, :] + theirs_ref[1 - n, :hidden, :]
@@ -176,7 +176,8 @@
         slope = sigma * (1.0 + gate_pre * (1.0 - sigma))
         grads_ref[n, :hidden, :] = (hidden_grad * up_pre * slope).astype(grads_ref.dtype)
         grads_ref[n, hidden:, :] = (hidden_grad * (gate_pre * sigma)).astype(grads_ref.dtype)
-    part_ref[...] = chip_sum(grads_ref[...], keep_ref[0], sib_ref[0]).astype(part_ref.dtype)
+    part_ref[...] = chip_sum(grads_ref[...], keep_ref[1], sib_ref[1]).astype(part_ref.dtype)
+    other_ref[...] = chip_sum(grads_ref[...], keep_ref[0], sib_ref[0]).astype(other_ref.dtype)
 
 
 def grads(mine, theirs, keep, sib):
@@ -184,13 +185,15 @@
     block = keep.shape[2]
     wide = depth // 3 * 2
     whole = pl.BlockSpec((CORES, depth, half), lambda i: (0, 0, 0))
-    weights = pl.BlockSpec((1, depth, block), lambda i: (CHIPS - 1, 0, 0))
+    weights = pl.BlockSpec((2, depth, block), lambda i: (1, 0, 0))
+    out = pl.BlockSpec((half, block), lambda i: (0, 0))
+    part = jax.ShapeDtypeStruct((half, block), jnp.bfloat16)
     return pl.pallas_call(
         grads_kernel,
         grid=(1,),
         in_specs=[whole, whole, weights, weights],
-        out_specs=[pl.BlockSpec((CORES, wide, half), lambda i: (0, 0, 0)), pl.BlockSpec((half, block), lambda i: (0, 0))],
-        out_shape=(jax.ShapeDtypeStruct((CORES, wide, half), jnp.bfloat16), jax.ShapeDtypeStruct((half, block), jnp.bfloat16)),
+        out_specs=[pl.BlockSpec((CORES, wide, half), lambda i: (0, 0, 0)), out, out],
+        out_shape=(jax.ShapeDtypeStruct((CORES, wide, half), jnp.bfloat16), part, part),
         compiler_params=BIG,
         name="grads",
     )(mine, theirs, keep, sib)
@@ -217,36 +220,34 @@
     )(grads_value, keep, sib, got)
 
 
-def rows_kernel(low_ref, high_ref, keep_ref, sib_ref, *refs):
-    def store(grads_ref, more):
+def total_kernel(low_ref, high_ref, keep_ref, sib_ref, *refs):
+    def store(grads_ref, far_ref, other_ref):
         value = chip_sum(grads_ref[...], keep_ref[0], sib_ref[0])
-        for ref in more:
-            value = value + ref[...].astype(jnp.float32)
+        value = value + far_ref[...].astype(jnp.float32) + other_ref[...].astype(jnp.float32)
         refs[-1][...] = value.astype(refs[-1].dtype)
 
     @pl.when(pl.program_id(0) == 0)
     def _():
-        store(low_ref, (refs[0], refs[2]) if len(refs) > 1 else ())
+        store(low_ref, refs[0], refs[1])
 
     @pl.when(pl.program_id(0) == 1)
     def _():
-        store(high_ref, (refs[1], refs[2]) if len(refs) > 1 else ())
-
-
-def all_rows(grads_values, keep, sib, at, more=()):
+        store(high_ref, refs[2], refs[3])
+
+
+def total(grads_values, keep, sib, more):
     _, wide, half = grads_values[0].shape
     _, depth, block = keep.shape
-    by_half = pl.BlockSpec((half, block), lambda i: (i, 0))
     whole = pl.BlockSpec((half, block), lambda i: (0, 0))
-    weights = pl.BlockSpec((1, depth, block), lambda i: (at, 0, 0))
-    return pl.pallas_call(
-        rows_kernel,
+    weights = pl.BlockSpec((1, depth, block), lambda i: (0, 0, 0))
+    return pl.pallas_call(
+        total_kernel,
         grid=(2,),
-        in_specs=[pl.BlockSpec((CORES, wide, half), lambda i: (0, 0, 0))] * 2 + [weights, weights] + [whole, whole, by_half][: len(more)],
-        out_specs=by_half,
+        in_specs=[pl.BlockSpec((CORES, wide, half), lambda i: (0, 0, 0))] * 2 + [weights, weights] + [whole] * 4,
+        out_specs=pl.BlockSpec((half, block), lambda i: (i, 0)),
         out_shape=jax.ShapeDtypeStruct((2 * half, block), jnp.bfloat16),
         compiler_params=BIG,
-        name="all_rows",
+        name="total",
     )(*grads_values, keep, sib, *more)
 
 
@@ -311,14 +312,13 @@
     other = [to_near_other(rows) for rows in halves]
     opposite = [from_near(rows) for rows in same]
     mine = first(own, *same, keep, sib)
-    values, far = [], []
+    values, more = [], []
     for part in range(2):
         rows = second(other[part], opposite[part], keep, sib, mine, part)
-        value, for_opposite = grads(rows, to_sibling(rows), keep, sib)
+        value, for_opposite, for_other = grads(rows, to_sibling(rows), keep, sib)
         values.append(value)
-        far.append(to_near(near(value, keep, sib, to_near(for_opposite))))
-    from_other = to_near_other(all_rows(values, keep, sib, 2))
-    return all_rows(values, keep, sib, 0, (*far, from_other))
+        more += [to_near(near(value, keep, sib, to_near(for_opposite))), to_near_other(for_other)]
+    return total(values, keep, sib, more)
 
 
 def shards(activations, out_grad, routes, gate_vals, w_gate, w_up, w_down):

time: 147 us -> 147 us (level)
  the two profiles are of different devices: /device:TPU:1 before, /device:TPU:6 now
where the time goes in v10:
time: 147 us; the launch traced here: 145 us
  starting transfers between devices  55.6 us (38%)
  waiting for transfers between devices  42.8 us (29%)
  blocking collectives  24.5 us (17%)
  Pallas kernels  19.5 us (13%)
  local copies, waits for them, and re-layouts  1.73 us (1%)
    ppermute x15, starting transfers between devices, send(): return lax.ppermute(value, 'tp', pairs)  39 us
    all_to_all x1, blocking collectives, exchange(): lax.all_to_all(blocks, 'tok', split_axis=0, concat_axis=0, tiled=True)  24.5 us
    ppermute x15, waiting for transfers between devices, send(): return lax.ppermute(value, 'tp', pairs)  23.2 us
    all_to_all x1, waiting for transfers between devices, exchange(): lax.all_to_all(blocks, 'tok', split_axis=0, concat_axis=0, tiled=True)  19.7 us
    all_to_all x1, starting transfers between devices, exchange(): lax.all_to_all(blocks, 'tok', split_axis=0, concat_axis=0, tiled=True)  16.6 us
    pallas_call x1, Pallas kernels, pack(): pl.pallas_call(pack_kernel, grid_spec=pltpu.PrefetchScalarGridSpec(num_sc...  5.83 us
  transfers between devices with their start and end apart: 16, of which 7 were waited for; matrix products, arithmetic and copies ran while one was open for 1% of the time, Pallas kernels for 10%

profile of v10, /device:TPU:6, one launch (start us, length us, event | category | flops | bytes accessed | tf_op | source)
XLA Modules:
  0.0 145.2 jit_solution(9625814939286404799)
XLA Ops:
  0.0 2.5 %dispatch.1 = bf16[512,1024]{1,0:T(8,128)(2,1)} custom-call(s32[2,128]{1,0:T(2,128)} %bitcast.26, bf16[128,512]{1,0:T(8,128)(2,1)} %x_ref.1, bf16[128,512]{1,0:T(8,128)(2,1)} %g_ref.1), custom_call_target="tpu_custom_call" | custom-call | tf_op jit(solution)/shard_map/dispatch/pallas_call | solution.py:44
  2.5 16.6 %all-to-all-start = ((bf16[64,8,1024]{2,1,0:T(8,128)(2,1)}), bf16[64,8,1024]{2,1,0:T(8,128)(2,1)S(1)}, u32[]{:S(2)}, u32[]{:S(2)}) async-start(bf16[64,8,1024]{2,1,0:T(8,128)(2,1)} %bitcast.24), calls=%async_computation | async-start | bytes 2097152 | tf_op jit(solution)/shard_map/all_to_all | solution.py:271
  19.1 0.1 fusion.1
  19.2 0.6 pad_add_fusion.blocks_ref
  19.8 5.8 %pack.1 = (bf16[4,576,512]{2,1,0:T(8,128)(2,1)}, bf16[4,576,512]{2,1,0:T(8,128)(2,1)}) custom-call(s32[8]{0:T(128)} %pad_add_fusion.blocks_ref, bf16[192,4096]{1,0:T(8,128)(2,1)} %bitcast.18, bf16[192,4096]{1,0:T(8,128)(2,1)} %bitcast.20, bf16[192,4096]{1,0:T(8,128)(2,1)} %bitcast.22, bf16[192,4096]{1,0:T(8,128)(2,1)} %bitcast.19, ...), custom_call_target="tpu_custom_call" | custom-call | tf_op jit(solution)/shard_map/pack/pallas_call | solution.py:83
  25.6 1.9 %collective-permute-start.3 = (bf16[4,576,512]{2,1,0:T(8,128)(2,1)}, bf16[4,576,512]{2,1,0:T(8,128)(2,1)S(1)}, u32[]{:S(2)}, u32[]{:S(2)}) collective-permute-start(bf16[4,576,512]{2,1,0:T(8,128)(2,1)} %get-tuple-element.34), channel_id=1, source_target_pairs={{0,1},{1,0},{2,3},{3,2},{4,5},{5,4},{6,7},{7,6},{8,9},{9,8},{10,11... | collective-permute-start | bytes 7077896 | tf_op jit(solution)/shard_map/ppermute | solution.py:279
  27.6 1.7 %mixer.1 = (bf16[128,512]{1,0:T(8,128)(2,1)}, bf16[128,512]{1,0:T(8,128)(2,1)}) custom-call(s32[2,128]{1,0:T(2,128)} %bitcast.27, f32[2,128]{1,0:T(2,128)} %bitcast.28), custom_call_target="tpu_custom_call" | custom-call | tf_op jit(solution)/shard_map/mixer/pallas_call | solution.py:61
  29.2 19.7 %all-to-all-done = bf16[64,8,1024]{2,1,0:T(8,128)(2,1)S(1)} async-done(((bf16[64,8,1024]{2,1,0:T(8,128)(2,1)}), bf16[64,8,1024]{2,1,0:T(8,128)(2,1)S(1)}, u32[]{:S(2)}, u32[]{:S(2)}) %all-to-all-start) | async-done | bytes 1048608 | tf_op jit(solution)/shard_map/all_to_all | solution.py:271
  48.9 0.1 fusion.4
  49.0 2.4 %collective-permute-start.1 = (bf16[256,1024]{1,0:T(8,128)(2,1)S(1)}, bf16[256,1024]{1,0:T(8,128)(2,1)S(1)}, u32[]{:S(2)}, u32[]{:S(2)}) collective-permute-start(bf16[256,1024]{1,0:T(8,128)(2,1)S(1)} %get-tuple-element.42), channel_id=1, source_target_pairs={{0,2},{1,7},{2,4},{3,1},{4,6},{5,3},{6,0},{7,5},{8,10},{9,15},{10,... | collective-permute-start | bytes 1572872 | tf_op jit(solution)/shard_map/ppermute | solution.py:279
  51.4 3.4 %collective-permute-start.4 = (bf16[256,1024]{1,0:T(8,128)(2,1)S(1)}, bf16[256,1024]{1,0:T(8,128)(2,1)S(1)}, u32[]{:S(2)}, u32[]{:S(2)}) collective-permute-start(bf16[256,1024]{1,0:T(8,128)(2,1)S(1)} %get-tuple-element.41), channel_id=1, source_target_pairs={{0,2},{1,7},{2,4},{3,1},{4,6},{5,3},{6,0},{7,5},{8,10},{9,15},{10,... | collective-permute-start | bytes 1572872 | tf_op jit(solution)/shard_map/ppermute | solution.py:279
  54.8 1.9 %collective-permute-start = (bf16[256,1024]{1,0:T(8,128)(2,1)S(1)}, bf16[256,1024]{1,0:T(8,128)(2,1)S(1)}, u32[]{:S(2)}, u32[]{:S(2)}) collective-permute-start(bf16[256,1024]{1,0:T(8,128)(2,1)S(1)} %get-tuple-element.42), channel_id=1, source_target_pairs={{0,7},{1,2},{2,1},{3,4},{4,3},{5,6},{6,5},{7,0},{8,15},{9,10},{10,... | collective-permute-start | bytes 1572872 | tf_op jit(solution)/shard_map/ppermute | solution.py:279
  56.7 3.7 %collective-permute-done.1.same_low_ref = bf16[256,1024]{1,0:T(8,128)(2,1)S(1)} collective-permute-done((bf16[256,1024]{1,0:T(8,128)(2,1)S(1)}, bf16[256,1024]{1,0:T(8,128)(2,1)S(1)}, u32[]{:S(2)}, u32[]{:S(2)}) %collective-permute-start.1) | collective-permute-done | bytes 524320 | tf_op jit(solution)/shard_map/ppermute | solution.py:279
  60.4 3.3 %collective-permute-start.2 = (bf16[256,1024]{1,0:T(8,128)(2,1)S(1)}, bf16[256,1024]{1,0:T(8,128)(2,1)S(1)}, u32[]{:S(2)}, u32[]{:S(2)}) collective-permute-start(bf16[256,1024]{1,0:T(8,128)(2,1)S(1)} %collective-permute-done.1.same_low_ref), channel_id=1, source_target_pairs={{0,2},{1,7},{2,4},{3,1},{4,6},{5,3},{6,0},{7,5},{8,10},{9,15},{10,... | collective-permute-start | bytes 1572872 | tf_op jit(solution)/shard_map/ppermute | solution.py:279
  63.6 1.9 %collective-permute-start.6 = (bf16[256,1024]{1,0:T(8,128)(2,1)S(1)}, bf16[256,1024]{1,0:T(8,128)(2,1)S(1)}, u32[]{:S(2)}, u32[]{:S(2)}) collective-permute-start(bf16[256,1024]{1,0:T(8,128)(2,1)S(1)} %get-tuple-element.41), channel_id=1, source_target_pairs={{0,7},{1,2},{2,1},{3,4},{4,3},{5,6},{6,5},{7,0},{8,15},{9,10},{10,... | collective-permute-start | bytes 1572872 | tf_op jit(solution)/shard_map/ppermute | solution.py:279
  65.6 6.0 %collective-permute-done.4.same_high_ref = bf16[256,1024]{1,0:T(8,128)(2,1)S(1)} collective-permute-done((bf16[256,1024]{1,0:T(8,128)(2,1)S(1)}, bf16[256,1024]{1,0:T(8,128)(2,1)S(1)}, u32[]{:S(2)}, u32[]{:S(2)}) %collective-permute-start.4) | collective-permute-done | bytes 524320 | tf_op jit(solution)/shard_map/ppermute | solution.py:279
  71.6 2.6 %collective-permute-start.7 = (bf16[256,1024]{1,0:T(8,128)(2,1)S(1)}, bf16[256,1024]{1,0:T(8,128)(2,1)S(1)}, u32[]{:S(2)}, u32[]{:S(2)}) collective-permute-start(bf16[256,1024]{1,0:T(8,128)(2,1)S(1)} %collective-permute-done.4.same_high_ref), channel_id=1, source_target_pairs={{0,2},{1,7},{2,4},{3,1},{4,6},{5,3},{6,0},{7,5},{8,10},{9,15},{10,... | collective-permute-start | bytes 1572872 | tf_op jit(solution)/shard_map/ppermute | solution.py:279
  74.2 0.0 collective-permute-done.3.sib_ref
  74.2 1.7 %copy-done = bf16[4,576,512]{2,1,0:T(8,128)(2,1)S(1)} copy-done((bf16[4,576,512]{2,1,0:T(8,128)(2,1)S(1)}, bf16[4,576,512]{2,1,0:T(8,128)(2,1)}, u32[]{:S(2)}) %copy-start) | copy-done | bytes 2359320
  75.9 2.0 %first.1.sum_ref = f32[2,576,512]{2,1,0:T(8,128)S(1)} custom-call(bf16[512,1024]{1,0:T(8,128)(2,1)S(1)} %bitcast.16, bf16[256,1024]{1,0:T(8,128)(2,1)S(1)} %collective-permute-done.1.same_low_ref, bf16[256,1024]{1,0:T(8,128)(2,1)S(1)} %collective-permute-done.4.same_high_ref, bf16[4,576,512]{2,1,0:T(8,128)(2,1)S(1)} %copy-done, ...), custom_call_target="tpu_custom_call" | custom-call | tf_op jit(solution)/shard_map/first/pallas_call | solution.py:127
  77.9 0.0 collective-permute-done.other_ref
  77.9 4.6 %collective-permute-done.2.opposite_ref = bf16[256,1024]{1,0:T(8,128)(2,1)S(1)} collective-permute-done((bf16[256,1024]{1,0:T(8,128)(2,1)S(1)}, bf16[256,1024]{1,0:T(8,128)(2,1)S(1)}, u32[]{:S(2)}, u32[]{:S(2)}) %collective-permute-start.2) | collective-permute-done | bytes 524320 | tf_op jit(solution)/shard_map/ppermute | solution.py:279
  82.5 0.9 second.2.mine_ref
  83.4 1.9 %collective-permute-start.5 = (f32[2,576,256]{2,1,0:T(8,128)S(1)}, f32[2,576,256]{2,1,0:T(8,128)S(1)}, u32[]{:S(2)}, u32[]{:S(2)}) collective-permute-start(f32[2,576,256]{2,1,0:T(8,128)S(1)} %second.2.mine_ref), channel_id=1, source_target_pairs={{0,1},{1,0},{2,3},{3,2},{4,5},{5,4},{6,7},{7,6},{8,9},{9,8},{10,11... | collective-permute-start | bytes 3538952 | tf_op jit(solution)/shard_map/ppermute | solution.py:279
  85.4 0.0 collective-permute-done.6.other_ref
  85.4 2.8 %collective-permute-done.7.opposite_ref = bf16[256,1024]{1,0:T(8,128)(2,1)S(1)} collective-permute-done((bf16[256,1024]{1,0:T(8,128)(2,1)S(1)}, bf16[256,1024]{1,0:T(8,128)(2,1)S(1)}, u32[]{:S(2)}, u32[]{:S(2)}) %collective-permute-start.7) | collective-permute-done | bytes 524320 | tf_op jit(solution)/shard_map/ppermute | solution.py:279
  88.1 0.9 second.3.mine_ref
  89.0 1.9 %collective-permute-start.8 = (f32[2,576,256]{2,1,0:T(8,128)S(1)}, f32[2,576,256]{2,1,0:T(8,128)S(1)}, u32[]{:S(2)}, u32[]{:S(2)}) collective-permute-start(f32[2,576,256]{2,1,0:T(8,128)S(1)} %second.3.mine_ref), channel_id=1, source_target_pairs={{0,1},{1,0},{2,3},{3,2},{4,5},{5,4},{6,7},{7,6},{8,9},{9,8},{10,11... | collective-permute-start | bytes 3538952 | tf_op jit(solution)/shard_map/ppermute | solution.py:279
  91.0 0.9 grads.2
  91.8 2.7 %collective-permute-start.9 = (bf16[256,512]{1,0:T(8,128)(2,1)S(1)}, bf16[256,512]{1,0:T(8,128)(2,1)S(1)}, u32[]{:S(2)}, u32[]{:S(2)}) collective-permute-start(bf16[256,512]{1,0:T(8,128)(2,1)S(1)} %get-tuple-element.37), channel_id=1, source_target_pairs={{0,6},{1,3},{2,0},{3,5},{4,2},{5,7},{6,4},{7,1},{8,14},{9,11},{10,... | collective-permute-start | bytes 786440 | tf_op jit(solution)/shard_map/ppermute | solution.py:279
  94.6 0.0 collective-permute-done.8.theirs_ref
  94.6 0.9 grads.3
  95.5 2.4 %collective-permute-start.12 = (bf16[256,512]{1,0:T(8,128)(2,1)S(1)}, bf16[256,512]{1,0:T(8,128)(2,1)S(1)}, u32[]{:S(2)}, u32[]{:S(2)}) collective-permute-start(bf16[256,512]{1,0:T(8,128)(2,1)S(1)} %get-tuple-element.39), channel_id=1, source_target_pairs={{0,6},{1,3},{2,0},{3,5},{4,2},{5,7},{6,4},{7,1},{8,14},{9,11},{10,... | collective-permute-start | bytes 786440 | tf_op jit(solution)/shard_map/ppermute | solution.py:279
  97.9 3.8 %collective-permute-start.11 = (bf16[256,512]{1,0:T(8,128)(2,1)S(1)}, bf16[256,512]{1,0:T(8,128)(2,1)S(1)}, u32[]{:S(2)}, u32[]{:S(2)}) collective-permute-start(bf16[256,512]{1,0:T(8,128)(2,1)S(1)} %get-tuple-element.38), channel_id=1, source_target_pairs={{0,7},{1,2},{2,1},{3,4},{4,3},{5,6},{6,5},{7,0},{8,15},{9,10},{10,... | collective-permute-start | bytes 786440 | tf_op jit(solution)/shard_map/ppermute | solution.py:279
  101.7 1.9 %collective-permute-start.14 = (bf16[256,512]{1,0:T(8,128)(2,1)S(1)}, bf16[256,512]{1,0:T(8,128)(2,1)S(1)}, u32[]{:S(2)}, u32[]{:S(2)}) collective-permute-start(bf16[256,512]{1,0:T(8,128)(2,1)S(1)} %get-tuple-element.40), channel_id=1, source_target_pairs={{0,7},{1,2},{2,1},{3,4},{4,3},{5,6},{6,5},{7,0},{8,15},{9,10},{10,... | collective-permute-start | bytes 786440 | tf_op jit(solution)/shard_map/ppermute | solution.py:279
  103.7 0.0 collective-permute-done.9.got_ref
  103.7 0.5 near.2
  104.1 3.5 %collective-permute-start.10 = (bf16[256,512]{1,0:T(8,128)(2,1)S(1)}, bf16[256,512]{1,0:T(8,128)(2,1)S(1)}, u32[]{:S(2)}, u32[]{:S(2)}) collective-permute-start(bf16[256,512]{1,0:T(8,128)(2,1)S(1)} %near.2), channel_id=1, source_target_pairs={{0,6},{1,3},{2,0},{3,5},{4,2},{5,7},{6,4},{7,1},{8,14},{9,11},{10,... | collective-permute-start | bytes 786440 | tf_op jit(solution)/shard_map/ppermute | solution.py:279
  107.6 0.0 collective-permute-done.12.got_ref
  107.6 0.5 near.3
  108.1 3.5 %collective-permute-start.13 = (bf16[256,512]{1,0:T(8,128)(2,1)S(1)}, bf16[256,512]{1,0:T(8,128)(2,1)S(1)}, u32[]{:S(2)}, u32[]{:S(2)}) collective-permute-start(bf16[256,512]{1,0:T(8,128)(2,1)S(1)} %near.3), channel_id=1, source_target_pairs={{0,6},{1,3},{2,0},{3,5},{4,2},{5,7},{6,4},{7,1},{8,14},{9,11},{10,... | collective-permute-start | bytes 786440 | tf_op jit(solution)/shard_map/ppermute | solution.py:279
  111.6 0.0 collective-permute-done.11.refs_1_
  111.6 0.0 collective-permute-done.14.refs_3_
  111.6 2.9 %collective-permute-done.10.refs_0_ = bf16[256,512]{1,0:T(8,128)(2,1)S(1)} collective-permute-done((bf16[256,512]{1,0:T(8,128)(2,1)S(1)}, bf16[256,512]{1,0:T(8,128)(2,1)S(1)}, u32[]{:S(2)}, u32[]{:S(2)}) %collective-permute-start.10) | collective-permute-done | bytes 262176 | tf_op jit(solution)/shard_map/ppermute | solution.py:279
  114.5 3.0 %collective-permute-done.13.refs_2_ = bf16[256,512]{1,0:T(8,128)(2,1)S(1)} collective-permute-done((bf16[256,512]{1,0:T(8,128)(2,1)S(1)}, bf16[256,512]{1,0:T(8,128)(2,1)S(1)}, u32[]{:S(2)}, u32[]{:S(2)}) %collective-permute-start.13) | collective-permute-done | bytes 262176 | tf_op jit(solution)/shard_map/ppermute | solution.py:279
  117.6 1.0 total.1
  118.6 24.5 %all_to_all.10 = bf16[64,8,512]{2,1,0:T(8,128)(2,1)} all-to-all(bf16[64,8,512]{2,1,0:T(8,128)(2,1)S(1)} %bitcast.17), channel_id=1, replica_groups=mesh['tok'=64,'tp'=8] {'tok'}, dimensions={0} | all-to-all | bytes 1048576 | tf_op jit(solution)/shard_map/all_to_all | solution.py:271
  143.1 2.1 %combine.1 = bf16[128,512]{1,0:T(8,128)(2,1)} custom-call(bf16[128,512]{1,0:T(8,128)(2,1)} %get-tuple-element.27.hi_ref, bf16[128,512]{1,0:T(8,128)(2,1)} %get-tuple-element.28.lo_ref, bf16[512,512]{1,0:T(8,128)(2,1)} %bitcast.25), custom_call_target="tpu_custom_call" | custom-call | tf_op jit(solution)/shard_map/combine/pallas_call | solution.py:262
  (2 shorter events, 0.0 us)
Async XLA Ops:
  2.5 46.4 %all-to-all-start = ((bf16[64,8,1024]{2,1,0:T(8,128)(2,1)}), bf16[64,8,1024]{2,1,0:T(8,128)(2,1)S(1)}, u32[]{:S(2)}, u32[]{:S(2)}) async-start(bf16[64,8,1024]{2,1,0:T(8,128)(2,1)} %bitcast.24), calls=%async_computation | async-start | bytes 2097152 | tf_op jit(solution)/shard_map/all_to_all | solution.py:271
  25.6 48.6 %collective-permute-start.3 = (bf16[4,576,512]{2,1,0:T(8,128)(2,1)}, bf16[4,576,512]{2,1,0:T(8,128)(2,1)S(1)}, u32[]{:S(2)}, u32[]{:S(2)}) collective-permute-start(bf16[4,576,512]{2,1,0:T(8,128)(2,1)} %get-tuple-element.34), channel_id=1, source_target_pairs={{0,1},{1,0},{2,3},{3,2},{4,5},{5,4},{6,7},{7,6},{8,9},{9,8},{10,11... | collective-permute-start | bytes 7077896 | tf_op jit(solution)/shard_map/ppermute | solution.py:279
  49.0 11.4 %collective-permute-start.1 = (bf16[256,1024]{1,0:T(8,128)(2,1)S(1)}, bf16[256,1024]{1,0:T(8,128)(2,1)S(1)}, u32[]{:S(2)}, u32[]{:S(2)}) collective-permute-start(bf16[256,1024]{1,0:T(8,128)(2,1)S(1)} %get-tuple-element.42), channel_id=1, source_target_pairs={{0,2},{1,7},{2,4},{3,1},{4,6},{5,3},{6,0},{7,5},{8,10},{9,15},{10,... | collective-permute-start | bytes 1572872 | tf_op jit(solution)/shard_map/ppermute | solution.py:279
  51.4 20.2 %collective-permute-start.4 = (bf16[256,1024]{1,0:T(8,128)(2,1)S(1)}, bf16[256,1024]{1,0:T(8,128)(2,1)S(1)}, u32[]{:S(2)}, u32[]{:S(2)}) collective-permute-start(bf16[256,1024]{1,0:T(8,128)(2,1)S(1)} %get-tuple-element.41), channel_id=1, source_target_pairs={{0,2},{1,7},{2,4},{3,1},{4,6},{5,3},{6,0},{7,5},{8,10},{9,15},{10,... | collective-permute-start | bytes 1572872 | tf_op jit(solution)/shard_map/ppermute | solution.py:279
  54.8 23.1 %collective-permute-start = (bf16[256,1024]{1,0:T(8,128)(2,1)S(1)}, bf16[256,1024]{1,0:T(8,128)(2,1)S(1)}, u32[]{:S(2)}, u32[]{:S(2)}) collective-permute-start(bf16[256,1024]{1,0:T(8,128)(2,1)S(1)} %get-tuple-element.42), channel_id=1, source_target_pairs={{0,7},{1,2},{2,1},{3,4},{4,3},{5,6},{6,5},{7,0},{8,15},{9,10},{10,... | collective-permute-start | bytes 1572872 | tf_op jit(solution)/shard_map/ppermute | solution.py:279
  60.4 22.1 %collective-permute-start.2 = (bf16[256,1024]{1,0:T(8,128)(2,1)S(1)}, bf16[256,1024]{1,0:T(8,128)(2,1)S(1)}, u32[]{:S(2)}, u32[]{:S(2)}) collective-permute-start(bf16[256,1024]{1,0:T(8,128)(2,1)S(1)} %collective-permute-done.1.same_low_ref), channel_id=1, source_target_pairs={{0,2},{1,7},{2,4},{3,1},{4,6},{5,3},{6,0},{7,5},{8,10},{9,15},{10,... | collective-permute-start | bytes 1572872 | tf_op jit(solution)/shard_map/ppermute | solution.py:279
  63.6 21.7 %collective-permute-start.6 = (bf16[256,1024]{1,0:T(8,128)(2,1)S(1)}, bf16[256,1024]{1,0:T(8,128)(2,1)S(1)}, u32[]{:S(2)}, u32[]{:S(2)}) collective-permute-start(bf16[256,1024]{1,0:T(8,128)(2,1)S(1)} %get-tuple-element.41), channel_id=1, source_target_pairs={{0,7},{1,2},{2,1},{3,4},{4,3},{5,6},{6,5},{7,0},{8,15},{9,10},{10,... | collective-permute-start | bytes 1572872 | tf_op jit(solution)/shard_map/ppermute | solution.py:279
  71.6 16.5 %collective-permute-start.7 = (bf16[256,1024]{1,0:T(8,128)(2,1)S(1)}, bf16[256,1024]{1,0:T(8,128)(2,1)S(1)}, u32[]{:S(2)}, u32[]{:S(2)}) collective-permute-start(bf16[256,1024]{1,0:T(8,128)(2,1)S(1)} %collective-permute-done.4.same_high_ref), channel_id=1, source_target_pairs={{0,2},{1,7},{2,4},{3,1},{4,6},{5,3},{6,0},{7,5},{8,10},{9,15},{10,... | collective-permute-start | bytes 1572872 | tf_op jit(solution)/shard_map/ppermute | solution.py:279
  74.2 1.7 %copy-start = (bf16[4,576,512]{2,1,0:T(8,128)(2,1)S(1)}, bf16[4,576,512]{2,1,0:T(8,128)(2,1)}, u32[]{:S(2)}) copy-start(bf16[4,576,512]{2,1,0:T(8,128)(2,1)} %get-tuple-element.33.keep_ref) | copy-start | bytes 7077892
  83.4 7.5 %collective-permute-start.5 = (f32[2,576,256]{2,1,0:T(8,128)S(1)}, f32[2,576,256]{2,1,0:T(8,128)S(1)}, u32[]{:S(2)}, u32[]{:S(2)}) collective-permute-start(f32[2,576,256]{2,1,0:T(8,128)S(1)} %second.2.mine_ref), channel_id=1, source_target_pairs={{0,1},{1,0},{2,3},{3,2},{4,5},{5,4},{6,7},{7,6},{8,9},{9,8},{10,11... | collective-permute-start | bytes 3538952 | tf_op jit(solution)/shard_map/ppermute | solution.py:279
  89.0 5.5 %collective-permute-start.8 = (f32[2,576,256]{2,1,0:T(8,128)S(1)}, f32[2,576,256]{2,1,0:T(8,128)S(1)}, u32[]{:S(2)}, u32[]{:S(2)}) collective-permute-start(f32[2,576,256]{2,1,0:T(8,128)S(1)} %second.3.mine_ref), channel_id=1, source_target_pairs={{0,1},{1,0},{2,3},{3,2},{4,5},{5,4},{6,7},{7,6},{8,9},{9,8},{10,11... | collective-permute-start | bytes 3538952 | tf_op jit(solution)/shard_map/ppermute | solution.py:279
  91.8 11.8 %collective-permute-start.9 = (bf16[256,512]{1,0:T(8,128)(2,1)S(1)}, bf16[256,512]{1,0:T(8,128)(2,1)S(1)}, u32[]{:S(2)}, u32[]{:S(2)}) collective-permute-start(bf16[256,512]{1,0:T(8,128)(2,1)S(1)} %get-tuple-element.37), channel_id=1, source_target_pairs={{0,6},{1,3},{2,0},{3,5},{4,2},{5,7},{6,4},{7,1},{8,14},{9,11},{10,... | collective-permute-start | bytes 786440 | tf_op jit(solution)/shard_map/ppermute | solution.py:279
  95.5 12.2 %collective-permute-start.12 = (bf16[256,512]{1,0:T(8,128)(2,1)S(1)}, bf16[256,512]{1,0:T(8,128)(2,1)S(1)}, u32[]{:S(2)}, u32[]{:S(2)}) collective-permute-start(bf16[256,512]{1,0:T(8,128)(2,1)S(1)} %get-tuple-element.39), channel_id=1, source_target_pairs={{0,6},{1,3},{2,0},{3,5},{4,2},{5,7},{6,4},{7,1},{8,14},{9,11},{10,... | collective-permute-start | bytes 786440 | tf_op jit(solution)/shard_map/ppermute | solution.py:279
  97.9 13.7 %collective-permute-start.11 = (bf16[256,512]{1,0:T(8,128)(2,1)S(1)}, bf16[256,512]{1,0:T(8,128)(2,1)S(1)}, u32[]{:S(2)}, u32[]{:S(2)}) collective-permute-start(bf16[256,512]{1,0:T(8,128)(2,1)S(1)} %get-tuple-element.38), channel_id=1, source_target_pairs={{0,7},{1,2},{2,1},{3,4},{4,3},{5,6},{6,5},{7,0},{8,15},{9,10},{10,... | collective-permute-start | bytes 786440 | tf_op jit(solution)/shard_map/ppermute | solution.py:279
  101.7 9.9 %collective-permute-start.14 = (bf16[256,512]{1,0:T(8,128)(2,1)S(1)}, bf16[256,512]{1,0:T(8,128)(2,1)S(1)}, u32[]{:S(2)}, u32[]{:S(2)}) collective-permute-start(bf16[256,512]{1,0:T(8,128)(2,1)S(1)} %get-tuple-element.40), channel_id=1, source_target_pairs={{0,7},{1,2},{2,1},{3,4},{4,3},{5,6},{6,5},{7,0},{8,15},{9,10},{10,... | collective-permute-start | bytes 786440 | tf_op jit(solution)/shard_map/ppermute | solution.py:279
  104.1 10.4 %collective-permute-start.10 = (bf16[256,512]{1,0:T(8,128)(2,1)S(1)}, bf16[256,512]{1,0:T(8,128)(2,1)S(1)}, u32[]{:S(2)}, u32[]{:S(2)}) collective-permute-start(bf16[256,512]{1,0:T(8,128)(2,1)S(1)} %near.2), channel_id=1, source_target_pairs={{0,6},{1,3},{2,0},{3,5},{4,2},{5,7},{6,4},{7,1},{8,14},{9,11},{10,... | collective-permute-start | bytes 786440 | tf_op jit(solution)/shard_map/ppermute | solution.py:279
  108.1 9.5 %collective-permute-start.13 = (bf16[256,512]{1,0:T(8,128)(2,1)S(1)}, bf16[256,512]{1,0:T(8,128)(2,1)S(1)}, u32[]{:S(2)}, u32[]{:S(2)}) collective-permute-start(bf16[256,512]{1,0:T(8,128)(2,1)S(1)} %near.3), channel_id=1, source_target_pairs={{0,6},{1,3},{2,0},{3,5},{4,2},{5,7},{6,4},{7,1},{8,14},{9,11},{10,... | collective-permute-start | bytes 786440 | tf_op jit(solution)/shard_map/ppermute | solution.py:279

commit v11 on v10

--- a/solution.py
+++ b/solution.py
@@ -166,7 +166,8 @@
     )
 
 
-def grads_kernel(mine_ref, theirs_ref, keep_ref, sib_ref, grads_ref, part_ref, other_ref):
+def grads_kernel(mine_ref, theirs_ref, keep_ref, sib_ref, *refs):
+    grads_ref, part_ref, other_ref = refs[-3:]
     hidden = mine_ref.shape[1] // 3
     for n in range(CORES):
         gate_pre = mine_ref[n, :hidden, :] + theirs_ref[1 - n, :hidden, :]
@@ -180,7 +181,7 @@
     other_ref[...] = chip_sum(grads_ref[...], keep_ref[0], sib_ref[0]).astype(other_ref.dtype)
 
 
-def grads(mine, theirs, keep, sib):
+def grads(mine, theirs, keep, sib, at, before):
     _, depth, half = mine.shape
     block = keep.shape[2]
     wide = depth // 3 * 2
@@ -191,12 +192,13 @@
     return pl.pallas_call(
         grads_kernel,
         grid=(1,),
-        in_specs=[whole, whole, weights, weights],
-        out_specs=[pl.BlockSpec((CORES, wide, half), lambda i: (0, 0, 0)), out, out],
-        out_shape=(jax.ShapeDtypeStruct((CORES, wide, half), jnp.bfloat16), part, part),
+        in_specs=[whole, whole, weights, weights] + [pl.BlockSpec(memory_space=pl.ANY) for _ in before],
+        out_specs=[pl.BlockSpec((CORES, wide, half), lambda i: (0, 0, 0)), out, pl.BlockSpec((half, block), lambda i: (at, 0))],
+        out_shape=(jax.ShapeDtypeStruct((CORES, wide, half), jnp.bfloat16), part, jax.ShapeDtypeStruct((2 * half, block), jnp.bfloat16)),
+        input_output_aliases={4: 2} if before else {},
         compiler_params=BIG,
         name="grads",
-    )(mine, theirs, keep, sib)
+    )(mine, theirs, keep, sib, *before)
 
 
 def near_kernel(grads_ref, keep_ref, sib_ref, got_ref, out_ref):
@@ -228,11 +230,11 @@
 
     @pl.when(pl.program_id(0) == 0)
     def _():
-        store(low_ref, refs[0], refs[1])
+        store(low_ref, refs[0], refs[2])
 
     @pl.when(pl.program_id(0) == 1)
     def _():
-        store(high_ref, refs[2], refs[3])
+        store(high_ref, refs[1], refs[2])
 
 
 def total(grads_values, keep, sib, more):
@@ -243,7 +245,7 @@
     return pl.pallas_call(
         total_kernel,
         grid=(2,),
-        in_specs=[pl.BlockSpec((CORES, wide, half), lambda i: (0, 0, 0))] * 2 + [weights, weights] + [whole] * 4,
+        in_specs=[pl.BlockSpec((CORES, wide, half), lambda i: (0, 0, 0))] * 2 + [weights, weights] + [whole, whole, pl.BlockSpec((half, block), lambda i: (i, 0))],
         out_specs=pl.BlockSpec((half, block), lambda i: (i, 0)),
         out_shape=jax.ShapeDtypeStruct((2 * half, block), jnp.bfloat16),
         compiler_params=BIG,
@@ -312,13 +314,14 @@
     other = [to_near_other(rows) for rows in halves]
     opposite = [from_near(rows) for rows in same]
     mine = first(own, *same, keep, sib)
-    values, more = [], []
+    values, more, other_parts = [], [], ()
     for part in range(2):
         rows = second(other[part], opposite[part], keep, sib, mine, part)
-        value, for_opposite, for_other = grads(rows, to_sibling(rows), keep, sib)
+        value, for_opposite, for_other = grads(rows, to_sibling(rows), keep, sib, part, other_parts)
+        other_parts = (for_other,)
         values.append(value)
-        more += [to_near(near(value, keep, sib, to_near(for_opposite))), to_near_other(for_other)]
-    return total(values, keep, sib, more)
+        more.append(to_near(near(value, keep, sib, to_near(for_opposite))))
+    return total(values, keep, sib, (*more, to_near_other(for_other)))
 
 
 def shards(activations, out_grad, routes, gate_vals, w_gate, w_up, w_down):

time: 147 us -> 147 us (level)
  starting transfers between devices: 55.6 us -> 51.5 us
  waiting for transfers between devices: 42.8 us -> 45.6 us
    ppermute x15 -> x14, starting transfers between devices: 39 us -> 34.9 us  [send(): return lax.ppermute(value, 'tp', pairs)]
    ppermute x15 -> x14, waiting for transfers between devices: 23.2 us -> 25.9 us  [send(): return lax.ppermute(value, 'tp', pairs)]
  transfers between devices with their start and end apart: 16 -> 15, of which waited for: 7 -> 9; matrix products, arithmetic and copies ran while one was open for 1% -> 1% of each run, Pallas kernels for 10% -> 10%
where the time goes in v11:
time: 147 us; the launch traced here: 144 us
  starting transfers between devices  51.5 us (35%)
  waiting for transfers between devices  45.6 us (31%)
  blocking collectives  25.2 us (17%)
  Pallas kernels  19.5 us (13%)
  local copies, waits for them, and re-layouts  1.73 us (1%)
    ppermute x14, starting transfers between devices, send(): return lax.ppermute(value, 'tp', pairs)  34.9 us
    ppermute x14, waiting for transfers between devices, send(): return lax.ppermute(value, 'tp', pairs)  25.9 us
    all_to_all x1, blocking collectives, exchange(): lax.all_to_all(blocks, 'tok', split_axis=0, concat_axis=0, tiled=True)  25.2 us
    all_to_all x1, waiting for transfers between devices, exchange(): lax.all_to_all(blocks, 'tok', split_axis=0, concat_axis=0, tiled=True)  19.7 us
    all_to_all x1, starting transfers between devices, exchange(): lax.all_to_all(blocks, 'tok', split_axis=0, concat_axis=0, tiled=True)  16.6 us
    pallas_call x1, Pallas kernels, pack(): pl.pallas_call(pack_kernel, grid_spec=pltpu.PrefetchScalarGridSpec(num_sc...  5.82 us
  transfers between devices with their start and end apart: 15, of which 9 were waited for; matrix products, arithmetic and copies ran while one was open for 1% of the time, Pallas kernels for 10%

profile of v11, /device:TPU:6, one launch (start us, length us, event | category | flops | bytes accessed | tf_op | source)
XLA Modules:
  0.0 144.5 jit_solution(16887500704484035562)
XLA Ops:
  0.0 2.5 %dispatch.1 = bf16[512,1024]{1,0:T(8,128)(2,1)} custom-call(s32[2,128]{1,0:T(2,128)} %bitcast.26, bf16[128,512]{1,0:T(8,128)(2,1)} %x_ref.1, bf16[128,512]{1,0:T(8,128)(2,1)} %g_ref.1), custom_call_target="tpu_custom_call" | custom-call | tf_op jit(solution)/shard_map/dispatch/pallas_call | solution.py:44
  2.5 16.6 %all-to-all-start = ((bf16[64,8,1024]{2,1,0:T(8,128)(2,1)}), bf16[64,8,1024]{2,1,0:T(8,128)(2,1)S(1)}, u32[]{:S(2)}, u32[]{:S(2)}) async-start(bf16[64,8,1024]{2,1,0:T(8,128)(2,1)} %bitcast.24), calls=%async_computation | async-start | bytes 2097152 | tf_op jit(solution)/shard_map/all_to_all | solution.py:273
  19.1 0.1 fusion.1
  19.2 0.6 pad_add_fusion.blocks_ref
  19.8 5.8 %pack.1 = (bf16[4,576,512]{2,1,0:T(8,128)(2,1)}, bf16[4,576,512]{2,1,0:T(8,128)(2,1)}) custom-call(s32[8]{0:T(128)} %pad_add_fusion.blocks_ref, bf16[192,4096]{1,0:T(8,128)(2,1)} %bitcast.18, bf16[192,4096]{1,0:T(8,128)(2,1)} %bitcast.20, bf16[192,4096]{1,0:T(8,128)(2,1)} %bitcast.22, bf16[192,4096]{1,0:T(8,128)(2,1)} %bitcast.19, ...), custom_call_target="tpu_custom_call" | custom-call | tf_op jit(solution)/shard_map/pack/pallas_call | solution.py:83
  25.6 1.9 %collective-permute-start.3 = (bf16[4,576,512]{2,1,0:T(8,128)(2,1)}, bf16[4,576,512]{2,1,0:T(8,128)(2,1)S(1)}, u32[]{:S(2)}, u32[]{:S(2)}) collective-permute-start(bf16[4,576,512]{2,1,0:T(8,128)(2,1)} %get-tuple-element.34), channel_id=1, source_target_pairs={{0,1},{1,0},{2,3},{3,2},{4,5},{5,4},{6,7},{7,6},{8,9},{9,8},{10,11... | collective-permute-start | bytes 7077896 | tf_op jit(solution)/shard_map/ppermute | solution.py:281
  27.5 1.7 %mixer.1 = (bf16[128,512]{1,0:T(8,128)(2,1)}, bf16[128,512]{1,0:T(8,128)(2,1)}) custom-call(s32[2,128]{1,0:T(2,128)} %bitcast.27, f32[2,128]{1,0:T(2,128)} %bitcast.28), custom_call_target="tpu_custom_call" | custom-call | tf_op jit(solution)/shard_map/mixer/pallas_call | solution.py:61
  29.2 19.7 %all-to-all-done = bf16[64,8,1024]{2,1,0:T(8,128)(2,1)S(1)} async-done(((bf16[64,8,1024]{2,1,0:T(8,128)(2,1)}), bf16[64,8,1024]{2,1,0:T(8,128)(2,1)S(1)}, u32[]{:S(2)}, u32[]{:S(2)}) %all-to-all-start) | async-done | bytes 1048608 | tf_op jit(solution)/shard_map/all_to_all | solution.py:273
  48.9 0.1 fusion.4
  49.0 2.4 %collective-permute-start.1 = (bf16[256,1024]{1,0:T(8,128)(2,1)S(1)}, bf16[256,1024]{1,0:T(8,128)(2,1)S(1)}, u32[]{:S(2)}, u32[]{:S(2)}) collective-permute-start(bf16[256,1024]{1,0:T(8,128)(2,1)S(1)} %get-tuple-element.42), channel_id=1, source_target_pairs={{0,2},{1,7},{2,4},{3,1},{4,6},{5,3},{6,0},{7,5},{8,10},{9,15},{10,... | collective-permute-start | bytes 1572872 | tf_op jit(solution)/shard_map/ppermute | solution.py:281
  51.4 3.4 %collective-permute-start.4 = (bf16[256,1024]{1,0:T(8,128)(2,1)S(1)}, bf16[256,1024]{1,0:T(8,128)(2,1)S(1)}, u32[]{:S(2)}, u32[]{:S(2)}) collective-permute-start(bf16[256,1024]{1,0:T(8,128)(2,1)S(1)} %get-tuple-element.41), channel_id=1, source_target_pairs={{0,2},{1,7},{2,4},{3,1},{4,6},{5,3},{6,0},{7,5},{8,10},{9,15},{10,... | collective-permute-start | bytes 1572872 | tf_op jit(solution)/shard_map/ppermute | solution.py:281
  54.8 1.9 %collective-permute-start = (bf16[256,1024]{1,0:T(8,128)(2,1)S(1)}, bf16[256,1024]{1,0:T(8,128)(2,1)S(1)}, u32[]{:S(2)}, u32[]{:S(2)}) collective-permute-start(bf16[256,1024]{1,0:T(8,128)(2,1)S(1)} %get-tuple-element.42), channel_id=1, source_target_pairs={{0,7},{1,2},{2,1},{3,4},{4,3},{5,6},{6,5},{7,0},{8,15},{9,10},{10,... | collective-permute-start | bytes 1572872 | tf_op jit(solution)/shard_map/ppermute | solution.py:281
  56.7 3.7 %collective-permute-done.1.same_low_ref = bf16[256,1024]{1,0:T(8,128)(2,1)S(1)} collective-permute-done((bf16[256,1024]{1,0:T(8,128)(2,1)S(1)}, bf16[256,1024]{1,0:T(8,128)(2,1)S(1)}, u32[]{:S(2)}, u32[]{:S(2)}) %collective-permute-start.1) | collective-permute-done | bytes 524320 | tf_op jit(solution)/shard_map/ppermute | solution.py:281
  60.4 3.3 %collective-permute-start.2 = (bf16[256,1024]{1,0:T(8,128)(2,1)S(1)}, bf16[256,1024]{1,0:T(8,128)(2,1)S(1)}, u32[]{:S(2)}, u32[]{:S(2)}) collective-permute-start(bf16[256,1024]{1,0:T(8,128)(2,1)S(1)} %collective-permute-done.1.same_low_ref), channel_id=1, source_target_pairs={{0,2},{1,7},{2,4},{3,1},{4,6},{5,3},{6,0},{7,5},{8,10},{9,15},{10,... | collective-permute-start | bytes 1572872 | tf_op jit(solution)/shard_map/ppermute | solution.py:281
  63.7 1.9 %collective-permute-start.6 = (bf16[256,1024]{1,0:T(8,128)(2,1)S(1)}, bf16[256,1024]{1,0:T(8,128)(2,1)S(1)}, u32[]{:S(2)}, u32[]{:S(2)}) collective-permute-start(bf16[256,1024]{1,0:T(8,128)(2,1)S(1)} %get-tuple-element.41), channel_id=1, source_target_pairs={{0,7},{1,2},{2,1},{3,4},{4,3},{5,6},{6,5},{7,0},{8,15},{9,10},{10,... | collective-permute-start | bytes 1572872 | tf_op jit(solution)/shard_map/ppermute | solution.py:281
  65.6 6.0 %collective-permute-done.4.same_high_ref = bf16[256,1024]{1,0:T(8,128)(2,1)S(1)} collective-permute-done((bf16[256,1024]{1,0:T(8,128)(2,1)S(1)}, bf16[256,1024]{1,0:T(8,128)(2,1)S(1)}, u32[]{:S(2)}, u32[]{:S(2)}) %collective-permute-start.4) | collective-permute-done | bytes 524320 | tf_op jit(solution)/shard_map/ppermute | solution.py:281
  71.6 2.6 %collective-permute-start.7 = (bf16[256,1024]{1,0:T(8,128)(2,1)S(1)}, bf16[256,1024]{1,0:T(8,128)(2,1)S(1)}, u32[]{:S(2)}, u32[]{:S(2)}) collective-permute-start(bf16[256,1024]{1,0:T(8,128)(2,1)S(1)} %collective-permute-done.4.same_high_ref), channel_id=1, source_target_pairs={{0,2},{1,7},{2,4},{3,1},{4,6},{5,3},{6,0},{7,5},{8,10},{9,15},{10,... | collective-permute-start | bytes 1572872 | tf_op jit(solution)/shard_map/ppermute | solution.py:281
  74.2 0.0 collective-permute-done.3.sib_ref
  74.2 0.0 copy-start
  74.2 1.7 %copy-done = bf16[4,576,512]{2,1,0:T(8,128)(2,1)S(1)} copy-done((bf16[4,576,512]{2,1,0:T(8,128)(2,1)S(1)}, bf16[4,576,512]{2,1,0:T(8,128)(2,1)}, u32[]{:S(2)}) %copy-start) | copy-done | bytes 2359320
  75.9 2.0 %first.1.sum_ref = f32[2,576,512]{2,1,0:T(8,128)S(1)} custom-call(bf16[512,1024]{1,0:T(8,128)(2,1)S(1)} %bitcast.16, bf16[256,1024]{1,0:T(8,128)(2,1)S(1)} %collective-permute-done.1.same_low_ref, bf16[256,1024]{1,0:T(8,128)(2,1)S(1)} %collective-permute-done.4.same_high_ref, bf16[4,576,512]{2,1,0:T(8,128)(2,1)S(1)} %copy-done, ...), custom_call_target="tpu_custom_call" | custom-call | tf_op jit(solution)/shard_map/first/pallas_call | solution.py:127
  77.9 0.0 collective-permute-done.other_ref
  77.9 4.6 %collective-permute-done.2.opposite_ref = bf16[256,1024]{1,0:T(8,128)(2,1)S(1)} collective-permute-done((bf16[256,1024]{1,0:T(8,128)(2,1)S(1)}, bf16[256,1024]{1,0:T(8,128)(2,1)S(1)}, u32[]{:S(2)}, u32[]{:S(2)}) %collective-permute-start.2) | collective-permute-done | bytes 524320 | tf_op jit(solution)/shard_map/ppermute | solution.py:281
  82.5 0.9 second.2.mine_ref
  83.4 1.9 %collective-permute-start.5 = (f32[2,576,256]{2,1,0:T(8,128)S(1)}, f32[2,576,256]{2,1,0:T(8,128)S(1)}, u32[]{:S(2)}, u32[]{:S(2)}) collective-permute-start(f32[2,576,256]{2,1,0:T(8,128)S(1)} %second.2.mine_ref), channel_id=1, source_target_pairs={{0,1},{1,0},{2,3},{3,2},{4,5},{5,4},{6,7},{7,6},{8,9},{9,8},{10,11... | collective-permute-start | bytes 3538952 | tf_op jit(solution)/shard_map/ppermute | solution.py:281
  85.4 0.0 collective-permute-done.6.other_ref
  85.4 2.8 %collective-permute-done.7.opposite_ref = bf16[256,1024]{1,0:T(8,128)(2,1)S(1)} collective-permute-done((bf16[256,1024]{1,0:T(8,128)(2,1)S(1)}, bf16[256,1024]{1,0:T(8,128)(2,1)S(1)}, u32[]{:S(2)}, u32[]{:S(2)}) %collective-permute-start.7) | collective-permute-done | bytes 524320 | tf_op jit(solution)/shard_map/ppermute | solution.py:281
  88.2 0.9 second.3.mine_ref
  89.0 1.9 %collective-permute-start.8 = (f32[2,576,256]{2,1,0:T(8,128)S(1)}, f32[2,576,256]{2,1,0:T(8,128)S(1)}, u32[]{:S(2)}, u32[]{:S(2)}) collective-permute-start(f32[2,576,256]{2,1,0:T(8,128)S(1)} %second.3.mine_ref), channel_id=1, source_target_pairs={{0,1},{1,0},{2,3},{3,2},{4,5},{5,4},{6,7},{7,6},{8,9},{9,8},{10,11... | collective-permute-start | bytes 3538952 | tf_op jit(solution)/shard_map/ppermute | solution.py:281
  91.0 0.0 collective-permute-done.5.theirs_ref
  91.0 0.9 grads.2
  91.8 2.7 %collective-permute-start.9 = (bf16[256,512]{1,0:T(8,128)(2,1)S(1)}, bf16[256,512]{1,0:T(8,128)(2,1)S(1)}, u32[]{:S(2)}, u32[]{:S(2)}) collective-permute-start(bf16[256,512]{1,0:T(8,128)(2,1)S(1)} %get-tuple-element.38), channel_id=1, source_target_pairs={{0,6},{1,3},{2,0},{3,5},{4,2},{5,7},{6,4},{7,1},{8,14},{9,11},{10,... | collective-permute-start | bytes 786440 | tf_op jit(solution)/shard_map/ppermute | solution.py:281
  94.6 0.0 collective-permute-done.8.theirs_ref
  94.6 0.9 grads.3
  95.5 2.4 %collective-permute-start.11 = (bf16[256,512]{1,0:T(8,128)(2,1)S(1)}, bf16[256,512]{1,0:T(8,128)(2,1)S(1)}, u32[]{:S(2)}, u32[]{:S(2)}) collective-permute-start(bf16[256,512]{1,0:T(8,128)(2,1)S(1)} %get-tuple-element.39), channel_id=1, source_target_pairs={{0,6},{1,3},{2,0},{3,5},{4,2},{5,7},{6,4},{7,1},{8,14},{9,11},{10,... | collective-permute-start | bytes 786440 | tf_op jit(solution)/shard_map/ppermute | solution.py:281
  97.9 3.8 %collective-permute-start.13 = (bf16[512,512]{1,0:T(8,128)(2,1)S(1)}, bf16[512,512]{1,0:T(8,128)(2,1)S(1)}, u32[]{:S(2)}, u32[]{:S(2)}) collective-permute-start(bf16[512,512]{1,0:T(8,128)(2,1)S(1)} %get-tuple-element.40), channel_id=1, source_target_pairs={{0,7},{1,2},{2,1},{3,4},{4,3},{5,6},{6,5},{7,0},{8,15},{9,10},{10,... | collective-permute-start | bytes 1572872 | tf_op jit(solution)/shard_map/ppermute | solution.py:281
  101.7 0.0 collective-permute-done.9.got_ref
  101.7 0.5 near.2
  102.2 2.2 %collective-permute-start.10 = (bf16[256,512]{1,0:T(8,128)(2,1)S(1)}, bf16[256,512]{1,0:T(8,128)(2,1)S(1)}, u32[]{:S(2)}, u32[]{:S(2)}) collective-permute-start(bf16[256,512]{1,0:T(8,128)(2,1)S(1)} %near.2), channel_id=1, source_target_pairs={{0,6},{1,3},{2,0},{3,5},{4,2},{5,7},{6,4},{7,1},{8,14},{9,11},{10,... | collective-permute-start | bytes 786440 | tf_op jit(solution)/shard_map/ppermute | solution.py:281
  104.5 0.5 collective-permute-done.11.got_ref
  104.9 0.5 near.3
  105.4 2.5 %collective-permute-start.12 = (bf16[256,512]{1,0:T(8,128)(2,1)S(1)}, bf16[256,512]{1,0:T(8,128)(2,1)S(1)}, u32[]{:S(2)}, u32[]{:S(2)}) collective-permute-start(bf16[256,512]{1,0:T(8,128)(2,1)S(1)} %near.3), channel_id=1, source_target_pairs={{0,6},{1,3},{2,0},{3,5},{4,2},{5,7},{6,4},{7,1},{8,14},{9,11},{10,... | collective-permute-start | bytes 786440 | tf_op jit(solution)/shard_map/ppermute | solution.py:281
  107.9 1.5 %collective-permute-done.13.refs_2_ = bf16[512,512]{1,0:T(8,128)(2,1)S(1)} collective-permute-done((bf16[512,512]{1,0:T(8,128)(2,1)S(1)}, bf16[512,512]{1,0:T(8,128)(2,1)S(1)}, u32[]{:S(2)}, u32[]{:S(2)}) %collective-permute-start.13) | collective-permute-done | bytes 524320 | tf_op jit(solution)/shard_map/ppermute | solution.py:281
  109.5 3.9 %collective-permute-done.10.refs_0_ = bf16[256,512]{1,0:T(8,128)(2,1)S(1)} collective-permute-done((bf16[256,512]{1,0:T(8,128)(2,1)S(1)}, bf16[256,512]{1,0:T(8,128)(2,1)S(1)}, u32[]{:S(2)}, u32[]{:S(2)}) %collective-permute-start.10) | collective-permute-done | bytes 262176 | tf_op jit(solution)/shard_map/ppermute | solution.py:281
  113.4 2.8 %collective-permute-done.12.refs_1_ = bf16[256,512]{1,0:T(8,128)(2,1)S(1)} collective-permute-done((bf16[256,512]{1,0:T(8,128)(2,1)S(1)}, bf16[256,512]{1,0:T(8,128)(2,1)S(1)}, u32[]{:S(2)}, u32[]{:S(2)}) %collective-permute-start.12) | collective-permute-done | bytes 262176 | tf_op jit(solution)/shard_map/ppermute | solution.py:281
  116.2 1.0 total.1
  117.1 25.2 %all_to_all.10 = bf16[64,8,512]{2,1,0:T(8,128)(2,1)} all-to-all(bf16[64,8,512]{2,1,0:T(8,128)(2,1)S(1)} %bitcast.17), channel_id=1, replica_groups=mesh['tok'=64,'tp'=8] {'tok'}, dimensions={0} | all-to-all | bytes 1048576 | tf_op jit(solution)/shard_map/all_to_all | solution.py:273
  142.3 2.1 %combine.1 = bf16[128,512]{1,0:T(8,128)(2,1)} custom-call(bf16[128,512]{1,0:T(8,128)(2,1)} %get-tuple-element.27.hi_ref, bf16[128,512]{1,0:T(8,128)(2,1)} %get-tuple-element.28.lo_ref, bf16[512,512]{1,0:T(8,128)(2,1)} %bitcast.25), custom_call_target="tpu_custom_call" | custom-call | tf_op jit(solution)/shard_map/combine/pallas_call | solution.py:264
Async XLA Ops:
  2.5 46.4 %all-to-all-start = ((bf16[64,8,1024]{2,1,0:T(8,128)(2,1)}), bf16[64,8,1024]{2,1,0:T(8,128)(2,1)S(1)}, u32[]{:S(2)}, u32[]{:S(2)}) async-start(bf16[64,8,1024]{2,1,0:T(8,128)(2,1)} %bitcast.24), calls=%async_computation | async-start | bytes 2097152 | tf_op jit(solution)/shard_map/all_to_all | solution.py:273
  25.6 48.6 %collective-permute-start.3 = (bf16[4,576,512]{2,1,0:T(8,128)(2,1)}, bf16[4,576,512]{2,1,0:T(8,128)(2,1)S(1)}, u32[]{:S(2)}, u32[]{:S(2)}) collective-permute-start(bf16[4,576,512]{2,1,0:T(8,128)(2,1)} %get-tuple-element.34), channel_id=1, source_target_pairs={{0,1},{1,0},{2,3},{3,2},{4,5},{5,4},{6,7},{7,6},{8,9},{9,8},{10,11... | collective-permute-start | bytes 7077896 | tf_op jit(solution)/shard_map/ppermute | solution.py:281
  49.0 11.4 %collective-permute-start.1 = (bf16[256,1024]{1,0:T(8,128)(2,1)S(1)}, bf16[256,1024]{1,0:T(8,128)(2,1)S(1)}, u32[]{:S(2)}, u32[]{:S(2)}) collective-permute-start(bf16[256,1024]{1,0:T(8,128)(2,1)S(1)} %get-tuple-element.42), channel_id=1, source_target_pairs={{0,2},{1,7},{2,4},{3,1},{4,6},{5,3},{6,0},{7,5},{8,10},{9,15},{10,... | collective-permute-start | bytes 1572872 | tf_op jit(solution)/shard_map/ppermute | solution.py:281
  51.4 20.2 %collective-permute-start.4 = (bf16[256,1024]{1,0:T(8,128)(2,1)S(1)}, bf16[256,1024]{1,0:T(8,128)(2,1)S(1)}, u32[]{:S(2)}, u32[]{:S(2)}) collective-permute-start(bf16[256,1024]{1,0:T(8,128)(2,1)S(1)} %get-tuple-element.41), channel_id=1, source_target_pairs={{0,2},{1,7},{2,4},{3,1},{4,6},{5,3},{6,0},{7,5},{8,10},{9,15},{10,... | collective-permute-start | bytes 1572872 | tf_op jit(solution)/shard_map/ppermute | solution.py:281
  54.8 23.1 %collective-permute-start = (bf16[256,1024]{1,0:T(8,128)(2,1)S(1)}, bf16[256,1024]{1,0:T(8,128)(2,1)S(1)}, u32[]{:S(2)}, u32[]{:S(2)}) collective-permute-start(bf16[256,1024]{1,0:T(8,128)(2,1)S(1)} %get-tuple-element.42), channel_id=1, source_target_pairs={{0,7},{1,2},{2,1},{3,4},{4,3},{5,6},{6,5},{7,0},{8,15},{9,10},{10,... | collective-permute-start | bytes 1572872 | tf_op jit(solution)/shard_map/ppermute | solution.py:281
  60.4 22.1 %collective-permute-start.2 = (bf16[256,1024]{1,0:T(8,128)(2,1)S(1)}, bf16[256,1024]{1,0:T(8,128)(2,1)S(1)}, u32[]{:S(2)}, u32[]{:S(2)}) collective-permute-start(bf16[256,1024]{1,0:T(8,128)(2,1)S(1)} %collective-permute-done.1.same_low_ref), channel_id=1, source_target_pairs={{0,2},{1,7},{2,4},{3,1},{4,6},{5,3},{6,0},{7,5},{8,10},{9,15},{10,... | collective-permute-start | bytes 1572872 | tf_op jit(solution)/shard_map/ppermute | solution.py:281
  63.7 21.7 %collective-permute-start.6 = (bf16[256,1024]{1,0:T(8,128)(2,1)S(1)}, bf16[256,1024]{1,0:T(8,128)(2,1)S(1)}, u32[]{:S(2)}, u32[]{:S(2)}) collective-permute-start(bf16[256,1024]{1,0:T(8,128)(2,1)S(1)} %get-tuple-element.41), channel_id=1, source_target_pairs={{0,7},{1,2},{2,1},{3,4},{4,3},{5,6},{6,5},{7,0},{8,15},{9,10},{10,... | collective-permute-start | bytes 1572872 | tf_op jit(solution)/shard_map/ppermute | solution.py:281
  71.6 16.5 %collective-permute-start.7 = (bf16[256,1024]{1,0:T(8,128)(2,1)S(1)}, bf16[256,1024]{1,0:T(8,128)(2,1)S(1)}, u32[]{:S(2)}, u32[]{:S(2)}) collective-permute-start(bf16[256,1024]{1,0:T(8,128)(2,1)S(1)} %collective-permute-done.4.same_high_ref), channel_id=1, source_target_pairs={{0,2},{1,7},{2,4},{3,1},{4,6},{5,3},{6,0},{7,5},{8,10},{9,15},{10,... | collective-permute-start | bytes 1572872 | tf_op jit(solution)/shard_map/ppermute | solution.py:281
  74.2 1.7 %copy-start = (bf16[4,576,512]{2,1,0:T(8,128)(2,1)S(1)}, bf16[4,576,512]{2,1,0:T(8,128)(2,1)}, u32[]{:S(2)}) copy-start(bf16[4,576,512]{2,1,0:T(8,128)(2,1)} %get-tuple-element.33.keep_ref) | copy-start | bytes 7077892
  83.4 7.5 %collective-permute-start.5 = (f32[2,576,256]{2,1,0:T(8,128)S(1)}, f32[2,576,256]{2,1,0:T(8,128)S(1)}, u32[]{:S(2)}, u32[]{:S(2)}) collective-permute-start(f32[2,576,256]{2,1,0:T(8,128)S(1)} %second.2.mine_ref), channel_id=1, source_target_pairs={{0,1},{1,0},{2,3},{3,2},{4,5},{5,4},{6,7},{7,6},{8,9},{9,8},{10,11... | collective-permute-start | bytes 3538952 | tf_op jit(solution)/shard_map/ppermute | solution.py:281
  89.0 5.5 %collective-permute-start.8 = (f32[2,576,256]{2,1,0:T(8,128)S(1)}, f32[2,576,256]{2,1,0:T(8,128)S(1)}, u32[]{:S(2)}, u32[]{:S(2)}) collective-permute-start(f32[2,576,256]{2,1,0:T(8,128)S(1)} %second.3.mine_ref), channel_id=1, source_target_pairs={{0,1},{1,0},{2,3},{3,2},{4,5},{5,4},{6,7},{7,6},{8,9},{9,8},{10,11... | collective-permute-start | bytes 3538952 | tf_op jit(solution)/shard_map/ppermute | solution.py:281
  91.8 9.9 %collective-permute-start.9 = (bf16[256,512]{1,0:T(8,128)(2,1)S(1)}, bf16[256,512]{1,0:T(8,128)(2,1)S(1)}, u32[]{:S(2)}, u32[]{:S(2)}) collective-permute-start(bf16[256,512]{1,0:T(8,128)(2,1)S(1)} %get-tuple-element.38), channel_id=1, source_target_pairs={{0,6},{1,3},{2,0},{3,5},{4,2},{5,7},{6,4},{7,1},{8,14},{9,11},{10,... | collective-permute-start | bytes 786440 | tf_op jit(solution)/shard_map/ppermute | solution.py:281
  95.5 9.5 %collective-permute-start.11 = (bf16[256,512]{1,0:T(8,128)(2,1)S(1)}, bf16[256,512]{1,0:T(8,128)(2,1)S(1)}, u32[]{:S(2)}, u32[]{:S(2)}) collective-permute-start(bf16[256,512]{1,0:T(8,128)(2,1)S(1)} %get-tuple-element.39), channel_id=1, source_target_pairs={{0,6},{1,3},{2,0},{3,5},{4,2},{5,7},{6,4},{7,1},{8,14},{9,11},{10,... | collective-permute-start | bytes 786440 | tf_op jit(solution)/shard_map/ppermute | solution.py:281
  97.9 11.6 %collective-permute-start.13 = (bf16[512,512]{1,0:T(8,128)(2,1)S(1)}, bf16[512,512]{1,0:T(8,128)(2,1)S(1)}, u32[]{:S(2)}, u32[]{:S(2)}) collective-permute-start(bf16[512,512]{1,0:T(8,128)(2,1)S(1)} %get-tuple-element.40), channel_id=1, source_target_pairs={{0,7},{1,2},{2,1},{3,4},{4,3},{5,6},{6,5},{7,0},{8,15},{9,10},{10,... | collective-permute-start | bytes 1572872 | tf_op jit(solution)/shard_map/ppermute | solution.py:281
  102.2 11.2 %collective-permute-start.10 = (bf16[256,512]{1,0:T(8,128)(2,1)S(1)}, bf16[256,512]{1,0:T(8,128)(2,1)S(1)}, u32[]{:S(2)}, u32[]{:S(2)}) collective-permute-start(bf16[256,512]{1,0:T(8,128)(2,1)S(1)} %near.2), channel_id=1, source_target_pairs={{0,6},{1,3},{2,0},{3,5},{4,2},{5,7},{6,4},{7,1},{8,14},{9,11},{10,... | collective-permute-start | bytes 786440 | tf_op jit(solution)/shard_map/ppermute | solution.py:281
  105.4 10.8 %collective-permute-start.12 = (bf16[256,512]{1,0:T(8,128)(2,1)S(1)}, bf16[256,512]{1,0:T(8,128)(2,1)S(1)}, u32[]{:S(2)}, u32[]{:S(2)}) collective-permute-start(bf16[256,512]{1,0:T(8,128)(2,1)S(1)} %near.3), channel_id=1, source_target_pairs={{0,6},{1,3},{2,0},{3,5},{4,2},{5,7},{6,4},{7,1},{8,14},{9,11},{10,... | collective-permute-start | bytes 786440 | tf_op jit(solution)/shard_map/ppermute | solution.py:281
